TPU v7x, 32 devices: a whole 2x2x4 slice. The times are simulated.
32 devices in a mesh: dp: 8 (over y, x, core), seq: 4 (over z).
Axes of the slice: x: 2, y: 2, z: 4, core: 2. Of those that a mesh axis runs over, the one named last changes fastest.
Arguments:
- tokens: bfloat16 [2, 8192, 1536], P(None, ('dp', 'seq')), may hold values from -6 to 6
- segment_ids: int32 [2, 8192], P(None, ('dp', 'seq')), may hold values from 0 to 31, never falling along the last dimension, each value on 1 to 1024 neighbouring positions
- out_grad: bfloat16 [2, 8192, 1536], P(None, ('dp', 'seq')), may hold values from -6 to 6
- w_q: bfloat16 [1536, 1536], P('dp'), may hold values from -0.15625 to 0.15625
- w_k: bfloat16 [1536, 1536], P('dp'), may hold values from -0.15625 to 0.15625
- w_v: bfloat16 [1536, 1536], P('dp'), may hold values from -0.15625 to 0.15625
- w_o: bfloat16 [1536, 1536], P('dp'), may hold values from -0.875 to 0.875
- w_gate: bfloat16 [1536, 4096], P('dp'), may hold values from -0.15625 to 0.15625
- w_up: bfloat16 [1536, 4096], P('dp'), may hold values from -0.15625 to 0.15625
- w_down: bfloat16 [4096, 1536], P('dp'), may hold values from -0.09375 to 0.09375
- gain_attn: bfloat16 [1536], P('dp'), may hold values from 0.5 to 1.5
- gain_ffn: bfloat16 [1536], P('dp'), may hold values from 0.5 to 1.5
Outputs:
- out: bfloat16 [2, 8192, 1536], P(None, ('dp', 'seq'))
- grad_tokens: float32 [2, 8192, 1536], P(None, ('dp', 'seq'))
- grad_w_q: float32 [1536, 1536], P('dp')
- grad_w_k: float32 [1536, 1536], P('dp')
- grad_w_v: float32 [1536, 1536], P('dp')
- grad_w_o: float32 [1536, 1536], P('dp')
- grad_w_gate: float32 [1536, 4096], P('dp')
- grad_w_up: float32 [1536, 4096], P('dp')
- grad_w_down: float32 [4096, 1536], P('dp')
- grad_gain_attn: float32 [1536], P('dp')
- grad_gain_ffn: float32 [1536], P('dp')
Inputs may be any that keep to these rules, and one draw needn't show every extreme that they name: `segment_ids`: along each micro-batch's 8192 tokens the ids never fall; a document holds 1 to 1024 tokens and may run on into the next sequence.
All inputs are finite; a program needn't handle non-finite values.
Results may differ from a plain program's by a relative error of at most 0.02.
Values may be sent and summed in bfloat16 or wider, within the bound.
A program may use at most 320 MiB of HBM per device.

v0:
```python
import math

import jax
import jax.numpy as jnp
from jax import lax
from jax.sharding import PartitionSpec as P

HEADS = 24
HD = 64


EPS = 1e-05


def positions_of(doc_row):
    count = doc_row.shape[0]
    place = jnp.arange(count, dtype=jnp.int32)
    before = jnp.concatenate([doc_row[:1], doc_row[:-1]])
    starts = (place == 0) | (doc_row != before)
    first_place = lax.cummax(jnp.where(starts, place, jnp.zeros_like(place)), axis=0)
    return place - first_place


def rope_tables(where_at, half):
    inverse = jnp.exp(jnp.arange(half, dtype=jnp.float32) * (-math.log(10000.0) / half))
    angle = where_at.astype(jnp.float32)[:, None] * inverse[None, :]
    return (jnp.cos(angle), jnp.sin(angle))


def rotate(values, cosine, sine):
    half = values.shape[-1] // 2
    first, second = (values[..., :half], values[..., half:])
    cos_heads, sin_heads = (cosine[:, None, :], sine[:, None, :])
    return jnp.concatenate(
        [first * cos_heads - second * sin_heads, second * cos_heads + first * sin_heads], axis=-1
    )


def rotate_back(grads, cosine, sine):
    half = grads.shape[-1] // 2
    first, second = (grads[..., :half], grads[..., half:])
    cos_heads, sin_heads = (cosine[:, None, :], sine[:, None, :])
    return jnp.concatenate(
        [first * cos_heads + second * sin_heads, second * cos_heads - first * sin_heads], axis=-1
    )


def rms_norm(values, gain):
    return values * lax.rsqrt(jnp.mean(values * values, axis=-1, keepdims=True) + EPS) * gain


def norm_backward(values, gain, grad_normed):
    scale = lax.rsqrt(jnp.mean(values * values, axis=-1, keepdims=True) + EPS)
    unit = values * scale
    grad_gain = jnp.sum(grad_normed * unit, axis=0)
    inner = grad_normed * gain
    grad_values = scale * (inner - unit * jnp.mean(inner * unit, axis=-1, keepdims=True))
    return (grad_gain, grad_values)


def block_scores(query_heads, key_heads, doc_row, start, block):
    length = doc_row.shape[0]
    place = jnp.arange(length, dtype=jnp.int32)
    query_block = lax.dynamic_slice_in_dim(query_heads, start, block, 0)
    doc_block = lax.dynamic_slice_in_dim(doc_row, start, block, 0)
    rows_block = start + jnp.arange(block, dtype=jnp.int32)
    allowed = (doc_block[:, None] == doc_row[None, :]) & (rows_block[:, None] >= place[None, :])
    scores = (
        jnp.einsum("qhd,khd->hqk", query_block, key_heads, preferred_element_type=jnp.float32)
        * 0.125
    )
    return (query_block, jnp.where(allowed[None], scores, -1e30))


def attention_forward(query, key, value, doc_row):
    length = query.shape[0]
    head_shape = (length, query.shape[1] // HD, HD)
    query_heads, key_heads, value_heads = (
        query.reshape(head_shape),
        key.reshape(head_shape),
        value.reshape(head_shape),
    )
    block = min(512, length)
    starts = jnp.arange(length // block, dtype=jnp.int32) * block

    def one_block(start):
        unused, scores = block_scores(query_heads, key_heads, doc_row, start, block)
        peak = jnp.max(scores, axis=-1, keepdims=True)
        expo = jnp.exp(scores - peak)
        total = jnp.sum(expo, axis=-1, keepdims=True)
        probs_low = (expo / total).astype(jnp.bfloat16)
        mixed = jnp.einsum(
            "hqk,khd->qhd", probs_low, value_heads, preferred_element_type=jnp.float32
        )
        return (mixed.astype(jnp.bfloat16), (peak + jnp.log(total))[..., 0])

    mixed, logsum = lax.map(one_block, starts)
    return (mixed.reshape(length, query.shape[1]), logsum)


def attention_backward(query, key, value, doc_row, logsum, grad_mixed, cosine, sine):
    length = query.shape[0]
    head_shape = (length, query.shape[1] // HD, HD)
    query_heads, key_heads, value_heads = (
        query.reshape(head_shape),
        key.reshape(head_shape),
        value.reshape(head_shape),
    )
    grad_heads = grad_mixed.reshape(head_shape)
    block = min(512, length)
    starts = jnp.arange(length // block, dtype=jnp.int32) * block

    def one_block(carry, item):
        grad_key, grad_value = carry
        start, logsum_block = item
        query_block, scores = block_scores(query_heads, key_heads, doc_row, start, block)
        probs = jnp.exp(scores - logsum_block[..., None])
        probs_low = probs.astype(jnp.bfloat16)
        grad_block = lax.dynamic_slice_in_dim(grad_heads, start, block, 0)
        grad_probs = jnp.einsum(
            "qhd,khd->hqk", grad_block, value_heads, preferred_element_type=jnp.float32
        )
        inner = jnp.sum(probs * grad_probs, axis=-1, keepdims=True)
        grad_scores = (probs * (grad_probs - inner)).astype(jnp.bfloat16)
        grad_query = (
            jnp.einsum("hqk,khd->qhd", grad_scores, key_heads, preferred_element_type=jnp.float32)
            * 0.125
        )
        grad_key = (
            grad_key
            + jnp.einsum(
                "hqk,qhd->khd", grad_scores, query_block, preferred_element_type=jnp.float32
            )
            * 0.125
        )
        grad_value = grad_value + jnp.einsum(
            "hqk,qhd->khd", probs_low, grad_block, preferred_element_type=jnp.float32
        )
        return ((grad_key, grad_value), grad_query)

    zeros_heads = jnp.zeros(head_shape, jnp.float32)
    (grad_key, grad_value), grad_query = lax.scan(
        one_block, (zeros_heads, zeros_heads), (starts, logsum)
    )
    grad_query = rotate_back(grad_query.reshape(head_shape), cosine, sine)
    grad_key = rotate_back(grad_key, cosine, sine)
    width_here = query.shape[1]
    return (
        grad_query.reshape(length, width_here).astype(jnp.bfloat16),
        grad_key.reshape(length, width_here).astype(jnp.bfloat16),
        grad_value.reshape(length, width_here).astype(jnp.bfloat16),
    )


def per_device(
    tokens, segment_ids, out_grad, w_q, w_k, w_v, w_o, w_gate, w_up, w_down, gain_attn, gain_ffn
):
    micro, rows, width = tokens.shape
    offset = lax.axis_index("seq") * rows
    shards = (w_q, w_k, w_v, w_o, w_gate, w_up, w_down, gain_attn, gain_ffn)
    gathered = (
        lax.all_gather(shards[0], "dp", axis=0, tiled=True),
        lax.all_gather(shards[1], "dp", axis=0, tiled=True),
        lax.all_gather(shards[2], "dp", axis=0, tiled=True),
        lax.all_gather(shards[3], "dp", axis=0, tiled=True),
        lax.all_gather(shards[4], "dp", axis=0, tiled=True),
        lax.all_gather(shards[5], "dp", axis=0, tiled=True),
        lax.all_gather(shards[6], "dp", axis=0, tiled=True),
        lax.all_gather(shards[7], "dp", axis=0, tiled=True),
        lax.all_gather(shards[8], "dp", axis=0, tiled=True),
    )
    docs = lax.all_gather(segment_ids, "seq", axis=1, tiled=True)
    full_q, full_k, full_v, full_o, full_gate, full_up, full_down, full_gain_a, full_gain_f = (
        gathered
    )
    gain_a = full_gain_a.astype(jnp.float32)
    gain_f = full_gain_f.astype(jnp.float32)
    row_heads = (rows, HEADS, HD)
    saved = []
    results = []
    for micro_index in range(micro):
        rows_in = tokens[micro_index].astype(jnp.float32)
        doc_row = docs[micro_index]
        cosine, sine = rope_tables(positions_of(doc_row), HD // 2)
        own_cos = lax.dynamic_slice_in_dim(cosine, offset, rows, 0)
        own_sin = lax.dynamic_slice_in_dim(sine, offset, rows, 0)
        normed = rms_norm(rows_in, gain_a).astype(jnp.bfloat16)
        query_rows = jnp.dot(normed, full_q, preferred_element_type=jnp.float32).reshape(row_heads)
        query_rows = rotate(query_rows, own_cos, own_sin).reshape(rows, width).astype(jnp.bfloat16)
        key_rows = jnp.dot(normed, full_k, preferred_element_type=jnp.float32).reshape(row_heads)
        key_rows = rotate(key_rows, own_cos, own_sin).reshape(rows, width).astype(jnp.bfloat16)
        value_rows = jnp.dot(normed, full_v, preferred_element_type=jnp.float32).astype(
            jnp.bfloat16
        )
        query, key, value = (
            lax.all_to_all(query_rows, "seq", split_axis=1, concat_axis=0, tiled=True),
            lax.all_to_all(key_rows, "seq", split_axis=1, concat_axis=0, tiled=True),
            lax.all_to_all(value_rows, "seq", split_axis=1, concat_axis=0, tiled=True),
        )
        mixed, logsum = attention_forward(query, key, value, doc_row)
        mixed_rows = lax.all_to_all(mixed, "seq", split_axis=0, concat_axis=1, tiled=True)
        middle = rows_in + jnp.dot(mixed_rows, full_o, preferred_element_type=jnp.float32)
        normed_ffn = rms_norm(middle, gain_f).astype(jnp.bfloat16)
        gate = jnp.dot(normed_ffn, full_gate, preferred_element_type=jnp.float32)
        up_value = jnp.dot(normed_ffn, full_up, preferred_element_type=jnp.float32)
        hidden = (jax.nn.silu(gate) * up_value).astype(jnp.bfloat16)
        result = middle + jnp.dot(hidden, full_down, preferred_element_type=jnp.float32)
        results.append(result.astype(jnp.bfloat16))
        saved.append(
            (
                rows_in,
                doc_row,
                cosine,
                sine,
                normed,
                query,
                key,
                value,
                logsum,
                mixed_rows,
                middle,
                normed_ffn,
                gate,
                up_value,
                hidden,
            )
        )
    back_weights = (
        lax.all_gather(shards[0], "dp", axis=0, tiled=True),
        lax.all_gather(shards[1], "dp", axis=0, tiled=True),
        lax.all_gather(shards[2], "dp", axis=0, tiled=True),
        lax.all_gather(shards[3], "dp", axis=0, tiled=True),
        lax.all_gather(shards[4], "dp", axis=0, tiled=True),
        lax.all_gather(shards[5], "dp", axis=0, tiled=True),
        lax.all_gather(shards[6], "dp", axis=0, tiled=True),
        lax.all_gather(shards[7], "dp", axis=0, tiled=True),
        lax.all_gather(shards[8], "dp", axis=0, tiled=True),
    )
    back_q, back_k, back_v, back_o, back_gate, back_up, back_down, back_gain_a, back_gain_f = (
        back_weights
    )
    gain_back_a = back_gain_a.astype(jnp.float32)
    gain_back_f = back_gain_f.astype(jnp.float32)
    totals = [jnp.zeros(weight.shape, jnp.float32) for weight in back_weights]
    grad_inputs = []
    for micro_index in range(micro):
        (
            rows_in,
            doc_row,
            cosine,
            sine,
            normed,
            query,
            key,
            value,
            logsum,
            mixed_rows,
            middle,
            normed_ffn,
            gate,
            up_value,
            hidden,
        ) = saved[micro_index]
        grad_out = out_grad[micro_index].astype(jnp.float32)
        grad_branch = grad_out.astype(jnp.bfloat16)
        totals[6] = totals[6] + jnp.einsum(
            "tf,td->fd", hidden, grad_branch, preferred_element_type=jnp.float32
        )
        grad_hidden = jnp.einsum(
            "td,fd->tf", grad_branch, back_down, preferred_element_type=jnp.float32
        )
        sigma = jax.nn.sigmoid(gate)
        grad_gate = (grad_hidden * up_value * sigma * (1.0 + gate * (1.0 - sigma))).astype(
            jnp.bfloat16
        )
        grad_up = (grad_hidden * jax.nn.silu(gate)).astype(jnp.bfloat16)
        totals[4] = totals[4] + jnp.einsum(
            "td,tf->df", normed_ffn, grad_gate, preferred_element_type=jnp.float32
        )
        totals[5] = totals[5] + jnp.einsum(
            "td,tf->df", normed_ffn, grad_up, preferred_element_type=jnp.float32
        )
        grad_normed_ffn = jnp.einsum(
            "tf,df->td", grad_gate, back_gate, preferred_element_type=jnp.float32
        )
        grad_normed_ffn = grad_normed_ffn + jnp.einsum(
            "tf,df->td", grad_up, back_up, preferred_element_type=jnp.float32
        )
        grad_gain_f, grad_middle = norm_backward(middle, gain_back_f, grad_normed_ffn)
        totals[8] = totals[8] + grad_gain_f
        grad_middle = grad_middle + grad_out
        grad_attn = grad_middle.astype(jnp.bfloat16)
        totals[3] = totals[3] + jnp.einsum(
            "ti,td->id", mixed_rows, grad_attn, preferred_element_type=jnp.float32
        )
        grad_mixed_rows = jnp.einsum(
            "td,id->ti", grad_attn, back_o, preferred_element_type=jnp.float32
        ).astype(jnp.bfloat16)
        grad_mixed = lax.all_to_all(grad_mixed_rows, "seq", split_axis=1, concat_axis=0, tiled=True)
        grad_query, grad_key, grad_value = attention_backward(
            query, key, value, doc_row, logsum, grad_mixed, cosine, sine
        )
        query_back, key_back, value_back = (
            lax.all_to_all(grad_query, "seq", split_axis=0, concat_axis=1, tiled=True),
            lax.all_to_all(grad_key, "seq", split_axis=0, concat_axis=1, tiled=True),
            lax.all_to_all(grad_value, "seq", split_axis=0, concat_axis=1, tiled=True),
        )
        totals[0] = totals[0] + jnp.einsum(
            "td,te->de", normed, query_back, preferred_element_type=jnp.float32
        )
        totals[1] = totals[1] + jnp.einsum(
            "td,te->de", normed, key_back, preferred_element_type=jnp.float32
        )
        totals[2] = totals[2] + jnp.einsum(
            "td,te->de", normed, value_back, preferred_element_type=jnp.float32
        )
        grad_normed = jnp.einsum(
            "te,de->td", query_back, back_q, preferred_element_type=jnp.float32
        )
        grad_normed = grad_normed + jnp.einsum(
            "te,de->td", key_back, back_k, preferred_element_type=jnp.float32
        )
        grad_normed = grad_normed + jnp.einsum(
            "te,de->td", value_back, back_v, preferred_element_type=jnp.float32
        )
        grad_gain_a, grad_rows = norm_backward(rows_in, gain_back_a, grad_normed)
        totals[7] = totals[7] + grad_gain_a
        grad_inputs.append(grad_rows + grad_middle)
    summed_all = (
        totals[0],
        totals[1],
        totals[2],
        totals[3],
        totals[4],
        totals[5],
        totals[6],
        totals[7],
        totals[8],
    )
    pieces = (
        lax.psum_scatter(
            summed_all[0].astype(jnp.bfloat16), "dp", scatter_dimension=0, tiled=True
        ).astype(jnp.float32),
        lax.psum_scatter(
            summed_all[1].astype(jnp.bfloat16), "dp", scatter_dimension=0, tiled=True
        ).astype(jnp.float32),
        lax.psum_scatter(
            summed_all[2].astype(jnp.bfloat16), "dp", scatter_dimension=0, tiled=True
        ).astype(jnp.float32),
        lax.psum_scatter(
            summed_all[3].astype(jnp.bfloat16), "dp", scatter_dimension=0, tiled=True
        ).astype(jnp.float32),
        lax.psum_scatter(
            summed_all[4].astype(jnp.bfloat16), "dp", scatter_dimension=0, tiled=True
        ).astype(jnp.float32),
        lax.psum_scatter(
            summed_all[5].astype(jnp.bfloat16), "dp", scatter_dimension=0, tiled=True
        ).astype(jnp.float32),
        lax.psum_scatter(
            summed_all[6].astype(jnp.bfloat16), "dp", scatter_dimension=0, tiled=True
        ).astype(jnp.float32),
        lax.psum_scatter(
            summed_all[7].astype(jnp.bfloat16), "dp", scatter_dimension=0, tiled=True
        ).astype(jnp.float32),
        lax.psum_scatter(
            summed_all[8].astype(jnp.bfloat16), "dp", scatter_dimension=0, tiled=True
        ).astype(jnp.float32),
    )
    pieces = (
        lax.psum(pieces[0].astype(jnp.bfloat16), "seq").astype(jnp.float32),
        lax.psum(pieces[1].astype(jnp.bfloat16), "seq").astype(jnp.float32),
        lax.psum(pieces[2].astype(jnp.bfloat16), "seq").astype(jnp.float32),
        lax.psum(pieces[3].astype(jnp.bfloat16), "seq").astype(jnp.float32),
        lax.psum(pieces[4].astype(jnp.bfloat16), "seq").astype(jnp.float32),
        lax.psum(pieces[5].astype(jnp.bfloat16), "seq").astype(jnp.float32),
        lax.psum(pieces[6].astype(jnp.bfloat16), "seq").astype(jnp.float32),
        lax.psum(pieces[7].astype(jnp.bfloat16), "seq").astype(jnp.float32),
        lax.psum(pieces[8].astype(jnp.bfloat16), "seq").astype(jnp.float32),
    )
    return (
        jnp.stack(results),
        jnp.stack(grad_inputs),
        pieces[0],
        pieces[1],
        pieces[2],
        pieces[3],
        pieces[4],
        pieces[5],
        pieces[6],
        pieces[7],
        pieces[8],
    )


def solution(mesh):
    placed = (
        P(None, ("dp", "seq"), None),
        P(None, ("dp", "seq")),
        P(None, ("dp", "seq"), None),
        P("dp", None),
        P("dp", None),
        P("dp", None),
        P("dp", None),
        P("dp", None),
        P("dp", None),
        P("dp", None),
        P("dp"),
        P("dp"),
    )
    return jax.shard_map(
        per_device,
        mesh=mesh,
        in_specs=placed,
        out_specs=(
            P(None, ("dp", "seq"), None),
            P(None, ("dp", "seq"), None),
            P("dp", None),
            P("dp", None),
            P("dp", None),
            P("dp", None),
            P("dp", None),
            P("dp", None),
            P("dp", None),
            P("dp"),
            P("dp"),
        ),
        check_vma=False,
    )
```

profile of v0, /device:TPU:0, one launch (start us, length us, event | category | flops | bytes accessed | tf_op | source)
XLA Modules:
  0.0 1494.6 jit_solution(15310913480453460365)
XLA Ops:
  13.0 16.3 %all-reduce.5 = (bf16[1536]{0:T(1024)(128)(2,1)S(1)}, bf16[1536]{0:T(1024)(128)(2,1)}) all-reduce(bf16[1536]{0:T(1024)(128)(2,1)S(1)} %dynamic-update-slice, bf16[1536]{0:T(1024)(128)(2,1)S(1)} %dynamic-update-slice.1), channel_id=1, replica_groups=mesh['dp'=8,'seq'=4] {'dp'}, use_global_device_ids=true, to_apply=%add | all-reduce | flops 3072 | bytes 12288
  29.3 12.1 all_gather.39
  51.6 6.6 copy.105
  58.3 34.2 %all-gather.8.cloned.1.call-done = bf16[1536,1536]{1,0:T(8,128)(2,1)} async-done(((bf16[192,1536]{1,0:T(8,128)(2,1)}), bf16[1536,1536]{1,0:T(8,128)(2,1)}) %all-gather.8.cloned.1.call-update) | async-done | bytes 4718608 | tf_op jit(solution)/shard_map/all_gather | solution.py:162
  92.5 6.6 copy.103
  111.9 19.6 %all-to-all-done.4 = bf16[256,4,384]{0,2,1:T(8,128)(2,1)S(1)} async-done(((bf16[256,4,384]{0,2,1:T(8,128)(2,1)}), bf16[256,4,384]{0,2,1:T(8,128)(2,1)S(1)}, u32[]{:S(2)}, u32[]{:S(2)}) %all-to-all-start.4) | async-done | bytes 786464 | tf_op jit(solution)/shard_map/all_to_all | solution.py:196
  140.4 14.3 all-to-all-done.5
  168.9 9.6 all-to-all-done.6
  184.7 17.6 %all-to-all-done = bf16[256,4,384]{0,2,1:T(8,128)(2,1)} async-done(((bf16[256,4,384]{0,2,1:T(8,128)(2,1)}), bf16[256,4,384]{0,2,1:T(8,128)(2,1)}, u32[]{:S(2)}, u32[]{:S(2)}) %all-to-all-start) | async-done | bytes 786464 | tf_op jit(solution)/shard_map/all_to_all | solution.py:196
  202.4 14.5 all-to-all-start.1
  221.7 14.6 all-to-all-done.1
  252.2 7.9 all-to-all-done.2
  265.1 33.5 %while.54 = (s32[]{:T(128)}, bf16[2,512,6,64]{1,3,2,0:T(8,128)(2,1)}, f32[2,6,512]{2,1,0:T(8,128)S(1)}, s32[2]{0:T(128)S(1)}, s32[1024]{0:T(1024)S(1)}, /*index=...) while((s32[]{:T(128)}, ...), condition=%wide.region_6.7_spmd, body=%wide.region_3.6_spmd.sunk | while | flops 844822016 | bytes 48630008 | solution.py:97
  312.2 33.6 %while.55 = (s32[]{:T(128)}, bf16[2,512,6,64]{1,3,2,0:T(8,128)(2,1)}, f32[2,6,512]{2,1,0:T(8,128)S(1)}, s32[2]{0:T(128)S(1)}, s32[1024]{0:T(1024)S(1)}, /*index=...) while((s32[]{:T(128)}, ...), condition=%wide.region_14.15_spmd, body=%wide.region_11.14_spmd.sunk | while | flops 844822016 | bytes 48630008 | solution.py:97
  365.5 14.2 all-to-all-done.7
  385.2 10.0 fusion.170
  395.2 9.6 fusion.171
  404.8 10.7 multiply_convert_fusion.4
  415.5 8.5 fusion.174
  424.1 11.2 multiply_reduce_fusion.3
  435.3 6.7 fusion.172
  442.0 9.6 fusion.173
  451.5 15.5 %multiply_convert_fusion.2 = (bf16[256,4096]{1,0:T(8,128)(2,1)}, bf16[256,4096]{1,0:T(8,128)(2,1)}, bf16[256,4096]{1,0:T(8,128)(2,1)}) fusion(f32[256,4096]{1,0:T(8,128)S(1)} %fusion.172, f32[256,4096]{1,0:T(8,128)} %fusion.173, bf16[4096,1536]{1,0:T(8,128)(2,1)} %all-gather.20.cloned.1.call-done, bf16[2,256,1536]{2,1,0:T(8,128)(2,1)S(1)} %copy-done.30), kind=kOutput, calls=%fused_computation.99 | convolution fusion | flops 3236954112 | bytes 28049408 | tf_op jit(solution)/shard_map/td,fd->tf/dot_general | solution.py:269
  467.1 7.7 fusion.176
  474.8 10.8 multiply_reduce_fusion.2
  500.2 15.0 %all-to-all-done.12 = bf16[256,4,384]{2,0,1:T(8,128)(2,1)} async-done(((bf16[256,4,384]{2,0,1:T(8,128)(2,1)}), bf16[256,4,384]{2,0,1:T(8,128)(2,1)}, u32[]{:S(2)}, u32[]{:S(2)}) %all-to-all-start.12) | async-done | bytes 786464 | tf_op jit(solution)/shard_map/all_to_all | solution.py:299
  528.8 10.2 all-to-all-done.8
  543.8 87.3 %while.56 = (s32[]{:T(128)}, f32[1024,6,64]{0,2,1:T(8,128)}, f32[1024,6,64]{0,2,1:T(8,128)}, f32[2,512,6,64]{1,0,3,2:T(2,128)}, s32[2]{0:T(128)S(1)}, /*index=5*...) while((s32[]{:T(128)}, f32[1024,6,64]{0,2,1:T(8,128)}, ...), condition=%wide.region_19.20_spmd.clone, body=%wide.region_17.19_spmd.clone.sunk | while | flops 2064184832 | bytes 245991888 | solution.py:142
  550.8 6.5 multiply_reduce_fusion.10
  569.5 6.4 bitcast_add_fusion.9
  578.8 7.3 dynamic_update_slice.37
  593.9 6.4 multiply_reduce_fusion.10
  612.9 6.6 bitcast_add_fusion.9
  622.3 7.3 dynamic_update_slice.37
  642.8 86.9 %while.57 = (s32[]{:T(128)}, f32[1024,6,64]{0,2,1:T(8,128)}, f32[1024,6,64]{0,2,1:T(8,128)}, f32[2,512,6,64]{1,0,3,2:T(2,128)}, s32[2]{0:T(128)S(1)}, /*index=5*...) while((s32[]{:T(128)}, f32[1024,6,64]{0,2,1:T(8,128)}, ...), condition=%wide.region_24.25_spmd.clone, body=%wide.region_22.24_spmd.clone.sunk | while | flops 2064184832 | bytes 245991888 | solution.py:142
  649.7 6.5 multiply_reduce_fusion.11
  668.3 6.1 bitcast_add_fusion.11
  677.3 7.3 dynamic_update_slice.38
  692.7 6.4 multiply_reduce_fusion.11
  711.6 6.6 bitcast_add_fusion.11
  721.1 7.3 dynamic_update_slice.38
  741.4 6.4 fusion.126
  747.8 12.4 all-to-all-done.13
  760.2 7.7 fusion.64
  778.8 14.9 all-to-all-done.10
  802.5 14.2 all-to-all-done.14
  816.8 7.8 fusion.65
  837.2 14.0 all-to-all-done.11
  860.0 14.3 all-to-all-done.15
  874.3 7.8 fusion.66
  883.2 13.4 fusion.178
  896.7 15.9 %add_convert_fusion.2 = bf16[1536,4096]{1,0:T(8,128)(2,1)} fusion(f32[1536,4096]{1,0:T(8,128)} %fusion.178, bf16[256,1536]{1,0:T(8,128)(2,1)S(1)} %copy-done.29, bf16[256,4096]{1,0:T(8,128)(2,1)} %get-tuple-element.486), kind=kOutput, calls=%fused_computation.90 | convolution fusion | flops 3233808384 | bytes 40632320 | tf_op jit(solution)/shard_map/td,tf->df/dot_general | solution.py:277
  912.7 12.0 fusion.179
  924.6 15.9 %add_convert_fusion.1 = bf16[1536,4096]{1,0:T(8,128)(2,1)} fusion(f32[1536,4096]{1,0:T(8,128)} %fusion.179, bf16[256,1536]{1,0:T(8,128)(2,1)S(1)} %copy-done.29, bf16[256,4096]{1,0:T(8,128)(2,1)} %get-tuple-element.485), kind=kOutput, calls=%fused_computation.89 | convolution fusion | flops 3233808384 | bytes 40632320 | tf_op jit(solution)/shard_map/td,tf->df/dot_general | solution.py:280
  942.0 16.6 %fusion.111 = f32[4096,1536]{1,0:T(8,128)} fusion(bf16[256,4096]{1,0:T(8,128)(2,1)} %get-tuple-element.484, bf16[2,256,1536]{2,1,0:T(8,128)(2,1)S(1)} %copy-done.32), kind=kOutput, calls=%fused_computation.190 | convolution fusion | flops 3221225472 | bytes 28049408 | tf_op jit(solution)/shard_map/tf,td->fd/dot_general | solution.py:266
  958.6 15.3 %add_convert_fusion = bf16[4096,1536]{1,0:T(8,128)(2,1)} fusion(f32[4096,1536]{1,0:T(8,128)} %fusion.111, bf16[256,4096]{1,0:T(8,128)(2,1)} %get-tuple-element.487, bf16[2,256,1536]{2,1,0:T(8,128)(2,1)S(1)} %copy-done.32), kind=kOutput, calls=%fused_computation.88 | convolution fusion | flops 3233808384 | bytes 40632320 | tf_op jit(solution)/shard_map/tf,td->fd/dot_general | solution.py:266
  974.7 56.1 %reduce-scatter.16.cloned.1.call-done = bf16[192,4096]{1,0:T(8,128)(2,1)} async-done(((bf16[1536,4096]{1,0:T(8,128)(2,1)}), bf16[192,4096]{1,0:T(8,128)(2,1)}) %reduce-scatter.16.cloned.1.call-update) | async-done | bytes 1572880 | tf_op jit(solution)/shard_map/reduce_scatter | solution.py:353
  1030.9 95.9 %reduce-scatter.18.cloned.1.call-done = bf16[192,4096]{1,0:T(8,128)(2,1)} async-done(((bf16[1536,4096]{1,0:T(8,128)(2,1)}), bf16[192,4096]{1,0:T(8,128)(2,1)}) %reduce-scatter.18.cloned.1.call-update) | async-done | bytes 1572880 | tf_op jit(solution)/shard_map/reduce_scatter | solution.py:356
  1126.8 95.8 %reduce-scatter.20.cloned.1.call-done = bf16[512,1536]{1,0:T(8,128)(2,1)} async-done(((bf16[4096,1536]{1,0:T(8,128)(2,1)}), bf16[512,1536]{1,0:T(8,128)(2,1)}) %reduce-scatter.20.cloned.1.call-update) | async-done | bytes 1572880 | tf_op jit(solution)/shard_map/reduce_scatter | solution.py:359
  1224.0 8.8 fusion.72
  1232.8 6.8 fusion.73
  1253.8 14.3 all-reduce.4
  1268.3 12.3 all-reduce.6
  1286.7 189.3 %all-reduce.10.cloned.1.call-done = (bf16[192,1536]{1,0:T(8,128)(2,1)}, bf16[192,1536]{1,0:T(8,128)(2,1)}, bf16[192,1536]{1,0:T(8,128)(2,1)}, bf16[192,1536]{1,0...) async-done(((bf16[192,1536]{1,0:T(8,128)(2,1)}, bf16[192,1536]{1,0:T(8,128)(2,1)}, bf16[192,1536]{1,0:T(8,128)(2,1)}, ...) | async-done | bytes 7077904 | tf_op jit(solution)/shard_map/psum | solution.py:370
  (526 shorter events, 399.1 us)
Async XLA Ops:
  7.2 44.5 %all-gather.10.cloned.1.call-start = ((), (), s32[]{:S(2)}) async-start(), calls=%async_computation.24 | async-start | bytes 5308416 | tf_op jit(solution)/shard_map/all_gather | solution.py:163
  7.9 84.6 %all-gather.8.cloned.1.call-start = ((), (), s32[]{:S(2)}) async-start(), calls=%async_computation.23 | async-start | bytes 5308416 | tf_op jit(solution)/shard_map/all_gather | solution.py:162
  8.7 20.6 %copy-start.92 = (s32[2,256]{1,0:T(2,128)S(1)}, s32[2,256]{1,0:T(2,128)}, u32[]{:S(2)}) copy-start(s32[2,256]{1,0:T(2,128)} %param.21) | copy-start | bytes 6148
  8.7 126.9 %all-gather.12.cloned.1.call-start = ((), (), s32[]{:S(2)}) async-start(), calls=%async_computation.25 | async-start | bytes 5308416 | tf_op jit(solution)/shard_map/all_gather | solution.py:164
  9.4 351.2 %all-gather.14.cloned.1.call-start = ((), (), s32[]{:S(2)}) async-start(), calls=%async_computation.26 | async-start | bytes 5308416 | tf_op jit(solution)/shard_map/all_gather | solution.py:165
  10.0 35.6 %copy-start.12 = (bf16[2,256,1536]{2,1,0:T(8,128)(2,1)S(1)}, bf16[2,256,1536]{2,1,0:T(8,128)(2,1)}, u32[]{:S(2)}) copy-start(bf16[2,256,1536]{2,1,0:T(8,128)(2,1)} %param.20) | copy-start | bytes 4718596
  10.0 375.2 %all-gather.16.cloned.1.call-start = ((), (), s32[]{:S(2)}) async-start(), calls=%async_computation.27 | async-start | bytes 14155776 | tf_op jit(solution)/shard_map/all_gather | solution.py:166
  10.6 384.6 %all-gather.18.cloned.1.call-start = ((), (), s32[]{:S(2)}) async-start(), calls=%async_computation.28 | async-start | bytes 14155776 | tf_op jit(solution)/shard_map/all_gather | solution.py:167
  29.3 187.6 %copy-start.77 = (f32[1536]{0:T(1024)}, f32[1536]{0:T(1024)S(1)}, u32[]{:S(2)}) copy-start(f32[1536]{0:T(1024)S(1)} %convert_element_type.287) | copy-start | bytes 18436
  41.9 16.3 %copy-start.63 = (s32[1,1024]{1,0:T(1,128)}, s32[1,1024]{1,0:T(1,128)S(1)}, u32[]{:S(2)}) copy-start(s32[1,1024]{1,0:T(1,128)S(1)} %get-tuple-element.895) | copy-start | bytes 12292
  45.6 12.7 copy-start.68
  45.6 12.7 copy-start.69
  45.6 89.4 %copy-start.70 = (f32[1024,32]{0,1:T(8,128)}, f32[1024,32]{0,1:T(8,128)S(1)}, u32[]{:S(2)}) copy-start(f32[1024,32]{0,1:T(8,128)S(1)} %get-tuple-element.523) | copy-start | bytes 393220
  45.6 89.4 %copy-start.72 = (f32[1024,32]{0,1:T(8,128)}, f32[1024,32]{0,1:T(8,128)S(1)}, u32[]{:S(2)}) copy-start(f32[1024,32]{0,1:T(8,128)S(1)} %get-tuple-element.524) | copy-start | bytes 393220
  46.0 89.6 %copy-start.87 = (f32[256]{0:T(256)}, f32[256]{0:T(256)S(1)}, u32[]{:S(2)}) copy-start(f32[256]{0:T(256)S(1)} %get-tuple-element.538) | copy-start | bytes 3076
  46.0 170.9 %copy-start.85 = (f32[256]{0:T(256)}, f32[256]{0:T(256)S(1)}, u32[]{:S(2)}) copy-start(f32[256]{0:T(256)S(1)} %get-tuple-element.539) | copy-start | bytes 3076
  106.4 25.1 %all-to-all-start.4 = ((bf16[256,4,384]{0,2,1:T(8,128)(2,1)}), bf16[256,4,384]{0,2,1:T(8,128)(2,1)S(1)}, u32[]{:S(2)}, u32[]{:S(2)}) async-start(bf16[256,4,384]{0,2,1:T(8,128)(2,1)} %bitcast.41), calls=%async_computation.4 | async-start | bytes 1572864 | tf_op jit(solution)/shard_map/all_to_all | solution.py:196
  131.5 23.2 %all-to-all-start.5 = ((bf16[256,4,384]{0,2,1:T(8,128)(2,1)}), bf16[256,4,384]{0,2,1:T(8,128)(2,1)S(1)}, u32[]{:S(2)}, u32[]{:S(2)}) async-start(bf16[256,4,384]{0,2,1:T(8,128)(2,1)} %bitcast.464), calls=%async_computation.5 | async-start | bytes 1572864 | tf_op jit(solution)/shard_map/all_to_all | solution.py:197
  154.6 23.8 %all-to-all-start.6 = ((bf16[256,4,384]{2,0,1:T(8,128)(2,1)}), bf16[256,4,384]{2,0,1:T(8,128)(2,1)}, u32[]{:S(2)}, u32[]{:S(2)}) async-start(bf16[256,4,384]{2,0,1:T(8,128)(2,1)} %bitcast.463), calls=%async_computation.6 | async-start | bytes 1572864 | tf_op jit(solution)/shard_map/all_to_all | solution.py:198
  178.5 23.9 %all-to-all-start = ((bf16[256,4,384]{0,2,1:T(8,128)(2,1)}), bf16[256,4,384]{0,2,1:T(8,128)(2,1)}, u32[]{:S(2)}, u32[]{:S(2)}) async-start(bf16[256,4,384]{0,2,1:T(8,128)(2,1)} %bitcast.465), calls=%async_computation | async-start | bytes 1572864 | tf_op jit(solution)/shard_map/all_to_all | solution.py:196
  202.4 33.9 %all-to-all-start.1 = ((bf16[256,4,384]{0,2,1:T(8,128)(2,1)}), bf16[256,4,384]{0,2,1:T(8,128)(2,1)}, u32[]{:S(2)}, u32[]{:S(2)}) async-start(bf16[256,4,384]{0,2,1:T(8,128)(2,1)} %bitcast.466), calls=%async_computation.1 | async-start | bytes 1572864 | tf_op jit(solution)/shard_map/all_to_all | solution.py:197
  236.3 23.9 %all-to-all-start.2 = ((bf16[256,4,384]{2,0,1:T(8,128)(2,1)}), bf16[256,4,384]{2,0,1:T(8,128)(2,1)}, u32[]{:S(2)}, u32[]{:S(2)}) async-start(bf16[256,4,384]{2,0,1:T(8,128)(2,1)} %bitcast.361), calls=%async_computation.2 | async-start | bytes 1572864 | tf_op jit(solution)/shard_map/all_to_all | solution.py:198
  240.5 164.3 %all-gather.20.cloned.1.call-start = ((), (), s32[]{:S(2)}) async-start(), calls=%async_computation.29 | async-start | bytes 14155776 | tf_op jit(solution)/shard_map/all_gather | solution.py:168
  298.6 9.1 copy-start.7
  298.6 9.1 copy-start.16
  298.6 9.1 copy-start.66
  307.7 47.4 %all-to-all-start.3 = ((bf16[4,256,384]{1,2,0:T(8,128)(2,1)}), bf16[4,256,384]{1,2,0:T(8,128)(2,1)S(1)}, u32[]{:S(2)}, u32[]{:S(2)}) async-start(bf16[4,256,384]{1,2,0:T(8,128)(2,1)} %copy.110), calls=%async_computation.3 | async-start | bytes 1572864 | tf_op jit(solution)/shard_map/all_to_all | solution.py:201
  345.8 9.3 copy-start.4
  349.5 11.0 copy-start.91
  349.6 11.1 copy-start.13
  355.1 10.4 copy-start.23
  355.1 24.6 %all-to-all-start.7 = ((bf16[4,256,384]{1,2,0:T(8,128)(2,1)}), bf16[4,256,384]{1,2,0:T(8,128)(2,1)S(1)}, u32[]{:S(2)}, u32[]{:S(2)}) async-start(bf16[4,256,384]{1,2,0:T(8,128)(2,1)} %copy.116), calls=%async_computation.7 | async-start | bytes 1572864 | tf_op jit(solution)/shard_map/all_to_all | solution.py:201
  385.2 10.0 copy-start.26
  395.2 9.6 copy-start.30
  467.1 21.8 %slice-start.4 = ((s8[4718592]{0:T(1024)(128)(4,1)}), s8[4194304]{0:T(1024)(128)(4,1)S(1)}, s32[]{:S(2)}) async-start(s8[4718592]{0:T(1024)(128)(4,1)} %bitcast.434), calls=%async_computation.42 | async-start | bytes 8388608
  474.8 10.8 copy-start.31
  474.8 14.1 slice-start.5
  488.8 30.6 %copy-start.20 = (f32[256,1536]{1,0:T(8,128)}, f32[256,1536]{1,0:T(8,128)S(1)}, u32[]{:S(2)}) copy-start(f32[256,1536]{1,0:T(8,128)S(1)} %get-tuple-element.506) | copy-start | bytes 4718596
  488.8 33.2 %copy-start.22 = (f32[256,1536]{1,0:T(8,128)}, f32[256,1536]{1,0:T(8,128)S(1)}, u32[]{:S(2)}) copy-start(f32[256,1536]{1,0:T(8,128)S(1)} %get-tuple-element.507) | copy-start | bytes 4718596
  491.3 23.9 %all-to-all-start.12 = ((bf16[256,4,384]{2,0,1:T(8,128)(2,1)}), bf16[256,4,384]{2,0,1:T(8,128)(2,1)}, u32[]{:S(2)}, u32[]{:S(2)}) async-start(bf16[256,4,384]{2,0,1:T(8,128)(2,1)} %bitcast.467), calls=%async_computation.12 | async-start | bytes 1572864 | tf_op jit(solution)/shard_map/all_to_all | solution.py:299
  515.2 23.9 %all-to-all-start.8 = ((bf16[256,4,384]{2,0,1:T(8,128)(2,1)}), bf16[256,4,384]{2,0,1:T(8,128)(2,1)}, u32[]{:S(2)}, u32[]{:S(2)}) async-start(bf16[256,4,384]{2,0,1:T(8,128)(2,1)} %bitcast.462), calls=%async_computation.8 | async-start | bytes 1572864 | tf_op jit(solution)/shard_map/all_to_all | solution.py:299
  519.4 455.3 %reduce-scatter.14.cloned.1.call-start = ((), (), s32[]{:S(2)}) async-start(), calls=%async_computation.33 | async-start | bytes 5308416 | tf_op jit(solution)/shard_map/reduce_scatter | solution.py:350
  562.3 13.6 slice-start
  605.4 14.1 slice-start
  637.0 99.4 %all-to-all-start.9 = ((bf16[4,256,384]{1,2,0:T(8,128)(2,1)}), bf16[4,256,384]{1,2,0:T(8,128)(2,1)}, u32[]{:S(2)}, u32[]{:S(2)}) async-start(bf16[4,256,384]{1,2,0:T(8,128)(2,1)} %copy.120), calls=%async_computation.9 | async-start | bytes 1572864 | tf_op jit(solution)/shard_map/all_to_all | solution.py:304
  661.3 13.2 slice-start.2
  704.1 14.1 slice-start.2
  736.3 23.8 %all-to-all-start.13 = ((bf16[4,256,384]{1,2,0:T(8,128)(2,1)}), bf16[4,256,384]{1,2,0:T(8,128)(2,1)S(1)}, u32[]{:S(2)}, u32[]{:S(2)}) async-start(bf16[4,256,384]{1,2,0:T(8,128)(2,1)} %copy.126), calls=%async_computation.13 | async-start | bytes 1572864 | tf_op jit(solution)/shard_map/all_to_all | solution.py:304
  741.4 233.3 %reduce-scatter.8.cloned.1.call-start = ((), (), s32[]{:S(2)}) async-start(), calls=%async_computation.30 | async-start | bytes 5308416 | tf_op jit(solution)/shard_map/reduce_scatter | solution.py:341
  741.4 18.8 %copy-start.88 = (f32[256]{0:T(256)S(1)}, f32[256]{0:T(256)}, u32[]{:S(2)}) copy-start(f32[256]{0:T(256)} %copy-done.87) | copy-start | bytes 3076
  770.6 23.1 %all-to-all-start.10 = ((bf16[4,256,384]{1,2,0:T(8,128)(2,1)}), bf16[4,256,384]{1,2,0:T(8,128)(2,1)S(1)}, u32[]{:S(2)}, u32[]{:S(2)}) async-start(bf16[4,256,384]{1,2,0:T(8,128)(2,1)} %copy.121), calls=%async_computation.10 | async-start | bytes 1572864 | tf_op jit(solution)/shard_map/all_to_all | solution.py:305
  793.7 8.8 copy-start.48
  793.7 23.1 %all-to-all-start.14 = ((bf16[4,256,384]{1,2,0:T(8,128)(2,1)}), bf16[4,256,384]{1,2,0:T(8,128)(2,1)S(1)}, u32[]{:S(2)}, u32[]{:S(2)}) async-start(bf16[4,256,384]{1,2,0:T(8,128)(2,1)} %copy.127), calls=%async_computation.14 | async-start | bytes 1572864 | tf_op jit(solution)/shard_map/all_to_all | solution.py:305
  797.2 177.5 %reduce-scatter.10.cloned.1.call-start = ((), (), s32[]{:S(2)}) async-start(), calls=%async_computation.31 | async-start | bytes 5308416 | tf_op jit(solution)/shard_map/reduce_scatter | solution.py:344
  827.7 23.5 %all-to-all-start.11 = ((bf16[4,256,384]{1,2,0:T(8,128)(2,1)}), bf16[4,256,384]{1,2,0:T(8,128)(2,1)S(1)}, u32[]{:S(2)}, u32[]{:S(2)}) async-start(bf16[4,256,384]{1,2,0:T(8,128)(2,1)} %copy.122), calls=%async_computation.11 | async-start | bytes 1572864 | tf_op jit(solution)/shard_map/all_to_all | solution.py:306
  851.2 23.1 %all-to-all-start.15 = ((bf16[4,256,384]{1,2,0:T(8,128)(2,1)}), bf16[4,256,384]{1,2,0:T(8,128)(2,1)S(1)}, u32[]{:S(2)}, u32[]{:S(2)}) async-start(bf16[4,256,384]{1,2,0:T(8,128)(2,1)} %copy.128), calls=%async_computation.15 | async-start | bytes 1572864 | tf_op jit(solution)/shard_map/all_to_all | solution.py:306
  854.7 120.1 %reduce-scatter.12.cloned.1.call-start = ((), (), s32[]{:S(2)}) async-start(), calls=%async_computation.32 | async-start | bytes 5308416 | tf_op jit(solution)/shard_map/reduce_scatter | solution.py:347
  882.1 14.5 copy-start.29
  882.1 148.7 %reduce-scatter.16.cloned.1.call-start = ((), (), s32[]{:S(2)}) async-start(), calls=%async_computation.34 | async-start | bytes 14155776 | tf_op jit(solution)/shard_map/reduce_scatter | solution.py:353
  912.6 214.2 %reduce-scatter.18.cloned.1.call-start = ((), (), s32[]{:S(2)}) async-start(), calls=%async_computation.35 | async-start | bytes 14155776 | tf_op jit(solution)/shard_map/reduce_scatter | solution.py:356
  940.6 282.0 %reduce-scatter.20.cloned.1.call-start = ((), (), s32[]{:S(2)}) async-start(), calls=%async_computation.36 | async-start | bytes 14155776 | tf_op jit(solution)/shard_map/reduce_scatter | solution.py:359
  973.9 502.1 %all-reduce.10.cloned.1.call-start = ((), (), s32[]{:S(2)}) async-start(), calls=%async_computation.37 | async-start | bytes 14155776 | tf_op jit(solution)/shard_map/psum | solution.py:370
  1224.0 16.9 %slice-start.8 = ((s8[4718592]{0:T(1024)(128)(4,1)}), s8[4194304]{0:T(1024)(128)(4,1)S(1)}, s32[]{:S(2)}) async-start(s8[4718592]{0:T(1024)(128)(4,1)} %bitcast.444), calls=%async_computation.46 | async-start | bytes 8388608
  1250.8 30.9 %copy-start.21 = (f32[256,1536]{1,0:T(8,128)S(1)}, f32[256,1536]{1,0:T(8,128)}, u32[]{:S(2)}) copy-start(f32[256,1536]{1,0:T(8,128)} %copy-done.20) | copy-start | bytes 4718596
  (93 other events, 403.2 us)
Sparse Core Ops, SparseCore 0:
  9.9 41.6 all-gather.9
  53.5 38.9 all-gather.7
  94.4 38.9 all-gather.11
  135.1 38.9 all-gather.13
  175.7 72.1 all-gather.15
  249.7 72.1 all-gather.17
  323.7 72.1 all-gather.19
  525.8 54.2 reduce-scatter.13
  768.0 52.0 reduce-scatter.7
  824.7 52.5 reduce-scatter.9
  882.3 52.7 reduce-scatter.11
  938.4 92.3 reduce-scatter.15
  1034.4 92.3 reduce-scatter.17
  1130.2 92.3 reduce-scatter.19
  1225.4 250.6 all-reduce.9
where the time goes:
time: 1510 us; the launch traced here: 1490 us
  waiting for transfers between devices  674 us (45%)
  matrix products  427 us (28%)
  local copies, waits for them, and re-layouts  142 us (9%)
  other arithmetic  86.6 us (6%)
  starting transfers between devices  76.6 us (5%)
  blocking collectives  55 us (4%)
  loops' own time  16.8 us (1%)
  between operations  16.8 us (1%)
    psum x1, waiting for transfers between devices, per_device(): lax.psum(pieces[0].astype(jnp.bfloat16), 'seq').astype(jnp.float32)  189 us
    reduce_scatter x1, waiting for transfers between devices, per_device(): lax.psum_scatter(summed_all[5].astype(jnp.bfloat16), 'dp', scatter_dimens...  95.9 us
    reduce_scatter x1, waiting for transfers between devices, per_device(): lax.psum_scatter(summed_all[6].astype(jnp.bfloat16), 'dp', scatter_dimens...  95.8 us
    reduce_scatter x1, waiting for transfers between devices, per_device(): lax.psum_scatter(summed_all[4].astype(jnp.bfloat16), 'dp', scatter_dimens...  56.1 us
    all_to_all x2, waiting for transfers between devices, per_device(): lax.all_to_all(query_rows, 'seq', split_axis=1, concat_axis=0, tiled=True)  37.2 us
    all_gather x1, waiting for transfers between devices, per_device(): lax.all_gather(shards[0], 'dp', axis=0, tiled=True)  34.2 us
    dynamic_update_slice x8, local copies, waits for them, and re-layouts, attention_backward(): lax.scan(one_block, (zeros_heads, zeros_heads), (starts, logsum))  32.3 us
    dot_general x2, matrix products, per_device(): jnp.einsum('tf,td->fd', hidden, grad_branch, preferred_element_type=jnp.f...  31.9 us
  transfers between devices with their start and end apart: 31, of which 20 were waited for; matrix products, arithmetic and copies ran while one was open for 35% of the time, Pallas kernels for 0%

commit v1 on v0

--- a/solution.py
+++ b/solution.py
@@ -3,6 +3,8 @@
 import jax
 import jax.numpy as jnp
 from jax import lax
+from jax.experimental import pallas as pl
+from jax.experimental.pallas import tpu as pltpu
 from jax.sharding import PartitionSpec as P
 
 HEADS = 24
@@ -392,6 +394,504 @@
     )
 
 
+BLK = 256
+LOG2E = 1.4426950408889634
+
+
+def swap_halves(v):
+    lane = lax.broadcasted_iota(jnp.int32, v.shape, 1)
+    width = v.shape[1]
+    up = pltpu.roll(v, width - 32, axis=1)
+    down = pltpu.roll(v, 32, axis=1)
+    return jnp.where(lane % 64 < 32, up, down)
+
+
+def nt(a, b):
+    return lax.dot_general(a, b, (((1,), (1,)), ((), ())), preferred_element_type=jnp.float32)
+
+
+def tn(a, b):
+    return lax.dot_general(a, b, (((0,), (0,)), ((), ())), preferred_element_type=jnp.float32)
+
+
+def attn_fwd_kernel(count_ref, q_ref, k_ref, v_ref, cos_ref, sin_ref, start_ref,
+                    qr_ref, kr_ref, vr_ref, mixed_ref, lse_ref):
+    pair = pl.program_id(0)
+    cosine, sine = cos_ref[...], sin_ref[...]
+    q = q_ref[...]
+    qr_ref[...] = (q * cosine + swap_halves(q) * sine).astype(jnp.bfloat16)
+    k = k_ref[...]
+    kr_ref[...] = (k * cosine + swap_halves(k) * sine).astype(jnp.bfloat16)
+    vr_ref[...] = v_ref[...].astype(jnp.bfloat16)
+    length = q_ref.shape[0]
+    lane = lax.broadcasted_iota(jnp.int32, (BLK, 128), 1)
+
+    def one_block(i, carry):
+        row0 = pl.multiple_of(i * BLK, BLK)
+        rows = pl.ds(row0, BLK)
+        for n in range(1, length // BLK + 1):
+            @pl.when(count_ref[i] == n)
+            def _():
+                width = n * BLK
+                key0 = pl.multiple_of((i - (n - 1)) * BLK, BLK)
+                keys = pl.ds(key0, width)
+                place = key0 + lax.broadcasted_iota(jnp.int32, (BLK, width), 1)
+                own = row0 + lax.broadcasted_iota(jnp.int32, (BLK, width), 0)
+                allowed = (place >= start_ref[rows, :]) & (place <= own)
+                for half in range(2):
+                    cols = slice(64 * half, 64 * half + 64)
+                    s = nt(qr_ref[rows, cols] * jnp.bfloat16(0.125), kr_ref[keys, cols])
+                    s = jnp.where(allowed, s, -1e30)
+                    peak = jnp.max(s, axis=-1, keepdims=True)
+                    expo = jnp.exp(s - peak)
+                    total = jnp.sum(expo, axis=-1, keepdims=True)
+                    out = jnp.dot(expo.astype(jnp.bfloat16), vr_ref[keys, cols],
+                                  preferred_element_type=jnp.float32)
+                    mixed_ref[rows, cols] = (out / total).astype(jnp.bfloat16)
+                    lse = peak + jnp.log(total)
+                    old = lse_ref[rows, :]
+                    lse_ref[rows, :] = jnp.where(lane == 2 * pair + half, lse, old)
+        return carry
+
+    lax.fori_loop(0, length // BLK, one_block, 0)
+
+
+def attn_fwd(qkv, cosine, sine, start, counts):
+    length, width = qkv.shape[0], qkv.shape[1] // 3
+    pairs = width // 128
+    col = pl.BlockSpec((length, 128), lambda p, c: (0, p))
+    key_col = pl.BlockSpec((length, 128), lambda p, c: (0, pairs + p))
+    value_col = pl.BlockSpec((length, 128), lambda p, c: (0, 2 * pairs + p))
+    fixed = pl.BlockSpec((length, 128), lambda p, c: (0, 0))
+    scol = pl.BlockSpec((length, 1), lambda p, c: (0, 0))
+    low = jax.ShapeDtypeStruct((length, width), jnp.bfloat16)
+    return pl.pallas_call(
+        attn_fwd_kernel,
+        grid_spec=pltpu.PrefetchScalarGridSpec(
+            num_scalar_prefetch=1, grid=(pairs,),
+            in_specs=[col, key_col, value_col, fixed, fixed, scol],
+            out_specs=[col, col, col, col, fixed],
+        ),
+        out_shape=[low, low, low, low, jax.ShapeDtypeStruct((length, 128), jnp.float32)],
+        compiler_params=pltpu.CompilerParams(vmem_limit_bytes=40 * 1024 * 1024),
+        cost_estimate=pl.CostEstimate(flops=8 * length * length * width // 2, bytes_accessed=20 * length * width,
+                                      transcendentals=length * length * pairs),
+        name="attn_fwd",
+    )(counts, qkv, qkv, qkv, cosine, sine, start)
+
+
+def attn_bwd_kernel(count_ref, q_ref, k_ref, v_ref, do_ref, cos_ref, sin_ref, start_ref, lse_ref,
+                    dq_ref, dk_ref, dv_ref, dk_acc, dv_acc, dq_acc):
+    length = q_ref.shape[0]
+    dk_acc[...] = jnp.zeros_like(dk_acc)
+    dv_acc[...] = jnp.zeros_like(dv_acc)
+
+    def one_block(i, carry):
+        row0 = pl.multiple_of(i * BLK, BLK)
+        rows = pl.ds(row0, BLK)
+        for n in range(1, length // BLK + 1):
+            @pl.when(count_ref[i] == n)
+            def _():
+                width = n * BLK
+                key0 = pl.multiple_of((i - (n - 1)) * BLK, BLK)
+                keys = pl.ds(key0, width)
+                place = key0 + lax.broadcasted_iota(jnp.int32, (width, BLK), 0)
+                own = row0 + lax.broadcasted_iota(jnp.int32, (width, BLK), 1)
+                allowed = (place >= start_ref[:, rows]) & (place <= own)
+                for half in range(2):
+                    cols = slice(64 * half, 64 * half + 64)
+                    q = q_ref[rows, cols] * jnp.bfloat16(0.125)
+                    k = k_ref[keys, cols]
+                    do = do_ref[rows, cols]
+                    s = nt(k, q)
+                    probs = jnp.where(allowed, jnp.exp(s - lse_ref[0, half:half + 1, rows]), 0.0)
+                    gp = nt(v_ref[keys, cols], do)
+                    inner = jnp.sum(probs * gp, axis=0, keepdims=True)
+                    gs = (probs * (gp - inner)).astype(jnp.bfloat16)
+                    dv_acc[keys, cols] += jnp.dot(probs.astype(jnp.bfloat16), do,
+                                                  preferred_element_type=jnp.float32)
+                    dk_acc[keys, cols] += jnp.dot(gs, q, preferred_element_type=jnp.float32)
+                    dq_acc[rows, cols] = tn(gs, k) * 0.125
+        return carry
+
+    lax.fori_loop(0, length // BLK, one_block, 0)
+    cosine, sine = cos_ref[...], sin_ref[...]
+    g = dq_acc[...]
+    dq_ref[...] = (g * cosine - swap_halves(g) * sine).astype(jnp.bfloat16)
+    g = dk_acc[...]
+    dk_ref[...] = (g * cosine - swap_halves(g) * sine).astype(jnp.bfloat16)
+    dv_ref[...] = dv_acc[...].astype(jnp.bfloat16)
+
+
+def attn_bwd(q, k, v, grad, cosine, sine, start_row, counts, lse):
+    length, width = q.shape
+    pairs = width // 128
+    col = pl.BlockSpec((length, 128), lambda p, c: (0, p))
+    fixed = pl.BlockSpec((length, 128), lambda p, c: (0, 0))
+    srow = pl.BlockSpec((1, length), lambda p, c: (0, 0))
+    lrow = pl.BlockSpec((1, 2, length), lambda p, c: (p, 0, 0))
+    low = jax.ShapeDtypeStruct((length, width), jnp.bfloat16)
+    return pl.pallas_call(
+        attn_bwd_kernel,
+        grid_spec=pltpu.PrefetchScalarGridSpec(
+            num_scalar_prefetch=1, grid=(pairs,),
+            in_specs=[col, col, col, col, fixed, fixed, srow, lrow],
+            out_specs=[col, col, col],
+            scratch_shapes=[pltpu.VMEM((length, 128), jnp.float32)] * 3,
+        ),
+        out_shape=[low, low, low],
+        compiler_params=pltpu.CompilerParams(vmem_limit_bytes=40 * 1024 * 1024),
+        cost_estimate=pl.CostEstimate(flops=20 * length * length * width // 2, bytes_accessed=14 * length * width,
+                                      transcendentals=length * length * pairs),
+        name="attn_bwd",
+    )(counts, q, k, v, grad, cosine, sine, start_row, lse)
+
+
+FAST_MESH = {"dp": 8, "seq": 4}
+CORE, ALONG_X, ALONG_Y = 1, 2, 4
+
+
+def swap(value, bit):
+    return lax.ppermute(value, "dp", [(i, i ^ bit) for i in range(8)])
+
+
+def after(value, *others):
+    return lax.optimization_barrier((value,) + others)[0]
+
+
+def ordered(own, other, core):
+    first = core == 0
+    return jnp.where(first, own, other), jnp.where(first, other, own)
+
+
+def reshard_pairs(turn, back):
+    pairs = []
+    for d in range(8):
+        for z in range(4):
+            target = ((d & 6) | (z >> 1)) * 4 + 2 * ((turn + z) % 2) + (d & 1)
+            pairs.append((target, d * 4 + z) if back else (d * 4 + z, target))
+    return pairs
+
+
+def to_sequence(blocks, seq_at):
+    got = []
+    for turn in range(2):
+        block = lax.dynamic_index_in_dim(blocks, (turn + seq_at) & 1, 0, keepdims=False)
+        got.append(lax.ppermute(block, ("dp", "seq"), reshard_pairs(turn, False)))
+    early = seq_at < 2
+    return jnp.concatenate(
+        [jnp.where(early, got[0], got[1]), jnp.where(early, got[1], got[0])], axis=0
+    )
+
+
+def from_sequence(half, seq_at):
+    rows = half.shape[0] // 2
+    early = seq_at < 2
+    got = []
+    for turn in range(2):
+        block = jnp.where(
+            early, half[rows * turn : rows * (turn + 1)], half[rows * (1 - turn) : rows * (2 - turn)]
+        )
+        got.append(lax.ppermute(block, ("dp", "seq"), reshard_pairs(turn, True)))
+    even = (seq_at & 1) == 0
+    return jnp.stack([jnp.where(even, got[0], got[1]), jnp.where(even, got[1], got[0])])
+
+
+def whole(half, core):
+    return jnp.concatenate(ordered(half, swap(half, CORE), core), axis=0)
+
+
+def relative_blocks(values, chip, axis):
+    size = values.shape[axis] // 4
+    return [lax.dynamic_slice_in_dim(values, size * (chip ^ k), size, axis) for k in range(4)]
+
+
+def relative(values, chip):
+    return jnp.concatenate(relative_blocks(values, chip, values.ndim - 1), axis=-1)
+
+
+def gather_start(piece_x, piece_y):
+    pieces = (piece_x, piece_y)
+    return (
+        pieces,
+        [swap(piece, ALONG_X) for piece in pieces],
+        [swap(piece, ALONG_Y) for piece in pieces],
+    )
+
+
+def gather_relay(started):
+    pieces, over_x, over_y = started
+    corner = [swap(over_x[0], ALONG_Y), swap(over_y[1], ALONG_X)]
+    return [[pieces[k], over_x[k], over_y[k], corner[k]] for k in range(2)]
+
+
+def dot(a, b):
+    return jnp.dot(a, b, preferred_element_type=jnp.float32)
+
+
+def low(value):
+    return value.astype(jnp.bfloat16)
+
+
+def wide(value):
+    return value.astype(jnp.float32)
+
+
+def scatter_first(send, bit):
+    return swap(low(send), bit)
+
+
+def scatter_second(keep, got, bit):
+    both = low(wide(keep) + wide(got))
+    rows = both.shape[0] // 2
+    return both[:rows], swap(both[rows:], bit)
+
+
+def sum_over_seq(value, seq_at):
+    one = low(wide(value) + wide(lax.ppermute(value, "seq", [(0, 1), (3, 2)])))
+    two = low(wide(one) + wide(lax.ppermute(one, "seq", [(1, 2), (2, 1)])))
+    ends = lax.ppermute(two, "seq", [(1, 0), (2, 3)])
+    return jnp.where((seq_at == 1) | (seq_at == 2), two, ends)
+
+
+def both_cores(reduced, core, blocks):
+    rows = reduced.shape[0] // 2
+    own = lax.dynamic_slice_in_dim(reduced, rows * core, rows, 0)
+    other = swap(lax.dynamic_slice_in_dim(reduced, rows * (1 - core), rows, 0), CORE)
+    width = reduced.shape[1]
+    shape = (rows, blocks, 1, width // blocks)
+    even, odd = ordered(own, other, core)
+    return wide(
+        jnp.concatenate([even.reshape(shape), odd.reshape(shape)], axis=2).reshape(rows, 2 * width)
+    )
+
+
+def column_device(
+    tokens, segment_ids, out_grad, w_q, w_k, w_v, w_o, w_gate, w_up, w_down, gain_attn, gain_ffn
+):
+    dp_at, seq_at = lax.axis_index("dp"), lax.axis_index("seq")
+    core, chip = dp_at & 1, dp_at >> 1
+    rows, width = tokens.shape[1], tokens.shape[2]
+    own_width = width // 2
+
+    def own_columns(weight, which):
+        parts = weight.reshape(weight.shape[0], 4, 2, weight.shape[1] // 8)
+        return lax.dynamic_index_in_dim(parts, which, 2, keepdims=False).reshape(
+            weight.shape[0], weight.shape[1] // 2
+        )
+
+    def chip_rows(weights):
+        own = jnp.concatenate([own_columns(weight, core) for weight in weights], axis=1)
+        other = jnp.concatenate([own_columns(weight, 1 - core) for weight in weights], axis=1)
+        return jnp.concatenate(ordered(own, swap(other, CORE), core), axis=0)
+
+    qkv = chip_rows((w_q, w_k, w_v))
+    third = own_width
+    qkv_x = jnp.concatenate([qkv[:, :third], qkv[:, 2 * third : 2 * third + third // 2]], axis=1)
+    qkv_y = jnp.concatenate(
+        [qkv[:, third : 2 * third], qkv[:, 2 * third + third // 2 :]], axis=1
+    )
+    gate_up = chip_rows((w_gate, w_up))
+    half_ff = gate_up.shape[1] // 2
+
+    gains = jnp.stack([gain_attn, gain_ffn])[None]
+    gains = jnp.concatenate(ordered(gains, swap(gains, CORE), core), axis=0)
+    gains = jnp.concatenate(ordered(gains, swap(gains, ALONG_X), chip & 1), axis=0)
+    gains = jnp.concatenate(ordered(gains, swap(gains, ALONG_Y), chip >> 1), axis=0)
+    gains = wide(gains.transpose(1, 0, 2).reshape(2, width))
+    gain_a, gain_f = gains[0], gains[1]
+
+    x_half = to_sequence(tokens, seq_at)
+    qkv_started = gather_start(qkv_x, qkv_y)
+    docs = to_sequence(segment_ids.reshape(2, 2, rows // 2), seq_at)
+    docs = whole(docs, core).reshape(4 * rows)
+    x_low = whole(x_half, core)
+    length = 4 * rows
+
+    qkv_pieces = gather_relay(qkv_started)
+    o_started = gather_start(
+        after(w_o[: w_o.shape[0] // 2], qkv_started[1][0], qkv_started[1][1]),
+        after(w_o[w_o.shape[0] // 2 :], qkv_started[2][0], qkv_started[2][1]),
+    )
+    o_pieces = gather_relay(o_started)
+    ff_started = gather_start(
+        after(gate_up[:, :half_ff], o_started[1][0], o_started[1][1], qkv_pieces[1][3]),
+        after(gate_up[:, half_ff:], o_started[2][0], o_started[2][1], qkv_pieces[0][3]),
+    )
+    ff_pieces = gather_relay(ff_started)
+    down_started = gather_start(
+        after(w_down[: w_down.shape[0] // 2], ff_started[1][0], ff_started[1][1]),
+        after(w_down[w_down.shape[0] // 2 :], ff_started[2][0], ff_started[2][1]),
+    )
+    down_pieces = gather_relay(down_started)
+    g_half = to_sequence(after(out_grad, x_half), seq_at)
+    grad_branch = whole(g_half, core)
+
+    full_qkv = jnp.concatenate(
+        [
+            jnp.concatenate(
+                [a[:, :third], b[:, :third], a[:, third:], b[:, third:]], axis=1
+            )
+            for a, b in zip(*qkv_pieces)
+        ],
+        axis=0,
+    )
+    full_gate = jnp.concatenate(ff_pieces[0], axis=0)
+    full_up = jnp.concatenate(ff_pieces[1], axis=0)
+
+    def in_chip_order(pieces):
+        rows_each = pieces[0][0].shape[0]
+        full = jnp.zeros((8 * rows_each, pieces[0][0].shape[1]), jnp.bfloat16)
+        for k in range(4):
+            for part in range(2):
+                full = lax.dynamic_update_slice_in_dim(
+                    full, pieces[part][k], rows_each * (2 * (chip ^ k) + part), 0
+                )
+        return full
+
+    full_o = in_chip_order(o_pieces)
+    full_down = in_chip_order(down_pieces)
+
+    place = jnp.arange(length, dtype=jnp.int32)
+    before = jnp.concatenate([docs[:1], docs[:-1]])
+    begins = (place == 0) | (docs != before)
+    start = lax.cummax(jnp.where(begins, place, jnp.zeros_like(place)), axis=0)
+    counts = place[: length // BLK] - start[::BLK] // BLK + 1
+    cosine, sine = rope_tables(place - start, HD // 2)
+    cosine = jnp.concatenate([cosine] * 4, axis=1)
+    sine = jnp.concatenate([-sine, sine, -sine, sine], axis=1)
+
+    x = wide(x_low)
+    normed = low(relative(rms_norm(x, gain_a), chip))
+    qkv_rows = dot(normed, full_qkv)
+    query, key, value, mixed, logsum = attn_fwd(qkv_rows, cosine, sine, start[:, None], counts)
+    logsum = logsum[:, : own_width // HD].T.reshape(own_width // 128, 2, length)
+    part = dot(mixed, full_o)
+    middle = x + part + wide(swap(low(part), CORE))
+    normed_ffn = low(relative(rms_norm(middle, gain_f), chip))
+    gate = dot(normed_ffn, full_gate)
+    up_value = dot(normed_ffn, full_up)
+    hidden = low(jax.nn.silu(gate) * up_value)
+    half_rows = length // 2
+
+    def of_core(values, which):
+        return lax.dynamic_slice_in_dim(values, half_rows * which, half_rows, 0)
+
+    out_other = swap(low(dot(of_core(hidden, 1 - core), full_down)), CORE)
+    result = of_core(middle, core) + dot(of_core(hidden, core), full_down) + wide(out_other)
+    result = from_sequence(low(result), seq_at)
+
+    def split_rows(blocks):
+        return (
+            jnp.concatenate([blocks[1], blocks[3]], axis=-1),
+            jnp.concatenate([blocks[0], blocks[2]], axis=-1),
+            jnp.concatenate([blocks[2], blocks[3]], axis=-1),
+            jnp.concatenate([blocks[0], blocks[1]], axis=-1),
+        )
+
+    def weight_grads(blocks, grad_x, grad_y):
+        send_x, keep_x, send_y, keep_y = split_rows(blocks)
+        got_x = scatter_first(tn(send_x, grad_x), ALONG_X)
+        got_y = scatter_first(tn(send_y, grad_y), ALONG_Y)
+        kept_x, last_x = scatter_second(tn(keep_x, grad_x), got_x, ALONG_Y)
+        kept_y, last_y = scatter_second(tn(keep_y, grad_y), got_y, ALONG_X)
+        return (
+            sum_over_seq(low(wide(kept_x) + wide(last_x)), seq_at),
+            sum_over_seq(low(wide(kept_y) + wide(last_y)), seq_at),
+        )
+
+    def static_blocks(values):
+        return jnp.split(values, 4, axis=1)
+
+    hidden_blocks = relative_blocks(hidden, chip, 1)
+    down_x, down_y = weight_grads(
+        hidden_blocks, grad_branch[:, :own_width], grad_branch[:, own_width:]
+    )
+    grad_hidden = nt(grad_branch, full_down)
+    sigma = jax.nn.sigmoid(gate)
+    grad_gate = low(grad_hidden * up_value * sigma * (1.0 + gate * (1.0 - sigma)))
+    grad_up = low(grad_hidden * (gate * sigma))
+    grad_nf = nt(grad_gate, full_gate) + nt(grad_up, full_up)
+    grad_nf_other = swap(low(grad_nf), CORE)
+    sum_gate, sum_up = weight_grads(static_blocks(normed_ffn), grad_gate, grad_up)
+    grad_nf = relative(grad_nf + wide(grad_nf_other), chip)
+    grad_gain_f, grad_middle = norm_backward(middle, gain_f, grad_nf)
+    grad_middle = grad_middle + wide(grad_branch)
+    grad_attn = low(grad_middle)
+
+    grad_mixed = low(nt(grad_attn, full_o))
+    grad_o = low(tn(mixed, grad_attn))
+    o_blocks = relative_blocks(grad_o, chip, 0)
+
+    def o_half(order, columns):
+        return jnp.concatenate([o_blocks[k][:, columns] for k in order], axis=0)
+
+    left, right = slice(0, own_width), slice(own_width, width)
+    kept_x, last_x = scatter_second(
+        o_half((0, 2), left), scatter_first(o_half((1, 3), left), ALONG_X), ALONG_Y
+    )
+    kept_y, last_y = scatter_second(
+        o_half((0, 1), right), scatter_first(o_half((2, 3), right), ALONG_Y), ALONG_X
+    )
+    sum_o = sum_over_seq(
+        jnp.concatenate(
+            [low(wide(kept_x) + wide(last_x)), low(wide(kept_y) + wide(last_y))], axis=1
+        ),
+        seq_at,
+    )
+    grad_query, grad_key, grad_value = attn_bwd(
+        query, key, value, grad_mixed, cosine, sine, start[None, :], counts, logsum
+    )
+    quarter = own_width // 2
+    qkv_sum_x, qkv_sum_y = weight_grads(
+        static_blocks(normed),
+        jnp.concatenate([grad_query, grad_value[:, :quarter]], axis=1),
+        jnp.concatenate([grad_key, grad_value[:, quarter:]], axis=1),
+    )
+    grad_qkv = jnp.concatenate([grad_query, grad_key, grad_value], axis=1)
+    normed_other = swap(low(nt(of_core(grad_qkv, 1 - core), full_qkv)), CORE)
+    grad_normed = nt(of_core(grad_qkv, core), full_qkv) + wide(normed_other)
+    grad_normed = relative(grad_normed, chip)
+    grad_gain_a, grad_rows = norm_backward(wide(x_half), gain_a, grad_normed)
+    grad_rows = grad_rows + of_core(grad_middle, core)
+    grad_tokens = wide(from_sequence(low(grad_rows), seq_at))
+
+    grad_gain_a = grad_gain_a + swap(grad_gain_a, CORE)
+    grad_gains = jnp.stack([grad_gain_a, grad_gain_f])
+    for bit in (ALONG_X, ALONG_Y):
+        grad_gains = grad_gains + swap(grad_gains, bit)
+    for bit in (1, 2):
+        grad_gains = grad_gains + lax.ppermute(
+            grad_gains, "seq", [(i, i ^ bit) for i in range(4)]
+        )
+    grad_gains = lax.dynamic_slice_in_dim(grad_gains, dp_at * (width // 8), width // 8, 1)
+
+    sum_qkv = jnp.concatenate(
+        [
+            qkv_sum_x[:, :own_width],
+            qkv_sum_y[:, :own_width],
+            qkv_sum_x[:, own_width:],
+            qkv_sum_y[:, own_width:],
+        ],
+        axis=1,
+    )
+    grads_qkv = both_cores(sum_qkv, core, 12)
+    grads_ff = both_cores(jnp.concatenate([sum_gate, sum_up], axis=1), core, 8)
+    return (
+        result,
+        grad_tokens,
+        grads_qkv[:, :width],
+        grads_qkv[:, width : 2 * width],
+        grads_qkv[:, 2 * width :],
+        wide(sum_o),
+        grads_ff[:, : w_gate.shape[1]],
+        grads_ff[:, w_gate.shape[1] :],
+        wide(jnp.concatenate([down_x, down_y], axis=1)),
+        grad_gains[0],
+        grad_gains[1],
+    )
+
+
 def solution(mesh):
     placed = (
         P(None, ("dp", "seq"), None),
@@ -408,7 +908,7 @@
         P("dp"),
     )
     return jax.shard_map(
-        per_device,
+        column_device if dict(mesh.shape) == FAST_MESH else per_device,
         mesh=mesh,
         in_specs=placed,
         out_specs=(

time: 1510 us -> 1150 us (0.76)
  matrix products: 427 us -> 165 us
  waiting for transfers between devices: 674 us -> 467 us
  starting transfers between devices: 76.6 us -> 176 us
  Pallas kernels: 0 us -> 81.7 us
  blocking collectives: 55 us -> 0 us
  local copies, waits for them, and re-layouts: 142 us -> 162 us
  loops' own time: 16.8 us -> 0 us
    ppermute x0 -> x90, waiting for transfers between devices: none -> 467 us  [the longest x57 223 us: swap(): return lax.ppermute(value, 'dp', [(i, i ^ bit) for i in range(8)])]
    dot_general x70 -> x25, matrix products: 427 us -> 165 us  [the longest x6 56.2 us: dot(): return jnp.dot(a, b, preferred_element_type=jnp.float32)]
    reduce_scatter x7 -> x0, waiting for transfers between devices: 248 us -> none  [the longest x1 95.9 us: per_device(): lax.psum_scatter(summed_all[5].astype(jnp.bfloat16), 'dp', scatter_dimens...]
    all_to_all x16 -> x0, waiting for transfers between devices: 193 us -> none  [the longest x2 37.2 us: per_device(): lax.all_to_all(query_rows, 'seq', split_axis=1, concat_axis=0, tiled=True)]
    psum x1 -> x0, waiting for transfers between devices: 189 us -> none  [per_device(): lax.psum(pieces[0].astype(jnp.bfloat16), 'seq').astype(jnp.float32)]
    ppermute x0 -> x90, starting transfers between devices: none -> 176 us  [the longest x57 69.2 us: swap(): return lax.ppermute(value, 'dp', [(i, i ^ bit) for i in range(8)])]
    pallas_call x0 -> x2, Pallas kernels: none -> 81.7 us  [the longest x1 45.2 us: attn_bwd(): pl.pallas_call(attn_bwd_kernel, grid_spec=pltpu.PrefetchScalarGridSpec(nu...]
    all_to_all x16 -> x0, starting transfers between devices: 76.1 us -> none  [the longest x2 18 us: per_device(): lax.all_to_all(key_rows, 'seq', split_axis=1, concat_axis=0, tiled=True)]
  transfers between devices with their start and end apart: 31 -> 90, of which waited for: 20 -> 28; matrix products, arithmetic and copies ran while one was open for 35% -> 28% of each run, Pallas kernels for 0% -> 7%
where the time goes in v1:
time: 1150 us; the launch traced here: 1140 us
  waiting for transfers between devices  467 us (41%)
  starting transfers between devices  176 us (15%)
  matrix products  165 us (14%)
  local copies, waits for them, and re-layouts  162 us (14%)
  other arithmetic  82.3 us (7%)
  Pallas kernels  81.7 us (7%)
    ppermute x57, waiting for transfers between devices, swap(): return lax.ppermute(value, 'dp', [(i, i ^ bit) for i in range(8)])  223 us
    ppermute x7, waiting for transfers between devices, sum_over_seq(): ends = lax.ppermute(two, 'seq', [(1, 0), (2, 3)])  141 us
    ppermute x57, starting transfers between devices, swap(): return lax.ppermute(value, 'dp', [(i, i ^ bit) for i in range(8)])  69.2 us
    dot_general x6, matrix products, dot(): return jnp.dot(a, b, preferred_element_type=jnp.float32)  56.2 us
    dot_general x6, matrix products, nt(): lax.dot_general(a, b, (((1,), (1,)), ((), ())), preferred_element_type=jn...  54.9 us
    dot_general x13, matrix products, tn(): lax.dot_general(a, b, (((0,), (0,)), ((), ())), preferred_element_type=jn...  53.9 us
    pallas_call x1, Pallas kernels, attn_bwd(): pl.pallas_call(attn_bwd_kernel, grid_spec=pltpu.PrefetchScalarGridSpec(nu...  45.2 us
    ppermute x7, starting transfers between devices, sum_over_seq(): one = low(wide(value) + wide(lax.ppermute(value, 'seq', [(0, 1), (3, 2)])))  44.9 us
  transfers between devices with their start and end apart: 90, of which 28 were waited for; matrix products, arithmetic and copies ran while one was open for 28% of the time, Pallas kernels for 7%

profile of v1, /device:TPU:0, one launch (start us, length us, event | category | flops | bytes accessed | tf_op | source)
XLA Modules:
  0.0 1137.0 jit_solution(12967017030034608760)
XLA Ops:
  3.9 4.1 collective-permute-start.4
  13.9 6.0 dynamic-slice_reduce_fusion.6
  22.3 11.2 dynamic-slice_reduce_fusion.4
  39.5 7.4 collective-permute-start
  58.8 19.7 %dynamic-slice_reduce_fusion = (bf16[192,4,512]{2,1,0:T(4,128)(2,1)S(1)}, bf16[192,4,512]{2,1,0:T(4,128)(2,1)S(1)}, bf16[192,4,512]{2,1,0:T(4,128)(2,1)S(1)}, bf16[192,4,512]{2,1,0:T(4,128)(2,1)S(1)}) fusion(bf16[192,4,2,512]{3,2,1,0:T(2,128)(2,1)S(1)} %reshape.236, s32[]{:T(128)S(6)} %select_n.389, s32[]{:T(128)S(6)} %select_n.388, ...), kind=kLoop, calls=%fused_computation.159 | loop fusion | bytes 6291464 | tf_op jit(solution)/shard_map/jit(dynamic_index_in_dim)/dynamic_slice | solution.py:679
  98.5 4.2 collective-permute-done.1
  105.2 4.3 collective-permute-start.40
  117.8 9.7 collective-permute-done.40
  133.4 15.0 %collective-permute-start.41 = (bf16[512,1536]{1,0:T(8,128)(2,1)}, bf16[512,1536]{1,0:T(8,128)(2,1)}, u32[]{:S(2)}, u32[]{:S(2)}) collective-permute-start(bf16[512,1536]{1,0:T(8,128)(2,1)} %pad_maximum_fusion.49), channel_id=1, source_target_pairs={{0,4},{4,0},{8,12},{12,8},{16,20},{20,16},{24,28},{28,24},{1,5},{5... | collective-permute-start | bytes 4718600 | tf_op jit(solution)/shard_map/ppermute | solution.py:555
  151.8 10.6 collective-permute-done.16
  165.2 3.8 collective-permute-done.18
  170.6 21.7 %collective-permute-done.20 = bf16[96,1536]{1,0:T(8,128)(2,1)S(1)} collective-permute-done((bf16[96,1536]{1,0:T(8,128)(2,1)S(1)}, bf16[96,1536]{1,0:T(8,128)(2,1)S(1)}, u32[]{:S(2)}, u32[]{:S(2)}) %collective-permute-start.20) | collective-permute-done | bytes 294944 | tf_op jit(solution)/shard_map/ppermute | solution.py:555
  196.6 4.6 fusion.2
  201.6 8.9 collective-permute-done.15
  214.9 9.9 fusion.15.q_ref.k_ref.v_ref
  227.5 36.5 %attn_fwd.1 = (bf16[1024,768]{1,0:T(8,128)(2,1)S(1)}, bf16[1024,768]{1,0:T(8,128)(2,1)S(1)}, bf16[1024,768]{1,0:T(8,128)(2,1)S(1)}, bf16[1024,768]{1,0:T(8,128)(2,1)S(1)}, f32[1024,128]{1,0:T(8,128)S(1)}) custom-call(s32[4]{0:T(128)S(1)} %subtract_add_fusion.count_ref, f32[1024,2304]{1,0:T(8,128)} %fusion.15.q_ref.k_ref.v_ref, ...), custom_call_target="tpu_custom_call" | custom-call | flops 3221225472 | bytes 15728640 | tf_op jit(solution)/shard_map/attn_fwd/pallas_call | solution.py:468
  272.9 4.3 fusion.108
  296.0 23.4 %collective-permute-done.30 = bf16[256,1536]{1,0:T(8,128)(2,1)} collective-permute-done((bf16[256,1536]{1,0:T(8,128)(2,1)S(1)}, bf16[256,1536]{1,0:T(8,128)(2,1)}, u32[]{:S(2)}, u32[]{:S(2)}) %collective-permute-start.30) | collective-permute-done | bytes 786464 | tf_op jit(solution)/shard_map/ppermute | solution.py:555
  329.5 42.5 %collective-permute-done.34 = bf16[256,1536]{1,0:T(8,128)(2,1)S(1)} collective-permute-done((bf16[256,1536]{1,0:T(8,128)(2,1)}, bf16[256,1536]{1,0:T(8,128)(2,1)S(1)}, u32[]{:S(2)}, u32[]{:S(2)}) %collective-permute-start.34) | collective-permute-done | bytes 786464 | tf_op jit(solution)/shard_map/ppermute | solution.py:555
  374.4 8.9 fusion.36
  386.1 10.8 fusion.64
  398.2 18.6 %multiply_convert_fusion.1 = (bf16[1024,2048]{1,0:T(8,128)(2,1)}, bf16[1024,2048]{1,0:T(8,128)(2,1)}, bf16[1024,2048]{1,0:T(8,128)(2,1)}) fusion(f32[1024,2048]{1,0:T(8,128)} %fusion.36, f32[1024,2048]{1,0:T(8,128)} %fusion.64, bf16[1536,2048]{1,0:T(8,128)(2,1)} %constant_dynamic-update-slice_fusion.7, bf16[1024,384]{1,0:T(8,128)(2,1)} %copy-done.78, ...), kind=kOutput, calls=%fused_computation.4 | convolution fusion | flops 6486491136 | bytes 38797312 | tf_op jit(solution)/shard_map/dot_general | solution.py:629
  416.8 12.0 %fusion.110 = f32[1024,1536]{1,0:T(8,128)} fusion(bf16[1024,2048]{1,0:T(8,128)(2,1)} %get-tuple-element.110, bf16[1536,2048]{1,0:T(8,128)(2,1)} %constant_dynamic-update-slice_fusion.11), kind=kOutput, calls=%fused_computation.363 | convolution fusion | flops 6442450944 | bytes 16777216 | tf_op jit(solution)/shard_map/dot_general | solution.py:410
  428.8 5.1 convolution_convert_fusion.1
  435.3 7.8 convolution_convert_fusion.6
  451.9 13.3 %fusion.109 = (bf16[1024,1536]{1,0:T(8,128)(2,1)}, f32[1024,1536]{1,0:T(8,128)}) fusion(f32[1024,1536]{1,0:T(8,128)} %fusion.110, bf16[1024,2048]{1,0:T(8,128)(2,1)} %get-tuple-element.109, bf16[1536,2048]{1,0:T(8,128)(2,1)} %constant_dynamic-update-slice_fusion.7), kind=kOutput, calls=%fused_computation.362 | convolution fusion | flops 6445596672 | bytes 26214400 | tf_op jit(solution)/shard_map/dot_general | solution.py:410
  465.2 21.6 %collective-permute-done.80 = bf16[1024,768]{0,1:T(8,128)(2,1)} collective-permute-done((bf16[1024,768]{0,1:T(8,128)(2,1)}, bf16[1024,768]{0,1:T(8,128)(2,1)}, u32[]{:S(2)}, u32[]{:S(2)}) %collective-permute-start.80) | collective-permute-done | bytes 1572896 | tf_op jit(solution)/shard_map/ppermute | solution.py:555
  486.7 4.0 add_convert_fusion.4
  491.6 4.9 fusion.23
  497.5 21.5 %collective-permute-start.38 = (bf16[256,1536]{1,0:T(8,128)(2,1)S(1)}, bf16[256,1536]{1,0:T(8,128)(2,1)S(1)}, u32[]{:S(2)}, u32[]{:S(2)}) collective-permute-start(bf16[256,1536]{1,0:T(8,128)(2,1)S(1)} %get-tuple-element.172), channel_id=1, source_target_pairs={{2,0},{0,1},{6,2},{4,3},{3,4},{1,5},{7,6},{5,7},{10,8},{8,9},{14,1... | collective-permute-start | bytes 2359304 | tf_op jit(solution)/shard_map/ppermute | solution.py:595
  523.1 5.0 convolution_convert_fusion.2
  529.2 41.3 %collective-permute-done.76 = bf16[512,768]{0,1:T(8,128)(2,1)S(1)} collective-permute-done((bf16[512,768]{0,1:T(8,128)(2,1)S(1)}, bf16[512,768]{0,1:T(8,128)(2,1)S(1)}, u32[]{:S(2)}, u32[]{:S(2)}) %collective-permute-start.76) | collective-permute-done | bytes 786464 | tf_op jit(solution)/shard_map/ppermute | solution.py:555
  571.4 22.9 %collective-permute-start.82 = (bf16[512,768]{0,1:T(8,128)(2,1)}, bf16[512,768]{0,1:T(8,128)(2,1)}, u32[]{:S(2)}, u32[]{:S(2)}) collective-permute-start(bf16[512,768]{0,1:T(8,128)(2,1)} %add_convert_fusion.20), channel_id=1, source_target_pairs={{0,1},{3,2},{4,5},{7,6},{8,9},{11,10},{12,13},{15,14},{16,17},{19,... | collective-permute-start | bytes 2359304 | tf_op jit(solution)/shard_map/ppermute | solution.py:651
  597.9 5.4 add_convert_fusion
  605.5 3.7 convert_add_fusion.2
  612.2 4.8 convert_add_fusion.1
  626.0 45.2 %attn_bwd.1 = (bf16[1024,768]{1,0:T(8,128)(2,1)S(1)}, bf16[1024,768]{1,0:T(8,128)(2,1)S(1)}, bf16[1024,768]{1,0:T(8,128)(2,1)S(1)}) custom-call(s32[4]{0:T(128)S(1)} %copy-done.4, bf16[1024,768]{1,0:T(8,128)(2,1)S(1)} %copy-done.6, bf16[1024,768]{1,0:T(8,128)(2,1)S(1)} %copy-done.8, bf16[1024,768]{1,0:T(8,128)(2,1)S(1)} %copy-done.10, ...), custom_call_target="tpu_custom_call" | custom-call | flops 8053063680 | bytes 11010048 | tf_op jit(solution)/shard_map/attn_bwd/pallas_call | solution.py:534
  671.6 9.9 convolution_convert_fusion.5
  681.6 6.8 add_convert_fusion.1
  700.1 6.0 collective-permute-done.60
  707.9 9.6 collective-permute-start.61
  723.9 4.3 collective-permute-done.61
  732.2 8.1 convolution_add_fusion.1
  749.9 8.8 collective-permute-done.65
  768.5 25.0 %collective-permute-done.87 = f32[2,1536]{1,0:T(2,128)S(1)} collective-permute-done((f32[2,1536]{1,0:T(2,128)S(1)}, f32[2,1536]{1,0:T(2,128)S(1)}, u32[]{:S(2)}, u32[]{:S(2)}) %collective-permute-start.87) | collective-permute-done | bytes 12320 | tf_op jit(solution)/shard_map/ppermute | solution.py:555
  796.4 30.1 %collective-permute-done.88 = f32[2,1536]{1,0:T(2,128)S(1)} collective-permute-done((f32[2,1536]{1,0:T(2,128)S(1)}, f32[2,1536]{1,0:T(2,128)S(1)}, u32[]{:S(2)}, u32[]{:S(2)}) %collective-permute-start.88) | collective-permute-done | bytes 12320 | tf_op jit(solution)/shard_map/ppermute | solution.py:864
  832.0 3.6 copy.95
  839.9 4.7 add_convert_fusion.2
  844.8 3.7 add_convert_fusion.3
  852.0 37.0 %collective-permute-done.45 = bf16[256,1536]{1,0:T(8,128)(2,1)S(1)} collective-permute-done((bf16[256,1536]{1,0:T(8,128)(2,1)S(1)}, bf16[256,1536]{1,0:T(8,128)(2,1)S(1)}, u32[]{:S(2)}, u32[]{:S(2)}) %collective-permute-start.45) | collective-permute-done | bytes 786464 | tf_op jit(solution)/shard_map/ppermute | solution.py:595
  892.5 4.6 collective-permute-start.53
  898.7 4.8 collective-permute-done.63
  909.0 17.3 %collective-permute-done.48 = bf16[384,1152]{1,0:T(8,128)(2,1)S(1)} collective-permute-done((bf16[384,1152]{1,0:T(8,128)(2,1)S(1)}, bf16[384,1152]{1,0:T(8,128)(2,1)S(1)}, u32[]{:S(2)}, u32[]{:S(2)}) %collective-permute-start.48) | collective-permute-done | bytes 884768 | tf_op jit(solution)/shard_map/ppermute | solution.py:651
  935.8 54.0 %collective-permute-done.55 = bf16[384,1152]{1,0:T(8,128)(2,1)S(1)} collective-permute-done((bf16[384,1152]{1,0:T(8,128)(2,1)S(1)}, bf16[384,1152]{1,0:T(8,128)(2,1)S(1)}, u32[]{:S(2)}, u32[]{:S(2)}) %collective-permute-start.55) | collective-permute-done | bytes 884768 | tf_op jit(solution)/shard_map/ppermute | solution.py:653
  990.0 18.8 %collective-permute-done.50 = bf16[384,1152]{1,0:T(8,128)(2,1)S(1)} collective-permute-done((bf16[384,1152]{1,0:T(8,128)(2,1)S(1)}, bf16[384,1152]{1,0:T(8,128)(2,1)S(1)}, u32[]{:S(2)}, u32[]{:S(2)}) %collective-permute-start.50) | collective-permute-done | bytes 884768 | tf_op jit(solution)/shard_map/ppermute | solution.py:653
  1012.4 30.1 %collective-permute-done.73 = bf16[384,2048]{1,0:T(8,128)(2,1)S(1)} collective-permute-done((bf16[384,2048]{1,0:T(8,128)(2,1)S(1)}, bf16[384,2048]{1,0:T(8,128)(2,1)S(1)}, u32[]{:S(2)}, u32[]{:S(2)}) %collective-permute-start.73) | collective-permute-done | bytes 1572896 | tf_op jit(solution)/shard_map/ppermute | solution.py:653
  1042.7 33.5 %collective-permute-done.68 = bf16[384,2048]{1,0:T(8,128)(2,1)S(1)} collective-permute-done((bf16[384,2048]{1,0:T(8,128)(2,1)S(1)}, bf16[384,2048]{1,0:T(8,128)(2,1)S(1)}, u32[]{:S(2)}, u32[]{:S(2)}) %collective-permute-start.68) | collective-permute-done | bytes 1572896 | tf_op jit(solution)/shard_map/ppermute | solution.py:653
  1085.1 4.4 maximum_convert_fusion.1
  1089.4 8.3 copy.91
  1097.7 7.0 reshape.245
  1104.7 3.8 fusion.103
  1112.5 8.9 copy.92
  1121.4 9.2 reshape.246
  1130.6 6.3 fusion.102
  (573 shorter events, 260.6 us)
Async XLA Ops:
  2.0 84.1 %collective-permute-start.3 = (s32[2,128]{1,0:T(2,128)}, s32[2,128]{1,0:T(2,128)}, u32[]{:S(2)}, u32[]{:S(2)}) collective-permute-start(s32[2,128]{1,0:T(2,128)} %get-tuple-element.196), channel_id=1, source_target_pairs={{0,0},{1,2},{2,4},{3,6},{4,1},{5,3},{6,5},{7,7},{8,8},{9,10},{10,1... | collective-permute-start | bytes 3080 | tf_op jit(solution)/shard_map/ppermute | solution.py:580
  3.9 82.3 %collective-permute-start.4 = (s32[2,128]{1,0:T(2,128)}, s32[2,128]{1,0:T(2,128)}, u32[]{:S(2)}, u32[]{:S(2)}) collective-permute-start(s32[2,128]{1,0:T(2,128)} %get-tuple-element.197), channel_id=1, source_target_pairs={{0,2},{1,0},{2,6},{3,4},{4,3},{5,1},{6,7},{7,5},{8,10},{9,8},{10,1... | collective-permute-start | bytes 3080 | tf_op jit(solution)/shard_map/ppermute | solution.py:580
  9.9 75.1 %collective-permute-start.6 = (bf16[1,2,192]{2,1,0:T(2,128)(2,1)}, bf16[1,2,192]{2,1,0:T(2,128)(2,1)}, u32[]{:S(2)}, u32[]{:S(2)}) collective-permute-start(bf16[1,2,192]{2,1,0:T(2,128)(2,1)} %maximum_bitcast_fusion), channel_id=1, source_target_pairs={{0,4},{4,0},{8,12},{12,8},{16,20},{20,16},{24,28},{28,24},{1,5},{5... | collective-permute-start | bytes 2312 | tf_op jit(solution)/shard_map/ppermute | solution.py:555
  38.3 72.1 %collective-permute-start.9 = (bf16[192,2304]{1,0:T(8,128)(2,1)}, bf16[192,2304]{1,0:T(8,128)(2,1)}, u32[]{:S(2)}, u32[]{:S(2)}) collective-permute-start(bf16[192,2304]{1,0:T(8,128)(2,1)} %pad_maximum_fusion.58), channel_id=1, source_target_pairs={{0,4},{4,0},{8,12},{12,8},{16,20},{20,16},{24,28},{28,24},{1,5},{5... | collective-permute-start | bytes 2654216 | tf_op jit(solution)/shard_map/ppermute | solution.py:555
  39.5 59.0 %collective-permute-start = (bf16[256,1536]{1,0:T(8,128)(2,1)}, bf16[256,1536]{1,0:T(8,128)(2,1)}, u32[]{:S(2)}, u32[]{:S(2)}) collective-permute-start(bf16[256,1536]{1,0:T(8,128)(2,1)} %get-tuple-element.175), channel_id=1, source_target_pairs={{0,0},{1,2},{2,4},{3,6},{4,1},{5,3},{6,5},{7,7},{8,8},{9,10},{10,1... | collective-permute-start | bytes 2359304 | tf_op jit(solution)/shard_map/ppermute | solution.py:580
  86.2 27.7 %collective-permute-start.23 = (bf16[192,4096]{1,0:T(8,128)(2,1)}, bf16[192,4096]{1,0:T(8,128)(2,1)}, u32[]{:S(2)}, u32[]{:S(2)}) collective-permute-start(bf16[192,4096]{1,0:T(8,128)(2,1)} %pad_maximum_fusion.47), channel_id=1, source_target_pairs={{0,4},{4,0},{8,12},{12,8},{16,20},{20,16},{24,28},{28,24},{1,5},{5... | collective-permute-start | bytes 4718600 | tf_op jit(solution)/shard_map/ppermute | solution.py:555
  104.3 91.0 %collective-permute-start.2 = (bf16[512,1536]{1,0:T(8,128)(2,1)S(1)}, bf16[512,1536]{1,0:T(8,128)(2,1)S(1)}, u32[]{:S(2)}, u32[]{:S(2)}) collective-permute-start(bf16[512,1536]{1,0:T(8,128)(2,1)S(1)} %pad_maximum_fusion.46), channel_id=1, source_target_pairs={{0,4},{4,0},{8,12},{12,8},{16,20},{20,16},{24,28},{28,24},{1,5},{5... | collective-permute-start | bytes 4718600 | tf_op jit(solution)/shard_map/ppermute | solution.py:555
  105.2 22.3 %collective-permute-start.40 = (bf16[256,1536]{1,0:T(8,128)(2,1)S(1)}, bf16[256,1536]{1,0:T(8,128)(2,1)S(1)}, u32[]{:S(2)}, u32[]{:S(2)}) collective-permute-start(bf16[256,1536]{1,0:T(8,128)(2,1)S(1)} %get-tuple-element.168), channel_id=1, source_target_pairs={{0,2},{1,0},{2,6},{3,4},{4,3},{5,1},{6,7},{7,5},{8,10},{9,8},{10,1... | collective-permute-start | bytes 2359304 | tf_op jit(solution)/shard_map/ppermute | solution.py:580
  113.9 35.0 %collective-permute-start.10 = (bf16[384,1152]{1,0:T(8,128)(2,1)S(1)}, bf16[384,1152]{1,0:T(8,128)(2,1)S(1)}, u32[]{:S(2)}, u32[]{:S(2)}) collective-permute-start(bf16[384,1152]{1,0:T(8,128)(2,1)S(1)} %pad_maximum_fusion.59), channel_id=1, source_target_pairs={{0,8},{4,12},{8,0},{12,4},{16,24},{20,28},{24,16},{28,20},{1,9},{5... | collective-permute-start | bytes 2654216 | tf_op jit(solution)/shard_map/ppermute | solution.py:555
  117.3 31.1 %collective-permute-start.13 = (bf16[384,1152]{1,0:T(8,128)(2,1)S(1)}, bf16[384,1152]{1,0:T(8,128)(2,1)S(1)}, u32[]{:S(2)}, u32[]{:S(2)}) collective-permute-start(bf16[384,1152]{1,0:T(8,128)(2,1)S(1)} %fusion.61), channel_id=1, source_target_pairs={{0,16},{4,20},{8,24},{12,28},{16,0},{20,4},{24,8},{28,12},{1,17},{... | collective-permute-start | bytes 2654216 | tf_op jit(solution)/shard_map/ppermute | solution.py:555
  133.4 143.8 %collective-permute-start.41 = (bf16[512,1536]{1,0:T(8,128)(2,1)}, bf16[512,1536]{1,0:T(8,128)(2,1)}, u32[]{:S(2)}, u32[]{:S(2)}) collective-permute-start(bf16[512,1536]{1,0:T(8,128)(2,1)} %pad_maximum_fusion.49), channel_id=1, source_target_pairs={{0,4},{4,0},{8,12},{12,8},{16,20},{20,16},{24,28},{28,24},{1,5},{5... | collective-permute-start | bytes 4718600 | tf_op jit(solution)/shard_map/ppermute | solution.py:555
  163.0 49.5 %collective-permute-start.14 = (bf16[384,1152]{1,0:T(8,128)(2,1)S(1)}, bf16[384,1152]{1,0:T(8,128)(2,1)S(1)}, u32[]{:S(2)}, u32[]{:S(2)}) collective-permute-start(bf16[384,1152]{1,0:T(8,128)(2,1)S(1)} %collective-permute-done.10), channel_id=1, source_target_pairs={{0,16},{4,20},{8,24},{12,28},{16,0},{20,4},{24,8},{28,12},{1,17},{... | collective-permute-start | bytes 2654216 | tf_op jit(solution)/shard_map/ppermute | solution.py:555
  164.5 27.8 %collective-permute-start.20 = (bf16[96,1536]{1,0:T(8,128)(2,1)S(1)}, bf16[96,1536]{1,0:T(8,128)(2,1)S(1)}, u32[]{:S(2)}, u32[]{:S(2)}) collective-permute-start(bf16[96,1536]{1,0:T(8,128)(2,1)S(1)} %collective-permute-done.16), channel_id=1, source_target_pairs={{0,16},{4,20},{8,24},{12,28},{16,0},{20,4},{24,8},{28,12},{1,17},{... | collective-permute-start | bytes 884744 | tf_op jit(solution)/shard_map/ppermute | solution.py:555
  169.1 24.8 %collective-permute-start.21 = (bf16[96,1536]{1,0:T(8,128)(2,1)S(1)}, bf16[96,1536]{1,0:T(8,128)(2,1)S(1)}, u32[]{:S(2)}, u32[]{:S(2)}) collective-permute-start(bf16[96,1536]{1,0:T(8,128)(2,1)S(1)} %collective-permute-done.19), channel_id=1, source_target_pairs={{0,8},{4,12},{8,0},{12,4},{16,24},{20,28},{24,16},{28,20},{1,9},{5... | collective-permute-start | bytes 884744 | tf_op jit(solution)/shard_map/ppermute | solution.py:555
  210.5 72.1 %collective-permute-start.25 = (bf16[384,2048]{1,0:T(8,128)(2,1)}, bf16[384,2048]{1,0:T(8,128)(2,1)}, u32[]{:S(2)}, u32[]{:S(2)}) collective-permute-start(bf16[384,2048]{1,0:T(8,128)(2,1)} %get-tuple-element.29), channel_id=1, source_target_pairs={{0,16},{4,20},{8,24},{12,28},{16,0},{20,4},{24,8},{28,12},{1,17},{... | collective-permute-start | bytes 4718600 | tf_op jit(solution)/shard_map/ppermute | solution.py:555
  211.5 71.3 %collective-permute-start.24 = (bf16[384,2048]{1,0:T(8,128)(2,1)}, bf16[384,2048]{1,0:T(8,128)(2,1)}, u32[]{:S(2)}, u32[]{:S(2)}) collective-permute-start(bf16[384,2048]{1,0:T(8,128)(2,1)} %get-tuple-element.29), channel_id=1, source_target_pairs={{0,8},{4,12},{8,0},{12,4},{16,24},{20,28},{24,16},{28,20},{1,9},{5... | collective-permute-start | bytes 4718600 | tf_op jit(solution)/shard_map/ppermute | solution.py:555
  212.5 70.2 %collective-permute-start.28 = (bf16[384,2048]{1,0:T(8,128)(2,1)}, bf16[384,2048]{1,0:T(8,128)(2,1)}, u32[]{:S(2)}, u32[]{:S(2)}) collective-permute-start(bf16[384,2048]{1,0:T(8,128)(2,1)} %get-tuple-element.30), channel_id=1, source_target_pairs={{0,16},{4,20},{8,24},{12,28},{16,0},{20,4},{24,8},{28,12},{1,17},{... | collective-permute-start | bytes 4718600 | tf_op jit(solution)/shard_map/ppermute | solution.py:555
  214.0 68.8 %collective-permute-start.27 = (bf16[384,2048]{1,0:T(8,128)(2,1)}, bf16[384,2048]{1,0:T(8,128)(2,1)}, u32[]{:S(2)}, u32[]{:S(2)}) collective-permute-start(bf16[384,2048]{1,0:T(8,128)(2,1)} %get-tuple-element.30), channel_id=1, source_target_pairs={{0,8},{4,12},{8,0},{12,4},{16,24},{20,28},{24,16},{28,20},{1,9},{5... | collective-permute-start | bytes 4718600 | tf_op jit(solution)/shard_map/ppermute | solution.py:555
  277.2 47.8 %collective-permute-start.22 = (bf16[1024,1536]{1,0:T(8,128)(2,1)}, bf16[1024,1536]{1,0:T(8,128)(2,1)S(1)}, u32[]{:S(2)}, u32[]{:S(2)}) collective-permute-start(bf16[1024,1536]{1,0:T(8,128)(2,1)} %get-tuple-element.198), channel_id=1, source_target_pairs={{0,4},{4,0},{8,12},{12,8},{16,20},{20,16},{24,28},{28,24},{1,5},{5... | collective-permute-start | bytes 9437192 | tf_op jit(solution)/shard_map/ppermute | solution.py:555
  282.7 40.0 %collective-permute-start.33 = (bf16[256,1536]{1,0:T(8,128)(2,1)S(1)}, bf16[256,1536]{1,0:T(8,128)(2,1)S(1)}, u32[]{:S(2)}, u32[]{:S(2)}) collective-permute-start(bf16[256,1536]{1,0:T(8,128)(2,1)S(1)} %copy-done.38), channel_id=1, source_target_pairs={{0,16},{4,20},{8,24},{12,28},{16,0},{20,4},{24,8},{28,12},{1,17},{... | collective-permute-start | bytes 2359304 | tf_op jit(solution)/shard_map/ppermute | solution.py:555
  282.7 39.5 %collective-permute-start.31 = (bf16[256,1536]{1,0:T(8,128)(2,1)S(1)}, bf16[256,1536]{1,0:T(8,128)(2,1)S(1)}, u32[]{:S(2)}, u32[]{:S(2)}) collective-permute-start(bf16[256,1536]{1,0:T(8,128)(2,1)S(1)} %copy-done.38), channel_id=1, source_target_pairs={{0,8},{4,12},{8,0},{12,4},{16,24},{20,28},{24,16},{28,20},{1,9},{5... | collective-permute-start | bytes 2359304 | tf_op jit(solution)/shard_map/ppermute | solution.py:555
  282.8 40.3 %collective-permute-start.32 = (bf16[256,1536]{1,0:T(8,128)(2,1)S(1)}, bf16[256,1536]{1,0:T(8,128)(2,1)S(1)}, u32[]{:S(2)}, u32[]{:S(2)}) collective-permute-start(bf16[256,1536]{1,0:T(8,128)(2,1)S(1)} %copy-done.37), channel_id=1, source_target_pairs={{0,16},{4,20},{8,24},{12,28},{16,0},{20,4},{24,8},{28,12},{1,17},{... | collective-permute-start | bytes 2359304 | tf_op jit(solution)/shard_map/ppermute | solution.py:555
  284.9 34.5 %collective-permute-start.30 = (bf16[256,1536]{1,0:T(8,128)(2,1)S(1)}, bf16[256,1536]{1,0:T(8,128)(2,1)}, u32[]{:S(2)}, u32[]{:S(2)}) collective-permute-start(bf16[256,1536]{1,0:T(8,128)(2,1)S(1)} %copy-done.37), channel_id=1, source_target_pairs={{0,8},{4,12},{8,0},{12,4},{16,24},{20,28},{24,16},{28,20},{1,9},{5... | collective-permute-start | bytes 2359304 | tf_op jit(solution)/shard_map/ppermute | solution.py:555
  319.3 77.5 %collective-permute-start.26 = (bf16[384,2048]{1,0:T(8,128)(2,1)}, bf16[384,2048]{1,0:T(8,128)(2,1)S(1)}, u32[]{:S(2)}, u32[]{:S(2)}) collective-permute-start(bf16[384,2048]{1,0:T(8,128)(2,1)} %collective-permute-done.24), channel_id=1, source_target_pairs={{0,16},{4,20},{8,24},{12,28},{16,0},{20,4},{24,8},{28,12},{1,17},{... | collective-permute-start | bytes 4718600 | tf_op jit(solution)/shard_map/ppermute | solution.py:555
  322.2 61.1 %collective-permute-start.29 = (bf16[384,2048]{1,0:T(8,128)(2,1)}, bf16[384,2048]{1,0:T(8,128)(2,1)}, u32[]{:S(2)}, u32[]{:S(2)}) collective-permute-start(bf16[384,2048]{1,0:T(8,128)(2,1)} %collective-permute-done.28), channel_id=1, source_target_pairs={{0,8},{4,12},{8,0},{12,4},{16,24},{20,28},{24,16},{28,20},{1,9},{5... | collective-permute-start | bytes 4718600 | tf_op jit(solution)/shard_map/ppermute | solution.py:555
  322.6 49.4 %collective-permute-start.34 = (bf16[256,1536]{1,0:T(8,128)(2,1)}, bf16[256,1536]{1,0:T(8,128)(2,1)S(1)}, u32[]{:S(2)}, u32[]{:S(2)}) collective-permute-start(bf16[256,1536]{1,0:T(8,128)(2,1)} %collective-permute-done.30), channel_id=1, source_target_pairs={{0,16},{4,20},{8,24},{12,28},{16,0},{20,4},{24,8},{28,12},{1,17},{... | collective-permute-start | bytes 2359304 | tf_op jit(solution)/shard_map/ppermute | solution.py:555
  323.2 51.1 %collective-permute-start.35 = (bf16[256,1536]{1,0:T(8,128)(2,1)S(1)}, bf16[256,1536]{1,0:T(8,128)(2,1)S(1)}, u32[]{:S(2)}, u32[]{:S(2)}) collective-permute-start(bf16[256,1536]{1,0:T(8,128)(2,1)S(1)} %collective-permute-done.33), channel_id=1, source_target_pairs={{0,8},{4,12},{8,0},{12,4},{16,24},{20,28},{24,16},{28,20},{1,9},{5... | collective-permute-start | bytes 2359304 | tf_op jit(solution)/shard_map/ppermute | solution.py:555
  443.1 48.4 %collective-permute-start.36 = (bf16[512,1536]{1,0:T(8,128)(2,1)}, bf16[512,1536]{1,0:T(8,128)(2,1)}, u32[]{:S(2)}, u32[]{:S(2)}) collective-permute-start(bf16[512,1536]{1,0:T(8,128)(2,1)} %convolution_convert_fusion.6), channel_id=1, source_target_pairs={{0,4},{4,0},{8,12},{12,8},{16,20},{20,16},{24,28},{28,24},{1,5},{5... | collective-permute-start | bytes 4718600 | tf_op jit(solution)/shard_map/ppermute | solution.py:555
  449.2 37.5 %collective-permute-start.80 = (bf16[1024,768]{0,1:T(8,128)(2,1)}, bf16[1024,768]{0,1:T(8,128)(2,1)}, u32[]{:S(2)}, u32[]{:S(2)}) collective-permute-start(bf16[1024,768]{0,1:T(8,128)(2,1)} %fusion.39), channel_id=1, source_target_pairs={{0,16},{4,20},{8,24},{12,28},{16,0},{20,4},{24,8},{28,12},{1,17},{... | collective-permute-start | bytes 4718600 | tf_op jit(solution)/shard_map/ppermute | solution.py:555
  450.0 47.5 %collective-permute-start.75 = (bf16[1024,768]{0,1:T(8,128)(2,1)}, bf16[1024,768]{0,1:T(8,128)(2,1)}, u32[]{:S(2)}, u32[]{:S(2)}) collective-permute-start(bf16[1024,768]{0,1:T(8,128)(2,1)} %fusion.40), channel_id=1, source_target_pairs={{0,8},{4,12},{8,0},{12,4},{16,24},{20,28},{24,16},{28,20},{1,9},{5... | collective-permute-start | bytes 4718600 | tf_op jit(solution)/shard_map/ppermute | solution.py:555
  450.8 147.1 %collective-permute-start.69 = (bf16[768,2048]{1,0:T(8,128)(2,1)}, bf16[768,2048]{1,0:T(8,128)(2,1)}, u32[]{:S(2)}, u32[]{:S(2)}) collective-permute-start(bf16[768,2048]{1,0:T(8,128)(2,1)} %convolution_convert_fusion.1), channel_id=1, source_target_pairs={{0,16},{4,20},{8,24},{12,28},{16,0},{20,4},{24,8},{28,12},{1,17},{... | collective-permute-start | bytes 9437192 | tf_op jit(solution)/shard_map/ppermute | solution.py:555
  465.2 140.1 %collective-permute-start.42 = (bf16[1024,1536]{1,0:T(8,128)(2,1)}, bf16[1024,1536]{1,0:T(8,128)(2,1)S(1)}, u32[]{:S(2)}, u32[]{:S(2)}) collective-permute-start(bf16[1024,1536]{1,0:T(8,128)(2,1)} %get-tuple-element.200), channel_id=1, source_target_pairs={{0,4},{4,0},{8,12},{12,8},{16,20},{20,16},{24,28},{28,24},{1,5},{5... | collective-permute-start | bytes 9437192 | tf_op jit(solution)/shard_map/ppermute | solution.py:555
  490.9 31.5 %collective-permute-start.81 = (bf16[512,768]{0,1:T(8,128)(2,1)S(1)}, bf16[512,768]{0,1:T(8,128)(2,1)S(1)}, u32[]{:S(2)}, u32[]{:S(2)}) collective-permute-start(bf16[512,768]{0,1:T(8,128)(2,1)S(1)} %slice.367), channel_id=1, source_target_pairs={{0,8},{4,12},{8,0},{12,4},{16,24},{20,28},{24,16},{28,20},{1,9},{5... | collective-permute-start | bytes 2359304 | tf_op jit(solution)/shard_map/ppermute | solution.py:555
  496.6 74.8 %collective-permute-start.37 = (bf16[256,1536]{1,0:T(8,128)(2,1)S(1)}, bf16[256,1536]{1,0:T(8,128)(2,1)S(1)}, u32[]{:S(2)}, u32[]{:S(2)}) collective-permute-start(bf16[256,1536]{1,0:T(8,128)(2,1)S(1)} %get-tuple-element.171), channel_id=1, source_target_pairs={{0,0},{2,1},{4,2},{6,3},{1,4},{3,5},{5,6},{7,7},{8,8},{10,9},{12,1... | collective-permute-start | bytes 2359304 | tf_op jit(solution)/shard_map/ppermute | solution.py:595
  497.5 96.8 %collective-permute-start.38 = (bf16[256,1536]{1,0:T(8,128)(2,1)S(1)}, bf16[256,1536]{1,0:T(8,128)(2,1)S(1)}, u32[]{:S(2)}, u32[]{:S(2)}) collective-permute-start(bf16[256,1536]{1,0:T(8,128)(2,1)S(1)} %get-tuple-element.172), channel_id=1, source_target_pairs={{2,0},{0,1},{6,2},{4,3},{3,4},{1,5},{7,6},{5,7},{10,8},{8,9},{14,1... | collective-permute-start | bytes 2359304 | tf_op jit(solution)/shard_map/ppermute | solution.py:595
  522.4 48.1 %collective-permute-start.76 = (bf16[512,768]{0,1:T(8,128)(2,1)S(1)}, bf16[512,768]{0,1:T(8,128)(2,1)S(1)}, u32[]{:S(2)}, u32[]{:S(2)}) collective-permute-start(bf16[512,768]{0,1:T(8,128)(2,1)S(1)} %slice.363), channel_id=1, source_target_pairs={{0,16},{4,20},{8,24},{12,28},{16,0},{20,4},{24,8},{28,12},{1,17},{... | collective-permute-start | bytes 2359304 | tf_op jit(solution)/shard_map/ppermute | solution.py:555
  570.5 111.0 %collective-permute-start.64 = (bf16[768,2048]{1,0:T(8,128)(2,1)}, bf16[768,2048]{1,0:T(8,128)(2,1)}, u32[]{:S(2)}, u32[]{:S(2)}) collective-permute-start(bf16[768,2048]{1,0:T(8,128)(2,1)} %convolution_convert_fusion.2), channel_id=1, source_target_pairs={{0,8},{4,12},{8,0},{12,4},{16,24},{20,28},{24,16},{28,20},{1,9},{5... | collective-permute-start | bytes 9437192 | tf_op jit(solution)/shard_map/ppermute | solution.py:555
  571.4 122.4 %collective-permute-start.82 = (bf16[512,768]{0,1:T(8,128)(2,1)}, bf16[512,768]{0,1:T(8,128)(2,1)}, u32[]{:S(2)}, u32[]{:S(2)}) collective-permute-start(bf16[512,768]{0,1:T(8,128)(2,1)} %add_convert_fusion.20), channel_id=1, source_target_pairs={{0,1},{3,2},{4,5},{7,6},{8,9},{11,10},{12,13},{15,14},{16,17},{19,... | collective-permute-start | bytes 2359304 | tf_op jit(solution)/shard_map/ppermute | solution.py:651
  594.3 104.3 %collective-permute-start.77 = (bf16[512,768]{0,1:T(8,128)(2,1)S(1)}, bf16[512,768]{0,1:T(8,128)(2,1)}, u32[]{:S(2)}, u32[]{:S(2)}) collective-permute-start(bf16[512,768]{0,1:T(8,128)(2,1)S(1)} %add_convert_fusion.23), channel_id=1, source_target_pairs={{0,1},{3,2},{4,5},{7,6},{8,9},{11,10},{12,13},{15,14},{16,17},{19,... | collective-permute-start | bytes 2359304 | tf_op jit(solution)/shard_map/ppermute | solution.py:651
  604.7 138.7 %collective-permute-start.70 = (bf16[384,2048]{1,0:T(8,128)(2,1)}, bf16[384,2048]{1,0:T(8,128)(2,1)}, u32[]{:S(2)}, u32[]{:S(2)}) collective-permute-start(bf16[384,2048]{1,0:T(8,128)(2,1)} %slice.357), channel_id=1, source_target_pairs={{0,8},{4,12},{8,0},{12,4},{16,24},{20,28},{24,16},{28,20},{1,9},{5... | collective-permute-start | bytes 4718600 | tf_op jit(solution)/shard_map/ppermute | solution.py:555
  621.8 73.7 %collective-permute-start.59 = (bf16[384,768]{1,0:T(8,128)(2,1)}, bf16[384,768]{1,0:T(8,128)(2,1)S(1)}, u32[]{:S(2)}, u32[]{:S(2)}) collective-permute-start(bf16[384,768]{1,0:T(8,128)(2,1)} %pad_maximum_fusion.61), channel_id=1, source_target_pairs={{0,16},{4,20},{8,24},{12,28},{16,0},{20,4},{24,8},{28,12},{1,17},{... | collective-permute-start | bytes 1769480 | tf_op jit(solution)/shard_map/ppermute | solution.py:555
  693.8 35.9 %collective-permute-start.43 = (bf16[512,1536]{1,0:T(8,128)(2,1)}, bf16[512,1536]{1,0:T(8,128)(2,1)S(1)}, u32[]{:S(2)}, u32[]{:S(2)}) collective-permute-start(bf16[512,1536]{1,0:T(8,128)(2,1)} %convolution_convert_fusion.5), channel_id=1, source_target_pairs={{0,4},{4,0},{8,12},{12,8},{16,20},{20,16},{24,28},{28,24},{1,5},{5... | collective-permute-start | bytes 4718600 | tf_op jit(solution)/shard_map/ppermute | solution.py:555
  695.4 25.8 %collective-permute-start.83 = (bf16[512,768]{0,1:T(8,128)(2,1)S(1)}, bf16[512,768]{0,1:T(8,128)(2,1)S(1)}, u32[]{:S(2)}, u32[]{:S(2)}) collective-permute-start(bf16[512,768]{0,1:T(8,128)(2,1)S(1)} %add_convert_fusion.19), channel_id=1, source_target_pairs={{1,2},{2,1},{5,6},{6,5},{9,10},{10,9},{13,14},{14,13},{17,18},{18,... | collective-permute-start | bytes 2359304 | tf_op jit(solution)/shard_map/ppermute | solution.py:652
  721.3 37.4 %collective-permute-start.65 = (bf16[384,2048]{1,0:T(8,128)(2,1)S(1)}, bf16[384,2048]{1,0:T(8,128)(2,1)S(1)}, u32[]{:S(2)}, u32[]{:S(2)}) collective-permute-start(bf16[384,2048]{1,0:T(8,128)(2,1)S(1)} %slice.355), channel_id=1, source_target_pairs={{0,16},{4,20},{8,24},{12,28},{16,0},{20,4},{24,8},{28,12},{1,17},{... | collective-permute-start | bytes 4718600 | tf_op jit(solution)/shard_map/ppermute | solution.py:555
  722.2 115.6 %collective-permute-start.51 = (bf16[768,1152]{1,0:T(8,128)(2,1)}, bf16[768,1152]{1,0:T(8,128)(2,1)}, u32[]{:S(2)}, u32[]{:S(2)}) collective-permute-start(bf16[768,1152]{1,0:T(8,128)(2,1)} %convolution_convert_fusion.3), channel_id=1, source_target_pairs={{0,16},{4,20},{8,24},{12,28},{16,0},{20,4},{24,8},{28,12},{1,17},{... | collective-permute-start | bytes 5308424 | tf_op jit(solution)/shard_map/ppermute | solution.py:555
  728.2 116.5 %collective-permute-start.46 = (bf16[768,1152]{1,0:T(8,128)(2,1)}, bf16[768,1152]{1,0:T(8,128)(2,1)}, u32[]{:S(2)}, u32[]{:S(2)}) collective-permute-start(bf16[768,1152]{1,0:T(8,128)(2,1)} %convolution_convert_fusion.4), channel_id=1, source_target_pairs={{0,8},{4,12},{8,0},{12,4},{16,24},{20,28},{24,16},{28,20},{1,9},{5... | collective-permute-start | bytes 5308424 | tf_op jit(solution)/shard_map/ppermute | solution.py:555
  730.9 36.8 %collective-permute-start.84 = (bf16[512,768]{0,1:T(8,128)(2,1)S(1)}, bf16[512,768]{0,1:T(8,128)(2,1)S(1)}, u32[]{:S(2)}, u32[]{:S(2)}) collective-permute-start(bf16[512,768]{0,1:T(8,128)(2,1)S(1)} %add_convert_fusion.18), channel_id=1, source_target_pairs={{1,0},{2,3},{5,4},{6,7},{9,8},{10,11},{13,12},{14,15},{17,16},{18,... | collective-permute-start | bytes 2359304 | tf_op jit(solution)/shard_map/ppermute | solution.py:653
  743.3 52.8 %collective-permute-start.79 = (bf16[512,768]{0,1:T(8,128)(2,1)S(1)}, bf16[512,768]{0,1:T(8,128)(2,1)S(1)}, u32[]{:S(2)}, u32[]{:S(2)}) collective-permute-start(bf16[512,768]{0,1:T(8,128)(2,1)S(1)} %add_convert_fusion.21), channel_id=1, source_target_pairs={{1,0},{2,3},{5,4},{6,7},{9,8},{10,11},{13,12},{14,15},{17,16},{18,... | collective-permute-start | bytes 2359304 | tf_op jit(solution)/shard_map/ppermute | solution.py:653
  766.2 82.5 %collective-permute-start.62 = (bf16[192,1536]{1,0:T(8,128)(2,1)S(1)}, bf16[192,1536]{1,0:T(8,128)(2,1)}, u32[]{:S(2)}, u32[]{:S(2)}) collective-permute-start(bf16[192,1536]{1,0:T(8,128)(2,1)S(1)} %add_convert_fusion.25), channel_id=1, source_target_pairs={{1,2},{2,1},{5,6},{6,5},{9,10},{10,9},{13,14},{14,13},{17,18},{18,... | collective-permute-start | bytes 1769480 | tf_op jit(solution)/shard_map/ppermute | solution.py:652
  767.7 25.8 %collective-permute-start.87 = (f32[2,1536]{1,0:T(2,128)S(1)}, f32[2,1536]{1,0:T(2,128)S(1)}, u32[]{:S(2)}, u32[]{:S(2)}) collective-permute-start(f32[2,1536]{1,0:T(2,128)S(1)} %fusion.96), channel_id=1, source_target_pairs={{0,16},{4,20},{8,24},{12,28},{16,0},{20,4},{24,8},{28,12},{1,17},{... | collective-permute-start | bytes 36872 | tf_op jit(solution)/shard_map/ppermute | solution.py:555
  793.5 111.2 %collective-permute-start.71 = (bf16[384,2048]{1,0:T(8,128)(2,1)}, bf16[384,2048]{1,0:T(8,128)(2,1)}, u32[]{:S(2)}, u32[]{:S(2)}) collective-permute-start(bf16[384,2048]{1,0:T(8,128)(2,1)} %add_convert_fusion.8), channel_id=1, source_target_pairs={{0,1},{3,2},{4,5},{7,6},{8,9},{11,10},{12,13},{15,14},{16,17},{19,... | collective-permute-start | bytes 4718600 | tf_op jit(solution)/shard_map/ppermute | solution.py:651
  796.2 30.3 %collective-permute-start.88 = (f32[2,1536]{1,0:T(2,128)S(1)}, f32[2,1536]{1,0:T(2,128)S(1)}, u32[]{:S(2)}, u32[]{:S(2)}) collective-permute-start(f32[2,1536]{1,0:T(2,128)S(1)} %fusion.131), channel_id=1, source_target_pairs={{0,1},{1,0},{2,3},{3,2},{4,5},{5,4},{6,7},{7,6},{8,9},{9,8},{10,11... | collective-permute-start | bytes 36872 | tf_op jit(solution)/shard_map/ppermute | solution.py:864
  835.7 91.7 %collective-permute-start.66 = (bf16[384,2048]{1,0:T(8,128)(2,1)}, bf16[384,2048]{1,0:T(8,128)(2,1)S(1)}, u32[]{:S(2)}, u32[]{:S(2)}) collective-permute-start(bf16[384,2048]{1,0:T(8,128)(2,1)} %add_convert_fusion.11), channel_id=1, source_target_pairs={{0,1},{3,2},{4,5},{7,6},{8,9},{11,10},{12,13},{15,14},{16,17},{19,... | collective-permute-start | bytes 4718600 | tf_op jit(solution)/shard_map/ppermute | solution.py:651
  844.7 44.3 %collective-permute-start.45 = (bf16[256,1536]{1,0:T(8,128)(2,1)S(1)}, bf16[256,1536]{1,0:T(8,128)(2,1)S(1)}, u32[]{:S(2)}, u32[]{:S(2)}) collective-permute-start(bf16[256,1536]{1,0:T(8,128)(2,1)S(1)} %copy-done.80), channel_id=1, source_target_pairs={{2,0},{0,1},{6,2},{4,3},{3,4},{1,5},{7,6},{5,7},{10,8},{8,9},{14,1... | collective-permute-start | bytes 2359304 | tf_op jit(solution)/shard_map/ppermute | solution.py:595
  848.6 43.6 %collective-permute-start.52 = (bf16[384,1152]{1,0:T(8,128)(2,1)S(1)}, bf16[384,1152]{1,0:T(8,128)(2,1)S(1)}, u32[]{:S(2)}, u32[]{:S(2)}) collective-permute-start(bf16[384,1152]{1,0:T(8,128)(2,1)S(1)} %slice.343), channel_id=1, source_target_pairs={{0,8},{4,12},{8,0},{12,4},{16,24},{20,28},{24,16},{28,20},{1,9},{5... | collective-permute-start | bytes 2654216 | tf_op jit(solution)/shard_map/ppermute | solution.py:555
  851.3 45.8 %collective-permute-start.47 = (bf16[384,1152]{1,0:T(8,128)(2,1)S(1)}, bf16[384,1152]{1,0:T(8,128)(2,1)S(1)}, u32[]{:S(2)}, u32[]{:S(2)}) collective-permute-start(bf16[384,1152]{1,0:T(8,128)(2,1)S(1)} %slice.340), channel_id=1, source_target_pairs={{0,16},{4,20},{8,24},{12,28},{16,0},{20,4},{24,8},{28,12},{1,17},{... | collective-permute-start | bytes 2654216 | tf_op jit(solution)/shard_map/ppermute | solution.py:555
  897.4 29.0 %collective-permute-start.48 = (bf16[384,1152]{1,0:T(8,128)(2,1)S(1)}, bf16[384,1152]{1,0:T(8,128)(2,1)S(1)}, u32[]{:S(2)}, u32[]{:S(2)}) collective-permute-start(bf16[384,1152]{1,0:T(8,128)(2,1)S(1)} %add_convert_fusion.17), channel_id=1, source_target_pairs={{0,1},{3,2},{4,5},{7,6},{8,9},{11,10},{12,13},{15,14},{16,17},{19,... | collective-permute-start | bytes 2654216 | tf_op jit(solution)/shard_map/ppermute | solution.py:651
  907.2 24.8 %collective-permute-start.72 = (bf16[384,2048]{1,0:T(8,128)(2,1)S(1)}, bf16[384,2048]{1,0:T(8,128)(2,1)S(1)}, u32[]{:S(2)}, u32[]{:S(2)}) collective-permute-start(bf16[384,2048]{1,0:T(8,128)(2,1)S(1)} %add_convert_fusion.7), channel_id=1, source_target_pairs={{1,2},{2,1},{5,6},{6,5},{9,10},{10,9},{13,14},{14,13},{17,18},{18,... | collective-permute-start | bytes 4718600 | tf_op jit(solution)/shard_map/ppermute | solution.py:652
  929.1 60.7 %collective-permute-start.55 = (bf16[384,1152]{1,0:T(8,128)(2,1)S(1)}, bf16[384,1152]{1,0:T(8,128)(2,1)S(1)}, u32[]{:S(2)}, u32[]{:S(2)}) collective-permute-start(bf16[384,1152]{1,0:T(8,128)(2,1)S(1)} %add_convert_fusion.12), channel_id=1, source_target_pairs={{1,0},{2,3},{5,4},{6,7},{9,8},{10,11},{13,12},{14,15},{17,16},{18,... | collective-permute-start | bytes 2654216 | tf_op jit(solution)/shard_map/ppermute | solution.py:653
  930.6 78.1 %collective-permute-start.50 = (bf16[384,1152]{1,0:T(8,128)(2,1)S(1)}, bf16[384,1152]{1,0:T(8,128)(2,1)S(1)}, u32[]{:S(2)}, u32[]{:S(2)}) collective-permute-start(bf16[384,1152]{1,0:T(8,128)(2,1)S(1)} %add_convert_fusion.15), channel_id=1, source_target_pairs={{1,0},{2,3},{5,4},{6,7},{9,8},{10,11},{13,12},{14,15},{17,16},{18,... | collective-permute-start | bytes 2654216 | tf_op jit(solution)/shard_map/ppermute | solution.py:653
  932.6 109.9 %collective-permute-start.73 = (bf16[384,2048]{1,0:T(8,128)(2,1)S(1)}, bf16[384,2048]{1,0:T(8,128)(2,1)S(1)}, u32[]{:S(2)}, u32[]{:S(2)}) collective-permute-start(bf16[384,2048]{1,0:T(8,128)(2,1)S(1)} %add_convert_fusion.6), channel_id=1, source_target_pairs={{1,0},{2,3},{5,4},{6,7},{9,8},{10,11},{13,12},{14,15},{17,16},{18,... | collective-permute-start | bytes 4718600 | tf_op jit(solution)/shard_map/ppermute | solution.py:653
  934.5 141.7 %collective-permute-start.68 = (bf16[384,2048]{1,0:T(8,128)(2,1)S(1)}, bf16[384,2048]{1,0:T(8,128)(2,1)S(1)}, u32[]{:S(2)}, u32[]{:S(2)}) collective-permute-start(bf16[384,2048]{1,0:T(8,128)(2,1)S(1)} %add_convert_fusion.9), channel_id=1, source_target_pairs={{1,0},{2,3},{5,4},{6,7},{9,8},{10,11},{13,12},{14,15},{17,16},{18,... | collective-permute-start | bytes 4718600 | tf_op jit(solution)/shard_map/ppermute | solution.py:653
  1009.3 69.6 %collective-permute-start.56 = (bf16[192,2304]{1,0:T(8,128)(2,1)S(1)}, bf16[192,2304]{1,0:T(8,128)(2,1)S(1)}, u32[]{:S(2)}, u32[]{:S(2)}) collective-permute-start(bf16[192,2304]{1,0:T(8,128)(2,1)S(1)} %constant_dynamic-slice_fusion.9), channel_id=1, source_target_pairs={{0,4},{4,0},{8,12},{12,8},{16,20},{20,16},{24,28},{28,24},{1,5},{5... | collective-permute-start | bytes 2654216 | tf_op jit(solution)/shard_map/ppermute | solution.py:555
  1077.6 30.9 %collective-permute-start.74 = (bf16[192,4096]{1,0:T(8,128)(2,1)}, bf16[192,4096]{1,0:T(8,128)(2,1)}, u32[]{:S(2)}, u32[]{:S(2)}) collective-permute-start(bf16[192,4096]{1,0:T(8,128)(2,1)} %fusion.46), channel_id=1, source_target_pairs={{0,4},{4,0},{8,12},{12,8},{16,20},{20,16},{24,28},{28,24},{1,5},{5... | collective-permute-start | bytes 4718600 | tf_op jit(solution)/shard_map/ppermute | solution.py:555
  (128 other events, 2619.4 us)

commit v2 on v0

--- a/solution.py
+++ b/solution.py
@@ -3,6 +3,8 @@
 import jax
 import jax.numpy as jnp
 from jax import lax
+from jax.experimental import pallas as pl
+from jax.experimental.pallas import tpu as pltpu
 from jax.sharding import PartitionSpec as P
 
 HEADS = 24
@@ -392,6 +394,939 @@
     )
 
 
+BLK = 256
+LOG2E = 1.4426950408889634
+
+
+def swap_halves(v):
+    lane = lax.broadcasted_iota(jnp.int32, v.shape, 1)
+    width = v.shape[1]
+    up = pltpu.roll(v, width - 32, axis=1)
+    down = pltpu.roll(v, 32, axis=1)
+    return jnp.where(lane % 64 < 32, up, down)
+
+
+def nt(a, b):
+    return lax.dot_general(a, b, (((1,), (1,)), ((), ())), preferred_element_type=jnp.float32)
+
+
+def tn(a, b):
+    return lax.dot_general(a, b, (((0,), (0,)), ((), ())), preferred_element_type=jnp.float32)
+
+
+def attn_fwd_kernel(count_ref, q_ref, k_ref, v_ref, cos_ref, sin_ref, start_ref,
+                    qr_ref, kr_ref, vr_ref, mixed_ref, lse_ref):
+    pair = pl.program_id(0)
+    cosine, sine = cos_ref[...], sin_ref[...]
+    q = q_ref[...]
+    qr_ref[...] = (q * cosine + swap_halves(q) * sine).astype(jnp.bfloat16)
+    k = k_ref[...]
+    kr_ref[...] = (k * cosine + swap_halves(k) * sine).astype(jnp.bfloat16)
+    vr_ref[...] = v_ref[...].astype(jnp.bfloat16)
+    length = q_ref.shape[0]
+    lane = lax.broadcasted_iota(jnp.int32, (BLK, 128), 1)
+
+    def one_block(i, carry):
+        row0 = pl.multiple_of(i * BLK, BLK)
+        rows = pl.ds(row0, BLK)
+        for n in range(1, length // BLK + 1):
+            @pl.when(count_ref[i] == n)
+            def _():
+                width = n * BLK
+                key0 = pl.multiple_of((i - (n - 1)) * BLK, BLK)
+                keys = pl.ds(key0, width)
+                place = key0 + lax.broadcasted_iota(jnp.int32, (BLK, width), 1)
+                own = row0 + lax.broadcasted_iota(jnp.int32, (BLK, width), 0)
+                allowed = (place >= start_ref[rows, :]) & (place <= own)
+                for half in range(2):
+                    cols = slice(64 * half, 64 * half + 64)
+                    s = nt(qr_ref[rows, cols] * jnp.bfloat16(0.125), kr_ref[keys, cols])
+                    s = jnp.where(allowed, s, -1e30)
+                    peak = jnp.max(s, axis=-1, keepdims=True)
+                    expo = jnp.exp(s - peak)
+                    total = jnp.sum(expo, axis=-1, keepdims=True)
+                    out = jnp.dot(expo.astype(jnp.bfloat16), vr_ref[keys, cols],
+                                  preferred_element_type=jnp.float32)
+                    mixed_ref[rows, cols] = (out / total).astype(jnp.bfloat16)
+                    lse = peak + jnp.log(total)
+                    old = lse_ref[rows, :]
+                    lse_ref[rows, :] = jnp.where(lane == 2 * pair + half, lse, old)
+        return carry
+
+    lax.fori_loop(0, length // BLK, one_block, 0)
+
+
+def attn_fwd(qkv, cosine, sine, start, counts):
+    length, width = qkv.shape[0], qkv.shape[1] // 3
+    pairs = width // 128
+    col = pl.BlockSpec((length, 128), lambda p, c: (0, p))
+    key_col = pl.BlockSpec((length, 128), lambda p, c: (0, pairs + p))
+    value_col = pl.BlockSpec((length, 128), lambda p, c: (0, 2 * pairs + p))
+    fixed = pl.BlockSpec((length, 128), lambda p, c: (0, 0))
+    scol = pl.BlockSpec((length, 1), lambda p, c: (0, 0))
+    low = jax.ShapeDtypeStruct((length, width), jnp.bfloat16)
+    return pl.pallas_call(
+        attn_fwd_kernel,
+        grid_spec=pltpu.PrefetchScalarGridSpec(
+            num_scalar_prefetch=1, grid=(pairs,),
+            in_specs=[col, key_col, value_col, fixed, fixed, scol],
+            out_specs=[col, col, col, col, fixed],
+        ),
+        out_shape=[low, low, low, low, jax.ShapeDtypeStruct((length, 128), jnp.float32)],
+        compiler_params=pltpu.CompilerParams(vmem_limit_bytes=40 * 1024 * 1024),
+        cost_estimate=pl.CostEstimate(flops=8 * length * length * width // 2, bytes_accessed=20 * length * width,
+                                      transcendentals=length * length * pairs),
+        name="attn_fwd",
+    )(counts, qkv, qkv, qkv, cosine, sine, start)
+
+
+def attn_bwd_kernel(count_ref, q_ref, k_ref, v_ref, do_ref, cos_ref, sin_ref, start_ref, lse_ref,
+                    dq_ref, dk_ref, dv_ref, dk_acc, dv_acc, dq_acc):
+    length = q_ref.shape[0]
+    dk_acc[...] = jnp.zeros_like(dk_acc)
+    dv_acc[...] = jnp.zeros_like(dv_acc)
+
+    def one_block(i, carry):
+        row0 = pl.multiple_of(i * BLK, BLK)
+        rows = pl.ds(row0, BLK)
+        for n in range(1, length // BLK + 1):
+            @pl.when(count_ref[i] == n)
+            def _():
+                width = n * BLK
+                key0 = pl.multiple_of((i - (n - 1)) * BLK, BLK)
+                keys = pl.ds(key0, width)
+                place = key0 + lax.broadcasted_iota(jnp.int32, (width, BLK), 0)
+                own = row0 + lax.broadcasted_iota(jnp.int32, (width, BLK), 1)
+                allowed = (place >= start_ref[:, rows]) & (place <= own)
+                for half in range(2):
+                    cols = slice(64 * half, 64 * half + 64)
+                    q = q_ref[rows, cols] * jnp.bfloat16(0.125)
+                    k = k_ref[keys, cols]
+                    do = do_ref[rows, cols]
+                    s = nt(k, q)
+                    probs = jnp.where(allowed, jnp.exp(s - lse_ref[0, half:half + 1, rows]), 0.0)
+                    gp = nt(v_ref[keys, cols], do)
+                    inner = jnp.sum(probs * gp, axis=0, keepdims=True)
+                    gs = (probs * (gp - inner)).astype(jnp.bfloat16)
+                    dv_acc[keys, cols] += jnp.dot(probs.astype(jnp.bfloat16), do,
+                                                  preferred_element_type=jnp.float32)
+                    dk_acc[keys, cols] += jnp.dot(gs, q, preferred_element_type=jnp.float32)
+                    dq_acc[rows, cols] = tn(gs, k) * 0.125
+        return carry
+
+    lax.fori_loop(0, length // BLK, one_block, 0)
+    cosine, sine = cos_ref[...], sin_ref[...]
+    g = dq_acc[...]
+    dq_ref[...] = (g * cosine - swap_halves(g) * sine).astype(jnp.bfloat16)
+    g = dk_acc[...]
+    dk_ref[...] = (g * cosine - swap_halves(g) * sine).astype(jnp.bfloat16)
+    dv_ref[...] = dv_acc[...].astype(jnp.bfloat16)
+
+
+def attn_bwd(q, k, v, grad, cosine, sine, start_row, counts, lse):
+    length, width = q.shape
+    pairs = width // 128
+    col = pl.BlockSpec((length, 128), lambda p, c: (0, p))
+    fixed = pl.BlockSpec((length, 128), lambda p, c: (0, 0))
+    srow = pl.BlockSpec((1, length), lambda p, c: (0, 0))
+    lrow = pl.BlockSpec((1, 2, length), lambda p, c: (p, 0, 0))
+    low = jax.ShapeDtypeStruct((length, width), jnp.bfloat16)
+    return pl.pallas_call(
+        attn_bwd_kernel,
+        grid_spec=pltpu.PrefetchScalarGridSpec(
+            num_scalar_prefetch=1, grid=(pairs,),
+            in_specs=[col, col, col, col, fixed, fixed, srow, lrow],
+            out_specs=[col, col, col],
+            scratch_shapes=[pltpu.VMEM((length, 128), jnp.float32)] * 3,
+        ),
+        out_shape=[low, low, low],
+        compiler_params=pltpu.CompilerParams(vmem_limit_bytes=40 * 1024 * 1024),
+        cost_estimate=pl.CostEstimate(flops=20 * length * length * width // 2, bytes_accessed=14 * length * width,
+                                      transcendentals=length * length * pairs),
+        name="attn_bwd",
+    )(counts, q, k, v, grad, cosine, sine, start_row, lse)
+
+
+FAST_MESH = {"dp": 8, "seq": 4}
+ANY = pl.BlockSpec(memory_space=pl.ANY)
+
+
+class Place:
+    def __init__(self):
+        self.dp, self.z = lax.axis_index("dp"), lax.axis_index("seq")
+        self.core = self.dp % 2
+        self.x = (self.dp // 2) % 2
+        self.y = self.dp // 4
+        self.over_core = self.dp + 1 - 2 * self.core
+        self.over_x = self.dp + 2 - 4 * self.x
+        self.over_y = self.dp + 4 - 8 * self.y
+        self.middle = (self.z == 1) | (self.z == 2)
+
+
+def enter(devices):
+    barrier = pltpu.get_barrier_semaphore()
+    for dp, seq in devices:
+        pl.semaphore_signal(
+            barrier, inc=1, device_id={"dp": dp, "seq": seq}, device_id_type=pl.DeviceIdType.MESH
+        )
+    pl.semaphore_wait(barrier, len(devices))
+
+
+def remote(src, dst, send_sem, recv_sem, dp, seq):
+    return pltpu.make_async_remote_copy(
+        src_ref=src,
+        dst_ref=dst,
+        send_sem=send_sem,
+        recv_sem=recv_sem,
+        device_id={"dp": dp, "seq": seq},
+        device_id_type=pl.DeviceIdType.MESH,
+    )
+
+
+def gather_kernel(
+    tokens, segments, out_grad, gains, w_q, w_k, w_v, w_o, w_gate, w_up, w_down,
+    x_out, seg_out, g_out, gains_out, qkv_out, o_out, ff_out, down_out,
+    send, recv, local, row_send, row_recv, row_local, gain_send, gain_recv,
+):
+    me = Place()
+    rows = tokens.shape[1]
+    plane = [(lax.rem(me.dp + k, 8), me.z) for k in range(1, 8)]
+    column = [
+        (me.dp - me.core + core, lax.rem(me.z + k, 4)) for k in range(1, 4) for core in range(2)
+    ]
+    enter(plane + column)
+    started = []
+
+    def begin(copy):
+        copy.start()
+        started.append(copy)
+
+    streams = ((tokens, x_out), (segments, seg_out), (out_grad, g_out))
+
+    def place_of(ref, seq):
+        return ref.at[pl.ds(rows * seq, rows)] if ref.shape[0] == 4 * rows else ref.at[seq]
+
+    def row_copies(index):
+        source, target = streams[index]
+        for m in range(2):
+            core, seq = me.z // 2, 2 * m + me.core
+            here = (core == me.core) & (seq == me.z)
+
+            @pl.when(here)
+            def _():
+                pltpu.make_async_copy(
+                    source.at[m], place_of(target, me.z), row_local.at[index]
+                ).start()
+
+            @pl.when(jnp.logical_not(here))
+            def _():
+                remote(
+                    source.at[m], place_of(target, me.z), row_send.at[index, m],
+                    row_recv.at[index, me.z % 2], me.dp - me.core + core, seq,
+                ).start()
+
+    def row_wait_send(index):
+        source, target = streams[index]
+        for m in range(2):
+            core, seq = me.z // 2, 2 * m + me.core
+            here = (core == me.core) & (seq == me.z)
+
+            @pl.when(jnp.logical_not(here))
+            def _():
+                remote(
+                    source.at[m], place_of(target, me.z), row_send.at[index, m],
+                    row_recv.at[index, me.z % 2], me.dp - me.core + core, seq,
+                ).wait_send()
+
+    def row_relay(index):
+        source, target = streams[index]
+        for slot in range(2):
+            seq = 2 * me.core + slot
+            block = place_of(target, seq)
+            here = (seq == me.z) & (me.z % 2 == me.core)
+
+            @pl.when(here)
+            def _():
+                pltpu.make_async_copy(block, block, row_local.at[index]).wait()
+
+            @pl.when(jnp.logical_not(here))
+            def _():
+                remote(
+                    block, block, row_send.at[index, slot], row_recv.at[index, slot], me.over_core, me.z
+                ).wait_recv()
+
+            begin(
+                remote(
+                    block, block, row_send.at[index, 2 + slot], row_recv.at[index, 2 + slot],
+                    me.over_core, me.z,
+                )
+            )
+
+    def row_finish(index):
+        source, target = streams[index]
+        for slot in range(2):
+            block = place_of(target, 2 * (1 - me.core) + slot)
+            remote(
+                block, block, row_send.at[index, 2 + slot], row_recv.at[index, 2 + slot], me.over_core, me.z
+            ).wait_recv()
+
+    by_columns = []
+    base = 0
+    for source in (w_q, w_k, w_v):
+        by_columns.append((source, qkv_out, base))
+        base += source.shape[1] // 2
+    by_columns.append((w_gate, ff_out, 0))
+    by_columns.append((w_up, ff_out, w_gate.shape[1] // 2))
+    by_rows = [(w_o, o_out), (w_down, down_out)]
+
+    def column_piece(index, owner):
+        source, target, first = by_columns[index]
+        depth, width = source.shape[0], source.shape[1] // 2
+        return target.at[pl.ds(depth * owner, depth), pl.ds(first, width)]
+
+    def columns_start(index):
+        source, target, first = by_columns[index]
+        width = source.shape[1] // 2
+        mine = column_piece(index, me.dp)
+        for core in range(2):
+            half = source.at[:, pl.ds(width * core, width)]
+            begin(remote(half, mine, send.at[index, core], recv.at[index, me.core],
+                         me.over_x - me.core + core, me.z))
+            begin(remote(half, mine, send.at[index, 2 + core], recv.at[index, 2 + me.core],
+                         me.over_y - me.core + core, me.z))
+
+            @pl.when(core == me.core)
+            def _():
+                pltpu.make_async_copy(half, mine, local.at[index]).start()
+
+            @pl.when(core != me.core)
+            def _():
+                remote(half, mine, send.at[index, 4], recv.at[index, 4], me.over_core, me.z).start()
+
+    def columns_relay(index):
+        piece = column_piece(index, me.over_x - me.core)
+        remote(piece, piece, send.at[index, 5], recv.at[index, 0], me.over_y, me.z).wait_recv()
+        begin(remote(piece, piece, send.at[index, 5], recv.at[index, 5], me.over_y, me.z))
+        piece = column_piece(index, me.over_y - me.core + 1)
+        remote(piece, piece, send.at[index, 6], recv.at[index, 3], me.over_x, me.z).wait_recv()
+        begin(remote(piece, piece, send.at[index, 6], recv.at[index, 6], me.over_x, me.z))
+
+    def columns_finish(index):
+        source, target, first = by_columns[index]
+        width = source.shape[1] // 2
+        corner = me.over_x + me.over_y - me.dp - me.core
+        for slot, owner in (
+            (1, me.over_x - me.core + 1), (2, me.over_y - me.core), (4, me.over_core),
+            (5, corner), (6, corner + 1),
+        ):
+            piece = column_piece(index, owner)
+            remote(piece, piece, send.at[index, 5], recv.at[index, slot], me.over_core, me.z).wait_recv()
+        mine = column_piece(index, me.dp)
+        pltpu.make_async_copy(mine, mine, local.at[index]).wait()
+        half = source.at[:, pl.ds(0, width)]
+        remote(half, mine, send.at[index, 4], recv.at[index, 4], me.over_core, me.z).wait_send()
+
+    def row_piece(which, owner):
+        source, target = by_rows[which]
+        depth = source.shape[0]
+        return target.at[pl.ds(depth * lax.rem(owner, 4), depth), :]
+
+    def rows_start(which):
+        source, target = by_rows[which]
+        index = 5 + which
+        mine = row_piece(which, me.dp)
+        begin(remote(source, mine, send.at[index, 0], recv.at[index, me.core],
+                     me.over_x - me.core + me.y, me.z))
+        begin(remote(source, mine, send.at[index, 1], recv.at[index, 2 + me.core],
+                     me.over_y - me.core + me.y, me.z))
+
+        @pl.when(me.core == me.y)
+        def _():
+            pltpu.make_async_copy(source, mine, local.at[index]).start()
+
+        @pl.when(me.core != me.y)
+        def _():
+            remote(source, mine, send.at[index, 4], recv.at[index, 4], me.over_core, me.z).start()
+
+    def rows_relay(which):
+        index = 5 + which
+
+        @pl.when(me.core == me.y)
+        def _():
+            piece = row_piece(which, me.over_x - me.core)
+            remote(piece, piece, send.at[index, 5], recv.at[index, 0], me.over_y, me.z).wait_recv()
+            remote(piece, piece, send.at[index, 5], recv.at[index, 5], me.over_y, me.z).start()
+
+        @pl.when(me.core != me.y)
+        def _():
+            piece = row_piece(which, me.over_y - me.core + 1)
+            remote(piece, piece, send.at[index, 6], recv.at[index, 3], me.over_x, me.z).wait_recv()
+            remote(piece, piece, send.at[index, 6], recv.at[index, 6], me.over_x, me.z).start()
+
+    def rows_finish(which):
+        source, target = by_rows[which]
+        index = 5 + which
+        corner = me.over_x + me.over_y - me.dp - me.core
+
+        def arrived(slot, owner):
+            piece = row_piece(which, owner)
+            remote(piece, piece, send.at[index, 5], recv.at[index, slot], me.over_core, me.z).wait_recv()
+
+        def left(slot):
+            piece = row_piece(which, me.dp)
+            remote(source, piece, send.at[index, slot], recv.at[index, slot], me.over_core, me.z).wait_send()
+
+        @pl.when(me.core == me.y)
+        def _():
+            arrived(1, me.over_x - me.core + 1)
+            arrived(4, me.over_core)
+            mine = row_piece(which, me.dp)
+            pltpu.make_async_copy(source, mine, local.at[index]).wait()
+            left(5)
+
+        @pl.when(me.core != me.y)
+        def _():
+            arrived(2, me.over_y - me.core)
+            arrived(5, corner)
+            arrived(6, corner + 1)
+            left(4)
+            left(6)
+
+    row_copies(0)
+    row_copies(1)
+    for index in range(3):
+        columns_start(index)
+    for k in range(1, 8):
+        begin(remote(gains, gains_out.at[me.dp], gain_send.at[k - 1], gain_recv.at[k - 1],
+                     lax.rem(me.dp + k, 8), me.z))
+    pltpu.make_async_copy(gains, gains_out.at[me.dp], gain_recv.at[7]).start()
+    rows_start(0)
+    row_copies(2)
+    for index in range(3):
+        columns_relay(index)
+    columns_start(3)
+    rows_relay(0)
+    columns_start(4)
+    row_relay(0)
+    row_relay(1)
+    columns_relay(3)
+    rows_start(1)
+    columns_relay(4)
+    row_relay(2)
+    rows_relay(1)
+    for index in range(5):
+        columns_finish(index)
+    for which in range(2):
+        rows_finish(which)
+    for index in range(3):
+        row_finish(index)
+        row_wait_send(index)
+    for k in range(1, 8):
+        piece = gains_out.at[lax.rem(me.dp + 8 - k, 8)]
+        remote(piece, piece, gain_send.at[k - 1], gain_recv.at[k - 1], me.over_core, me.z).wait_recv()
+    pltpu.make_async_copy(gains, gains_out.at[me.dp], gain_recv.at[7]).wait()
+    for copy in started:
+        copy.wait_send()
+
+
+def gather_all(tokens, segments, out_grad, gains, weights):
+    rows, width = tokens.shape[1], tokens.shape[2]
+    ff = weights[4].shape[1]
+    low = jnp.bfloat16
+    shapes = [
+        jax.ShapeDtypeStruct((4 * rows, width), low),
+        jax.ShapeDtypeStruct((4,) + segments.shape[1:], jnp.int32),
+        jax.ShapeDtypeStruct((4 * rows, width), low),
+        jax.ShapeDtypeStruct((8,) + gains.shape, low),
+        jax.ShapeDtypeStruct((width, 3 * width // 2), low),
+        jax.ShapeDtypeStruct((width // 2, width), low),
+        jax.ShapeDtypeStruct((width, ff), low),
+        jax.ShapeDtypeStruct((ff // 2, width), low),
+    ]
+    dma = pltpu.SemaphoreType.DMA
+    return pl.pallas_call(
+        gather_kernel,
+        in_specs=[ANY] * 11,
+        out_specs=[ANY] * 8,
+        out_shape=shapes,
+        scratch_shapes=[
+            dma((7, 7)), dma((7, 7)), dma((7,)), dma((3, 4)), dma((3, 4)), dma((3,)), dma((7,)), dma((8,)),
+        ],
+        compiler_params=pltpu.CompilerParams(collective_id=0, has_side_effects=True),
+        cost_estimate=pl.CostEstimate(flops=0, bytes_accessed=500_000_000, transcendentals=0),
+        name="gather_all",
+    )(tokens, segments, out_grad, gains, *weights)
+
+
+class ColumnJob:
+    def __init__(self, me, refs, source, target, first, width, half, x_first):
+        self.me, self.refs, self.x_first = me, refs, x_first
+        self.source, self.target = source, target
+        self.cols = pl.ds(first, width)
+        which, inside = first // half, first % half
+        self.out_first, self.half, self.width = 2 * half * which + inside, half, width
+        self.rows = source.shape[0] // 4
+
+    def chip_rows(self, x, y):
+        return self.source.at[pl.ds(self.rows * (2 * y + x), self.rows), self.cols]
+
+    def first_copies(self, sends_only=False):
+        me, (got, keep) = self.me, (self.refs[0], self.refs[1])
+        copies, loads = [], []
+        for k in range(2):
+            part = pl.ds(self.rows * k, self.rows)
+            if self.x_first:
+                sent, kept, to = self.chip_rows(1 - me.x, k), self.chip_rows(me.x, k), me.over_x
+            else:
+                sent, kept, to = self.chip_rows(k, 1 - me.y), self.chip_rows(k, me.y), me.over_y
+            copies.append(remote(sent, got.at[part], self.sem(0, k), self.sem(1, k), to, me.z))
+            if not sends_only:
+                loads.append(pltpu.make_async_copy(kept, keep.at[part], self.sem(2, k)))
+        return copies, loads
+
+    def sem(self, kind, k):
+        return self.refs[4].at[kind, k]
+
+    def second_copy(self):
+        me, (got, keep, second) = self.me, self.refs[:3]
+        at, to = (me.y, me.over_y) if self.x_first else (me.x, me.over_x)
+        part = keep.at[pl.ds(self.rows * (1 - at), self.rows)]
+        return remote(part, second, self.sem(0, 2), self.sem(1, 2), to, me.z)
+
+    def start(self):
+        for copy in sum(self.first_copies(), []):
+            copy.start()
+
+    def pass_second(self):
+        copies, loads = self.first_copies()
+        for k in range(2):
+            loads[k].wait()
+            copies[k].wait_recv()
+        got, keep = self.refs[:2]
+        add_rows(keep, 0, got, 2 * self.rows)
+        self.second_copy().start()
+
+    def reduce_plane(self):
+        me, (got, keep, second) = self.me, self.refs[:3]
+        at = me.y if self.x_first else me.x
+        self.second_copy().wait_recv()
+        add_rows(second, self.rows * at, keep, self.rows)
+
+    active = None
+
+    def out_piece(self, row_first, rows, core):
+        first = pl.multiple_of(self.out_first + self.half * core, 128)
+        return self.target.at[pl.ds(row_first, rows), pl.ds(first, self.width)]
+
+    def last_copy(self, final):
+        me, rows = self.me, self.rows // 2
+        part = final.at[pl.ds(rows * (1 - me.core), rows)]
+        return remote(
+            part, self.out_piece(0, rows, me.core), self.sem(0, 3), self.sem(1, 3), me.over_core, me.z
+        )
+
+    def own_copy(self, final):
+        me, rows = self.me, self.rows // 2
+        part = final.at[pl.ds(rows * me.core, rows)]
+        return pltpu.make_async_copy(part, self.out_piece(0, rows, me.core), self.sem(2, 0))
+
+    def finish(self, final):
+        self.last_copy(final).start()
+        self.own_copy(final).start()
+
+    def drain(self, final):
+        me, rows = self.me, self.rows // 2
+        for copy in self.first_copies(True)[0]:
+            copy.wait_send()
+        self.second_copy().wait_send()
+        self.last_copy(final).wait_send()
+        self.own_copy(final).wait()
+        part = final.at[pl.ds(rows * me.core, rows)]
+        remote(
+            part, self.out_piece(0, rows, 1 - me.core), self.sem(0, 3), self.sem(1, 3), me.over_core, me.z
+        ).wait_recv()
+
+
+class RowJob:
+    def __init__(self, me, refs, source, target, first, width):
+        self.me, self.refs = me, refs
+        self.source, self.target = source, target
+        self.cols = pl.ds(first, width)
+        self.rows = source.shape[0] // 2
+        self.active = me.core == me.y
+
+    sem = ColumnJob.sem
+
+    def first_copy(self):
+        me, got = self.me, self.refs[0]
+        sent = self.source.at[pl.ds(self.rows * (1 - me.x), self.rows), self.cols]
+        return remote(sent, got, self.sem(0, 0), self.sem(1, 0), me.over_x, me.z)
+
+    def load(self):
+        kept = self.source.at[pl.ds(self.rows * self.me.x, self.rows), self.cols]
+        return pltpu.make_async_copy(kept, self.refs[1], self.sem(2, 0))
+
+    def second_copy(self):
+        me, (got, keep, second) = self.me, self.refs[:3]
+        return remote(keep, second, self.sem(0, 2), self.sem(1, 2), me.over_y, me.z)
+
+    def start(self):
+        self.first_copy().start()
+        self.load().start()
+
+    def pass_second(self):
+        self.load().wait()
+        self.first_copy().wait_recv()
+        got, keep = self.refs[:2]
+        add_rows(keep, 0, got, self.rows)
+
+        @pl.when(jnp.logical_not(self.active))
+        def _():
+            self.second_copy().start()
+
+    def reduce_plane(self):
+        got, keep, second = self.refs[:3]
+
+        @pl.when(self.active)
+        def _():
+            self.second_copy().wait_recv()
+            add_rows(second, 0, keep, self.rows)
+
+    def last_copy(self, final):
+        me, rows = self.me, self.rows // 2
+        part = final.at[pl.ds(rows * (1 - me.core), rows)]
+        target = self.target.at[:, self.cols]
+        return remote(part, target, self.sem(0, 3), self.sem(1, 3), me.over_core, me.z)
+
+    def own_copy(self, final):
+        me, rows = self.me, self.rows // 2
+        part = final.at[pl.ds(rows * me.core, rows)]
+        return pltpu.make_async_copy(part, self.target.at[:, self.cols], self.sem(2, 1))
+
+    def finish(self, final):
+        @pl.when(self.active)
+        def _():
+            self.last_copy(final).start()
+            self.own_copy(final).start()
+
+    def drain(self, final):
+        self.first_copy().wait_send()
+
+        @pl.when(self.active)
+        def _():
+            self.last_copy(final).wait_send()
+            self.own_copy(final).wait()
+
+        @pl.when(jnp.logical_not(self.active))
+        def _():
+            self.second_copy().wait_send()
+            self.last_copy(final).wait_recv()
+
+
+def add_rows(target, first, other, rows, step=64):
+    def chunk(k, carry):
+        at = pl.multiple_of(k * step, step)
+        source = pl.multiple_of(first + k * step, step)
+        target[pl.ds(at, step), :] += other[pl.ds(source, step), :]
+        return carry
+
+    lax.fori_loop(0, rows // step, chunk, 0)
+
+
+def both(active, condition):
+    return condition if active is None else active & condition
+
+
+def final_of(job):
+    return job.refs[0].at[pl.ds(0, job.rows)]
+
+
+def seq_copy(job, step):
+    me, total, over, sem = job.me, job.refs[2], job.refs[3], job.refs[5]
+    inner = me.z + 1 - 2 * (me.z // 2)
+    opposite = 3 - me.z
+    outer = 3 * (me.z // 2)
+    if step == 0:
+        return remote(total, over.at[0], sem.at[0, 0], sem.at[1, 0], me.dp, inner)
+    if step == 1:
+        return remote(total, over.at[1], sem.at[0, 1], sem.at[1, 1], me.dp, opposite)
+    return remote(final_of(job), final_of(job), sem.at[0, 2], sem.at[1, 2], me.dp, outer)
+
+
+def plane_and_seq_first(job):
+    job.reduce_plane()
+
+    @pl.when(both(job.active, jnp.logical_not(job.me.middle)))
+    def _():
+        seq_copy(job, 0).start()
+
+
+def seq_second(job):
+    @pl.when(both(job.active, job.me.middle))
+    def _():
+        seq_copy(job, 0).wait_recv()
+        add_rows(job.refs[2], 0, job.refs[3].at[0], job.rows)
+        seq_copy(job, 1).start()
+
+
+def seq_third(job):
+    @pl.when(both(job.active, job.me.middle))
+    def _():
+        seq_copy(job, 1).wait_recv()
+        final, total, over, step = final_of(job), job.refs[2], job.refs[3].at[1], 64
+
+        def chunk(k, carry):
+            part = pl.ds(pl.multiple_of(k * step, step), step)
+            final[part, :] = total[part, :] + over[part, :]
+            return carry
+
+        lax.fori_loop(0, job.rows // step, chunk, 0)
+        seq_copy(job, 2).start()
+
+
+def finish(job):
+    @pl.when(both(job.active, jnp.logical_not(job.me.middle)))
+    def _():
+        seq_copy(job, 2).wait_recv()
+
+    job.finish(final_of(job))
+
+
+def drain(job):
+    job.drain(final_of(job))
+
+    @pl.when(both(job.active, jnp.logical_not(job.me.middle)))
+    def _():
+        seq_copy(job, 0).wait_send()
+
+    @pl.when(both(job.active, job.me.middle))
+    def _():
+        seq_copy(job, 1).wait_send()
+        seq_copy(job, 2).wait_send()
+
+
+STAGES = (
+    (0, lambda job: job.start()),
+    (2, lambda job: job.pass_second()),
+    (3, plane_and_seq_first),
+    (4, seq_second),
+    (5, seq_third),
+    (6, finish),
+)
+
+
+def run_jobs(jobs):
+    for tick in range(len(jobs) + STAGES[-1][0]):
+        for late, stage in reversed(STAGES):
+            if 0 <= tick - late < len(jobs):
+                stage(jobs[tick - late])
+    for job in jobs:
+        drain(job)
+
+
+def job_plan(d_model, ff):
+    half = d_model // 2
+    down = [("down", 384 * k, 384, True) for k in range(d_model // 384)]
+    wide_ff = [("ff", 512 * k, 512, False) for k in range(ff // 512)]
+    rest = [("o", half * k, half, True) for k in range(2)]
+    qkv = [("qkv", 384 * k, 384, k % 2 == 1) for k in range(3 * half // 384)]
+    return [job for pair in zip(down, wide_ff) for job in pair] + wide_ff[len(down) :] + rest + qkv
+
+
+def reduce_all(g_qkv, g_o, g_ff, g_down):
+    d_model, ff = g_o.shape[1], g_ff.shape[1]
+    plan = job_plan(d_model, ff)
+    sources = {"qkv": g_qkv, "o": g_o, "ff": g_ff, "down": g_down}
+    names = ("qkv", "o", "ff", "down")
+    halves = {"qkv": d_model // 2, "ff": ff // 2}
+    outs = [
+        jax.ShapeDtypeStruct((d_model // 8, 3 * d_model), jnp.bfloat16),
+        jax.ShapeDtypeStruct((d_model // 8, d_model), jnp.bfloat16),
+        jax.ShapeDtypeStruct((d_model // 8, 2 * ff), jnp.bfloat16),
+        jax.ShapeDtypeStruct((ff // 8, d_model), jnp.bfloat16),
+    ]
+    scratch = []
+    dma = pltpu.SemaphoreType.DMA
+    for name, first, width, x_first in plan:
+        by_columns = name in halves
+        rows = sources[name].shape[0] // (4 if by_columns else 2)
+        many = 2 * rows if by_columns else rows
+
+        def vmem(*shape):
+            return pltpu.VMEM(shape, jnp.bfloat16)
+
+        scratch += [
+            vmem(many, width), vmem(many, width), vmem(rows, width), vmem(2, rows, width), dma((3, 4)), dma((2, 3)),
+        ]
+
+    def kernel(*refs):
+        source = dict(zip(names, refs[:4]))
+        target = dict(zip(names, refs[4:8]))
+        buffers = refs[8:]
+        me = Place()
+        enter(
+            [(me.over_core, me.z)]
+            + [(me.over_x, me.z), (me.over_y, me.z)]
+            + [(me.dp, lax.rem(me.z + k, 4)) for k in range(1, 4)]
+        )
+        jobs = []
+        for k, (name, first, width, x_first) in enumerate(plan):
+            own = buffers[6 * k : 6 * k + 6]
+            if name in halves:
+                jobs.append(
+                    ColumnJob(me, own, source[name], target[name], first, width, halves[name], x_first)
+                )
+            else:
+                jobs.append(RowJob(me, own, source[name], target[name], first, width))
+        run_jobs(jobs)
+
+    return pl.pallas_call(
+        kernel,
+        in_specs=[ANY] * 4,
+        out_specs=[ANY] * 4,
+        out_shape=outs,
+        scratch_shapes=scratch,
+        compiler_params=pltpu.CompilerParams(
+            collective_id=1, has_side_effects=True, vmem_limit_bytes=61 * 1024 * 1024
+        ),
+        cost_estimate=pl.CostEstimate(flops=0, bytes_accessed=800_000_000, transcendentals=0),
+        name="reduce_all",
+    )(g_qkv, g_o, g_ff, g_down)
+
+
+def swap_core(value):
+    return lax.ppermute(value, "dp", [(i, i ^ 1) for i in range(8)])
+
+
+def reshard_pairs(turn):
+    pairs = []
+    for d in range(8):
+        for z in range(4):
+            target = ((d & 6) | (z >> 1)) * 4 + 2 * ((turn + z) % 2) + (d & 1)
+            pairs.append((target, d * 4 + z))
+    return pairs
+
+
+def from_sequence(half, seq_at):
+    rows = half.shape[0] // 2
+    early = seq_at < 2
+    got = []
+    for turn in range(2):
+        block = jnp.where(
+            early, half[rows * turn : rows * (turn + 1)], half[rows * (1 - turn) : rows * (2 - turn)]
+        )
+        got.append(lax.ppermute(block, ("dp", "seq"), reshard_pairs(turn)))
+    even = (seq_at & 1) == 0
+    return jnp.stack([jnp.where(even, got[0], got[1]), jnp.where(even, got[1], got[0])])
+
+
+def dot(a, b):
+    return jnp.dot(a, b, preferred_element_type=jnp.float32)
+
+
+def low(value):
+    return value.astype(jnp.bfloat16)
+
+
+def wide(value):
+    return value.astype(jnp.float32)
+
+
+def column_device(
+    tokens, segment_ids, out_grad, w_q, w_k, w_v, w_o, w_gate, w_up, w_down, gain_attn, gain_ffn
+):
+    dp_at, seq_at = lax.axis_index("dp"), lax.axis_index("seq")
+    core = dp_at & 1
+    rows, width = tokens.shape[1], tokens.shape[2]
+    own_width = width // 2
+    length = 4 * rows
+    pad = -gain_attn.shape[0] % 128
+    gains = jnp.pad(jnp.stack([gain_attn, gain_ffn]), ((0, 0), (0, pad)))
+    x_low, docs, grad_branch, gains, full_qkv, full_o, full_ff, full_down = gather_all(
+        tokens, segment_ids.reshape(2, 1, rows), out_grad, gains,
+        (w_q, w_k, w_v, w_o, w_gate, w_up, w_down),
+    )
+    docs = docs.reshape(length)
+    gains = wide(gains[:, :, : width // 8].transpose(1, 0, 2).reshape(2, width))
+    gain_a, gain_f = gains[0], gains[1]
+    half_ff = full_ff.shape[1] // 2
+
+    place = jnp.arange(length, dtype=jnp.int32)
+    before = jnp.concatenate([docs[:1], docs[:-1]])
+    begins = (place == 0) | (docs != before)
+    start = lax.cummax(jnp.where(begins, place, jnp.zeros_like(place)), axis=0)
+    counts = place[: length // BLK] - start[::BLK] // BLK + 1
+    cosine, sine = rope_tables(place - start, HD // 2)
+    cosine = jnp.concatenate([cosine] * 4, axis=1)
+    sine = jnp.concatenate([-sine, sine, -sine, sine], axis=1)
+
+    def of_core(values, which):
+        return lax.dynamic_slice_in_dim(values, length // 2 * which, length // 2, 0)
+
+    x = wide(x_low)
+    normed = low(rms_norm(x, gain_a))
+    qkv_rows = dot(normed, full_qkv)
+    query, key, value, mixed, logsum = attn_fwd(qkv_rows, cosine, sine, start[:, None], counts)
+    logsum = logsum[:, : own_width // HD].T.reshape(own_width // 128, 2, length)
+    part = dot(mixed, full_o)
+    middle = x + part + wide(swap_core(low(part)))
+    normed_ffn = low(rms_norm(middle, gain_f))
+    gate = dot(normed_ffn, full_ff[:, :half_ff])
+    up_value = dot(normed_ffn, full_ff[:, half_ff:])
+    hidden = low(jax.nn.silu(gate) * up_value)
+    out_other = swap_core(low(dot(of_core(hidden, 1 - core), full_down)))
+    result = of_core(middle, core) + dot(of_core(hidden, core), full_down) + wide(out_other)
+    result = from_sequence(low(result), seq_at)
+
+    g_down = low(tn(hidden, grad_branch))
+    grad_hidden = nt(grad_branch, full_down)
+    sigma = jax.nn.sigmoid(gate)
+    grad_gate = low(grad_hidden * up_value * sigma * (1.0 + gate * (1.0 - sigma)))
+    grad_up = low(grad_hidden * (gate * sigma))
+    grad_ff = jnp.concatenate([grad_gate, grad_up], axis=1)
+    g_ff = low(tn(normed_ffn, grad_ff))
+    grad_nf = nt(grad_ff, full_ff)
+    grad_nf = grad_nf + wide(swap_core(low(grad_nf)))
+    grad_gain_f, grad_middle = norm_backward(middle, gain_f, grad_nf)
+    grad_middle = grad_middle + wide(grad_branch)
+    grad_attn = low(grad_middle)
+
+    grad_mixed = low(nt(grad_attn, full_o))
+    g_o = low(tn(mixed, grad_attn))
+    grad_qkv = jnp.concatenate(
+        attn_bwd(query, key, value, grad_mixed, cosine, sine, start[None, :], counts, logsum), axis=1
+    )
+    g_qkv = low(tn(normed, grad_qkv))
+    normed_other = swap_core(low(nt(of_core(grad_qkv, 1 - core), full_qkv)))
+    grad_normed = nt(of_core(grad_qkv, core), full_qkv) + wide(normed_other)
+    grad_gain_a, grad_rows = norm_backward(of_core(x, core), gain_a, grad_normed)
+    grad_rows = grad_rows + of_core(grad_middle, core)
+    grad_tokens = wide(from_sequence(low(grad_rows), seq_at))
+
+    grad_gain_a = grad_gain_a + swap_core(grad_gain_a)
+    grad_gains = jnp.stack([grad_gain_a, grad_gain_f])
+    for bit in (2, 4):
+        grad_gains = grad_gains + lax.ppermute(grad_gains, "dp", [(i, i ^ bit) for i in range(8)])
+    for bit in (1, 2):
+        grad_gains = grad_gains + lax.ppermute(grad_gains, "seq", [(i, i ^ bit) for i in range(4)])
+    grad_gains = lax.dynamic_slice_in_dim(grad_gains, dp_at * (width // 8), width // 8, 1)
+
+    r_qkv, r_o, r_ff, r_down = reduce_all(g_qkv, g_o, g_ff, g_down)
+    return (
+        result,
+        grad_tokens,
+        wide(r_qkv[:, :width]),
+        wide(r_qkv[:, width : 2 * width]),
+        wide(r_qkv[:, 2 * width :]),
+        wide(r_o),
+        wide(r_ff[:, : w_gate.shape[1]]),
+        wide(r_ff[:, w_gate.shape[1] :]),
+        wide(r_down),
+        grad_gains[0],
+        grad_gains[1],
+    )
+
+
 def solution(mesh):
     placed = (
         P(None, ("dp", "seq"), None),
@@ -408,7 +1343,7 @@
         P("dp"),
     )
     return jax.shard_map(
-        per_device,
+        column_device if dict(mesh.shape) == FAST_MESH else per_device,
         mesh=mesh,
         in_specs=placed,
         out_specs=(

time: 1510 us -> 896 us (0.59)
  waiting for transfers between devices: 674 us -> 57.7 us
  Pallas kernels: 0 us -> 611 us
  matrix products: 427 us -> 157 us
  local copies, waits for them, and re-layouts: 142 us -> 7.84 us
  starting transfers between devices: 76.6 us -> 16.4 us
  blocking collectives: 55 us -> 0 us
  other arithmetic: 86.6 us -> 42.3 us
  loops' own time: 16.8 us -> 0 us
  between operations: 16.8 us -> 1.59 us
    pallas_call x0 -> x4, Pallas kernels: none -> 611 us  [the longest x1 302 us: reduce_all(): pl.pallas_call(kernel, in_specs=[ANY] * 4, out_specs=[ANY] * 4, out_shape...]
    dot_general x70 -> x15, matrix products: 427 us -> 157 us  [the longest x6 63.5 us: dot(): return jnp.dot(a, b, preferred_element_type=jnp.float32)]
    reduce_scatter x7 -> x0, waiting for transfers between devices: 248 us -> none  [the longest x1 95.9 us: per_device(): lax.psum_scatter(summed_all[5].astype(jnp.bfloat16), 'dp', scatter_dimens...]
    all_to_all x16 -> x0, waiting for transfers between devices: 193 us -> none  [the longest x2 37.2 us: per_device(): lax.all_to_all(query_rows, 'seq', split_axis=1, concat_axis=0, tiled=True)]
    psum x1 -> x0, waiting for transfers between devices: 189 us -> none  [per_device(): lax.psum(pieces[0].astype(jnp.bfloat16), 'seq').astype(jnp.float32)]
    all_to_all x16 -> x0, starting transfers between devices: 76.1 us -> none  [the longest x2 18 us: per_device(): lax.all_to_all(key_rows, 'seq', split_axis=1, concat_axis=0, tiled=True)]
    ppermute x0 -> x13, waiting for transfers between devices: none -> 57.7 us  [the longest x2 29.8 us: column_device(): lax.ppermute(grad_gains, 'seq', [(i, i ^ bit) for i in range(4)])]
    all_gather x7 -> x0, waiting for transfers between devices: 39.8 us -> none  [the longest x1 34.2 us: per_device(): lax.all_gather(shards[0], 'dp', axis=0, tiled=True)]
  transfers between devices with their start and end apart: 31 -> 13, of which waited for: 20 -> 3; matrix products, arithmetic and copies ran while one was open for 35% -> 11% of each run, Pallas kernels for 0% -> 34%
where the time goes in v2:
time: 896 us; the launch traced here: 894 us
  Pallas kernels  611 us (68%)
  matrix products  157 us (18%)
  waiting for transfers between devices  57.7 us (6%)
  other arithmetic  42.3 us (5%)
  starting transfers between devices  16.4 us (2%)
    pallas_call x1, Pallas kernels, reduce_all(): pl.pallas_call(kernel, in_specs=[ANY] * 4, out_specs=[ANY] * 4, out_shape...  302 us
    pallas_call x1, Pallas kernels, gather_all(): pl.pallas_call(gather_kernel, in_specs=[ANY] * 11, out_specs=[ANY] * 8, o...  235 us
    dot_general x6, matrix products, dot(): return jnp.dot(a, b, preferred_element_type=jnp.float32)  63.5 us
    dot_general x5, matrix products, nt(): lax.dot_general(a, b, (((1,), (1,)), ((), ())), preferred_element_type=jn...  51.8 us
    dot_general x4, matrix products, tn(): lax.dot_general(a, b, (((0,), (0,)), ((), ())), preferred_element_type=jn...  41.9 us
    pallas_call x1, Pallas kernels, attn_bwd(): pl.pallas_call(attn_bwd_kernel, grid_spec=pltpu.PrefetchScalarGridSpec(nu...  40 us
    pallas_call x1, Pallas kernels, attn_fwd(): pl.pallas_call(attn_fwd_kernel, grid_spec=pltpu.PrefetchScalarGridSpec(nu...  33.9 us
    ppermute x2, waiting for transfers between devices, column_device(): lax.ppermute(grad_gains, 'seq', [(i, i ^ bit) for i in range(4)])  29.8 us
  transfers between devices with their start and end apart: 13, of which 3 were waited for; matrix products, arithmetic and copies ran while one was open for 11% of the time, Pallas kernels for 34%

profile of v2, /device:TPU:0, one launch (start us, length us, event | category | flops | bytes accessed | tf_op | source)
XLA Modules:
  0.0 894.3 jit_solution(13920771519151395449)
XLA Ops:
  0.7 0.7 stack.36
  1.3 0.7 stack.37
  2.0 1.3 reshape.147.segments
  3.2 0.6 fusion.31.gains
  3.8 235.0 %gather_all.1 = (bf16[1024,1536]{1,0:T(8,128)(2,1)}, s32[4,1,256]{2,1,0:T(1,128)}, bf16[1024,1536]{1,0:T(8,128)(2,1)}, bf16[8,2,256]{2,1,0:T(2,128)(2,1)}, bf16[...) custom-call(bf16[2,256,1536]{2,1,0:T(8,128)(2,1)} %tokens.1, ...), custom_call_target="tpu_custom_call" | custom-call | bytes 500000000 | tf_op jit(solution)/shard_map/gather_all/pallas_call | solution.py:847
  238.8 1.2 slice.77
  240.0 1.5 fusion.21
  241.4 0.3 reduce-window.9
  241.8 0.1 slice_reduce_fusion.2
  242.1 0.2 copy.27.start_ref
  242.3 2.6 multiply_reduce_fusion.3
  244.9 0.7 convert_bitcast_fusion
  245.8 1.9 fusion.19
  247.7 0.9 pad_maximum_fusion.4
  248.6 13.2 %fusion.18.q_ref.k_ref.v_ref = f32[1024,2304]{1,0:T(8,128)} fusion(bf16[1536,2304]{1,0:T(8,128)(2,1)} %get-tuple-element.34, bf16[1024,1536]{1,0:T(8,128)(2,1)S(1)} %copy-done.15, f32[1536]{0:T(1024)S(1)} %mul.175, f32[1024]{0:T(1024)S(1)} %add_rsqrt_fusion.1), kind=kOutput, calls=%fused_computation.46 | convolution fusion | flops 7254048768 | bytes 19671040 | tf_op jit(solution)/shard_map/dot_general | solution.py:1224
  261.8 33.9 %attn_fwd.1 = (bf16[1024,768]{1,0:T(8,128)(2,1)S(1)}, bf16[1024,768]{1,0:T(8,128)(2,1)S(1)}, bf16[1024,768]{1,0:T(8,128)(2,1)S(1)}, bf16[1024,768]{1,0:T(8,128)(2,1)S(1)}, f32[1024,128]{1,0:T(8,128)S(1)}) custom-call(s32[4]{0:T(128)S(1)} %subtract_add_fusion.count_ref, f32[1024,2304]{1,0:T(8,128)} %fusion.18.q_ref.k_ref.v_ref, ...), custom_call_target="tpu_custom_call" | custom-call | flops 3221225472 | bytes 15728640 | tf_op jit(solution)/shard_map/attn_fwd/pallas_call | solution.py:468
  295.8 5.1 fusion.36
  300.9 1.9 collective-permute-start
  302.7 5.4 convert_element_type.109
  308.2 0.2 copy.28
  308.5 2.2 multiply_reduce_fusion.6
  310.7 0.6 add_rsqrt_fusion.2
  311.2 12.4 %fusion.38 = f32[1024,2048]{1,0:T(8,128)} fusion(bf16[1024,1536]{1,0:T(8,128)(2,1)} %get-tuple-element.42, bf16[2048,1536]{1,0:T(8,128)(2,1)} %get-tuple-element.38), kind=kOutput, calls=%fused_computation.108 | convolution fusion | flops 6442450944 | bytes 17825792 | tf_op jit(solution)/shard_map/dot_general | solution.py:410
  323.7 5.1 multiply_reduce_fusion.2
  328.8 0.6 multiply_convert_fusion.3
  329.4 2.0 copy-done.14
  331.4 10.8 %fusion.1 = f32[1024,2048]{1,0:T(8,128)} fusion(bf16[1024,1536]{1,0:T(8,128)(2,1)S(1)} %multiply_convert_fusion.3, bf16[1536,4096]{1,0:T(8,128)(2,1)} %get-tuple-element.37), kind=kOutput, calls=%fused_computation.13 | convolution fusion | flops 6442450944 | bytes 17825792 | tf_op jit(solution)/shard_map/dot_general | solution.py:1224
  342.2 18.0 %multiply_convert_fusion.1 = (bf16[1024,2048]{1,0:T(8,128)(2,1)}, bf16[1024,2048]{1,0:T(8,128)(2,1)}, bf16[1024,2048]{1,0:T(8,128)(2,1)}) fusion(f32[1024,2048]{1,0:T(8,128)} %fusion.38, f32[1024,2048]{1,0:T(8,128)} %fusion.1, bf16[1024,1536]{1,0:T(8,128)(2,1)S(1)} %multiply_convert_fusion.3, bf16[1536,4096]{1,0:T(8,128)(2,1)} %get-tuple-element.37), kind=kOutput, calls=%fused_computation.4 | convolution fusion | flops 6473908224 | bytes 38797312 | tf_op jit(solution)/shard_map/dot_general | solution.py:1224
  360.2 8.1 convolution_convert_fusion.5
  368.4 18.9 %fusion.37 = (bf16[1024,1536]{1,0:T(8,128)(2,1)}, f32[1024,1536]{1,0:T(8,128)}) fusion(bf16[1536,4096]{1,0:T(8,128)(2,1)} %get-tuple-element.37, bf16[1024,2048]{1,0:T(8,128)(2,1)} %get-tuple-element.62, bf16[1024,2048]{1,0:T(8,128)(2,1)S(1)} %copy-done.32), kind=kOutput, calls=%fused_computation.107 | convolution fusion | flops 12903251968 | bytes 30408704 | tf_op jit(solution)/shard_map/dot_general | solution.py:410
  387.3 19.3 %convolution_convert_fusion.refs_2_ = bf16[1536,4096]{1,0:T(8,128)(2,1)} fusion(bf16[1024,1536]{1,0:T(8,128)(2,1)S(1)} %multiply_convert_fusion.3, bf16[1024,2048]{1,0:T(8,128)(2,1)} %get-tuple-element.62, bf16[1024,2048]{1,0:T(8,128)(2,1)} %get-tuple-element.61), kind=kOutput, calls=%fused_computation | convolution fusion | flops 12907970560 | bytes 24117248 | tf_op jit(solution)/shard_map/dot_general | solution.py:414
  406.5 0.5 collective-permute-start.4
  407.0 8.4 add_convert_fusion.1
  415.4 0.1 broadcast_select_fusion.3
  415.6 0.7 collective-permute-start.2
  416.3 2.8 collective-permute-start.3
  419.1 8.9 convolution_convert_fusion.2.refs_3_
  428.0 26.2 %collective-permute-done.3 = bf16[256,1536]{1,0:T(8,128)(2,1)S(1)} collective-permute-done((bf16[256,1536]{1,0:T(8,128)(2,1)S(1)}, bf16[256,1536]{1,0:T(8,128)(2,1)S(1)}, u32[]{:S(2)}, u32[]{:S(2)}) %collective-permute-start.3) | collective-permute-done | bytes 786464 | tf_op jit(solution)/shard_map/ppermute | solution.py:1218
  454.3 1.3 pad_maximum_fusion.3
  455.6 2.5 multiply_reduce_fusion
  458.1 2.4 convert_add_fusion
  460.6 6.2 convolution_convert_fusion.6.do_ref
  466.8 4.0 convolution_convert_fusion.3.refs_1_
  470.9 40.0 %attn_bwd.1 = (bf16[1024,768]{1,0:T(8,128)(2,1)S(1)}, bf16[1024,768]{1,0:T(8,128)(2,1)S(1)}, bf16[1024,768]{1,0:T(8,128)(2,1)S(1)}) custom-call(s32[4]{0:T(128)S(1)} %copy-done.7, bf16[1024,768]{1,0:T(8,128)(2,1)S(1)} %get-tuple-element.39.q_ref, bf16[1024,768]{1,0:T(8,128)(2,1)S(1)} %copy-done.9, bf16[1024,768]{1,0:T(8,128)(2,1)S(1)} %copy-done.11, ...), custom_call_target="tpu_custom_call" | custom-call | flops 8053063680 | bytes 11010048 | tf_op jit(solution)/shard_map/attn_bwd/pallas_call | solution.py:534
  511.3 5.0 convolution_convert_fusion.4
  516.3 9.8 %convolution_convert_fusion.1.refs_0_ = bf16[1536,2304]{1,0:T(8,128)(2,1)} fusion(bf16[1024,2304]{1,0:T(8,128)(2,1)S(1)} %constant_dynamic-update-slice_fusion, bf16[1024,1536]{1,0:T(8,128)(2,1)S(1)} %copy-done.17, f32[1536]{0:T(1024)S(1)} %copy-done.26, f32[1024]{0:T(1024)S(1)} %copy-done.29), kind=kOutput, calls=%fused_computation.1 | convolution fusion | flops 7257587712 | bytes 14952448 | tf_op jit(solution)/shard_map/dot_general | solution.py:414
  526.1 302.4 %reduce_all.1 = (bf16[192,4608]{1,0:T(8,128)(2,1)}, bf16[192,1536]{1,0:T(8,128)(2,1)}, bf16[192,8192]{1,0:T(8,128)(2,1)}, bf16[512,1536]{1,0:T(8,128)(2,1)}) custom-call(bf16[1536,2304]{1,0:T(8,128)(2,1)} %convolution_convert_fusion.1.refs_0_, bf16[768,1536]{1,0:T(8,128)(2,1)} %convolution_convert_fusion.3.refs_1_, ...), custom_call_target="tpu_custom_call" | custom-call | bytes 800000000 | tf_op jit(solution)/shard_map/reduce_all/pallas_call | solution.py:1183
  828.5 9.4 %multiply_reduce_fusion.4 = (f32[1536]{0:T(1024)S(1)}, f32[512]{0:T(512)S(1)}, f32[512,1536]{1,0:T(8,128)S(1)}) fusion(f32[1024,1536]{1,0:T(8,128)} %convert_element_type.109, s32[]{:T(128)S(6)} %select_n.66, f32[512]{0:T(512)S(1)} %copy-done.27, f32[1536]{0:T(1024)S(1)} %copy-done.26, bf16[512,1536]{1,0:T(8,128)(2,1)} %collective-permute-done.5, ...), kind=kOutput, calls=%fused_computation.24 | convolution fusion | flops 3630168064 | bytes 17318912 | tf_op jit(solution)/shard_map/dot_general | solution.py:410
  837.9 0.4 collective-permute-start.8
  838.3 3.5 slice_convert_fusion
  841.8 2.3 collective-permute-start.9
  844.1 1.7 collective-permute-done.9
  845.8 2.1 collective-permute-start.10
  847.9 2.7 add_convert_fusion
  850.8 0.1 broadcast_select_fusion.1
  850.9 0.8 collective-permute-start.6
  851.7 3.1 collective-permute-start.7
  854.9 1.5 collective-permute-start.12
  856.4 1.9 slice_convert_fusion.2
  858.4 2.1 convert_element_type.142
  860.4 1.1 convert_element_type.139
  861.6 29.8 %collective-permute-done.12 = f32[2,1536]{1,0:T(2,128)S(1)} collective-permute-done((f32[2,1536]{1,0:T(2,128)S(1)}, f32[2,1536]{1,0:T(2,128)S(1)}, u32[]{:S(2)}, u32[]{:S(2)}) %collective-permute-start.12) | collective-permute-done | bytes 12320 | tf_op jit(solution)/shard_map/ppermute | solution.py:1311
  891.5 0.6 fusion.35
  892.2 1.9 maximum_convert_fusion
  (127 shorter events, 1.6 us)
Async XLA Ops:
  242.0 19.8 %copy-start.4 = (s32[8,128]{1,0:T(8,128)}, s32[8,128]{1,0:T(8,128)S(1)}, u32[]{:S(2)}) copy-start(s32[8,128]{1,0:T(8,128)S(1)} %get-tuple-element.60) | copy-start | bytes 12292
  244.9 16.9 %copy-start.28 = (f32[1024]{0:T(1024)}, f32[1024]{0:T(1024)S(1)}, u32[]{:S(2)}) copy-start(f32[1024]{0:T(1024)S(1)} %add_rsqrt_fusion.1) | copy-start | bytes 12292
  245.8 16.0 %copy-start.25 = (f32[1536]{0:T(1024)}, f32[1536]{0:T(1024)S(1)}, u32[]{:S(2)}) copy-start(f32[1536]{0:T(1024)S(1)} %mul.175) | copy-start | bytes 18436
  245.8 2.9 copy-start.15
  247.7 14.1 %copy-start.6 = (s32[4]{0:T(128)}, s32[4]{0:T(128)S(1)}, u32[]{:S(2)}) copy-start(s32[4]{0:T(128)S(1)} %subtract_add_fusion.count_ref) | copy-start | bytes 52
  248.6 13.2 %copy-start = (f32[1024,128]{1,0:T(8,128)}, f32[1024,128]{1,0:T(8,128)S(1)}, u32[]{:S(2)}) copy-start(f32[1024,128]{1,0:T(8,128)S(1)} %get-tuple-element.87.cos_ref) | copy-start | bytes 1572868
  248.6 13.2 %copy-start.2 = (f32[1024,128]{1,0:T(8,128)}, f32[1024,128]{1,0:T(8,128)S(1)}, u32[]{:S(2)}) copy-start(f32[1024,128]{1,0:T(8,128)S(1)} %get-tuple-element.88.sin_ref) | copy-start | bytes 1572868
  261.8 34.0 %copy-start.30 = (bf16[768,1536]{1,0:T(8,128)(2,1)S(1)}, bf16[768,1536]{1,0:T(8,128)(2,1)}, u32[]{:S(2)}) copy-start(bf16[768,1536]{1,0:T(8,128)(2,1)} %get-tuple-element.36) | copy-start | bytes 7077892
  295.8 5.1 copy-start.8
  295.8 5.1 copy-start.10
  295.8 5.1 copy-start.12
  300.9 22.8 %collective-permute-start = (bf16[1024,1536]{1,0:T(8,128)(2,1)}, bf16[1024,1536]{1,0:T(8,128)(2,1)}, u32[]{:S(2)}, u32[]{:S(2)}) collective-permute-start(bf16[1024,1536]{1,0:T(8,128)(2,1)} %get-tuple-element.82), channel_id=1, source_target_pairs={{0,4},{4,0},{8,12},{12,8},{16,20},{20,16},{24,28},{28,24},{1,5},{5... | collective-permute-start | bytes 9437192 | tf_op jit(solution)/shard_map/ppermute | solution.py:1198
  311.2 12.4 %copy-start.16 = (bf16[1024,1536]{1,0:T(8,128)(2,1)S(1)}, bf16[1024,1536]{1,0:T(8,128)(2,1)}, u32[]{:S(2)}) copy-start(bf16[1024,1536]{1,0:T(8,128)(2,1)} %get-tuple-element.31) | copy-start | bytes 9437188
  328.8 2.6 copy-start.14
  360.2 8.1 copy-start.32
  368.4 38.7 %collective-permute-start.1 = (bf16[512,1536]{1,0:T(8,128)(2,1)}, bf16[512,1536]{1,0:T(8,128)(2,1)}, u32[]{:S(2)}, u32[]{:S(2)}) collective-permute-start(bf16[512,1536]{1,0:T(8,128)(2,1)} %convolution_convert_fusion.5), channel_id=1, source_target_pairs={{0,4},{4,0},{8,12},{12,8},{16,20},{20,16},{24,28},{28,24},{1,5},{5... | collective-permute-start | bytes 4718600 | tf_op jit(solution)/shard_map/ppermute | solution.py:1198
  406.5 12.6 %copy-start.20 = (bf16[1024,1536]{1,0:T(8,128)(2,1)S(1)}, bf16[1024,1536]{1,0:T(8,128)(2,1)}, u32[]{:S(2)}) copy-start(bf16[1024,1536]{1,0:T(8,128)(2,1)} %get-tuple-element.42) | copy-start | bytes 9437188
  406.5 12.6 %copy-start.31 = (bf16[1024,2048]{1,0:T(8,128)(2,1)S(1)}, bf16[1024,2048]{1,0:T(8,128)(2,1)}, u32[]{:S(2)}) copy-start(bf16[1024,2048]{1,0:T(8,128)(2,1)} %get-tuple-element.63) | copy-start | bytes 12582916
  406.5 49.0 %collective-permute-start.4 = (bf16[1024,1536]{1,0:T(8,128)(2,1)}, bf16[1024,1536]{1,0:T(8,128)(2,1)S(1)}, u32[]{:S(2)}, u32[]{:S(2)}) collective-permute-start(bf16[1024,1536]{1,0:T(8,128)(2,1)} %get-tuple-element.84), channel_id=1, source_target_pairs={{0,4},{4,0},{8,12},{12,8},{16,20},{20,16},{24,28},{28,24},{1,5},{5... | collective-permute-start | bytes 9437192 | tf_op jit(solution)/shard_map/ppermute | solution.py:1198
  415.6 12.5 %collective-permute-start.2 = (bf16[256,1536]{1,0:T(8,128)(2,1)S(1)}, bf16[256,1536]{1,0:T(8,128)(2,1)S(1)}, u32[]{:S(2)}, u32[]{:S(2)}) collective-permute-start(bf16[256,1536]{1,0:T(8,128)(2,1)S(1)} %get-tuple-element.75), channel_id=1, source_target_pairs={{0,0},{2,1},{4,2},{6,3},{1,4},{3,5},{5,6},{7,7},{8,8},{10,9},{12,1... | collective-permute-start | bytes 2359304 | tf_op jit(solution)/shard_map/ppermute | solution.py:1218
  416.3 39.3 %slice-start = ((s8[6291456]{0:T(1024)(128)(4,1)}), s8[4194304]{0:T(1024)(128)(4,1)S(1)}, s32[]{:S(2)}) async-start(s8[6291456]{0:T(1024)(128)(4,1)} %bitcast.48), calls=%async_computation | async-start | bytes 8388608
  416.3 39.3 %slice-start.4 = ((s8[6291456]{0:T(1024)(128)(4,1)}), s8[4194304]{0:T(1024)(128)(4,1)S(1)}, s32[]{:S(2)}) async-start(s8[6291456]{0:T(1024)(128)(4,1)} %bitcast.52), calls=%async_computation.4 | async-start | bytes 8388608
  416.3 39.3 %slice-start.1 = ((s8[6291456]{0:T(1024)(128)(4,1)}), s8[2097152]{0:T(1024)(128)(4,1)S(1)}, s32[]{:S(2)}) async-start(s8[6291456]{0:T(1024)(128)(4,1)} %bitcast.48), calls=%async_computation.1 | async-start | bytes 4194304
  416.3 39.3 %slice-start.5 = ((s8[6291456]{0:T(1024)(128)(4,1)}), s8[2097152]{0:T(1024)(128)(4,1)S(1)}, s32[]{:S(2)}) async-start(s8[6291456]{0:T(1024)(128)(4,1)} %bitcast.52), calls=%async_computation.5 | async-start | bytes 4194304
  416.3 37.9 %collective-permute-start.3 = (bf16[256,1536]{1,0:T(8,128)(2,1)S(1)}, bf16[256,1536]{1,0:T(8,128)(2,1)S(1)}, u32[]{:S(2)}, u32[]{:S(2)}) collective-permute-start(bf16[256,1536]{1,0:T(8,128)(2,1)S(1)} %get-tuple-element.76), channel_id=1, source_target_pairs={{2,0},{0,1},{6,2},{4,3},{3,4},{1,5},{7,6},{5,7},{10,8},{8,9},{14,1... | collective-permute-start | bytes 2359304 | tf_op jit(solution)/shard_map/ppermute | solution.py:1218
  460.5 6.2 copy-start.18
  460.6 6.2 copy-start.13
  466.8 4.1 copy-start.1
  466.8 4.1 copy-start.3
  466.8 4.1 copy-start.5
  466.8 4.0 copy-start.7
  466.8 4.0 copy-start.9
  466.8 4.0 copy-start.11
  466.8 44.4 %slice-start.6 = ((s8[7077888]{0:T(1024)(128)(4,1)}), s8[2883584]{0:T(1024)(128)(4,1)S(1)}, s32[]{:S(2)}) async-start(s8[7077888]{0:T(1024)(128)(4,1)} %bitcast.59), calls=%async_computation.6 | async-start | bytes 5767168
  470.9 40.4 %slice-start.7 = ((s8[7077888]{0:T(1024)(128)(4,1)}), s8[4194304]{0:T(1024)(128)(4,1)S(1)}, s32[]{:S(2)}) async-start(s8[7077888]{0:T(1024)(128)(4,1)} %bitcast.59), calls=%async_computation.7 | async-start | bytes 8388608
  511.3 5.0 copy-start.24
  511.3 5.0 copy-start.17
  511.3 5.0 copy-start.26
  511.3 5.0 copy-start.29
  516.3 312.2 %collective-permute-start.5 = (bf16[512,1536]{1,0:T(8,128)(2,1)}, bf16[512,1536]{1,0:T(8,128)(2,1)}, u32[]{:S(2)}, u32[]{:S(2)}) collective-permute-start(bf16[512,1536]{1,0:T(8,128)(2,1)} %convolution_convert_fusion.4), channel_id=1, source_target_pairs={{0,4},{4,0},{8,12},{12,8},{16,20},{20,16},{24,28},{28,24},{1,5},{5... | collective-permute-start | bytes 4718600 | tf_op jit(solution)/shard_map/ppermute | solution.py:1198
  526.1 302.4 %copy-start.27 = (f32[512]{0:T(512)S(1)}, f32[512]{0:T(512)}, u32[]{:S(2)}) copy-start(f32[512]{0:T(512)} %add_rsqrt_fusion.2) | copy-start | bytes 6148
  526.1 321.9 %slice-start.2 = ((s8[6291456]{0:T(1024)(128)(4,1)}), s8[2097152]{0:T(1024)(128)(4,1)S(1)}, s32[]{:S(2)}) async-start(s8[6291456]{0:T(1024)(128)(4,1)} %bitcast.50), calls=%async_computation.2 | async-start | bytes 4194304
  828.5 9.8 %copy-start.19 = (bf16[192,8192]{1,0:T(8,128)(2,1)S(1)}, bf16[192,8192]{1,0:T(8,128)(2,1)}, u32[]{:S(2)}) copy-start(bf16[192,8192]{1,0:T(8,128)(2,1)} %get-tuple-element.49) | copy-start | bytes 9437188
  828.5 19.5 %slice-start.3 = ((s8[6291456]{0:T(1024)(128)(4,1)}), s8[4194304]{0:T(1024)(128)(4,1)S(1)}, s32[]{:S(2)}) async-start(s8[6291456]{0:T(1024)(128)(4,1)} %bitcast.50), calls=%async_computation.3 | async-start | bytes 8388608
  837.9 3.9 collective-permute-start.8
  841.8 4.0 collective-permute-start.9
  845.8 4.9 collective-permute-start.10
  850.6 5.8 copy-start.21
  850.7 7.7 copy-start.22
  850.7 4.2 collective-permute-start.11
  850.9 41.2 %collective-permute-start.6 = (bf16[256,1536]{1,0:T(8,128)(2,1)S(1)}, bf16[256,1536]{1,0:T(8,128)(2,1)S(1)}, u32[]{:S(2)}, u32[]{:S(2)}) collective-permute-start(bf16[256,1536]{1,0:T(8,128)(2,1)S(1)} %get-tuple-element.71), channel_id=1, source_target_pairs={{0,0},{2,1},{4,2},{6,3},{1,4},{3,5},{5,6},{7,7},{8,8},{10,9},{12,1... | collective-permute-start | bytes 2359304 | tf_op jit(solution)/shard_map/ppermute | solution.py:1218
  851.7 40.3 %collective-permute-start.7 = (bf16[256,1536]{1,0:T(8,128)(2,1)S(1)}, bf16[256,1536]{1,0:T(8,128)(2,1)S(1)}, u32[]{:S(2)}, u32[]{:S(2)}) collective-permute-start(bf16[256,1536]{1,0:T(8,128)(2,1)S(1)} %get-tuple-element.72), channel_id=1, source_target_pairs={{2,0},{0,1},{6,2},{4,3},{3,4},{1,5},{7,6},{5,7},{10,8},{8,9},{14,1... | collective-permute-start | bytes 2359304 | tf_op jit(solution)/shard_map/ppermute | solution.py:1218
  854.9 36.5 %collective-permute-start.12 = (f32[2,1536]{1,0:T(2,128)S(1)}, f32[2,1536]{1,0:T(2,128)S(1)}, u32[]{:S(2)}, u32[]{:S(2)}) collective-permute-start(f32[2,1536]{1,0:T(2,128)S(1)} %add.117), channel_id=1, source_target_pairs={{0,2},{1,3},{2,0},{3,1},{4,6},{5,7},{6,4},{7,5},{8,10},{9,11},{10,... | collective-permute-start | bytes 36872 | tf_op jit(solution)/shard_map/ppermute | solution.py:1311
  856.4 4.0 copy-start.23

commit v3 on v2

--- a/solution.py
+++ b/solution.py
@@ -1115,25 +1115,107 @@
 )
 
 
-def run_jobs(jobs):
+GAIN_HOPS = 5
+
+
+class GainSums:
+    def __init__(self, me, source, target, buffer, sem):
+        self.me, self.source, self.target, self.buffer, self.sem = me, source, target, buffer, sem
+
+    def hop(self, k):
+        me = self.me
+        across = me.z + 2 - 4 * (me.z // 2)
+        beside = me.z + 1 - 2 * (me.z % 2)
+        dp = (me.over_core, me.over_x, me.over_y, me.dp, me.dp)[k]
+        seq = (me.z, me.z, me.z, beside, across)[k]
+        return remote(
+            self.buffer.at[k, 0], self.buffer.at[k, 1], self.sem.at[0, k], self.sem.at[1, k], dp, seq
+        )
+
+    def start(self):
+        self.buffer[0, 0] = self.source[...]
+        self.hop(0).start()
+
+    def step(self, k):
+        self.hop(k).wait_recv()
+        total = self.buffer[k, 0] + self.buffer[k, 1]
+        if k + 1 < GAIN_HOPS:
+            self.buffer[k + 1, 0] = total
+            self.hop(k + 1).start()
+        else:
+            self.target[...] = total
+
+    def drain(self):
+        for k in range(GAIN_HOPS):
+            self.hop(k).wait_send()
+
+
+class RowsBack:
+    def __init__(self, me, source, target, sem):
+        self.me, self.source, self.target, self.sem = me, source, target, sem
+
+    def each(self, local, elsewhere):
+        me = self.me
+        rows = self.source.shape[0] // 2
+        for slot in range(2):
+            core, seq = me.z % 2, 2 * me.core + slot
+            here = (core == me.core) & (seq == me.z)
+            block, target = self.source.at[pl.ds(rows * slot, rows)], self.target.at[me.z // 2]
+
+            @pl.when(here)
+            def _():
+                local(pltpu.make_async_copy(block, target, self.sem.at[2, 0]))
+
+            @pl.when(jnp.logical_not(here))
+            def _():
+                elsewhere(
+                    remote(
+                        block, target, self.sem.at[0, slot], self.sem.at[1, me.z // 2],
+                        me.dp - me.core + core, seq,
+                    )
+                )
+
+    def start(self):
+        self.each(lambda copy: copy.start(), lambda copy: copy.start())
+
+    def drain(self):
+        me = self.me
+        self.each(lambda copy: copy.wait(), lambda copy: copy.wait_send())
+        rows = self.source.shape[0] // 2
+        for m in range(2):
+            here = (me.z == 2 * m + me.core) & (me.core == me.z // 2)
+
+            @pl.when(jnp.logical_not(here))
+            def _():
+                remote(
+                    self.source.at[pl.ds(0, rows)], self.target.at[m], self.sem.at[0, 0],
+                    self.sem.at[1, m], me.over_core, me.z,
+                ).wait_recv()
+
+
+def run_jobs(jobs, gains):
     for tick in range(len(jobs) + STAGES[-1][0]):
         for late, stage in reversed(STAGES):
             if 0 <= tick - late < len(jobs):
                 stage(jobs[tick - late])
+        if tick % 2 == 1 and tick // 2 < GAIN_HOPS:
+            gains.step(tick // 2)
     for job in jobs:
         drain(job)
+    gains.drain()
 
 
 def job_plan(d_model, ff):
     half = d_model // 2
     down = [("down", 384 * k, 384, True) for k in range(d_model // 384)]
-    wide_ff = [("ff", 512 * k, 512, False) for k in range(ff // 512)]
-    rest = [("o", half * k, half, True) for k in range(2)]
-    qkv = [("qkv", 384 * k, 384, k % 2 == 1) for k in range(3 * half // 384)]
-    return [job for pair in zip(down, wide_ff) for job in pair] + wide_ff[len(down) :] + rest + qkv
-
-
-def reduce_all(g_qkv, g_o, g_ff, g_down):
+    by_y = [("ff", 512 * k, 512, False) for k in range(len(down))]
+    by_turns = [("ff", 512 * k, 512, k % 2 == 0) for k in range(len(down), ff // 512)]
+    rest = [("o", half, half, True), ("qkv", 0, 384, False), ("o", 0, half, True), ("qkv", 384, 384, False)]
+    qkv = [("qkv", 384 * k, 384, k % 2 == 0) for k in range(2, 3 * half // 384)]
+    return [job for pair in zip(down, by_y) for job in pair] + by_turns + rest + qkv
+
+
+def reduce_all(g_qkv, g_o, g_ff, g_down, half_rows, gain_sums):
     d_model, ff = g_o.shape[1], g_ff.shape[1]
     plan = job_plan(d_model, ff)
     sources = {"qkv": g_qkv, "o": g_o, "ff": g_ff, "down": g_down}
@@ -1144,9 +1226,15 @@
         jax.ShapeDtypeStruct((d_model // 8, d_model), jnp.bfloat16),
         jax.ShapeDtypeStruct((d_model // 8, 2 * ff), jnp.bfloat16),
         jax.ShapeDtypeStruct((ff // 8, d_model), jnp.bfloat16),
+        jax.ShapeDtypeStruct((2, half_rows.shape[0] // 2, d_model), jnp.bfloat16),
+        jax.ShapeDtypeStruct(gain_sums.shape, jnp.float32),
     ]
-    scratch = []
     dma = pltpu.SemaphoreType.DMA
+    scratch = [
+        dma((3, 2)),
+        pltpu.VMEM((GAIN_HOPS, 2) + gain_sums.shape, jnp.float32),
+        dma((2, GAIN_HOPS)),
+    ]
     for name, first, width, x_first in plan:
         by_columns = name in halves
         rows = sources[name].shape[0] // (4 if by_columns else 2)
@@ -1161,14 +1249,23 @@
 
     def kernel(*refs):
         source = dict(zip(names, refs[:4]))
-        target = dict(zip(names, refs[4:8]))
-        buffers = refs[8:]
+        target = dict(zip(names, refs[6:10]))
+        row_sem, gain_buffer, gain_sem = refs[12:15]
+        buffers = refs[15:]
         me = Place()
         enter(
             [(me.over_core, me.z)]
             + [(me.over_x, me.z), (me.over_y, me.z)]
-            + [(me.dp, lax.rem(me.z + k, 4)) for k in range(1, 4)]
-        )
+            + [
+                (me.dp - me.core + core, lax.rem(me.z + k, 4))
+                for k in range(1, 4)
+                for core in range(2)
+            ]
+        )
+        rows_back = RowsBack(me, refs[4], refs[10], row_sem)
+        gains = GainSums(me, refs[5], refs[11], gain_buffer, gain_sem)
+        rows_back.start()
+        gains.start()
         jobs = []
         for k, (name, first, width, x_first) in enumerate(plan):
             own = buffers[6 * k : 6 * k + 6]
@@ -1178,12 +1275,13 @@
                 )
             else:
                 jobs.append(RowJob(me, own, source[name], target[name], first, width))
-        run_jobs(jobs)
+        run_jobs(jobs, gains)
+        rows_back.drain()
 
     return pl.pallas_call(
         kernel,
-        in_specs=[ANY] * 4,
-        out_specs=[ANY] * 4,
+        in_specs=[ANY] * 5 + [pl.BlockSpec(memory_space=pltpu.VMEM)],
+        out_specs=[ANY] * 5 + [pl.BlockSpec(memory_space=pltpu.VMEM)],
         out_shape=outs,
         scratch_shapes=scratch,
         compiler_params=pltpu.CompilerParams(
@@ -1191,7 +1289,7 @@
         ),
         cost_estimate=pl.CostEstimate(flops=0, bytes_accessed=800_000_000, transcendentals=0),
         name="reduce_all",
-    )(g_qkv, g_o, g_ff, g_down)
+    )(g_qkv, g_o, g_ff, g_down, half_rows, gain_sums)
 
 
 def swap_core(value):
@@ -1301,20 +1399,14 @@
     grad_normed = nt(of_core(grad_qkv, core), full_qkv) + wide(normed_other)
     grad_gain_a, grad_rows = norm_backward(of_core(x, core), gain_a, grad_normed)
     grad_rows = grad_rows + of_core(grad_middle, core)
-    grad_tokens = wide(from_sequence(low(grad_rows), seq_at))
-
-    grad_gain_a = grad_gain_a + swap_core(grad_gain_a)
-    grad_gains = jnp.stack([grad_gain_a, grad_gain_f])
-    for bit in (2, 4):
-        grad_gains = grad_gains + lax.ppermute(grad_gains, "dp", [(i, i ^ bit) for i in range(8)])
-    for bit in (1, 2):
-        grad_gains = grad_gains + lax.ppermute(grad_gains, "seq", [(i, i ^ bit) for i in range(4)])
+    gain_sums = jnp.stack([grad_gain_a, 0.5 * grad_gain_f])
+    r_qkv, r_o, r_ff, r_down, grad_tokens, grad_gains = reduce_all(
+        g_qkv, g_o, g_ff, g_down, low(grad_rows), gain_sums
+    )
     grad_gains = lax.dynamic_slice_in_dim(grad_gains, dp_at * (width // 8), width // 8, 1)
-
-    r_qkv, r_o, r_ff, r_down = reduce_all(g_qkv, g_o, g_ff, g_down)
     return (
         result,
-        grad_tokens,
+        wide(grad_tokens),
         wide(r_qkv[:, :width]),
         wide(r_qkv[:, width : 2 * width]),
         wide(r_qkv[:, 2 * width :]),

time: 896 us -> 838 us (0.935)
  waiting for transfers between devices: 57.7 us -> 28.1 us
  Pallas kernels: 611 us -> 588 us
  starting transfers between devices: 16.4 us -> 6.14 us
    ppermute x4 -> x0, waiting for transfers between devices: 31.5 us -> none  [the longest x2 29.8 us: column_device(): lax.ppermute(grad_gains, 'seq', [(i, i ^ bit) for i in range(4)])]
    pallas_call x1, Pallas kernels: 302 us -> 283 us  [reduce_all(): pl.pallas_call(kernel, in_specs=[ANY] * 5 + [pl.BlockSpec(memory_space=pl...]
    ppermute x4 -> x2, waiting for transfers between devices: 26.2 us -> 28.1 us  [from_sequence(): got.append(lax.ppermute(block, ('dp', 'seq'), reshard_pairs(turn)))]
  transfers between devices with their start and end apart: 13 -> 6, of which waited for: 3 -> 1; matrix products, arithmetic and copies ran while one was open for 11% -> 11% of each run, Pallas kernels for 34% -> 0%
where the time goes in v3:
time: 838 us; the launch traced here: 833 us
  Pallas kernels  588 us (70%)
  matrix products  156 us (19%)
  other arithmetic  44 us (5%)
  waiting for transfers between devices  28.1 us (3%)
  local copies, waits for them, and re-layouts  8.91 us (1%)
    pallas_call x1, Pallas kernels, reduce_all(): pl.pallas_call(kernel, in_specs=[ANY] * 5 + [pl.BlockSpec(memory_space=pl...  283 us
    pallas_call x1, Pallas kernels, gather_all(): pl.pallas_call(gather_kernel, in_specs=[ANY] * 11, out_specs=[ANY] * 8, o...  235 us
    dot_general x6, matrix products, dot(): return jnp.dot(a, b, preferred_element_type=jnp.float32)  63.7 us
    dot_general x5, matrix products, nt(): lax.dot_general(a, b, (((1,), (1,)), ((), ())), preferred_element_type=jn...  49.5 us
    dot_general x4, matrix products, tn(): lax.dot_general(a, b, (((0,), (0,)), ((), ())), preferred_element_type=jn...  42.4 us
    pallas_call x1, Pallas kernels, attn_bwd(): pl.pallas_call(attn_bwd_kernel, grid_spec=pltpu.PrefetchScalarGridSpec(nu...  37.9 us
    pallas_call x1, Pallas kernels, attn_fwd(): pl.pallas_call(attn_fwd_kernel, grid_spec=pltpu.PrefetchScalarGridSpec(nu...  32.8 us
    ppermute x2, waiting for transfers between devices, from_sequence(): got.append(lax.ppermute(block, ('dp', 'seq'), reshard_pairs(turn)))  28.1 us
  transfers between devices with their start and end apart: 6, of which 1 were waited for; matrix products, arithmetic and copies ran while one was open for 11% of the time, Pallas kernels for 0%

profile of v3, /device:TPU:0, one launch (start us, length us, event | category | flops | bytes accessed | tf_op | source)
XLA Modules:
  0.0 832.5 jit_solution(2090005998836201914)
XLA Ops:
  0.7 0.7 stack.25
  1.3 0.7 stack.26
  2.0 1.3 reshape.156.segments
  3.2 0.6 fusion.30.gains
  3.8 235.0 %gather_all.1 = (bf16[1024,1536]{1,0:T(8,128)(2,1)}, s32[4,1,256]{2,1,0:T(1,128)}, bf16[1024,1536]{1,0:T(8,128)(2,1)}, bf16[8,2,256]{2,1,0:T(2,128)(2,1)}, bf16[...) custom-call(bf16[2,256,1536]{2,1,0:T(8,128)(2,1)} %tokens.1, ...), custom_call_target="tpu_custom_call" | custom-call | bytes 500000000 | tf_op jit(solution)/shard_map/gather_all/pallas_call | solution.py:847
  238.8 1.2 slice.69
  240.0 1.5 fusion.21
  241.4 0.3 reduce-window.9
  241.7 0.1 slice.71
  241.8 0.1 slice_reduce_fusion.2
  241.9 0.1 subtract_convert_fusion
  242.0 0.1 slice.73
  242.1 0.2 copy.27.start_ref
  242.3 2.6 multiply_reduce_fusion.3
  244.9 0.7 convert_bitcast_fusion
  245.8 1.9 fusion.19
  247.7 0.9 pad_maximum_fusion.4
  248.6 13.2 %fusion.18.q_ref.k_ref.v_ref = f32[1024,2304]{1,0:T(8,128)} fusion(bf16[1536,2304]{1,0:T(8,128)(2,1)} %get-tuple-element.36, bf16[1024,1536]{1,0:T(8,128)(2,1)S(1)} %copy-done.15, f32[1536]{0:T(1024)S(1)} %mul.191, f32[1024]{0:T(1024)S(1)} %add_rsqrt_fusion.1), kind=kOutput, calls=%fused_computation.45 | convolution fusion | flops 7254048768 | bytes 19671040 | tf_op jit(solution)/shard_map/dot_general | solution.py:1322
  261.9 32.8 %attn_fwd.1 = (bf16[1024,768]{1,0:T(8,128)(2,1)S(1)}, bf16[1024,768]{1,0:T(8,128)(2,1)S(1)}, bf16[1024,768]{1,0:T(8,128)(2,1)S(1)}, bf16[1024,768]{1,0:T(8,128)(2,1)S(1)}, f32[1024,128]{1,0:T(8,128)S(1)}) custom-call(s32[4]{0:T(128)S(1)} %subtract_add_fusion.count_ref, f32[1024,2304]{1,0:T(8,128)} %fusion.18.q_ref.k_ref.v_ref, ...), custom_call_target="tpu_custom_call" | custom-call | flops 3221225472 | bytes 15728640 | tf_op jit(solution)/shard_map/attn_fwd/pallas_call | solution.py:468
  294.7 5.1 fusion.34
  299.8 1.9 collective-permute-start
  301.7 5.4 convert_element_type.109
  307.2 0.2 copy.28
  307.4 2.2 multiply_reduce_fusion.6
  309.6 0.6 add_rsqrt_fusion.2
  310.2 12.5 %fusion.36 = f32[1024,2048]{1,0:T(8,128)} fusion(bf16[1024,1536]{1,0:T(8,128)(2,1)} %get-tuple-element.44, bf16[2048,1536]{1,0:T(8,128)(2,1)} %get-tuple-element.40), kind=kOutput, calls=%fused_computation.101 | convolution fusion | flops 6442450944 | bytes 17825792 | tf_op jit(solution)/shard_map/dot_general | solution.py:410
  322.7 5.1 multiply_reduce_fusion.2
  327.8 0.6 multiply_convert_fusion.3
  328.4 2.1 copy-done.14
  330.5 10.8 %fusion.1 = f32[1024,2048]{1,0:T(8,128)} fusion(bf16[1024,1536]{1,0:T(8,128)(2,1)S(1)} %multiply_convert_fusion.3, bf16[1536,4096]{1,0:T(8,128)(2,1)} %get-tuple-element.39), kind=kOutput, calls=%fused_computation.13 | convolution fusion | flops 6442450944 | bytes 17825792 | tf_op jit(solution)/shard_map/dot_general | solution.py:1322
  341.3 18.1 %multiply_convert_fusion.1 = (bf16[1024,2048]{1,0:T(8,128)(2,1)}, bf16[1024,2048]{1,0:T(8,128)(2,1)}, bf16[1024,2048]{1,0:T(8,128)(2,1)}) fusion(f32[1024,2048]{1,0:T(8,128)} %fusion.36, f32[1024,2048]{1,0:T(8,128)} %fusion.1, bf16[1024,1536]{1,0:T(8,128)(2,1)S(1)} %multiply_convert_fusion.3, bf16[1536,4096]{1,0:T(8,128)(2,1)} %get-tuple-element.39), kind=kOutput, calls=%fused_computation.4 | convolution fusion | flops 6473908224 | bytes 38797312 | tf_op jit(solution)/shard_map/dot_general | solution.py:1322
  359.3 8.1 convolution_convert_fusion.5
  367.5 18.9 %fusion.35 = (bf16[1024,1536]{1,0:T(8,128)(2,1)}, f32[1024,1536]{1,0:T(8,128)}) fusion(bf16[1536,4096]{1,0:T(8,128)(2,1)} %get-tuple-element.39, bf16[1024,2048]{1,0:T(8,128)(2,1)} %get-tuple-element.66, bf16[1024,2048]{1,0:T(8,128)(2,1)S(1)} %copy-done.30), kind=kOutput, calls=%fused_computation.100 | convolution fusion | flops 12903251968 | bytes 30408704 | tf_op jit(solution)/shard_map/dot_general | solution.py:410
  386.4 19.2 %convolution_convert_fusion.refs_2_ = bf16[1536,4096]{1,0:T(8,128)(2,1)} fusion(bf16[1024,1536]{1,0:T(8,128)(2,1)S(1)} %multiply_convert_fusion.3, bf16[1024,2048]{1,0:T(8,128)(2,1)} %get-tuple-element.66, bf16[1024,2048]{1,0:T(8,128)(2,1)} %get-tuple-element.65), kind=kOutput, calls=%fused_computation | convolution fusion | flops 12907970560 | bytes 24117248 | tf_op jit(solution)/shard_map/dot_general | solution.py:414
  405.6 0.5 collective-permute-start.4
  406.1 8.4 %add_convert_fusion.1 = bf16[512,1536]{1,0:T(8,128)(2,1)S(1)} fusion(bf16[512,1536]{1,0:T(8,128)(2,1)} %collective-permute-done.1, f32[1024,1536]{1,0:T(8,128)} %copy-done.14, s32[]{:T(128)S(6)} %select_n.50, bf16[2048,1536]{1,0:T(8,128)(2,1)} %get-tuple-element.40, bf16[1024,2048]{1,0:T(8,128)(2,1)} %get-tuple-element.67), kind=kOutput, calls=%fused_computation.29 | convolution fusion | flops 3224371200 | bytes 14681088 | tf_op jit(solution)/shard_map/dot_general | solution.py:1322
  414.5 0.1 broadcast_select_fusion.1
  414.6 0.7 collective-permute-start.2
  415.4 3.0 collective-permute-start.3
  418.4 9.0 %convolution_convert_fusion.2.refs_3_ = bf16[2048,1536]{1,0:T(8,128)(2,1)} fusion(bf16[1024,2048]{1,0:T(8,128)(2,1)S(1)} %copy-done.29, bf16[1024,1536]{1,0:T(8,128)(2,1)S(1)} %copy-done.18), kind=kOutput, calls=%fused_computation.8 | convolution fusion | flops 6445596672 | bytes 13631488 | tf_op jit(solution)/shard_map/dot_general | solution.py:414
  427.4 28.1 %collective-permute-done.3 = bf16[256,1536]{1,0:T(8,128)(2,1)S(1)} collective-permute-done((bf16[256,1536]{1,0:T(8,128)(2,1)S(1)}, bf16[256,1536]{1,0:T(8,128)(2,1)S(1)}, u32[]{:S(2)}, u32[]{:S(2)}) %collective-permute-start.3) | collective-permute-done | bytes 786464 | tf_op jit(solution)/shard_map/ppermute | solution.py:1316
  455.5 0.1 select_bitcast_fusion.1
  455.6 1.3 pad_maximum_fusion.3
  457.0 2.5 multiply_reduce_fusion
  459.4 2.4 convert_add_fusion
  461.8 4.4 convolution_convert_fusion.6.do_ref
  466.3 4.0 convolution_convert_fusion.3.refs_1_
  470.4 37.9 %attn_bwd.1 = (bf16[1024,768]{1,0:T(8,128)(2,1)S(1)}, bf16[1024,768]{1,0:T(8,128)(2,1)S(1)}, bf16[1024,768]{1,0:T(8,128)(2,1)S(1)}) custom-call(s32[4]{0:T(128)S(1)} %copy-done.7, bf16[1024,768]{1,0:T(8,128)(2,1)S(1)} %get-tuple-element.41.q_ref, bf16[1024,768]{1,0:T(8,128)(2,1)S(1)} %copy-done.9, bf16[1024,768]{1,0:T(8,128)(2,1)S(1)} %copy-done.11, ...), custom_call_target="tpu_custom_call" | custom-call | flops 8053063680 | bytes 11010048 | tf_op jit(solution)/shard_map/attn_bwd/pallas_call | solution.py:534
  508.3 0.1 constant_dynamic-update-slice_fusion.2
  508.4 0.1 constant_dynamic-update-slice_fusion.1
  508.5 0.1 constant_dynamic-update-slice_fusion
  508.7 7.0 convolution_convert_fusion.4
  515.8 10.2 %convolution_convert_fusion.1.refs_0_ = bf16[1536,2304]{1,0:T(8,128)(2,1)} fusion(bf16[1024,2304]{1,0:T(8,128)(2,1)S(1)} %constant_dynamic-update-slice_fusion, bf16[1024,1536]{1,0:T(8,128)(2,1)S(1)} %copy-done.17, f32[1536]{0:T(1024)S(1)} %copy-done.24, f32[1024]{0:T(1024)S(1)} %copy-done.27), kind=kOutput, calls=%fused_computation.1 | convolution fusion | flops 7257587712 | bytes 14952448 | tf_op jit(solution)/shard_map/dot_general | solution.py:414
  526.1 6.7 multiply_reduce_fusion.4
  532.9 0.6 pad_maximum_fusion.6.refs_5_
  533.5 1.9 add_convert_fusion.refs_4_
  535.4 282.5 %reduce_all.1 = (bf16[192,4608]{1,0:T(8,128)(2,1)}, bf16[192,1536]{1,0:T(8,128)(2,1)}, bf16[192,8192]{1,0:T(8,128)(2,1)}, bf16[512,1536]{1,0:T(8,128)(2,1)}, bf1...) custom-call(bf16[1536,2304]{1,0:T(8,128)(2,1)} %convolution_convert_fusion.1.refs_0_, ...), custom_call_target="tpu_custom_call" | custom-call | bytes 800000000 | tf_op jit(solution)/shard_map/reduce_all/pallas_call | solution.py:1281
  818.0 5.5 slice_convert_fusion
  823.5 1.9 slice_convert_fusion.2
  825.4 0.2 copy-done.21
  825.6 2.1 convert_element_type.135
  827.7 2.1 convert_element_type.142
  829.8 1.1 convert_element_type.139
  830.9 1.4 fusion.33
  (98 shorter events, 0.6 us)
Async XLA Ops:
  242.0 19.8 %copy-start.4 = (s32[8,128]{1,0:T(8,128)}, s32[8,128]{1,0:T(8,128)S(1)}, u32[]{:S(2)}) copy-start(s32[8,128]{1,0:T(8,128)S(1)} %get-tuple-element.64) | copy-start | bytes 12292
  244.9 16.9 %copy-start.26 = (f32[1024]{0:T(1024)}, f32[1024]{0:T(1024)S(1)}, u32[]{:S(2)}) copy-start(f32[1024]{0:T(1024)S(1)} %add_rsqrt_fusion.1) | copy-start | bytes 12292
  245.8 16.1 %copy-start.23 = (f32[1536]{0:T(1024)}, f32[1536]{0:T(1024)S(1)}, u32[]{:S(2)}) copy-start(f32[1536]{0:T(1024)S(1)} %mul.191) | copy-start | bytes 18436
  245.8 2.9 copy-start.15
  247.7 14.2 %copy-start.6 = (s32[4]{0:T(128)}, s32[4]{0:T(128)S(1)}, u32[]{:S(2)}) copy-start(s32[4]{0:T(128)S(1)} %subtract_add_fusion.count_ref) | copy-start | bytes 52
  248.6 13.3 %copy-start = (f32[1024,128]{1,0:T(8,128)}, f32[1024,128]{1,0:T(8,128)S(1)}, u32[]{:S(2)}) copy-start(f32[1024,128]{1,0:T(8,128)S(1)} %get-tuple-element.87.cos_ref) | copy-start | bytes 1572868
  248.6 13.3 %copy-start.2 = (f32[1024,128]{1,0:T(8,128)}, f32[1024,128]{1,0:T(8,128)S(1)}, u32[]{:S(2)}) copy-start(f32[1024,128]{1,0:T(8,128)S(1)} %get-tuple-element.88.sin_ref) | copy-start | bytes 1572868
  261.9 32.9 %copy-start.28 = (bf16[768,1536]{1,0:T(8,128)(2,1)S(1)}, bf16[768,1536]{1,0:T(8,128)(2,1)}, u32[]{:S(2)}) copy-start(bf16[768,1536]{1,0:T(8,128)(2,1)} %get-tuple-element.38) | copy-start | bytes 7077892
  294.7 5.1 copy-start.8
  294.7 5.1 copy-start.10
  294.7 5.1 copy-start.12
  299.8 22.9 %collective-permute-start = (bf16[1024,1536]{1,0:T(8,128)(2,1)}, bf16[1024,1536]{1,0:T(8,128)(2,1)}, u32[]{:S(2)}, u32[]{:S(2)}) collective-permute-start(bf16[1024,1536]{1,0:T(8,128)(2,1)} %get-tuple-element.82), channel_id=1, source_target_pairs={{0,4},{4,0},{8,12},{12,8},{16,20},{20,16},{24,28},{28,24},{1,5},{5... | collective-permute-start | bytes 9437192 | tf_op jit(solution)/shard_map/ppermute | solution.py:1296
  310.2 12.5 %copy-start.16 = (bf16[1024,1536]{1,0:T(8,128)(2,1)S(1)}, bf16[1024,1536]{1,0:T(8,128)(2,1)}, u32[]{:S(2)}) copy-start(bf16[1024,1536]{1,0:T(8,128)(2,1)} %get-tuple-element.33) | copy-start | bytes 9437188
  327.8 2.7 copy-start.14
  359.3 8.1 copy-start.30
  367.5 38.6 %collective-permute-start.1 = (bf16[512,1536]{1,0:T(8,128)(2,1)}, bf16[512,1536]{1,0:T(8,128)(2,1)}, u32[]{:S(2)}, u32[]{:S(2)}) collective-permute-start(bf16[512,1536]{1,0:T(8,128)(2,1)} %convolution_convert_fusion.5), channel_id=1, source_target_pairs={{0,4},{4,0},{8,12},{12,8},{16,20},{20,16},{24,28},{28,24},{1,5},{5... | collective-permute-start | bytes 4718600 | tf_op jit(solution)/shard_map/ppermute | solution.py:1296
  405.6 12.8 %copy-start.18 = (bf16[1024,1536]{1,0:T(8,128)(2,1)S(1)}, bf16[1024,1536]{1,0:T(8,128)(2,1)}, u32[]{:S(2)}) copy-start(bf16[1024,1536]{1,0:T(8,128)(2,1)} %get-tuple-element.44) | copy-start | bytes 9437188
  405.6 12.8 %copy-start.29 = (bf16[1024,2048]{1,0:T(8,128)(2,1)S(1)}, bf16[1024,2048]{1,0:T(8,128)(2,1)}, u32[]{:S(2)}) copy-start(bf16[1024,2048]{1,0:T(8,128)(2,1)} %get-tuple-element.67) | copy-start | bytes 12582916
  405.6 51.3 %collective-permute-start.4 = (bf16[1024,1536]{1,0:T(8,128)(2,1)}, bf16[1024,1536]{1,0:T(8,128)(2,1)S(1)}, u32[]{:S(2)}, u32[]{:S(2)}) collective-permute-start(bf16[1024,1536]{1,0:T(8,128)(2,1)} %get-tuple-element.84), channel_id=1, source_target_pairs={{0,4},{4,0},{8,12},{12,8},{16,20},{20,16},{24,28},{28,24},{1,5},{5... | collective-permute-start | bytes 9437192 | tf_op jit(solution)/shard_map/ppermute | solution.py:1296
  414.6 12.8 %collective-permute-start.2 = (bf16[256,1536]{1,0:T(8,128)(2,1)S(1)}, bf16[256,1536]{1,0:T(8,128)(2,1)S(1)}, u32[]{:S(2)}, u32[]{:S(2)}) collective-permute-start(bf16[256,1536]{1,0:T(8,128)(2,1)S(1)} %get-tuple-element.75), channel_id=1, source_target_pairs={{0,0},{2,1},{4,2},{6,3},{1,4},{3,5},{5,6},{7,7},{8,8},{10,9},{12,1... | collective-permute-start | bytes 2359304 | tf_op jit(solution)/shard_map/ppermute | solution.py:1316
  415.3 41.6 %slice-start = ((s8[6291456]{0:T(1024)(128)(4,1)}), s8[4194304]{0:T(1024)(128)(4,1)S(1)}, s32[]{:S(2)}) async-start(s8[6291456]{0:T(1024)(128)(4,1)} %bitcast.44), calls=%async_computation | async-start | bytes 8388608
  415.4 41.6 %slice-start.4 = ((s8[6291456]{0:T(1024)(128)(4,1)}), s8[4194304]{0:T(1024)(128)(4,1)S(1)}, s32[]{:S(2)}) async-start(s8[6291456]{0:T(1024)(128)(4,1)} %bitcast.48), calls=%async_computation.4 | async-start | bytes 8388608
  415.4 41.6 %slice-start.1 = ((s8[6291456]{0:T(1024)(128)(4,1)}), s8[2097152]{0:T(1024)(128)(4,1)S(1)}, s32[]{:S(2)}) async-start(s8[6291456]{0:T(1024)(128)(4,1)} %bitcast.44), calls=%async_computation.1 | async-start | bytes 4194304
  415.4 41.5 %slice-start.5 = ((s8[6291456]{0:T(1024)(128)(4,1)}), s8[2097152]{0:T(1024)(128)(4,1)S(1)}, s32[]{:S(2)}) async-start(s8[6291456]{0:T(1024)(128)(4,1)} %bitcast.48), calls=%async_computation.5 | async-start | bytes 4194304
  415.4 40.1 %collective-permute-start.3 = (bf16[256,1536]{1,0:T(8,128)(2,1)S(1)}, bf16[256,1536]{1,0:T(8,128)(2,1)S(1)}, u32[]{:S(2)}, u32[]{:S(2)}) collective-permute-start(bf16[256,1536]{1,0:T(8,128)(2,1)S(1)} %get-tuple-element.76), channel_id=1, source_target_pairs={{2,0},{0,1},{6,2},{4,3},{3,4},{1,5},{7,6},{5,7},{10,8},{8,9},{14,1... | collective-permute-start | bytes 2359304 | tf_op jit(solution)/shard_map/ppermute | solution.py:1316
  461.8 4.4 copy-start.13
  466.3 4.1 copy-start.1
  466.3 4.1 copy-start.3
  466.3 4.1 copy-start.5
  466.3 4.0 copy-start.7
  466.3 4.0 copy-start.9
  466.3 4.0 copy-start.11
  508.6 7.2 copy-start.17
  508.6 7.2 copy-start.24
  508.6 7.2 copy-start.27
  508.7 17.4 %slice-start.2 = ((s8[6291456]{0:T(1024)(128)(4,1)}), s8[4194304]{0:T(1024)(128)(4,1)S(1)}, s32[]{:S(2)}) async-start(s8[6291456]{0:T(1024)(128)(4,1)} %bitcast.46), calls=%async_computation.2 | async-start | bytes 8388608
  515.7 10.4 %collective-permute-start.5 = (bf16[512,1536]{1,0:T(8,128)(2,1)S(1)}, bf16[512,1536]{1,0:T(8,128)(2,1)S(1)}, u32[]{:S(2)}, u32[]{:S(2)}) collective-permute-start(bf16[512,1536]{1,0:T(8,128)(2,1)S(1)} %convolution_convert_fusion.4), channel_id=1, source_target_pairs={{0,4},{4,0},{8,12},{12,8},{16,20},{20,16},{24,28},{28,24},{1,5},{5... | collective-permute-start | bytes 4718600 | tf_op jit(solution)/shard_map/ppermute | solution.py:1296
  515.8 10.3 %slice-start.3 = ((s8[6291456]{0:T(1024)(128)(4,1)}), s8[2097152]{0:T(1024)(128)(4,1)S(1)}, s32[]{:S(2)}) async-start(s8[6291456]{0:T(1024)(128)(4,1)} %bitcast.46), calls=%async_computation.3 | async-start | bytes 4194304
  515.8 10.3 %copy-start.25 = (f32[512]{0:T(512)S(1)}, f32[512]{0:T(512)}, u32[]{:S(2)}) copy-start(f32[512]{0:T(512)} %add_rsqrt_fusion.2) | copy-start | bytes 6148
  818.0 5.5 copy-start.19
  823.4 2.2 copy-start.21
  823.4 4.3 copy-start.20
  825.6 4.2 copy-start.22

commit v4 on v3

--- a/solution.py
+++ b/solution.py
@@ -584,9 +584,14 @@
 
 
 def gather_kernel(
-    tokens, segments, out_grad, gains, w_q, w_k, w_v, w_o, w_gate, w_up, w_down,
+    tokens, segments, out_grad, gains, cosine, sine, w_q, w_k, w_v, w_o, w_gate, w_up, w_down,
     x_out, seg_out, g_out, gains_out, qkv_out, o_out, ff_out, down_out,
+    normed_out, heads_out, mixed_out, lse_out, middle_out, nf_out, slope_gate_out, slope_up_out,
+    hidden_out, g_down_out, start_out,
     send, recv, local, row_send, row_recv, row_local, gain_send, gain_recv,
+    x_v, seg_v, gains_v, normed_v, w_qkv_v, heads_v, mixed_v, w_o_v, middle_v, part_send, part_recv,
+    nf_v, w_ff_v, branch_v, tile_v, g_tile_v, lse_v, start_v,
+    part_sem, load_sem, w_sem, tile_sem, store_sem,
 ):
     me = Place()
     rows = tokens.shape[1]
@@ -792,6 +797,20 @@
             left(4)
             left(6)
 
+    def load(source, target, k):
+        return pltpu.make_async_copy(source, target, load_sem.at[k])
+
+    stores = []
+
+    def store(source, target):
+        copy = pltpu.make_async_copy(source, target, store_sem.at[len(stores)])
+        stores.append(copy)
+        copy.start()
+
+    length, width = x_v.shape
+    own_width = width // 2
+    half_ff = ff_out.shape[1] // 2
+
     row_copies(0)
     row_copies(1)
     for index in range(3):
@@ -800,62 +819,285 @@
         begin(remote(gains, gains_out.at[me.dp], gain_send.at[k - 1], gain_recv.at[k - 1],
                      lax.rem(me.dp + k, 8), me.z))
     pltpu.make_async_copy(gains, gains_out.at[me.dp], gain_recv.at[7]).start()
-    rows_start(0)
     row_copies(2)
     for index in range(3):
         columns_relay(index)
-    columns_start(3)
-    rows_relay(0)
-    columns_start(4)
+    rows_start(0)
     row_relay(0)
     row_relay(1)
-    columns_relay(3)
-    rows_start(1)
-    columns_relay(4)
-    row_relay(2)
-    rows_relay(1)
-    for index in range(5):
-        columns_finish(index)
-    for which in range(2):
-        rows_finish(which)
-    for index in range(3):
-        row_finish(index)
-        row_wait_send(index)
     for k in range(1, 8):
         piece = gains_out.at[lax.rem(me.dp + 8 - k, 8)]
         remote(piece, piece, gain_send.at[k - 1], gain_recv.at[k - 1], me.over_core, me.z).wait_recv()
     pltpu.make_async_copy(gains, gains_out.at[me.dp], gain_recv.at[7]).wait()
+    load(gains_out, gains_v, 0).start()
+    row_finish(1)
+    load(seg_out, seg_v, 1).start()
+    row_finish(0)
+    load(x_out, x_v, 2).start()
+    load(gains_out, gains_v, 0).wait()
+    load(seg_out, seg_v, 1).wait()
+    load(x_out, x_v, 2).wait()
+    both_gains = gains_v[0].astype(jnp.float32)
+    for k in range(1, 8):
+        both_gains = both_gains + gains_v[k].astype(jnp.float32)
+    gain_a, gain_f = both_gains[0:1], both_gains[1:2]
+
+    norm_rows(lambda part: x_v[part, :].astype(jnp.float32), gain_a, normed_v, length)
+    store(normed_v, normed_out)
+
+    docs = jnp.concatenate([seg_v[k] for k in range(4)], axis=1)
+    for k in range(4):
+        square = lax.broadcasted_iota(jnp.int32, (rows, rows), 0) == lax.broadcasted_iota(
+            jnp.int32, (rows, rows), 1
+        )
+        ids = jnp.sum(jnp.where(square, seg_v[k], 0), axis=1, keepdims=True)
+        start_v[pl.ds(rows * k, rows), :] = jnp.sum(
+            jnp.where(docs < ids, 1, 0), axis=1, keepdims=True
+        )
+    store(start_v, start_out)
+
+    for index in range(3):
+        columns_finish(index)
+    columns_start(3)
+    columns_start(4)
+    rows_relay(0)
+    tile = 256
+    tiles = own_width // tile
+    for t in range(tiles):
+        for kind in range(3):
+            part = pl.ds(own_width * kind + tile * t, tile)
+            pltpu.make_async_copy(qkv_out.at[:, part], w_qkv_v.at[:, part], w_sem.at[kind, t]).start()
+    for t in range(tiles):
+        for kind in range(3):
+            part = pl.ds(own_width * kind + tile * t, tile)
+            pltpu.make_async_copy(qkv_out.at[:, part], w_qkv_v.at[:, part], w_sem.at[kind, t]).wait()
+            product = jnp.dot(normed_v[...], w_qkv_v[:, part], preferred_element_type=jnp.float32)
+            for k in range(tile // 128):
+                piece = product[:, 128 * k : 128 * k + 128]
+                if kind < 2:
+                    piece = piece * cosine[...] + swap_halves(piece) * sine[...]
+                heads_v[:, pl.ds(own_width * kind + tile * t + 128 * k, 128)] = piece.astype(jnp.bfloat16)
+
+        def pair_step(pair, carry):
+            attend(pair, own_width, heads_v, start_v, mixed_v, lse_v)
+            return carry
+
+        lax.fori_loop(tile // 128 * t, tile // 128 * (t + 1), pair_step, 0)
+        if t == 0:
+            row_relay(2)
+        if t == 1:
+            rows_start(1)
+    store(heads_v, heads_out)
+    store(mixed_v, mixed_out)
+    store(lse_v, lse_out)
+
+    rows_finish(0)
+    load(o_out, w_o_v, 0).start()
+    row_finish(2)
+    load(g_out, branch_v, 1).start()
+    load(o_out, w_o_v, 0).wait()
+    chunk = width // 3
+
+    def part_copy(k):
+        part = pl.ds(chunk * k, chunk)
+        return remote(
+            part_send.at[:, part], part_recv.at[:, part], part_sem.at[0, k], part_sem.at[1, k], me.over_core, me.z
+        )
+
+    for k in range(3):
+        for at in range(chunk * k, chunk * (k + 1), tile):
+            part = pl.ds(at, tile)
+            product = jnp.dot(mixed_v[...], w_o_v[:, part], preferred_element_type=jnp.float32)
+            part_send[:, part] = product.astype(jnp.bfloat16)
+            middle_v[:, part] = x_v[:, part].astype(jnp.float32) + product
+        part_copy(k).start()
+    columns_relay(3)
+    columns_relay(4)
+    for k in range(3):
+        part_copy(k).wait_recv()
+
+    def middle_rows(part):
+        value = middle_v[part, :] + part_recv[part, :].astype(jnp.float32)
+        middle_v[part, :] = value
+        return value
+
+    norm_rows(middle_rows, gain_f, nf_v, length)
+    store(middle_v, middle_out)
+    store(nf_v, nf_out)
+    load(g_out, branch_v, 1).wait()
+    rows_relay(1)
+    columns_finish(3)
+    columns_finish(4)
+
+    def ff_load(n, slot, kind):
+        first = pl.multiple_of(half_ff * kind + tile * n, 128)
+        return pltpu.make_async_copy(
+            ff_out.at[:, pl.ds(first, tile)], w_ff_v.at[slot, kind], tile_sem.at[0, slot, kind]
+        )
+
+    def tile_store(n, slot, kind):
+        part = pl.ds(pl.multiple_of(tile * n, 128), tile)
+        target = (slope_gate_out, slope_up_out, hidden_out)[kind]
+        return pltpu.make_async_copy(tile_v.at[slot, kind], target.at[:, part], tile_sem.at[1, slot, kind])
+
+    def grad_store(n, slot):
+        part = pl.ds(pl.multiple_of(tile * n, tile), tile)
+        return pltpu.make_async_copy(g_tile_v.at[slot], g_down_out.at[part, :], tile_sem.at[2, slot, 0])
+
+    count = half_ff // tile
+    for kind in range(2):
+        ff_load(0, 0, kind).start()
+
+    def ff_step(n, carry):
+        slot = lax.rem(n, 2)
+        for kind in range(2):
+            ff_load(n, slot, kind).wait()
+
+        @pl.when(n + 1 < count)
+        def _():
+            for kind in range(2):
+                ff_load(n + 1, 1 - slot, kind).start()
+
+        @pl.when(n >= 2)
+        def _():
+            for kind in range(3):
+                tile_store(n - 2, slot, kind).wait()
+            grad_store(n - 2, slot).wait()
+
+        gate = jnp.dot(nf_v[...], w_ff_v[slot, 0], preferred_element_type=jnp.float32)
+        up_value = jnp.dot(nf_v[...], w_ff_v[slot, 1], preferred_element_type=jnp.float32)
+        sigma = jax.nn.sigmoid(gate)
+        silu = gate * sigma
+        tile_v[slot, 0] = (up_value * sigma * (1.0 + gate * (1.0 - sigma))).astype(jnp.bfloat16)
+        tile_v[slot, 1] = silu.astype(jnp.bfloat16)
+        hidden = (silu * up_value).astype(jnp.bfloat16)
+        tile_v[slot, 2] = hidden
+        g_tile_v[slot] = jnp.dot(
+            hidden.T, branch_v[...], preferred_element_type=jnp.float32
+        ).astype(jnp.bfloat16)
+        for kind in range(3):
+            tile_store(n, slot, kind).start()
+        grad_store(n, slot).start()
+        return carry
+
+    lax.fori_loop(0, count, ff_step, 0)
+    for n in range(count - 2, count):
+        for kind in range(3):
+            tile_store(n, n % 2, kind).wait()
+        grad_store(n, n % 2).wait()
+    rows_finish(1)
+    for copy in stores:
+        copy.wait()
+    for k in range(3):
+        part_copy(k).wait_send()
+    for index in range(3):
+        row_wait_send(index)
     for copy in started:
         copy.wait_send()
 
 
-def gather_all(tokens, segments, out_grad, gains, weights):
+def norm_rows(read, gain, target, length, step=64):
+    def chunk(k, carry):
+        part = pl.ds(pl.multiple_of(k * step, step), step)
+        values = read(part)
+        scale = lax.rsqrt(jnp.mean(values * values, axis=-1, keepdims=True) + EPS)
+        target[part, :] = (values * scale * gain).astype(target.dtype)
+        return carry
+
+    lax.fori_loop(0, length // step, chunk, 0)
+
+
+def attend(pair, width, heads, start, mixed, lse):
+    length = heads.shape[0]
+    lane = lax.broadcasted_iota(jnp.int32, (BLK, 128), 1)
+    cols = [pl.ds(pl.multiple_of(width * kind + 128 * pair, 128), 128) for kind in range(3)]
+    for i in range(length // BLK):
+        own_rows, keys = slice(BLK * i, BLK * (i + 1)), BLK * (i + 1)
+        place = lax.broadcasted_iota(jnp.int32, (BLK, keys), 1)
+        own = BLK * i + lax.broadcasted_iota(jnp.int32, (BLK, keys), 0)
+        allowed = (place >= start[own_rows, :]) & (place <= own)
+        query = heads[own_rows, cols[0]] * jnp.bfloat16(0.125)
+        key, value = heads[0:keys, cols[1]], heads[0:keys, cols[2]]
+        kept = lse[own_rows, :]
+        outs = []
+        for half in range(2):
+            part = slice(64 * half, 64 * half + 64)
+            scores = jnp.where(allowed, nt(query[:, part], key[:, part]), -1e30)
+            peak = jnp.max(scores, axis=-1, keepdims=True)
+            expo = jnp.exp(scores - peak)
+            total = jnp.sum(expo, axis=-1, keepdims=True)
+            out = jnp.dot(expo.astype(jnp.bfloat16), value[:, part], preferred_element_type=jnp.float32)
+            outs.append((out / total).astype(jnp.bfloat16))
+            kept = jnp.where(lane == 2 * pair + half, peak + jnp.log(total), kept)
+        mixed[own_rows, cols[0]] = jnp.concatenate(outs, axis=1)
+        lse[own_rows, :] = kept
+
+
+def gather_all(tokens, segments, out_grad, gains, cosine, sine, weights):
     rows, width = tokens.shape[1], tokens.shape[2]
-    ff = weights[4].shape[1]
+    length, half, ff = 4 * rows, width // 2, weights[4].shape[1]
+    half_ff = ff // 2
     low = jnp.bfloat16
+
+    def shape(*dims, dtype=low):
+        return jax.ShapeDtypeStruct(dims, dtype)
+
     shapes = [
-        jax.ShapeDtypeStruct((4 * rows, width), low),
-        jax.ShapeDtypeStruct((4,) + segments.shape[1:], jnp.int32),
-        jax.ShapeDtypeStruct((4 * rows, width), low),
-        jax.ShapeDtypeStruct((8,) + gains.shape, low),
-        jax.ShapeDtypeStruct((width, 3 * width // 2), low),
-        jax.ShapeDtypeStruct((width // 2, width), low),
-        jax.ShapeDtypeStruct((width, ff), low),
-        jax.ShapeDtypeStruct((ff // 2, width), low),
+        shape(length, width),
+        shape(4, *segments.shape[1:], dtype=jnp.int32),
+        shape(length, width),
+        shape(8, *gains.shape),
+        shape(width, 3 * half),
+        shape(half, width),
+        shape(width, ff),
+        shape(half_ff, width),
+        shape(length, width),
+        shape(length, 3 * half),
+        shape(length, half),
+        shape(length, 128, dtype=jnp.float32),
+        shape(length, width, dtype=jnp.float32),
+        shape(length, width),
+        shape(length, half_ff),
+        shape(length, half_ff),
+        shape(length, half_ff),
+        shape(half_ff, width),
+        shape(length, 1, dtype=jnp.int32),
     ]
-    dma = pltpu.SemaphoreType.DMA
+    dma, vmem = pltpu.SemaphoreType.DMA, pltpu.VMEM
+    whole = pl.BlockSpec(memory_space=pltpu.VMEM)
     return pl.pallas_call(
         gather_kernel,
-        in_specs=[ANY] * 11,
-        out_specs=[ANY] * 8,
+        in_specs=[ANY] * 4 + [whole] * 2 + [ANY] * 7,
+        out_specs=[ANY] * len(shapes),
         out_shape=shapes,
         scratch_shapes=[
             dma((7, 7)), dma((7, 7)), dma((7,)), dma((3, 4)), dma((3, 4)), dma((3,)), dma((7,)), dma((8,)),
+            vmem((length, width), low),
+            vmem((4,) + segments.shape[1:], jnp.int32),
+            vmem((8,) + gains.shape, low),
+            vmem((length, width), low),
+            vmem((width, 3 * half), low),
+            vmem((length, 3 * half), low),
+            vmem((length, half), low),
+            vmem((half, width), low),
+            vmem((length, width), jnp.float32),
+            vmem((length, width), low),
+            vmem((length, width), low),
+            vmem((length, width), low),
+            vmem((2, 2, width, 256), low),
+            vmem((length, width), low),
+            vmem((2, 3, length, 256), low),
+            vmem((2, 256, width), low),
+            vmem((length, 128), jnp.float32),
+            vmem((length, 1), jnp.int32),
+            dma((2, 3)), dma((3,)), dma((3, 3)), dma((3, 2, 3)), dma((7,)),
         ],
-        compiler_params=pltpu.CompilerParams(collective_id=0, has_side_effects=True),
+        compiler_params=pltpu.CompilerParams(
+            collective_id=0, has_side_effects=True, vmem_limit_bytes=61 * 1024 * 1024
+        ),
         cost_estimate=pl.CostEstimate(flops=0, bytes_accessed=500_000_000, transcendentals=0),
         name="gather_all",
-    )(tokens, segments, out_grad, gains, *weights)
+    )(tokens, segments, out_grad, gains, cosine, sine, *weights)
 
 
 class ColumnJob:
@@ -1338,50 +1580,42 @@
     rows, width = tokens.shape[1], tokens.shape[2]
     own_width = width // 2
     length = 4 * rows
-    pad = -gain_attn.shape[0] % 128
-    gains = jnp.pad(jnp.stack([gain_attn, gain_ffn]), ((0, 0), (0, pad)))
-    x_low, docs, grad_branch, gains, full_qkv, full_o, full_ff, full_down = gather_all(
-        tokens, segment_ids.reshape(2, 1, rows), out_grad, gains,
-        (w_q, w_k, w_v, w_o, w_gate, w_up, w_down),
-    )
-    docs = docs.reshape(length)
-    gains = wide(gains[:, :, : width // 8].transpose(1, 0, 2).reshape(2, width))
-    gain_a, gain_f = gains[0], gains[1]
-    half_ff = full_ff.shape[1] // 2
-
+    gains = lax.dynamic_update_slice_in_dim(
+        jnp.zeros((2, width), jnp.bfloat16),
+        jnp.stack([gain_attn, gain_ffn]),
+        dp_at * gain_attn.shape[0],
+        1,
+    )
     place = jnp.arange(length, dtype=jnp.int32)
-    before = jnp.concatenate([docs[:1], docs[:-1]])
-    begins = (place == 0) | (docs != before)
-    start = lax.cummax(jnp.where(begins, place, jnp.zeros_like(place)), axis=0)
-    counts = place[: length // BLK] - start[::BLK] // BLK + 1
-    cosine, sine = rope_tables(place - start, HD // 2)
+    cosine, sine = rope_tables(place, HD // 2)
     cosine = jnp.concatenate([cosine] * 4, axis=1)
     sine = jnp.concatenate([-sine, sine, -sine, sine], axis=1)
+    (
+        x_low, docs, grad_branch, gains, full_qkv, full_o, full_ff, full_down, normed, heads, mixed,
+        logsum, middle, normed_ffn, slope_gate, slope_up, hidden, g_down, start,
+    ) = gather_all(
+        tokens, segment_ids.reshape(2, 1, rows), out_grad, gains, cosine, sine,
+        (w_q, w_k, w_v, w_o, w_gate, w_up, w_down),
+    )
+    gains = jnp.sum(wide(gains), axis=0)
+    gain_a, gain_f = gains[0], gains[1]
+    start = start.reshape(length)
+    counts = place[: length // BLK] - start[::BLK] // BLK + 1
+    logsum = logsum[:, : own_width // HD].T.reshape(own_width // 128, 2, length)
+    query, key, value = jnp.split(heads, 3, axis=1)
+    x = wide(x_low)
 
     def of_core(values, which):
         return lax.dynamic_slice_in_dim(values, length // 2 * which, length // 2, 0)
 
-    x = wide(x_low)
-    normed = low(rms_norm(x, gain_a))
-    qkv_rows = dot(normed, full_qkv)
-    query, key, value, mixed, logsum = attn_fwd(qkv_rows, cosine, sine, start[:, None], counts)
-    logsum = logsum[:, : own_width // HD].T.reshape(own_width // 128, 2, length)
-    part = dot(mixed, full_o)
-    middle = x + part + wide(swap_core(low(part)))
-    normed_ffn = low(rms_norm(middle, gain_f))
-    gate = dot(normed_ffn, full_ff[:, :half_ff])
-    up_value = dot(normed_ffn, full_ff[:, half_ff:])
-    hidden = low(jax.nn.silu(gate) * up_value)
     out_other = swap_core(low(dot(of_core(hidden, 1 - core), full_down)))
     result = of_core(middle, core) + dot(of_core(hidden, core), full_down) + wide(out_other)
     result = from_sequence(low(result), seq_at)
 
-    g_down = low(tn(hidden, grad_branch))
     grad_hidden = nt(grad_branch, full_down)
-    sigma = jax.nn.sigmoid(gate)
-    grad_gate = low(grad_hidden * up_value * sigma * (1.0 + gate * (1.0 - sigma)))
-    grad_up = low(grad_hidden * (gate * sigma))
-    grad_ff = jnp.concatenate([grad_gate, grad_up], axis=1)
+    grad_ff = jnp.concatenate(
+        [low(grad_hidden * wide(slope_gate)), low(grad_hidden * wide(slope_up))], axis=1
+    )
     g_ff = low(tn(normed_ffn, grad_ff))
     grad_nf = nt(grad_ff, full_ff)
     grad_nf = grad_nf + wide(swap_core(low(grad_nf)))

time: 838 us -> 757 us (0.903)
  matrix products: 156 us -> 99.3 us
  Pallas kernels: 588 us -> 558 us
  other arithmetic: 44 us -> 30.5 us
    dot_general x6 -> x2, matrix products: 63.7 us -> 16.3 us  [dot(): return jnp.dot(a, b, preferred_element_type=jnp.float32)]
    pallas_call x2 -> x1, Pallas kernels: 268 us -> 241 us  [gather_all(): pl.pallas_call(gather_kernel, in_specs=[ANY] * 4 + [whole] * 2 + [ANY] *...]
    dot_general x4 -> x3, matrix products: 42.4 us -> 34.2 us  [tn(): lax.dot_general(a, b, (((0,), (0,)), ((), ())), preferred_element_type=jn...]
    convert_element_type x7 -> x5, other arithmetic: 18.8 us -> 12.2 us  [wide(): return value.astype(jnp.float32)]
  transfers between devices with their start and end apart: 6 -> 5, of which waited for: 1 -> 1; matrix products, arithmetic and copies ran while one was open for 11% -> 11% of each run, Pallas kernels for 0% -> 0%
where the time goes in v4:
time: 757 us; the launch traced here: 745 us
  Pallas kernels  558 us (74%)
  matrix products  99.3 us (13%)
  waiting for transfers between devices  32.2 us (4%)
  other arithmetic  30.5 us (4%)
  local copies, waits for them, and re-layouts  12.9 us (2%)
  starting transfers between devices  10.1 us (1%)
    pallas_call x1, Pallas kernels, reduce_all(): pl.pallas_call(kernel, in_specs=[ANY] * 5 + [pl.BlockSpec(memory_space=pl...  278 us
    pallas_call x1, Pallas kernels, gather_all(): pl.pallas_call(gather_kernel, in_specs=[ANY] * 4 + [whole] * 2 + [ANY] *...  241 us
    dot_general x5, matrix products, nt(): lax.dot_general(a, b, (((1,), (1,)), ((), ())), preferred_element_type=jn...  48.8 us
    pallas_call x1, Pallas kernels, attn_bwd(): pl.pallas_call(attn_bwd_kernel, grid_spec=pltpu.PrefetchScalarGridSpec(nu...  40 us
    dot_general x3, matrix products, tn(): lax.dot_general(a, b, (((0,), (0,)), ((), ())), preferred_element_type=jn...  34.2 us
    ppermute x2, waiting for transfers between devices, from_sequence(): got.append(lax.ppermute(block, ('dp', 'seq'), reshard_pairs(turn)))  32.2 us
    dot_general x2, matrix products, dot(): return jnp.dot(a, b, preferred_element_type=jnp.float32)  16.3 us
  transfers between devices with their start and end apart: 5, of which 1 were waited for; matrix products, arithmetic and copies ran while one was open for 11% of the time, Pallas kernels for 0%

profile of v4, /device:TPU:0, one launch (start us, length us, event | category | flops | bytes accessed | tf_op | source)
XLA Modules:
  0.0 744.7 jit_solution(13867760931394486679)
XLA Ops:
  0.7 1.3 reshape.73.segments
  1.9 0.7 stack.26
  2.6 0.7 stack.25
  3.3 1.9 fusion.20
  5.2 0.2 dynamic_update_slice.3.gains
  5.4 0.0 copy-start.11
  5.4 1.8 pad_maximum_fusion.4
  7.2 240.8 %gather_all.1 = (bf16[1024,1536]{1,0:T(8,128)(2,1)}, s32[4,1,256]{2,1,0:T(1,128)}, bf16[1024,1536]{1,0:T(8,128)(2,1)}, bf16[8,2,1536]{2,1,0:T(2,128)(2,1)}, bf16...) custom-call(bf16[2,256,1536]{2,1,0:T(8,128)(2,1)} %tokens.1, ...), custom_call_target="tpu_custom_call" | custom-call | bytes 500000000 | tf_op jit(solution)/shard_map/gather_all/pallas_call | solution.py:1068
  248.0 0.0 slice-start.4
  248.0 0.0 slice-start.5
  248.0 8.1 %convolution_convert_fusion.4 = bf16[512,1536]{1,0:T(8,128)(2,1)} fusion(bf16[2048,1536]{1,0:T(8,128)(2,1)} %get-tuple-element.40, bf16[1024,2048]{1,0:T(8,128)(2,1)} %get-tuple-element.39, s32[]{:T(128)S(6)} %select_n.46), kind=kOutput, calls=%fused_computation.28 | convolution fusion | flops 3222011904 | bytes 9961476 | tf_op jit(solution)/shard_map/dot_general | solution.py:1564
  256.1 5.7 collective-permute-start
  261.8 13.6 %multiply_convert_fusion.1 = (bf16[1024,2048]{1,0:T(8,128)(2,1)}, bf16[1024,2048]{1,0:T(8,128)(2,1)}) fusion(bf16[1024,2048]{1,0:T(8,128)(2,1)} %get-tuple-element.45, bf16[1024,2048]{1,0:T(8,128)(2,1)} %get-tuple-element.46, bf16[1024,1536]{1,0:T(8,128)(2,1)S(1)} %copy-done.5, bf16[2048,1536]{1,0:T(8,128)(2,1)} %get-tuple-element.40), kind=kOutput, calls=%fused_computation.4 | convolution fusion | flops 6455033856 | bytes 26214400 | tf_op jit(solution)/shard_map/dot_general | solution.py:410
  275.4 17.2 %fusion.29 = (bf16[1024,1536]{1,0:T(8,128)(2,1)}, f32[1024,1536]{1,0:T(8,128)}) fusion(bf16[1536,4096]{1,0:T(8,128)(2,1)S(1)} %bitcast.29, bf16[1024,2048]{1,0:T(8,128)(2,1)} %get-tuple-element.72, bf16[1024,2048]{1,0:T(8,128)(2,1)} %get-tuple-element.71), kind=kOutput, calls=%fused_computation.82 | convolution fusion | flops 12903251968 | bytes 30408704 | tf_op jit(solution)/shard_map/dot_general | solution.py:410
  292.6 0.0 collective-permute-start.3
  292.6 20.3 %convolution_convert_fusion.refs_2_ = bf16[1536,4096]{1,0:T(8,128)(2,1)} fusion(bf16[1024,1536]{1,0:T(8,128)(2,1)} %get-tuple-element.55, bf16[1024,2048]{1,0:T(8,128)(2,1)} %get-tuple-element.72, bf16[1024,2048]{1,0:T(8,128)(2,1)} %get-tuple-element.71), kind=kOutput, calls=%fused_computation | convolution fusion | flops 12907970560 | bytes 24117248 | tf_op jit(solution)/shard_map/dot_general | solution.py:414
  312.9 1.2 reduce
  314.1 0.1 slice.47
  314.2 0.1 convert_reduce_fusion
  314.3 1.9 slice_bitcast_fusion
  316.2 3.4 multiply_reduce_fusion.2
  319.6 0.3 copy-done.2
  319.9 0.4 fusion.10
  320.3 1.2 copy.26
  321.6 0.0 collective-permute-done
  321.6 8.2 %add_convert_fusion = bf16[512,1536]{1,0:T(8,128)(2,1)S(1)} fusion(bf16[512,1536]{1,0:T(8,128)(2,1)} %collective-permute-done, bf16[2048,1536]{1,0:T(8,128)(2,1)} %get-tuple-element.40, f32[1024,1536]{1,0:T(8,128)} %get-tuple-element.38, s32[]{:T(128)S(6)} %select_n.45, bf16[1024,2048]{1,0:T(8,128)(2,1)} %get-tuple-element.39), kind=kOutput, calls=%fused_computation.26 | convolution fusion | flops 3224371200 | bytes 14681088 | tf_op jit(solution)/shard_map/dot_general | solution.py:1564
  329.8 0.0 slice-start.2
  329.8 0.1 broadcast_select_fusion.1
  329.9 0.8 collective-permute-start.1
  330.7 3.5 collective-permute-start.2
  334.2 0.0 slice-start
  334.3 0.0 slice-start.1
  334.3 0.0 slice-start.3
  334.3 2.8 fusion.27
  337.1 0.0 collective-permute-done.1
  337.1 32.2 %collective-permute-done.2 = bf16[256,1536]{1,0:T(8,128)(2,1)S(1)} collective-permute-done((bf16[256,1536]{1,0:T(8,128)(2,1)S(1)}, bf16[256,1536]{1,0:T(8,128)(2,1)S(1)}, u32[]{:S(2)}, u32[]{:S(2)}) %collective-permute-start.2) | collective-permute-done | bytes 786464 | tf_op jit(solution)/shard_map/ppermute | solution.py:1558
  369.3 0.1 select_bitcast_fusion.1
  369.4 1.3 pad_maximum_fusion.3
  370.7 0.0 collective-permute-done.3
  370.8 2.9 multiply_reduce_fusion
  373.7 2.3 convert_add_fusion
  376.0 0.0 copy-start
  376.1 0.0 copy-start.1
  376.1 4.4 convolution_convert_fusion.5.do_ref
  380.5 40.0 %attn_bwd.1 = (bf16[1024,768]{1,0:T(8,128)(2,1)S(1)}, bf16[1024,768]{1,0:T(8,128)(2,1)S(1)}, bf16[1024,768]{1,0:T(8,128)(2,1)S(1)}) custom-call(s32[4]{0:T(128)S(1)} %subtract_add_fusion.count_ref, bf16[1024,768]{1,0:T(8,128)(2,1)S(1)} %get-tuple-element.75.q_ref, bf16[1024,768]{1,0:T(8,128)(2,1)S(1)} %get-tuple-element.74.k_ref, ...), custom_call_target="tpu_custom_call" | custom-call | flops 8053063680 | bytes 11010048 | tf_op jit(solution)/shard_map/attn_bwd/pallas_call | solution.py:534
  420.5 0.1 constant_dynamic-update-slice_fusion.2
  420.6 1.3 copy-done.13
  421.9 4.1 convolution_convert_fusion.2.refs_1_
  426.0 0.1 constant_dynamic-update-slice_fusion.1
  426.1 0.1 constant_dynamic-update-slice_fusion
  426.2 7.0 convolution_convert_fusion.3
  433.3 0.1 collective-permute-start.4
  433.4 9.8 %convolution_convert_fusion.1.refs_0_ = bf16[1536,2304]{1,0:T(8,128)(2,1)} fusion(bf16[1024,1536]{1,0:T(8,128)(2,1)S(1)} %copy-done.12, bf16[1024,2304]{1,0:T(8,128)(2,1)S(1)} %constant_dynamic-update-slice_fusion), kind=kOutput, calls=%fused_computation.1 | convolution fusion | flops 7251296256 | bytes 14942208 | tf_op jit(solution)/shard_map/dot_general | solution.py:414
  443.2 6.7 fusion.9
  449.9 2.0 fusion.8.refs_4_
  452.0 0.6 pad_maximum_fusion.6.refs_5_
  452.6 277.6 %reduce_all.1 = (bf16[192,4608]{1,0:T(8,128)(2,1)}, bf16[192,1536]{1,0:T(8,128)(2,1)}, bf16[192,8192]{1,0:T(8,128)(2,1)}, bf16[512,1536]{1,0:T(8,128)(2,1)}, bf1...) custom-call(bf16[1536,2304]{1,0:T(8,128)(2,1)} %convolution_convert_fusion.1.refs_0_, ...), custom_call_target="tpu_custom_call" | custom-call | bytes 800000000 | tf_op jit(solution)/shard_map/reduce_all/pallas_call | solution.py:1523
  730.1 3.6 convert_element_type.126
  733.8 1.9 slice_convert_fusion.2
  735.7 1.1 convert_element_type.130
  736.8 0.7 copy-done.4
  737.5 3.5 slice_convert_fusion
  741.0 2.1 convert_element_type.133
  743.1 1.4 fusion.28
  (49 shorter events, 0.2 us)
Async XLA Ops:
  5.4 1.9 copy-start.11
  248.0 13.8 %copy-start.5 = (bf16[1024,1536]{1,0:T(8,128)(2,1)S(1)}, bf16[1024,1536]{1,0:T(8,128)(2,1)}, u32[]{:S(2)}) copy-start(bf16[1024,1536]{1,0:T(8,128)(2,1)} %get-tuple-element.44) | copy-start | bytes 9437188
  248.0 27.4 %slice-start.4 = ((s8[12582912]{0:T(1024)(128)(4,1)}), s8[4194304]{0:T(1024)(128)(4,1)S(1)}, s32[]{:S(2)}) async-start(s8[12582912]{0:T(1024)(128)(4,1)} %bitcast.28), calls=%async_computation.4 | async-start | bytes 8388608
  248.0 27.4 %slice-start.5 = ((s8[12582912]{0:T(1024)(128)(4,1)}), s8[4194304]{0:T(1024)(128)(4,1)S(1)}, s32[]{:S(2)}) async-start(s8[12582912]{0:T(1024)(128)(4,1)} %bitcast.28), calls=%async_computation.5 | async-start | bytes 8388608
  256.1 65.4 %collective-permute-start = (bf16[512,1536]{1,0:T(8,128)(2,1)}, bf16[512,1536]{1,0:T(8,128)(2,1)}, u32[]{:S(2)}, u32[]{:S(2)}) collective-permute-start(bf16[512,1536]{1,0:T(8,128)(2,1)} %convolution_convert_fusion.4), channel_id=1, source_target_pairs={{0,4},{4,0},{8,12},{12,8},{16,20},{20,16},{24,28},{28,24},{1,5},{5... | collective-permute-start | bytes 4718600 | tf_op jit(solution)/shard_map/ppermute | solution.py:1538
  261.8 13.6 %slice-start.6 = ((s8[12582912]{0:T(1024)(128)(4,1)}), s8[4194304]{0:T(1024)(128)(4,1)S(1)}, s32[]{:S(2)}) async-start(s8[12582912]{0:T(1024)(128)(4,1)} %bitcast.28), calls=%async_computation.6 | async-start | bytes 8388608
  292.6 78.1 %collective-permute-start.3 = (bf16[1024,1536]{1,0:T(8,128)(2,1)}, bf16[1024,1536]{1,0:T(8,128)(2,1)S(1)}, u32[]{:S(2)}, u32[]{:S(2)}) collective-permute-start(bf16[1024,1536]{1,0:T(8,128)(2,1)} %get-tuple-element.90), channel_id=1, source_target_pairs={{0,4},{4,0},{8,12},{12,8},{16,20},{20,16},{24,28},{28,24},{1,5},{5... | collective-permute-start | bytes 9437192 | tf_op jit(solution)/shard_map/ppermute | solution.py:1538
  292.6 21.6 %copy-start.10 = (bf16[8,2,1536]{2,1,0:T(2,128)(2,1)S(1)}, bf16[8,2,1536]{2,1,0:T(2,128)(2,1)}, u32[]{:S(2)}) copy-start(bf16[8,2,1536]{2,1,0:T(2,128)(2,1)} %get-tuple-element.48) | copy-start | bytes 147460
  316.2 3.7 copy-start.2
  329.8 41.0 %slice-start.2 = ((s8[6291456]{0:T(1024)(128)(4,1)}), s8[4194304]{0:T(1024)(128)(4,1)S(1)}, s32[]{:S(2)}) async-start(s8[6291456]{0:T(1024)(128)(4,1)} %bitcast.24), calls=%async_computation.2 | async-start | bytes 8388608
  329.9 7.2 collective-permute-start.1
  330.7 38.6 %collective-permute-start.2 = (bf16[256,1536]{1,0:T(8,128)(2,1)S(1)}, bf16[256,1536]{1,0:T(8,128)(2,1)S(1)}, u32[]{:S(2)}, u32[]{:S(2)}) collective-permute-start(bf16[256,1536]{1,0:T(8,128)(2,1)S(1)} %get-tuple-element.84), channel_id=1, source_target_pairs={{2,0},{0,1},{6,2},{4,3},{3,4},{1,5},{7,6},{5,7},{10,8},{8,9},{14,1... | collective-permute-start | bytes 2359304 | tf_op jit(solution)/shard_map/ppermute | solution.py:1558
  334.2 36.5 %slice-start = ((s8[6291456]{0:T(1024)(128)(4,1)}), s8[4194304]{0:T(1024)(128)(4,1)S(1)}, s32[]{:S(2)}) async-start(s8[6291456]{0:T(1024)(128)(4,1)} %bitcast.22), calls=%async_computation | async-start | bytes 8388608
  334.3 36.5 %slice-start.1 = ((s8[6291456]{0:T(1024)(128)(4,1)}), s8[2097152]{0:T(1024)(128)(4,1)S(1)}, s32[]{:S(2)}) async-start(s8[6291456]{0:T(1024)(128)(4,1)} %bitcast.22), calls=%async_computation.1 | async-start | bytes 4194304
  334.3 36.5 %slice-start.3 = ((s8[6291456]{0:T(1024)(128)(4,1)}), s8[2097152]{0:T(1024)(128)(4,1)S(1)}, s32[]{:S(2)}) async-start(s8[6291456]{0:T(1024)(128)(4,1)} %bitcast.24), calls=%async_computation.3 | async-start | bytes 4194304
  370.8 2.9 copy-start.6
  376.0 4.4 copy-start
  376.1 4.4 copy-start.1
  420.5 1.4 copy-start.13
  426.2 7.1 copy-start.12
  433.3 9.9 %collective-permute-start.4 = (bf16[512,1536]{1,0:T(8,128)(2,1)S(1)}, bf16[512,1536]{1,0:T(8,128)(2,1)S(1)}, u32[]{:S(2)}, u32[]{:S(2)}) collective-permute-start(bf16[512,1536]{1,0:T(8,128)(2,1)S(1)} %convolution_convert_fusion.3), channel_id=1, source_target_pairs={{0,4},{4,0},{8,12},{12,8},{16,20},{20,16},{24,28},{28,24},{1,5},{5... | collective-permute-start | bytes 4718600 | tf_op jit(solution)/shard_map/ppermute | solution.py:1538
  433.4 9.8 %copy-start.3 = (bf16[1024,1536]{1,0:T(8,128)(2,1)S(1)}, bf16[1024,1536]{1,0:T(8,128)(2,1)}, u32[]{:S(2)}) copy-start(bf16[1024,1536]{1,0:T(8,128)(2,1)} %get-tuple-element.57) | copy-start | bytes 9437188
  730.1 3.6 copy-start.7
  733.8 1.9 copy-start.9
  733.8 3.8 copy-start.4
  737.5 3.5 copy-start.8

commit v5 on v4

--- a/solution.py
+++ b/solution.py
@@ -1,7 +1,9 @@
+import functools
 import math
 
 import jax
 import jax.numpy as jnp
+import numpy as np
 from jax import lax
 from jax.experimental import pallas as pl
 from jax.experimental.pallas import tpu as pltpu
@@ -414,139 +416,6 @@
     return lax.dot_general(a, b, (((0,), (0,)), ((), ())), preferred_element_type=jnp.float32)
 
 
-def attn_fwd_kernel(count_ref, q_ref, k_ref, v_ref, cos_ref, sin_ref, start_ref,
-                    qr_ref, kr_ref, vr_ref, mixed_ref, lse_ref):
-    pair = pl.program_id(0)
-    cosine, sine = cos_ref[...], sin_ref[...]
-    q = q_ref[...]
-    qr_ref[...] = (q * cosine + swap_halves(q) * sine).astype(jnp.bfloat16)
-    k = k_ref[...]
-    kr_ref[...] = (k * cosine + swap_halves(k) * sine).astype(jnp.bfloat16)
-    vr_ref[...] = v_ref[...].astype(jnp.bfloat16)
-    length = q_ref.shape[0]
-    lane = lax.broadcasted_iota(jnp.int32, (BLK, 128), 1)
-
-    def one_block(i, carry):
-        row0 = pl.multiple_of(i * BLK, BLK)
-        rows = pl.ds(row0, BLK)
-        for n in range(1, length // BLK + 1):
-            @pl.when(count_ref[i] == n)
-            def _():
-                width = n * BLK
-                key0 = pl.multiple_of((i - (n - 1)) * BLK, BLK)
-                keys = pl.ds(key0, width)
-                place = key0 + lax.broadcasted_iota(jnp.int32, (BLK, width), 1)
-                own = row0 + lax.broadcasted_iota(jnp.int32, (BLK, width), 0)
-                allowed = (place >= start_ref[rows, :]) & (place <= own)
-                for half in range(2):
-                    cols = slice(64 * half, 64 * half + 64)
-                    s = nt(qr_ref[rows, cols] * jnp.bfloat16(0.125), kr_ref[keys, cols])
-                    s = jnp.where(allowed, s, -1e30)
-                    peak = jnp.max(s, axis=-1, keepdims=True)
-                    expo = jnp.exp(s - peak)
-                    total = jnp.sum(expo, axis=-1, keepdims=True)
-                    out = jnp.dot(expo.astype(jnp.bfloat16), vr_ref[keys, cols],
-                                  preferred_element_type=jnp.float32)
-                    mixed_ref[rows, cols] = (out / total).astype(jnp.bfloat16)
-                    lse = peak + jnp.log(total)
-                    old = lse_ref[rows, :]
-                    lse_ref[rows, :] = jnp.where(lane == 2 * pair + half, lse, old)
-        return carry
-
-    lax.fori_loop(0, length // BLK, one_block, 0)
-
-
-def attn_fwd(qkv, cosine, sine, start, counts):
-    length, width = qkv.shape[0], qkv.shape[1] // 3
-    pairs = width // 128
-    col = pl.BlockSpec((length, 128), lambda p, c: (0, p))
-    key_col = pl.BlockSpec((length, 128), lambda p, c: (0, pairs + p))
-    value_col = pl.BlockSpec((length, 128), lambda p, c: (0, 2 * pairs + p))
-    fixed = pl.BlockSpec((length, 128), lambda p, c: (0, 0))
-    scol = pl.BlockSpec((length, 1), lambda p, c: (0, 0))
-    low = jax.ShapeDtypeStruct((length, width), jnp.bfloat16)
-    return pl.pallas_call(
-        attn_fwd_kernel,
-        grid_spec=pltpu.PrefetchScalarGridSpec(
-            num_scalar_prefetch=1, grid=(pairs,),
-            in_specs=[col, key_col, value_col, fixed, fixed, scol],
-            out_specs=[col, col, col, col, fixed],
-        ),
-        out_shape=[low, low, low, low, jax.ShapeDtypeStruct((length, 128), jnp.float32)],
-        compiler_params=pltpu.CompilerParams(vmem_limit_bytes=40 * 1024 * 1024),
-        cost_estimate=pl.CostEstimate(flops=8 * length * length * width // 2, bytes_accessed=20 * length * width,
-                                      transcendentals=length * length * pairs),
-        name="attn_fwd",
-    )(counts, qkv, qkv, qkv, cosine, sine, start)
-
-
-def attn_bwd_kernel(count_ref, q_ref, k_ref, v_ref, do_ref, cos_ref, sin_ref, start_ref, lse_ref,
-                    dq_ref, dk_ref, dv_ref, dk_acc, dv_acc, dq_acc):
-    length = q_ref.shape[0]
-    dk_acc[...] = jnp.zeros_like(dk_acc)
-    dv_acc[...] = jnp.zeros_like(dv_acc)
-
-    def one_block(i, carry):
-        row0 = pl.multiple_of(i * BLK, BLK)
-        rows = pl.ds(row0, BLK)
-        for n in range(1, length // BLK + 1):
-            @pl.when(count_ref[i] == n)
-            def _():
-                width = n * BLK
-                key0 = pl.multiple_of((i - (n - 1)) * BLK, BLK)
-                keys = pl.ds(key0, width)
-                place = key0 + lax.broadcasted_iota(jnp.int32, (width, BLK), 0)
-                own = row0 + lax.broadcasted_iota(jnp.int32, (width, BLK), 1)
-                allowed = (place >= start_ref[:, rows]) & (place <= own)
-                for half in range(2):
-                    cols = slice(64 * half, 64 * half + 64)
-                    q = q_ref[rows, cols] * jnp.bfloat16(0.125)
-                    k = k_ref[keys, cols]
-                    do = do_ref[rows, cols]
-                    s = nt(k, q)
-                    probs = jnp.where(allowed, jnp.exp(s - lse_ref[0, half:half + 1, rows]), 0.0)
-                    gp = nt(v_ref[keys, cols], do)
-                    inner = jnp.sum(probs * gp, axis=0, keepdims=True)
-                    gs = (probs * (gp - inner)).astype(jnp.bfloat16)
-                    dv_acc[keys, cols] += jnp.dot(probs.astype(jnp.bfloat16), do,
-                                                  preferred_element_type=jnp.float32)
-                    dk_acc[keys, cols] += jnp.dot(gs, q, preferred_element_type=jnp.float32)
-                    dq_acc[rows, cols] = tn(gs, k) * 0.125
-        return carry
-
-    lax.fori_loop(0, length // BLK, one_block, 0)
-    cosine, sine = cos_ref[...], sin_ref[...]
-    g = dq_acc[...]
-    dq_ref[...] = (g * cosine - swap_halves(g) * sine).astype(jnp.bfloat16)
-    g = dk_acc[...]
-    dk_ref[...] = (g * cosine - swap_halves(g) * sine).astype(jnp.bfloat16)
-    dv_ref[...] = dv_acc[...].astype(jnp.bfloat16)
-
-
-def attn_bwd(q, k, v, grad, cosine, sine, start_row, counts, lse):
-    length, width = q.shape
-    pairs = width // 128
-    col = pl.BlockSpec((length, 128), lambda p, c: (0, p))
-    fixed = pl.BlockSpec((length, 128), lambda p, c: (0, 0))
-    srow = pl.BlockSpec((1, length), lambda p, c: (0, 0))
-    lrow = pl.BlockSpec((1, 2, length), lambda p, c: (p, 0, 0))
-    low = jax.ShapeDtypeStruct((length, width), jnp.bfloat16)
-    return pl.pallas_call(
-        attn_bwd_kernel,
-        grid_spec=pltpu.PrefetchScalarGridSpec(
-            num_scalar_prefetch=1, grid=(pairs,),
-            in_specs=[col, col, col, col, fixed, fixed, srow, lrow],
-            out_specs=[col, col, col],
-            scratch_shapes=[pltpu.VMEM((length, 128), jnp.float32)] * 3,
-        ),
-        out_shape=[low, low, low],
-        compiler_params=pltpu.CompilerParams(vmem_limit_bytes=40 * 1024 * 1024),
-        cost_estimate=pl.CostEstimate(flops=20 * length * length * width // 2, bytes_accessed=14 * length * width,
-                                      transcendentals=length * length * pairs),
-        name="attn_bwd",
-    )(counts, q, k, v, grad, cosine, sine, start_row, lse)
-
-
 FAST_MESH = {"dp": 8, "seq": 4}
 ANY = pl.BlockSpec(memory_space=pl.ANY)
 
@@ -586,11 +455,11 @@
 def gather_kernel(
     tokens, segments, out_grad, gains, cosine, sine, w_q, w_k, w_v, w_o, w_gate, w_up, w_down,
     x_out, seg_out, g_out, gains_out, qkv_out, o_out, ff_out, down_out,
-    normed_out, heads_out, mixed_out, lse_out, middle_out, nf_out, slope_gate_out, slope_up_out,
-    hidden_out, g_down_out, start_out,
+    heads_out, lse_out, middle_out, slope_gate_out, slope_up_out, hidden_out, g_down_out, start_out,
+    gain_out, normed_t_out, nf_t_out, mixed_t_out,
     send, recv, local, row_send, row_recv, row_local, gain_send, gain_recv,
     x_v, seg_v, gains_v, normed_v, w_qkv_v, heads_v, mixed_v, w_o_v, middle_v, part_send, part_recv,
-    nf_v, w_ff_v, branch_v, tile_v, g_tile_v, lse_v, start_v,
+    nf_v, w_ff_v, branch_v, tile_v, g_tile_v, lse_v, start_v, lse_t_v, start_row_v, gain_v, turned_v, mixed_t_v,
     part_sem, load_sem, w_sem, tile_sem, store_sem,
 ):
     me = Place()
@@ -806,6 +675,7 @@
         copy = pltpu.make_async_copy(source, target, store_sem.at[len(stores)])
         stores.append(copy)
         copy.start()
+        return copy
 
     length, width = x_v.shape
     own_width = width // 2
@@ -841,11 +711,13 @@
     for k in range(1, 8):
         both_gains = both_gains + gains_v[k].astype(jnp.float32)
     gain_a, gain_f = both_gains[0:1], both_gains[1:2]
+    gain_v[...] = both_gains
+    store(gain_v, gain_out)
 
     norm_rows(lambda part: x_v[part, :].astype(jnp.float32), gain_a, normed_v, length)
-    store(normed_v, normed_out)
 
     docs = jnp.concatenate([seg_v[k] for k in range(4)], axis=1)
+    start_row = jnp.zeros((1, length), jnp.int32)
     for k in range(4):
         square = lax.broadcasted_iota(jnp.int32, (rows, rows), 0) == lax.broadcasted_iota(
             jnp.int32, (rows, rows), 1
@@ -854,7 +726,11 @@
         start_v[pl.ds(rows * k, rows), :] = jnp.sum(
             jnp.where(docs < ids, 1, 0), axis=1, keepdims=True
         )
-    store(start_v, start_out)
+        start_row = start_row + jnp.sum(jnp.where(ids < docs, 1, 0), axis=0, keepdims=True)
+    start_row_v[...] = start_row
+    store(start_row_v, start_out)
+    turn(normed_v, turned_v)
+    normed_store = store(turned_v, normed_t_out)
 
     for index in range(3):
         columns_finish(index)
@@ -888,8 +764,10 @@
         if t == 1:
             rows_start(1)
     store(heads_v, heads_out)
-    store(mixed_v, mixed_out)
-    store(lse_v, lse_out)
+    lse_t_v[...] = lse_v[...].T
+    store(lse_t_v, lse_out)
+    turn(mixed_v, mixed_t_v)
+    store(mixed_t_v, mixed_t_out)
 
     rows_finish(0)
     load(o_out, w_o_v, 0).start()
@@ -923,7 +801,9 @@
 
     norm_rows(middle_rows, gain_f, nf_v, length)
     store(middle_v, middle_out)
-    store(nf_v, nf_out)
+    normed_store.wait()
+    turn(nf_v, turned_v)
+    store(turned_v, nf_t_out)
     load(g_out, branch_v, 1).wait()
     rows_relay(1)
     columns_finish(3)
@@ -987,13 +867,19 @@
         grad_store(n, n % 2).wait()
     rows_finish(1)
     for copy in stores:
-        copy.wait()
+        if copy is not normed_store:
+            copy.wait()
     for k in range(3):
         part_copy(k).wait_send()
     for index in range(3):
         row_wait_send(index)
     for copy in started:
         copy.wait_send()
+
+
+def turn(source, target):
+    for k in range(source.shape[1] // 256):
+        target[256 * k : 256 * (k + 1), :] = source[:, 256 * k : 256 * (k + 1)].T
 
 
 def norm_rows(read, gain, target, length, step=64):
@@ -1051,17 +937,18 @@
         shape(half, width),
         shape(width, ff),
         shape(half_ff, width),
-        shape(length, width),
         shape(length, 3 * half),
-        shape(length, half),
-        shape(length, 128, dtype=jnp.float32),
+        shape(128, length, dtype=jnp.float32),
         shape(length, width, dtype=jnp.float32),
-        shape(length, width),
         shape(length, half_ff),
         shape(length, half_ff),
         shape(length, half_ff),
         shape(half_ff, width),
-        shape(length, 1, dtype=jnp.int32),
+        shape(1, length, dtype=jnp.int32),
+        shape(2, width, dtype=jnp.float32),
+        shape(width, length),
+        shape(width, length),
+        shape(half, length),
     ]
     dma, vmem = pltpu.SemaphoreType.DMA, pltpu.VMEM
     whole = pl.BlockSpec(memory_space=pltpu.VMEM)
@@ -1090,7 +977,12 @@
             vmem((2, 256, width), low),
             vmem((length, 128), jnp.float32),
             vmem((length, 1), jnp.int32),
-            dma((2, 3)), dma((3,)), dma((3, 3)), dma((3, 2, 3)), dma((7,)),
+            vmem((128, length), jnp.float32),
+            vmem((1, length), jnp.int32),
+            vmem((2, width), jnp.float32),
+            vmem((width, length), low),
+            vmem((half, length), low),
+            dma((2, 3)), dma((3,)), dma((3, 3)), dma((3, 2, 3)), dma((9,)),
         ],
         compiler_params=pltpu.CompilerParams(
             collective_id=0, has_side_effects=True, vmem_limit_bytes=61 * 1024 * 1024
@@ -1100,169 +992,25 @@
     )(tokens, segments, out_grad, gains, cosine, sine, *weights)
 
 
-class ColumnJob:
-    def __init__(self, me, refs, source, target, first, width, half, x_first):
-        self.me, self.refs, self.x_first = me, refs, x_first
-        self.source, self.target = source, target
-        self.cols = pl.ds(first, width)
-        which, inside = first // half, first % half
-        self.out_first, self.half, self.width = 2 * half * which + inside, half, width
-        self.rows = source.shape[0] // 4
-
-    def chip_rows(self, x, y):
-        return self.source.at[pl.ds(self.rows * (2 * y + x), self.rows), self.cols]
-
-    def first_copies(self, sends_only=False):
-        me, (got, keep) = self.me, (self.refs[0], self.refs[1])
-        copies, loads = [], []
-        for k in range(2):
-            part = pl.ds(self.rows * k, self.rows)
-            if self.x_first:
-                sent, kept, to = self.chip_rows(1 - me.x, k), self.chip_rows(me.x, k), me.over_x
-            else:
-                sent, kept, to = self.chip_rows(k, 1 - me.y), self.chip_rows(k, me.y), me.over_y
-            copies.append(remote(sent, got.at[part], self.sem(0, k), self.sem(1, k), to, me.z))
-            if not sends_only:
-                loads.append(pltpu.make_async_copy(kept, keep.at[part], self.sem(2, k)))
-        return copies, loads
-
-    def sem(self, kind, k):
-        return self.refs[4].at[kind, k]
-
-    def second_copy(self):
-        me, (got, keep, second) = self.me, self.refs[:3]
-        at, to = (me.y, me.over_y) if self.x_first else (me.x, me.over_x)
-        part = keep.at[pl.ds(self.rows * (1 - at), self.rows)]
-        return remote(part, second, self.sem(0, 2), self.sem(1, 2), to, me.z)
-
-    def start(self):
-        for copy in sum(self.first_copies(), []):
-            copy.start()
-
-    def pass_second(self):
-        copies, loads = self.first_copies()
-        for k in range(2):
-            loads[k].wait()
-            copies[k].wait_recv()
-        got, keep = self.refs[:2]
-        add_rows(keep, 0, got, 2 * self.rows)
-        self.second_copy().start()
-
-    def reduce_plane(self):
-        me, (got, keep, second) = self.me, self.refs[:3]
-        at = me.y if self.x_first else me.x
-        self.second_copy().wait_recv()
-        add_rows(second, self.rows * at, keep, self.rows)
-
-    active = None
-
-    def out_piece(self, row_first, rows, core):
-        first = pl.multiple_of(self.out_first + self.half * core, 128)
-        return self.target.at[pl.ds(row_first, rows), pl.ds(first, self.width)]
-
-    def last_copy(self, final):
-        me, rows = self.me, self.rows // 2
-        part = final.at[pl.ds(rows * (1 - me.core), rows)]
-        return remote(
-            part, self.out_piece(0, rows, me.core), self.sem(0, 3), self.sem(1, 3), me.over_core, me.z
-        )
-
-    def own_copy(self, final):
-        me, rows = self.me, self.rows // 2
-        part = final.at[pl.ds(rows * me.core, rows)]
-        return pltpu.make_async_copy(part, self.out_piece(0, rows, me.core), self.sem(2, 0))
-
-    def finish(self, final):
-        self.last_copy(final).start()
-        self.own_copy(final).start()
-
-    def drain(self, final):
-        me, rows = self.me, self.rows // 2
-        for copy in self.first_copies(True)[0]:
-            copy.wait_send()
-        self.second_copy().wait_send()
-        self.last_copy(final).wait_send()
-        self.own_copy(final).wait()
-        part = final.at[pl.ds(rows * me.core, rows)]
-        remote(
-            part, self.out_piece(0, rows, 1 - me.core), self.sem(0, 3), self.sem(1, 3), me.over_core, me.z
-        ).wait_recv()
-
-
-class RowJob:
-    def __init__(self, me, refs, source, target, first, width):
-        self.me, self.refs = me, refs
-        self.source, self.target = source, target
-        self.cols = pl.ds(first, width)
-        self.rows = source.shape[0] // 2
-        self.active = me.core == me.y
-
-    sem = ColumnJob.sem
-
-    def first_copy(self):
-        me, got = self.me, self.refs[0]
-        sent = self.source.at[pl.ds(self.rows * (1 - me.x), self.rows), self.cols]
-        return remote(sent, got, self.sem(0, 0), self.sem(1, 0), me.over_x, me.z)
-
-    def load(self):
-        kept = self.source.at[pl.ds(self.rows * self.me.x, self.rows), self.cols]
-        return pltpu.make_async_copy(kept, self.refs[1], self.sem(2, 0))
-
-    def second_copy(self):
-        me, (got, keep, second) = self.me, self.refs[:3]
-        return remote(keep, second, self.sem(0, 2), self.sem(1, 2), me.over_y, me.z)
-
-    def start(self):
-        self.first_copy().start()
-        self.load().start()
-
-    def pass_second(self):
-        self.load().wait()
-        self.first_copy().wait_recv()
-        got, keep = self.refs[:2]
-        add_rows(keep, 0, got, self.rows)
-
-        @pl.when(jnp.logical_not(self.active))
-        def _():
-            self.second_copy().start()
-
-    def reduce_plane(self):
-        got, keep, second = self.refs[:3]
-
-        @pl.when(self.active)
-        def _():
-            self.second_copy().wait_recv()
-            add_rows(second, 0, keep, self.rows)
-
-    def last_copy(self, final):
-        me, rows = self.me, self.rows // 2
-        part = final.at[pl.ds(rows * (1 - me.core), rows)]
-        target = self.target.at[:, self.cols]
-        return remote(part, target, self.sem(0, 3), self.sem(1, 3), me.over_core, me.z)
-
-    def own_copy(self, final):
-        me, rows = self.me, self.rows // 2
-        part = final.at[pl.ds(rows * me.core, rows)]
-        return pltpu.make_async_copy(part, self.target.at[:, self.cols], self.sem(2, 1))
-
-    def finish(self, final):
-        @pl.when(self.active)
-        def _():
-            self.last_copy(final).start()
-            self.own_copy(final).start()
-
-    def drain(self, final):
-        self.first_copy().wait_send()
-
-        @pl.when(self.active)
-        def _():
-            self.last_copy(final).wait_send()
-            self.own_copy(final).wait()
-
-        @pl.when(jnp.logical_not(self.active))
-        def _():
-            self.second_copy().wait_send()
-            self.last_copy(final).wait_recv()
+def guard(condition, action):
+    if isinstance(condition, (bool, np.bool_)):
+        if condition:
+            action()
+    else:
+        pl.when(condition)(action)
+
+
+def everything(*conditions):
+    known = [c for c in conditions if isinstance(c, (bool, np.bool_))]
+    if not all(known):
+        return False
+    rest = [c for c in conditions if not isinstance(c, (bool, np.bool_))]
+    if not rest:
+        return True
+    total = rest[0]
+    for c in rest[1:]:
+        total = total & c
+    return total
 
 
 def add_rows(target, first, other, rows, step=64):
@@ -1275,94 +1023,331 @@
     lax.fori_loop(0, rows // step, chunk, 0)
 
 
-def both(active, condition):
-    return condition if active is None else active & condition
-
-
-def final_of(job):
-    return job.refs[0].at[pl.ds(0, job.rows)]
-
-
-def seq_copy(job, step):
-    me, total, over, sem = job.me, job.refs[2], job.refs[3], job.refs[5]
-    inner = me.z + 1 - 2 * (me.z // 2)
-    opposite = 3 - me.z
-    outer = 3 * (me.z // 2)
-    if step == 0:
-        return remote(total, over.at[0], sem.at[0, 0], sem.at[1, 0], me.dp, inner)
-    if step == 1:
-        return remote(total, over.at[1], sem.at[0, 1], sem.at[1, 1], me.dp, opposite)
-    return remote(final_of(job), final_of(job), sem.at[0, 2], sem.at[1, 2], me.dp, outer)
-
-
-def plane_and_seq_first(job):
-    job.reduce_plane()
-
-    @pl.when(both(job.active, jnp.logical_not(job.me.middle)))
-    def _():
-        seq_copy(job, 0).start()
-
-
-def seq_second(job):
-    @pl.when(both(job.active, job.me.middle))
-    def _():
-        seq_copy(job, 0).wait_recv()
-        add_rows(job.refs[2], 0, job.refs[3].at[0], job.rows)
-        seq_copy(job, 1).start()
-
-
-def seq_third(job):
-    @pl.when(both(job.active, job.me.middle))
-    def _():
-        seq_copy(job, 1).wait_recv()
-        final, total, over, step = final_of(job), job.refs[2], job.refs[3].at[1], 64
-
-        def chunk(k, carry):
-            part = pl.ds(pl.multiple_of(k * step, step), step)
-            final[part, :] = total[part, :] + over[part, :]
-            return carry
-
-        lax.fori_loop(0, job.rows // step, chunk, 0)
-        seq_copy(job, 2).start()
-
-
-def finish(job):
-    @pl.when(both(job.active, jnp.logical_not(job.me.middle)))
-    def _():
-        seq_copy(job, 2).wait_recv()
-
-    job.finish(final_of(job))
-
-
-def drain(job):
-    job.drain(final_of(job))
-
-    @pl.when(both(job.active, jnp.logical_not(job.me.middle)))
-    def _():
-        seq_copy(job, 0).wait_send()
-
-    @pl.when(both(job.active, job.me.middle))
-    def _():
-        seq_copy(job, 1).wait_send()
-        seq_copy(job, 2).wait_send()
-
-
-STAGES = (
-    (0, lambda job: job.start()),
-    (2, lambda job: job.pass_second()),
-    (3, plane_and_seq_first),
-    (4, seq_second),
-    (5, seq_third),
-    (6, finish),
-)
+JOB = 256
+
+
+class Stream:
+    active = True
+
+    def tick(self, t):
+        for late, stage in reversed(self.stages):
+            k = t - late
+            guard(everything(k >= 0, k < self.count), functools.partial(stage, k))
+
+    @property
+    def ticks(self):
+        return self.count + self.stages[-1][0]
+
+    def slot(self, k):
+        return k % self.slots if isinstance(k, int) else lax.rem(k, self.slots)
+
+    def column(self, k, base=0):
+        return pl.ds(pl.multiple_of(base + JOB * k, 128), JOB)
+
+    def total(self, k):
+        return self.second.at[self.slot(k)]
+
+    def final(self, k):
+        return self.got.at[self.slot(k), pl.ds(0, self.rows)]
+
+    def seq_copy(self, k, step):
+        me, slot, sem = self.me, self.slot(k), self.seq_sem
+        inner = me.z + 1 - 2 * (me.z // 2)
+        opposite = 3 - me.z
+        outer = 3 * (me.z // 2)
+        if step == 0:
+            return remote(self.total(k), self.over.at[slot, 0], sem.at[slot, 0, 0], sem.at[slot, 1, 0], me.dp, inner)
+        if step == 1:
+            return remote(
+                self.total(k), self.over.at[slot, 1], sem.at[slot, 0, 1], sem.at[slot, 1, 1], me.dp, opposite
+            )
+        return remote(self.final(k), self.final(k), sem.at[slot, 0, 2], sem.at[slot, 1, 2], me.dp, outer)
+
+    def plane_and_ends(self, k):
+        self.reduce_plane(k)
+        guard(
+            everything(self.active, jnp.logical_not(self.me.middle)),
+            lambda: self.seq_copy(k, 0).start(),
+        )
+
+    def across(self, k):
+        def action():
+            self.seq_copy(k, 0).wait_recv()
+            add_rows(self.total(k), 0, self.over.at[self.slot(k), 0], self.rows)
+            self.seq_copy(k, 1).start()
+
+        guard(everything(self.active, self.me.middle), action)
+
+    def back(self, k):
+        def action():
+            self.seq_copy(k, 1).wait_recv()
+            final, total, over, step = self.final(k), self.total(k), self.over.at[self.slot(k), 1], 64
+
+            def chunk(at, carry):
+                part = pl.ds(pl.multiple_of(at * step, step), step)
+                final[part, :] = total[part, :] + over[part, :]
+                return carry
+
+            lax.fori_loop(0, self.rows // step, chunk, 0)
+            self.seq_copy(k, 2).start()
+
+        guard(everything(self.active, self.me.middle), action)
+
+    def finish(self, k):
+        guard(
+            everything(self.active, jnp.logical_not(self.me.middle)),
+            lambda: self.seq_copy(k, 2).wait_recv(),
+        )
+        self.output(k)
+
+    def drain(self, k):
+        self.drain_plane(k)
+
+        def ends():
+            self.seq_copy(k, 0).wait_send()
+
+        def middles():
+            self.seq_copy(k, 1).wait_send()
+            self.seq_copy(k, 2).wait_send()
+
+        guard(everything(self.active, jnp.logical_not(self.me.middle)), ends)
+        guard(everything(self.active, self.me.middle), middles)
+
+
+class ColumnStream(Stream):
+    def __init__(self, me, source, target, ff_jobs, d_model, ff, refs):
+        self.me, self.source, self.target = me, source, target
+        self.got, self.keep, self.second, self.over, self.sem, self.seq_sem, self.credit = refs
+        self.slots, self.rows = self.got.shape[0], source.shape[0] // 4
+        self.count, self.ff_jobs = source.shape[1] // JOB, ff_jobs
+        self.ff, self.d_model = ff, d_model
+        self.stages = (
+            (0, self.start), (3, self.pass_second), (4, self.plane_and_ends), (5, self.across),
+            (6, self.back), (7, self.finish), (8, self.drain),
+        )
+
+    def x_first(self, k):
+        late = k // self.ff_jobs
+        return (1 - late) * ((k // (self.ff_jobs // 2)) % 2) * ((k + 1) % 2) + late * (k % 2)
+
+    def first_copy(self, k, part):
+        me, slot, x_first = self.me, self.slot(k), self.x_first(k)
+        block = x_first * (2 * part + 1 - me.x) + (1 - x_first) * (2 * (1 - me.y) + part)
+        sent = self.source.at[pl.ds(pl.multiple_of(self.rows * block, self.rows), self.rows), self.column(k)]
+        to = x_first * me.over_x + (1 - x_first) * me.over_y
+        return remote(
+            sent, self.got.at[slot, pl.ds(self.rows * part, self.rows)],
+            self.sem.at[slot, 0, part], self.sem.at[slot, 1, part], to, me.z,
+        )
+
+    def keep_copy(self, k, part):
+        me, slot, x_first = self.me, self.slot(k), self.x_first(k)
+        block = x_first * (2 * part + me.x) + (1 - x_first) * (2 * me.y + part)
+        kept = self.source.at[pl.ds(pl.multiple_of(self.rows * block, self.rows), self.rows), self.column(k)]
+        return pltpu.make_async_copy(
+            kept, self.keep.at[slot, pl.ds(self.rows * part, self.rows)], self.sem.at[slot, 2, part]
+        )
+
+    def at(self, k):
+        x_first = self.x_first(k)
+        return x_first * self.me.y + (1 - x_first) * self.me.x
+
+    def second_copy(self, k):
+        me, slot, x_first = self.me, self.slot(k), self.x_first(k)
+        row = pl.multiple_of(self.rows * (1 - self.at(k)), self.rows)
+        to = x_first * me.over_y + (1 - x_first) * me.over_x
+        return remote(
+            self.keep.at[slot, pl.ds(row, self.rows)], self.second.at[slot],
+            self.sem.at[slot, 0, 2], self.sem.at[slot, 1, 2], to, me.z,
+        )
+
+    def start(self, k):
+        def credits():
+            slot = self.slot(k)
+
+            @pl.when(self.me.middle)
+            def _():
+                pl.semaphore_wait(self.credit.at[slot], 5)
+
+            @pl.when(jnp.logical_not(self.me.middle))
+            def _():
+                pl.semaphore_wait(self.credit.at[slot], 4)
+
+        guard(k >= self.slots, credits)
+        for part in range(2):
+            self.first_copy(k, part).start()
+            self.keep_copy(k, part).start()
+
+    def pass_second(self, k):
+        for part in range(2):
+            self.keep_copy(k, part).wait()
+            self.first_copy(k, part).wait_recv()
+        slot = self.slot(k)
+        add_rows(self.keep.at[slot], 0, self.got.at[slot], 2 * self.rows)
+        self.second_copy(k).start()
+
+    def reduce_plane(self, k):
+        self.second_copy(k).wait_recv()
+        add_rows(self.total(k), self.rows * self.at(k), self.keep.at[self.slot(k)], self.rows)
+
+    def out_column(self, k, core, late):
+        if late:
+            m, half = k - self.ff_jobs, self.d_model // 2
+            tiles = half // JOB
+            first = 2 * self.ff + self.d_model * (m // tiles) + JOB * (m % tiles) + half * core
+        else:
+            first = self.ff * (k % 2) + JOB * (k // 2) + self.ff // 2 * core
+        return self.target.at[:, pl.ds(pl.multiple_of(first, 128), JOB)]
+
+    def last_copy(self, k, late=False):
+        me, slot, rows = self.me, self.slot(k), self.rows // 2
+        part = self.got.at[slot, pl.ds(pl.multiple_of(rows * (1 - me.core), rows), rows)]
+        return remote(
+            part, self.out_column(k, me.core, late), self.sem.at[slot, 0, 3], self.sem.at[slot, 1, 3],
+            me.over_core, me.z,
+        )
+
+    def own_copy(self, k, late=False):
+        me, slot, rows = self.me, self.slot(k), self.rows // 2
+        part = self.got.at[slot, pl.ds(pl.multiple_of(rows * me.core, rows), rows)]
+        return pltpu.make_async_copy(part, self.out_column(k, me.core, late), self.sem.at[slot, 2, 0])
+
+    def output(self, k):
+        def begin(late):
+            self.last_copy(k, late).start()
+            self.own_copy(k, late).start()
+
+        guard(k < self.ff_jobs, lambda: begin(False))
+        guard(k >= self.ff_jobs, lambda: begin(True))
+
+    def drain_plane(self, k):
+        for part in range(2):
+            self.first_copy(k, part).wait_send()
+        self.second_copy(k).wait_send()
+
+        def end(late):
+            self.last_copy(k, late).wait()
+            self.own_copy(k, late).wait()
+
+        guard(k < self.ff_jobs, lambda: end(False))
+        guard(k >= self.ff_jobs, lambda: end(True))
+
+    def drain(self, k):
+        super().drain(k)
+
+        def signal(dp, seq):
+            pl.semaphore_signal(
+                self.credit.at[self.slot(k)], inc=1, device_id={"dp": dp, "seq": seq},
+                device_id_type=pl.DeviceIdType.MESH,
+            )
+
+        def free():
+            me = self.me
+            for dp in (me.over_core, me.over_x, me.over_y):
+                signal(dp, me.z)
+
+            @pl.when(me.middle)
+            def _():
+                signal(me.dp, 3 - me.z)
+                signal(me.dp, 3 * (me.z // 2))
+
+            @pl.when(jnp.logical_not(me.middle))
+            def _():
+                signal(me.dp, me.z + 1 - 2 * (me.z // 2))
+
+        guard(k + self.slots < self.count, free)
+
+
+class RowStream(Stream):
+    def __init__(self, me, source, target, refs):
+        self.me, self.source, self.target = me, source, target
+        self.got, self.second, self.over, self.stage, self.sem, self.seq_sem = refs
+        self.slots, self.rows = self.got.shape[0], source.shape[0] // 2
+        self.count = source.shape[1] // JOB
+        self.active = me.core == me.y
+        self.stages = (
+            (0, self.start), (1, self.load), (2, self.pass_second), (3, self.plane_and_ends), (4, self.across),
+            (5, self.back), (6, self.finish), (7, self.drain),
+        )
+
+    def first_copy(self, k):
+        me, slot = self.me, self.slot(k)
+        sent = self.source.at[pl.ds(pl.multiple_of(self.rows * (1 - me.x), self.rows), self.rows), self.column(k)]
+        return remote(sent, self.got.at[slot], self.sem.at[slot, 0, 0], self.sem.at[slot, 1, 0], me.over_x, me.z)
+
+    def load_copy(self, k):
+        kept = self.source.at[
+            pl.ds(pl.multiple_of(self.rows * self.me.x, self.rows), self.rows), self.column(k)
+        ]
+        return pltpu.make_async_copy(kept, self.stage, self.sem.at[self.slot(k), 2, 0])
+
+    def second_copy(self, k):
+        me, slot = self.me, self.slot(k)
+        return remote(
+            self.got.at[slot], self.second.at[slot], self.sem.at[slot, 0, 2], self.sem.at[slot, 1, 2],
+            me.over_y, me.z,
+        )
+
+    def start(self, k):
+        self.first_copy(k).start()
+
+    def load(self, k):
+        self.load_copy(k).start()
+
+    def pass_second(self, k):
+        self.load_copy(k).wait()
+        self.first_copy(k).wait_recv()
+        add_rows(self.got.at[self.slot(k)], 0, self.stage, self.rows)
+        guard(jnp.logical_not(self.active), lambda: self.second_copy(k).start())
+
+    def reduce_plane(self, k):
+        def action():
+            self.second_copy(k).wait_recv()
+            add_rows(self.total(k), 0, self.got.at[self.slot(k)], self.rows)
+
+        guard(self.active, action)
+
+    def last_copy(self, k):
+        me, slot, rows = self.me, self.slot(k), self.rows // 2
+        part = self.got.at[slot, pl.ds(pl.multiple_of(rows * (1 - me.core), rows), rows)]
+        return remote(
+            part, self.target.at[:, self.column(k)], self.sem.at[slot, 0, 3], self.sem.at[slot, 1, 3],
+            me.over_core, me.z,
+        )
+
+    def own_copy(self, k):
+        me, slot, rows = self.me, self.slot(k), self.rows // 2
+        part = self.got.at[slot, pl.ds(pl.multiple_of(rows * me.core, rows), rows)]
+        return pltpu.make_async_copy(part, self.target.at[:, self.column(k)], self.sem.at[slot, 2, 1])
+
+    def output(self, k):
+        def action():
+            self.last_copy(k).start()
+            self.own_copy(k).start()
+
+        guard(self.active, action)
+
+    def drain_plane(self, k):
+        self.first_copy(k).wait_send()
+
+        def active():
+            self.last_copy(k).wait_send()
+            self.own_copy(k).wait()
+
+        def passive():
+            self.second_copy(k).wait_send()
+            self.last_copy(k).wait_recv()
+
+        guard(self.active, active)
+        guard(jnp.logical_not(self.active), passive)
 
 
 GAIN_HOPS = 5
 
 
 class GainSums:
-    def __init__(self, me, source, target, buffer, sem):
-        self.me, self.source, self.target, self.buffer, self.sem = me, source, target, buffer, sem
+    def __init__(self, me, target, buffer, sem):
+        self.me, self.target, self.buffer, self.sem = me, target, buffer, sem
 
     def hop(self, k):
         me = self.me
@@ -1375,7 +1360,6 @@
         )
 
     def start(self):
-        self.buffer[0, 0] = self.source[...]
         self.hop(0).start()
 
     def step(self, k):
@@ -1435,219 +1419,569 @@
                 ).wait_recv()
 
 
-def run_jobs(jobs, gains):
-    for tick in range(len(jobs) + STAGES[-1][0]):
-        for late, stage in reversed(STAGES):
-            if 0 <= tick - late < len(jobs):
-                stage(jobs[tick - late])
-        if tick % 2 == 1 and tick // 2 < GAIN_HOPS:
-            gains.step(tick // 2)
-    for job in jobs:
-        drain(job)
+def attend_back(pair, width, heads, grad_mixed, start, lse, grads, key_sum, value_sum, query_sum, cosine, sine):
+    length = heads.shape[0]
+    cols = [pl.ds(pl.multiple_of(width * kind + 128 * pair, 128), 128) for kind in range(3)]
+    key_sum[...] = jnp.zeros_like(key_sum)
+    value_sum[...] = jnp.zeros_like(value_sum)
+    for i in range(length // BLK):
+        own_rows, keys = slice(BLK * i, BLK * (i + 1)), BLK * (i + 1)
+        place = lax.broadcasted_iota(jnp.int32, (keys, BLK), 0)
+        own = BLK * i + lax.broadcasted_iota(jnp.int32, (keys, BLK), 1)
+        allowed = (place >= start[:, own_rows]) & (place <= own)
+        query = heads[own_rows, cols[0]] * jnp.bfloat16(0.125)
+        key, value = heads[0:keys, cols[1]], heads[0:keys, cols[2]]
+        grad = grad_mixed[own_rows, cols[0]]
+        for half in range(2):
+            part = slice(64 * half, 64 * half + 64)
+            scores = nt(key[:, part], query[:, part])
+            logsum = lse[pl.ds(2 * pair + half, 1), own_rows]
+            probs = jnp.where(allowed, jnp.exp(scores - logsum), 0.0)
+            grad_probs = nt(value[:, part], grad[:, part])
+            inner = jnp.sum(probs * grad_probs, axis=0, keepdims=True)
+            grad_scores = (probs * (grad_probs - inner)).astype(jnp.bfloat16)
+            value_sum[0:keys, part] += dot(probs.astype(jnp.bfloat16), grad[:, part])
+            key_sum[0:keys, part] += dot(grad_scores, query[:, part])
+            query_sum[own_rows, part] = tn(grad_scores, key[:, part]) * 0.125
+    for kind, total in enumerate((query_sum, key_sum)):
+        value = total[...]
+        grads[:, cols[kind]] = (value * cosine[...] - swap_halves(value) * sine[...]).astype(jnp.bfloat16)
+    grads[:, cols[2]] = value_sum[...].astype(jnp.bfloat16)
+
+
+def backward_kernel(
+    branch_h, slope_gate_h, slope_up_h, hidden_h, nf_t_h, normed_t_h, mixed_t_h, heads_h, lse_h, middle_h, x_h,
+    g_down_h, w_qkv_h, w_o_h, w_ff_h, w_down_h, start_ref, gain_ref, cosine, sine,
+    out_o, tokens_o, cols_o, o_o, down_o, gains_o, g_cols_h, g_o_h, kept_h, rows_h, grad_nf_h,
+    col_got, col_keep, col_second, col_over, col_sem, col_seq, col_credit,
+    down_got, down_second, down_over, down_stage, down_sem, down_seq,
+    o_got, o_second, o_over, o_stage, o_sem, o_seq,
+    wide_recv, half_recv, half_free, wide_sem, half_sem,
+    gain_buffer, gain_sem, row_sem, load_sem, tile_sem, store_sem,
+):
+    me = Place()
+    enter(
+        [(me.over_core, me.z), (me.over_x, me.z), (me.over_y, me.z)]
+        + [(me.dp - me.core + core, lax.rem(me.z + k, 4)) for k in range(1, 4) for core in range(2)]
+    )
+    length, width = branch_h.shape
+    half_rows, own_width, half_ff = length // 2, width // 2, slope_gate_h.shape[1]
+    bf16, f32 = jnp.bfloat16, jnp.float32
+    vmem = pltpu.VMEM
+    ff_jobs = 2 * half_ff // JOB
+    cols = ColumnStream(
+        me, g_cols_h, cols_o, ff_jobs, width, 2 * half_ff,
+        (col_got, col_keep, col_second, col_over, col_sem, col_seq, col_credit),
+    )
+    downs = RowStream(
+        me, g_down_h, down_o, (down_got, down_second, down_over, down_stage, down_sem, down_seq)
+    )
+    outs = RowStream(me, g_o_h, o_o, (o_got, o_second, o_over, o_stage, o_sem, o_seq))
+    back_out = RowsBack(me, rows_h.at[0], out_o, row_sem.at[0])
+    back_tokens = RowsBack(me, rows_h.at[1], tokens_o, row_sem.at[1])
+    gains = GainSums(me, gains_o, gain_buffer, gain_sem)
+
+    def load(source, target, k=0):
+        return pltpu.make_async_copy(source, target, load_sem.at[k])
+
+    def fetch(*pairs):
+        for k, (source, target) in enumerate(pairs):
+            load(source, target, k).start()
+        for k, (source, target) in enumerate(pairs):
+            load(source, target, k).wait()
+
+    def lanes(n, size=JOB, base=0):
+        return pl.ds(pl.multiple_of(base + size * n, 128), size)
+
+    def sublanes(n, size):
+        return pl.ds(pl.multiple_of(n * size, size), size)
+
+    def grad_store(buffer, slot, target, n, k):
+        return pltpu.make_async_copy(buffer.at[slot], target.at[:, lanes(n)], store_sem.at[slot, k])
+
+    downs.tick(0)
+
+    def feed_forward(grad_ff):
+        steps = half_ff // JOB
+
+        def hidden_grads(branch, w_tile, slopes, nf_t, g_tile):
+            def tile_loads(n, slot):
+                return (
+                    pltpu.make_async_copy(w_down_h.at[sublanes(n, JOB), :], w_tile.at[slot], tile_sem.at[slot, 0]),
+                    pltpu.make_async_copy(slope_gate_h.at[:, lanes(n)], slopes.at[slot, 0], tile_sem.at[slot, 1]),
+                    pltpu.make_async_copy(slope_up_h.at[:, lanes(n)], slopes.at[slot, 1], tile_sem.at[slot, 2]),
+                )
+
+            for copy in tile_loads(0, 0):
+                copy.start()
+            fetch((branch_h, branch), (nf_t_h, nf_t))
+            downs.tick(1)
+
+            def step(n, carry):
+                slot = lax.rem(n, 2)
+                for copy in tile_loads(n, slot):
+                    copy.wait()
+
+                @pl.when(n + 1 < steps)
+                def _():
+                    for copy in tile_loads(n + 1, 1 - slot):
+                        copy.start()
+
+                grad_hidden = nt(branch[...], w_tile[slot])
+
+                @pl.when(n > 0)
+                def _():
+                    for kind in range(2):
+                        grad_store(g_tile, kind, g_cols_h, 2 * n - 2 + kind, 0).wait()
+
+                for kind in range(2):
+                    grad = (grad_hidden * slopes[slot, kind].astype(f32)).astype(bf16)
+                    grad_ff[:, lanes(n, JOB, half_ff * kind)] = grad
+                    g_tile[kind] = dot(nf_t[...], grad).astype(bf16)
+                    grad_store(g_tile, kind, g_cols_h, 2 * n + kind, 0).start()
+
+                @pl.when(lax.rem(n, 2) == 1)
+                def _():
+                    cols.tick(n // 2)
+
+                @pl.when((lax.rem(n, 2) == 0) & (n > 0))
+                def _():
+                    downs.tick(1 + n // 2)
+
+                return carry
+
+            lax.fori_loop(0, steps, step, 0)
+            for kind in range(2):
+                grad_store(g_tile, kind, g_cols_h, 2 * steps - 2 + kind, 0).wait()
+
+        pl.run_scoped(
+            hidden_grads, vmem((length, width), bf16), vmem((2, JOB, width), bf16),
+            vmem((2, 2, length, JOB), bf16), vmem((width, length), bf16), vmem((2, width, JOB), bf16),
+        )
+
+        def layer_out(hidden, w_down, send, total):
+            other, own = 1 - me.core, me.core
+            fetch((w_down_h, w_down), (hidden_h.at[sublanes(other, half_rows), :], hidden))
+            load(middle_h.at[sublanes(own, half_rows), :], total, 2).start()
+
+            def other_tile(n, carry):
+                send[:, lanes(n)] = dot(hidden[...], w_down[:, lanes(n)]).astype(bf16)
+                return carry
+
+            lax.fori_loop(0, width // JOB, other_tile, 0)
+            exchange = remote(send, half_recv, half_sem.at[0, 0], half_sem.at[1, 0], me.over_core, me.z)
+            exchange.start()
+            fetch((hidden_h.at[sublanes(own, half_rows), :], hidden))
+            load(middle_h.at[sublanes(own, half_rows), :], total, 2).wait()
+
+            def own_tile(n, carry):
+                total[:, lanes(n)] += dot(hidden[...], w_down[:, lanes(n)])
+                return carry
+
+            lax.fori_loop(0, width // JOB, own_tile, 0)
+            exchange.wait()
+
+            def combine(k, carry):
+                part = sublanes(k, 64)
+                send[part, :] = (total[part, :] + half_recv[part, :].astype(f32)).astype(bf16)
+                return carry
+
+            lax.fori_loop(0, half_rows // 64, combine, 0)
+            pl.semaphore_signal(
+                half_free, inc=1, device_id={"dp": me.over_core, "seq": me.z},
+                device_id_type=pl.DeviceIdType.MESH,
+            )
+            fetch((send, rows_h.at[0]))
+
+        pl.run_scoped(
+            layer_out, vmem((half_rows, half_ff), bf16), vmem((half_ff, width), bf16),
+            vmem((half_rows, width), bf16), vmem((half_rows, width), f32),
+        )
+        back_out.start()
+        cols.tick(steps // 2)
+        downs.tick(1 + steps // 2)
+
+    chunk = 2 * JOB
+    chunks = width // chunk
+
+    def wide_copy(send, k):
+        part = pl.ds(chunk * k, chunk)
+        return remote(
+            send.at[:, part], wide_recv.at[:, part], wide_sem.at[0, k], wide_sem.at[1, k], me.over_core, me.z
+        )
+
+    def with_grad_ff(grad_ff):
+        feed_forward(grad_ff)
+
+        def input_grads(w_tile, send, parts):
+            def tile_load(n, kind):
+                return pltpu.make_async_copy(
+                    w_ff_h.at[sublanes(n, JOB), pl.ds(half_ff * kind, half_ff)], w_tile.at[kind],
+                    tile_sem.at[kind, 0],
+                )
+
+            def part_store(n, slot):
+                return pltpu.make_async_copy(parts.at[slot], grad_nf_h.at[:, lanes(n)], store_sem.at[slot, 0])
+
+            for kind in range(2):
+                tile_load(0, kind).start()
+            count = width // JOB
+
+            def step(n, carry):
+                slot = lax.rem(n, 2)
+                tile_load(n, 0).wait()
+                part = nt(grad_ff[:, 0:half_ff], w_tile[0])
+
+                @pl.when(n + 1 < count)
+                def _():
+                    tile_load(n + 1, 0).start()
+
+                tile_load(n, 1).wait()
+                part = part + nt(grad_ff[:, half_ff : 2 * half_ff], w_tile[1])
+
+                @pl.when(n + 1 < count)
+                def _():
+                    tile_load(n + 1, 1).start()
+
+                @pl.when(n >= 2)
+                def _():
+                    part_store(n - 2, slot).wait()
+
+                parts[slot] = part
+                part_store(n, slot).start()
+                send[:, lanes(n)] = part.astype(bf16)
+                for k in range(chunks):
+                    @pl.when(n == 2 * k + 1)
+                    def _():
+                        wide_copy(send, k).start()
+
+                @pl.when(lax.rem(n, 2) == 1)
+                def _():
+                    cols.tick(5 + n // 2)
+
+                @pl.when(lax.rem(n, 2) == 0)
+                def _():
+                    downs.tick(6 + n // 2)
+
+                return carry
+
+            lax.fori_loop(0, count, step, 0)
+            for n in range(count - 2, count):
+                part_store(n, n % 2).wait()
+            for k in range(chunks):
+                wide_copy(send, k).wait()
+
+        pl.run_scoped(
+            input_grads, vmem((2, JOB, half_ff), bf16), vmem((length, width), bf16), vmem((2, length, JOB), f32)
+        )
+
+    pl.run_scoped(with_grad_ff, vmem((length, 2 * half_ff), bf16))
+
+    def to_attention(grad_attn):
+        def norm_back(grad_nf, middle, branch):
+            fetch((middle_h, middle), (branch_h, branch), (grad_nf_h, grad_nf))
+            gain = gain_ref[1:2, :]
+
+            def rows(k, total):
+                part = sublanes(k, 64)
+                grad = grad_nf[part, :] + wide_recv[part, :].astype(f32)
+                gained, values = norm_rows_back(middle[part, :], gain, grad)
+                values = values + branch[part, :].astype(f32)
+                grad_nf[part, :] = values
+                grad_attn[part, :] = values.astype(bf16)
+                return total + gained
+
+            total = lax.fori_loop(0, length // 64, rows, jnp.zeros((1, width), f32))
+            gain_buffer[0, 0, 1:2, :] = 0.5 * total
+            kept = load(grad_nf.at[sublanes(me.core, half_rows), :], kept_h, 0)
+            kept.start()
+            cols.tick(8)
+            kept.wait()
+
+        pl.run_scoped(
+            norm_back, vmem((length, width), f32), vmem((length, width), f32), vmem((length, width), bf16)
+        )
+
+        def out_projection(w_o, mixed_t, g_tile, grad_mixed):
+            fetch((w_o_h, w_o), (mixed_t_h, mixed_t))
+            for n in range(own_width // JOB):
+                grad_mixed[:, JOB * n : JOB * (n + 1)] = nt(
+                    grad_attn[...], w_o[JOB * n : JOB * (n + 1), :]
+                ).astype(bf16)
+            placed = load(grad_mixed, wide_recv.at[:, pl.ds(0, own_width)], 3)
+            placed.start()
+            count = width // JOB
+
+            def step(n, carry):
+                slot = lax.rem(n, 2)
+
+                @pl.when(n >= 2)
+                def _():
+                    grad_store(g_tile, slot, g_o_h, n - 2, 1).wait()
+
+                g_tile[slot] = dot(mixed_t[...], grad_attn[:, lanes(n)]).astype(bf16)
+                grad_store(g_tile, slot, g_o_h, n, 1).start()
+
+                @pl.when(lax.rem(n, 3) == 2)
+                def _():
+                    cols.tick(9 + n // 3)
+
+                return carry
+
+            lax.fori_loop(0, count, step, 0)
+            for n in range(count - 2, count):
+                grad_store(g_tile, n % 2, g_o_h, n, 1).wait()
+            placed.wait()
+
+        pl.run_scoped(
+            out_projection, vmem((own_width, width), bf16), vmem((own_width, length), bf16),
+            vmem((2, own_width, JOB), bf16), vmem((length, own_width), bf16),
+        )
+
+    pl.run_scoped(to_attention, vmem((length, width), bf16))
+
+    def attention(grads):
+        def heads_back(heads, lse, key_sum, value_sum, query_sum):
+            fetch((heads_h, heads), (lse_h, lse))
+
+            def step(pair, carry):
+                attend_back(
+                    pair, own_width, heads, wide_recv, start_ref, lse, grads, key_sum, value_sum, query_sum, cosine, sine
+                )
+                outs.tick(pair)
+
+                @pl.when(pair > 0)
+                def _():
+                    cols.tick(10 + pair)
+
+                @pl.when(pair < 4)
+                def _():
+                    downs.tick(9 + pair)
+
+                return carry
+
+            lax.fori_loop(0, own_width // 128, step, 0)
+
+        pl.run_scoped(
+            heads_back, vmem((length, 3 * own_width), bf16), vmem((128, length), f32),
+            *[vmem((length, 128), f32)] * 3,
+        )
+
+        def projection_grads(normed_t, g_tile):
+            fetch((normed_t_h, normed_t))
+            count = 3 * own_width // JOB
+
+            def step(n, carry):
+                slot = lax.rem(n, 2)
+                g_tile[slot] = dot(normed_t[...], grads[:, lanes(n)]).astype(bf16)
+
+                @pl.when(n >= 1)
+                def _():
+                    grad_store(g_tile, 1 - slot, g_cols_h, ff_jobs + n - 1, 1).wait()
+
+                grad_store(g_tile, slot, g_cols_h, ff_jobs + n, 1).start()
+
+                @pl.when(n >= 1)
+                def _():
+                    cols.tick(15 + n)
+
+                @pl.when(n < 7)
+                def _():
+                    outs.tick(6 + n)
+
+                return carry
+
+            lax.fori_loop(0, count, step, 0)
+            grad_store(g_tile, (count - 1) % 2, g_cols_h, ff_jobs + count - 1, 1).wait()
+
+        pl.run_scoped(projection_grads, vmem((width, length), bf16), vmem((2, width, JOB), bf16))
+
+        def tokens_back(w_tile, send, total, x_rows, kept):
+            def tile_load(n, slot):
+                return pltpu.make_async_copy(w_qkv_h.at[sublanes(n, JOB), :], w_tile.at[slot], tile_sem.at[slot, 0])
+
+            tile_load(0, 0).start()
+            load(x_h.at[sublanes(me.core, half_rows), :], x_rows, 0).start()
+            load(kept_h, kept, 1).start()
+            count = width // JOB
+
+            def step(n, carry):
+                slot = lax.rem(n, 2)
+                tile_load(n, slot).wait()
+
+                @pl.when(n + 1 < count)
+                def _():
+                    tile_load(n + 1, 1 - slot).start()
+
+                send[:, lanes(n)] = nt(grads[sublanes(1 - me.core, half_rows), :], w_tile[slot]).astype(bf16)
+                total[:, lanes(n)] = nt(grads[sublanes(me.core, half_rows), :], w_tile[slot])
+                return carry
+
+            lax.fori_loop(0, count, step, 0)
+            pl.semaphore_wait(half_free, 1)
+            exchange = remote(send, half_recv, half_sem.at[0, 0], half_sem.at[1, 0], me.over_core, me.z)
+            exchange.start()
+            cols.tick(15 + 3 * own_width // JOB)
+            load(x_h.at[sublanes(me.core, half_rows), :], x_rows, 0).wait()
+            load(kept_h, kept, 1).wait()
+            exchange.wait()
+            gain = gain_ref[0:1, :]
+
+            def rows(k, sums):
+                part = sublanes(k, 64)
+                grad = total[part, :] + half_recv[part, :].astype(f32)
+                gained, values = norm_rows_back(x_rows[part, :].astype(f32), gain, grad)
+                send[part, :] = (values + kept[part, :]).astype(bf16)
+                return sums + gained
+
+            gain_buffer[0, 0, 0:1, :] = lax.fori_loop(0, half_rows // 64, rows, jnp.zeros((1, width), f32))
+            gains.start()
+            fetch((send, rows_h.at[1]))
+
+        pl.run_scoped(
+            tokens_back, vmem((2, JOB, 3 * own_width), bf16), vmem((half_rows, width), bf16),
+            vmem((half_rows, width), f32), vmem((half_rows, width), bf16), vmem((half_rows, width), f32),
+        )
+        back_tokens.start()
+
+    pl.run_scoped(attention, vmem((length, 3 * own_width), bf16))
+
+    first = 16 + 3 * own_width // JOB
+
+    def rest(t, carry):
+        cols.tick(t)
+        for k in range(GAIN_HOPS):
+            @pl.when(t == first + 1 + k)
+            def _():
+                gains.step(k)
+
+        return carry
+
+    lax.fori_loop(first, cols.ticks, rest, 0)
     gains.drain()
-
-
-def job_plan(d_model, ff):
-    half = d_model // 2
-    down = [("down", 384 * k, 384, True) for k in range(d_model // 384)]
-    by_y = [("ff", 512 * k, 512, False) for k in range(len(down))]
-    by_turns = [("ff", 512 * k, 512, k % 2 == 0) for k in range(len(down), ff // 512)]
-    rest = [("o", half, half, True), ("qkv", 0, 384, False), ("o", 0, half, True), ("qkv", 384, 384, False)]
-    qkv = [("qkv", 384 * k, 384, k % 2 == 0) for k in range(2, 3 * half // 384)]
-    return [job for pair in zip(down, by_y) for job in pair] + by_turns + rest + qkv
-
-
-def reduce_all(g_qkv, g_o, g_ff, g_down, half_rows, gain_sums):
-    d_model, ff = g_o.shape[1], g_ff.shape[1]
-    plan = job_plan(d_model, ff)
-    sources = {"qkv": g_qkv, "o": g_o, "ff": g_ff, "down": g_down}
-    names = ("qkv", "o", "ff", "down")
-    halves = {"qkv": d_model // 2, "ff": ff // 2}
-    outs = [
-        jax.ShapeDtypeStruct((d_model // 8, 3 * d_model), jnp.bfloat16),
-        jax.ShapeDtypeStruct((d_model // 8, d_model), jnp.bfloat16),
-        jax.ShapeDtypeStruct((d_model // 8, 2 * ff), jnp.bfloat16),
-        jax.ShapeDtypeStruct((ff // 8, d_model), jnp.bfloat16),
-        jax.ShapeDtypeStruct((2, half_rows.shape[0] // 2, d_model), jnp.bfloat16),
-        jax.ShapeDtypeStruct(gain_sums.shape, jnp.float32),
+    back_out.drain()
+    back_tokens.drain()
+
+
+def norm_rows_back(values, gain, grad):
+    scale = lax.rsqrt(jnp.mean(values * values, axis=-1, keepdims=True) + EPS)
+    unit = values * scale
+    inner = grad * gain
+    return (
+        jnp.sum(grad * unit, axis=0, keepdims=True),
+        scale * (inner - unit * jnp.mean(inner * unit, axis=-1, keepdims=True)),
+    )
+
+
+COLUMN_SLOTS = 10
+
+
+def backward(branch, slopes, hidden, turned, heads, lse, middle, x, g_down, weights, start, gain, cosine, sine):
+    length, width = branch.shape
+    half, half_ff = width // 2, hidden.shape[1]
+    rows = length // 4
+    bf16, f32 = jnp.bfloat16, jnp.float32
+
+    def shape(*dims, dtype=bf16):
+        return jax.ShapeDtypeStruct(dims, dtype)
+
+    columns = 2 * half_ff + 3 * half
+    shapes = [
+        shape(2, rows, width),
+        shape(2, rows, width),
+        shape(width // 8, 2 * columns),
+        shape(width // 8, width),
+        shape(half_ff // 4, width),
+        shape(2, width, dtype=f32),
+        shape(width, columns),
+        shape(half, width),
+        shape(length // 2, width, dtype=f32),
+        shape(2, length // 2, width),
+        shape(length, width, dtype=f32),
     ]
-    dma = pltpu.SemaphoreType.DMA
-    scratch = [
-        dma((3, 2)),
-        pltpu.VMEM((GAIN_HOPS, 2) + gain_sums.shape, jnp.float32),
-        dma((2, GAIN_HOPS)),
-    ]
-    for name, first, width, x_first in plan:
-        by_columns = name in halves
-        rows = sources[name].shape[0] // (4 if by_columns else 2)
-        many = 2 * rows if by_columns else rows
-
-        def vmem(*shape):
-            return pltpu.VMEM(shape, jnp.bfloat16)
-
-        scratch += [
-            vmem(many, width), vmem(many, width), vmem(rows, width), vmem(2, rows, width), dma((3, 4)), dma((2, 3)),
+    dma, vmem = pltpu.SemaphoreType.DMA, pltpu.VMEM
+    whole = pl.BlockSpec(memory_space=pltpu.VMEM)
+    ring, row = COLUMN_SLOTS, width // 4
+    jobs = width // JOB
+    row_buffers = []
+    for depth in (half_ff // 2, half // 2):
+        row_buffers += [
+            vmem((jobs, depth, JOB), bf16), vmem((jobs, depth, JOB), bf16), vmem((jobs, 2, depth, JOB), bf16),
+            vmem((depth, JOB), bf16), dma((jobs, 3, 4)), dma((jobs, 2, 3)),
         ]
-
-    def kernel(*refs):
-        source = dict(zip(names, refs[:4]))
-        target = dict(zip(names, refs[6:10]))
-        row_sem, gain_buffer, gain_sem = refs[12:15]
-        buffers = refs[15:]
-        me = Place()
-        enter(
-            [(me.over_core, me.z)]
-            + [(me.over_x, me.z), (me.over_y, me.z)]
-            + [
-                (me.dp - me.core + core, lax.rem(me.z + k, 4))
-                for k in range(1, 4)
-                for core in range(2)
-            ]
-        )
-        rows_back = RowsBack(me, refs[4], refs[10], row_sem)
-        gains = GainSums(me, refs[5], refs[11], gain_buffer, gain_sem)
-        rows_back.start()
-        gains.start()
-        jobs = []
-        for k, (name, first, width, x_first) in enumerate(plan):
-            own = buffers[6 * k : 6 * k + 6]
-            if name in halves:
-                jobs.append(
-                    ColumnJob(me, own, source[name], target[name], first, width, halves[name], x_first)
-                )
-            else:
-                jobs.append(RowJob(me, own, source[name], target[name], first, width))
-        run_jobs(jobs, gains)
-        rows_back.drain()
-
     return pl.pallas_call(
-        kernel,
-        in_specs=[ANY] * 5 + [pl.BlockSpec(memory_space=pltpu.VMEM)],
-        out_specs=[ANY] * 5 + [pl.BlockSpec(memory_space=pltpu.VMEM)],
-        out_shape=outs,
-        scratch_shapes=scratch,
+        backward_kernel,
+        in_specs=[ANY] * 16 + [whole] * 4,
+        out_specs=[ANY] * 5 + [whole] + [ANY] * 5,
+        out_shape=shapes,
+        scratch_shapes=[
+            vmem((ring, 2 * row, JOB), bf16), vmem((ring, 2 * row, JOB), bf16), vmem((ring, row, JOB), bf16),
+            vmem((ring, 2, row, JOB), bf16), dma((ring, 3, 4)), dma((ring, 2, 3)),
+            pltpu.SemaphoreType.REGULAR((ring,)),
+        ]
+        + row_buffers
+        + [
+            vmem((length, width), bf16), vmem((length // 2, width), bf16), pltpu.SemaphoreType.REGULAR,
+            dma((2, 3)), dma((2, 1)),
+            vmem((GAIN_HOPS, 2, 2, width), f32), dma((2, GAIN_HOPS)), dma((2, 3, 2)), dma((4,)), dma((2, 3)),
+            dma((2, 2)),
+        ],
         compiler_params=pltpu.CompilerParams(
-            collective_id=1, has_side_effects=True, vmem_limit_bytes=61 * 1024 * 1024
+            collective_id=1, has_side_effects=True, vmem_limit_bytes=63 * 1024 * 1024
         ),
         cost_estimate=pl.CostEstimate(flops=0, bytes_accessed=800_000_000, transcendentals=0),
-        name="reduce_all",
-    )(g_qkv, g_o, g_ff, g_down, half_rows, gain_sums)
-
-
-def swap_core(value):
-    return lax.ppermute(value, "dp", [(i, i ^ 1) for i in range(8)])
-
-
-def reshard_pairs(turn):
-    pairs = []
-    for d in range(8):
-        for z in range(4):
-            target = ((d & 6) | (z >> 1)) * 4 + 2 * ((turn + z) % 2) + (d & 1)
-            pairs.append((target, d * 4 + z))
-    return pairs
-
-
-def from_sequence(half, seq_at):
-    rows = half.shape[0] // 2
-    early = seq_at < 2
-    got = []
-    for turn in range(2):
-        block = jnp.where(
-            early, half[rows * turn : rows * (turn + 1)], half[rows * (1 - turn) : rows * (2 - turn)]
-        )
-        got.append(lax.ppermute(block, ("dp", "seq"), reshard_pairs(turn)))
-    even = (seq_at & 1) == 0
-    return jnp.stack([jnp.where(even, got[0], got[1]), jnp.where(even, got[1], got[0])])
+        name="backward",
+    )(
+        branch, *slopes, hidden, *turned, heads, lse, middle, x, g_down, *weights, start, gain, cosine, sine
+    )
+
+
+def wide(value):
+    return value.astype(jnp.float32)
 
 
 def dot(a, b):
     return jnp.dot(a, b, preferred_element_type=jnp.float32)
-
-
-def low(value):
-    return value.astype(jnp.bfloat16)
-
-
-def wide(value):
-    return value.astype(jnp.float32)
 
 
 def column_device(
     tokens, segment_ids, out_grad, w_q, w_k, w_v, w_o, w_gate, w_up, w_down, gain_attn, gain_ffn
 ):
-    dp_at, seq_at = lax.axis_index("dp"), lax.axis_index("seq")
-    core = dp_at & 1
+    dp_at = lax.axis_index("dp")
     rows, width = tokens.shape[1], tokens.shape[2]
-    own_width = width // 2
-    length = 4 * rows
+    length, ff = 4 * rows, w_gate.shape[1]
     gains = lax.dynamic_update_slice_in_dim(
         jnp.zeros((2, width), jnp.bfloat16),
         jnp.stack([gain_attn, gain_ffn]),
         dp_at * gain_attn.shape[0],
         1,
     )
-    place = jnp.arange(length, dtype=jnp.int32)
-    cosine, sine = rope_tables(place, HD // 2)
+    cosine, sine = rope_tables(jnp.arange(length, dtype=jnp.int32), HD // 2)
     cosine = jnp.concatenate([cosine] * 4, axis=1)
     sine = jnp.concatenate([-sine, sine, -sine, sine], axis=1)
     (
-        x_low, docs, grad_branch, gains, full_qkv, full_o, full_ff, full_down, normed, heads, mixed,
-        logsum, middle, normed_ffn, slope_gate, slope_up, hidden, g_down, start,
+        x_low, docs, grad_branch, gains, full_qkv, full_o, full_ff, full_down, heads, lse, middle,
+        slope_gate, slope_up, hidden, g_down, start, gain, normed_t, nf_t, mixed_t,
     ) = gather_all(
         tokens, segment_ids.reshape(2, 1, rows), out_grad, gains, cosine, sine,
         (w_q, w_k, w_v, w_o, w_gate, w_up, w_down),
     )
-    gains = jnp.sum(wide(gains), axis=0)
-    gain_a, gain_f = gains[0], gains[1]
-    start = start.reshape(length)
-    counts = place[: length // BLK] - start[::BLK] // BLK + 1
-    logsum = logsum[:, : own_width // HD].T.reshape(own_width // 128, 2, length)
-    query, key, value = jnp.split(heads, 3, axis=1)
-    x = wide(x_low)
-
-    def of_core(values, which):
-        return lax.dynamic_slice_in_dim(values, length // 2 * which, length // 2, 0)
-
-    out_other = swap_core(low(dot(of_core(hidden, 1 - core), full_down)))
-    result = of_core(middle, core) + dot(of_core(hidden, core), full_down) + wide(out_other)
-    result = from_sequence(low(result), seq_at)
-
-    grad_hidden = nt(grad_branch, full_down)
-    grad_ff = jnp.concatenate(
-        [low(grad_hidden * wide(slope_gate)), low(grad_hidden * wide(slope_up))], axis=1
-    )
-    g_ff = low(tn(normed_ffn, grad_ff))
-    grad_nf = nt(grad_ff, full_ff)
-    grad_nf = grad_nf + wide(swap_core(low(grad_nf)))
-    grad_gain_f, grad_middle = norm_backward(middle, gain_f, grad_nf)
-    grad_middle = grad_middle + wide(grad_branch)
-    grad_attn = low(grad_middle)
-
-    grad_mixed = low(nt(grad_attn, full_o))
-    g_o = low(tn(mixed, grad_attn))
-    grad_qkv = jnp.concatenate(
-        attn_bwd(query, key, value, grad_mixed, cosine, sine, start[None, :], counts, logsum), axis=1
-    )
-    g_qkv = low(tn(normed, grad_qkv))
-    normed_other = swap_core(low(nt(of_core(grad_qkv, 1 - core), full_qkv)))
-    grad_normed = nt(of_core(grad_qkv, core), full_qkv) + wide(normed_other)
-    grad_gain_a, grad_rows = norm_backward(of_core(x, core), gain_a, grad_normed)
-    grad_rows = grad_rows + of_core(grad_middle, core)
-    gain_sums = jnp.stack([grad_gain_a, 0.5 * grad_gain_f])
-    r_qkv, r_o, r_ff, r_down, grad_tokens, grad_gains = reduce_all(
-        g_qkv, g_o, g_ff, g_down, low(grad_rows), gain_sums
-    )
+    result, grad_tokens, g_cols, g_o, g_down, grad_gains = backward(
+        grad_branch, (slope_gate, slope_up), hidden, (nf_t, normed_t, mixed_t), heads, lse, middle, x_low, g_down,
+        (full_qkv, full_o, full_ff, full_down), start, gain, cosine, sine,
+    )[:6]
     grad_gains = lax.dynamic_slice_in_dim(grad_gains, dp_at * (width // 8), width // 8, 1)
+    first = 2 * ff
     return (
         result,
         wide(grad_tokens),
-        wide(r_qkv[:, :width]),
-        wide(r_qkv[:, width : 2 * width]),
-        wide(r_qkv[:, 2 * width :]),
-        wide(r_o),
-        wide(r_ff[:, : w_gate.shape[1]]),
-        wide(r_ff[:, w_gate.shape[1] :]),
-        wide(r_down),
+        wide(g_cols[:, first : first + width]),
+        wide(g_cols[:, first + width : first + 2 * width]),
+        wide(g_cols[:, first + 2 * width :]),
+        wide(g_o),
+        wide(g_cols[:, :ff]),
+        wide(g_cols[:, ff:first]),
+        wide(g_down),
         grad_gains[0],
         grad_gains[1],
     )

time: 757 us -> 646 us (0.85); the launches traced: 745 us -> 641 us
  matrix products: 99.3 us -> 0 us
  Pallas kernels: 558 us -> 619 us
  waiting for transfers between devices: 32.2 us -> 0 us
  other arithmetic: 30.5 us -> 17.9 us
  starting transfers between devices: 10.1 us -> 0 us
  local copies, waits for them, and re-layouts: 12.9 us -> 3.67 us
    dot_general x10 -> x0, matrix products: 99.3 us -> none  [the longest x5 48.8 us: nt(): lax.dot_general(a, b, (((1,), (1,)), ((), ())), preferred_element_type=jn...]
    pallas_call x2 -> x1, Pallas kernels: 318 us -> 378 us  [backward(): pl.pallas_call(backward_kernel, in_specs=[ANY] * 16 + [whole] * 4, out_sp...]
    ppermute x5 -> x0, waiting for transfers between devices: 32.2 us -> none  [the longest x2 32.2 us: from_sequence(): got.append(lax.ppermute(block, ('dp', 'seq'), reshard_pairs(turn)))]
    ppermute x5 -> x0, starting transfers between devices: 10.1 us -> none  [the longest x3 5.75 us: swap_core(): return lax.ppermute(value, 'dp', [(i, i ^ 1) for i in range(8)])]
  transfers between devices with their start and end apart: 5 -> 0, of which waited for: 1 -> 0; matrix products, arithmetic and copies ran while one was open for 11% -> 0% of each run, Pallas kernels for 0% -> 0%
where the time goes in v5:
time: 646 us; the launch traced here: 641 us
  Pallas kernels  619 us (96%)
  other arithmetic  17.9 us (3%)
    pallas_call x1, Pallas kernels, backward(): pl.pallas_call(backward_kernel, in_specs=[ANY] * 16 + [whole] * 4, out_sp...  378 us
    pallas_call x1, Pallas kernels, gather_all(): pl.pallas_call(gather_kernel, in_specs=[ANY] * 4 + [whole] * 2 + [ANY] *...  241 us
    convert_element_type x5, other arithmetic, wide(): return value.astype(jnp.float32)  14.1 us

profile of v5, /device:TPU:0, one launch (start us, length us, event | category | flops | bytes accessed | tf_op | source)
XLA Modules:
  0.0 641.4 jit_solution(17528933124119057970)
XLA Ops:
  0.6 0.0 copy-start.6
  0.7 0.0 copy-start.7
  0.7 0.0 copy-start.5
  0.7 1.9 fusion
  2.6 1.8 pad_maximum_fusion
  4.5 0.0 copy-done.6
  4.5 0.0 copy-done.7
  4.5 0.5 dynamic_update_slice.3.gains
  5.0 0.0 copy-done.5
  5.0 0.0 copy-start.4
  5.0 0.6 reshape.34.segments
  5.6 0.0 copy-done.4
  5.6 240.8 %gather_all.1 = (bf16[1024,1536]{1,0:T(8,128)(2,1)}, s32[4,1,256]{2,1,0:T(1,128)}, bf16[1024,1536]{1,0:T(8,128)(2,1)}, bf16[8,2,1536]{2,1,0:T(2,128)(2,1)}, bf16...) custom-call(bf16[2,256,1536]{2,1,0:T(8,128)(2,1)} %tokens.1, ...), custom_call_target="tpu_custom_call" | custom-call | bytes 500000000 | tf_op jit(solution)/shard_map/gather_all/pallas_call | solution.py:955
  246.4 378.1 %backward.1 = (bf16[2,256,1536]{2,1,0:T(8,128)(2,1)}, bf16[2,256,1536]{2,1,0:T(8,128)(2,1)}, bf16[192,12800]{1,0:T(8,128)(2,1)}, bf16[192,1536]{1,0:T(8,128)(2,1...) custom-call(bf16[1024,1536]{1,0:T(8,128)(2,1)} %get-tuple-element.35, ...), custom_call_target="tpu_custom_call" | custom-call | bytes 800000000 | tf_op jit(solution)/shard_map/backward/pallas_call | solution.py:1912
  624.5 5.4 slice_convert_fusion
  629.8 0.0 copy-start.2
  629.8 3.5 slice_convert_fusion.2
  633.3 0.0 copy-start.1
  633.3 0.0 copy-done.2
  633.3 2.1 convert_element_type.46
  635.4 0.0 copy-start.3
  635.4 0.0 copy-done.1
  635.4 0.0 copy-start
  635.4 2.1 convert_element_type.53
  637.4 0.0 copy-done.3
  637.4 1.1 convert_element_type.50
  638.6 1.4 fusion.1
  640.0 0.0 copy-done
  640.0 1.1 copy.26
  (6 shorter events, 0.0 us)
Async XLA Ops:
  0.6 3.8 copy-start.6
  0.7 3.8 copy-start.7
  0.7 4.4 copy-start.5
  5.0 0.6 copy-start.4
  629.8 3.5 copy-start.2
  633.3 2.1 copy-start.1
  635.4 2.1 copy-start.3
  635.4 4.6 copy-start

commit v6 on v5

--- a/solution.py
+++ b/solution.py
@@ -1013,7 +1013,13 @@
     return total
 
 
-def add_rows(target, first, other, rows, step=64):
+def chunk_of(rows):
+    return 384 if rows % 384 == 0 else 512
+
+
+def add_rows(target, first, other, rows):
+    step = chunk_of(rows)
+
     def chunk(k, carry):
         at = pl.multiple_of(k * step, step)
         source = pl.multiple_of(first + k * step, step)
@@ -1081,7 +1087,8 @@
     def back(self, k):
         def action():
             self.seq_copy(k, 1).wait_recv()
-            final, total, over, step = self.final(k), self.total(k), self.over.at[self.slot(k), 1], 64
+            final, total, over = self.final(k), self.total(k), self.over.at[self.slot(k), 1]
+            step = chunk_of(self.rows)
 
             def chunk(at, carry):
                 part = pl.ds(pl.multiple_of(at * step, step), step)
@@ -1122,8 +1129,8 @@
         self.count, self.ff_jobs = source.shape[1] // JOB, ff_jobs
         self.ff, self.d_model = ff, d_model
         self.stages = (
-            (0, self.start), (3, self.pass_second), (4, self.plane_and_ends), (5, self.across),
-            (6, self.back), (7, self.finish), (8, self.drain),
+            (0, self.start), (2, self.pass_second), (4, self.plane_and_ends), (6, self.across),
+            (8, self.back), (9, self.finish), (10, self.drain),
         )
 
     def x_first(self, k):
@@ -1259,16 +1266,17 @@
 
 
 class RowStream(Stream):
-    def __init__(self, me, source, target, refs):
+    def __init__(self, me, source, target, lates, refs):
         self.me, self.source, self.target = me, source, target
         self.got, self.second, self.over, self.stage, self.sem, self.seq_sem = refs
         self.slots, self.rows = self.got.shape[0], source.shape[0] // 2
         self.count = source.shape[1] // JOB
         self.active = me.core == me.y
-        self.stages = (
-            (0, self.start), (1, self.load), (2, self.pass_second), (3, self.plane_and_ends), (4, self.across),
-            (5, self.back), (6, self.finish), (7, self.drain),
-        )
+        steps = (
+            self.start, self.load, self.pass_second, self.plane_and_ends, self.across, self.back, self.finish,
+            self.drain,
+        )
+        self.stages = tuple(zip(lates, steps))
 
     def first_copy(self, k):
         me, slot = self.me, self.slot(k)
@@ -1474,9 +1482,9 @@
         (col_got, col_keep, col_second, col_over, col_sem, col_seq, col_credit),
     )
     downs = RowStream(
-        me, g_down_h, down_o, (down_got, down_second, down_over, down_stage, down_sem, down_seq)
-    )
-    outs = RowStream(me, g_o_h, o_o, (o_got, o_second, o_over, o_stage, o_sem, o_seq))
+        me, g_down_h, down_o, (0, 2, 3, 5, 7, 8, 9, 10), (down_got, down_second, down_over, down_stage, down_sem, down_seq)
+    )
+    outs = RowStream(me, g_o_h, o_o, (0, 1, 2, 4, 6, 7, 8, 9), (o_got, o_second, o_over, o_stage, o_sem, o_seq))
     back_out = RowsBack(me, rows_h.at[0], out_o, row_sem.at[0])
     back_tokens = RowsBack(me, rows_h.at[1], tokens_o, row_sem.at[1])
     gains = GainSums(me, gains_o, gain_buffer, gain_sem)
@@ -1540,13 +1548,13 @@
                     g_tile[kind] = dot(nf_t[...], grad).astype(bf16)
                     grad_store(g_tile, kind, g_cols_h, 2 * n + kind, 0).start()
 
-                @pl.when(lax.rem(n, 2) == 1)
+                @pl.when((n >= 2) & (n != 5))
                 def _():
-                    cols.tick(n // 2)
-
-                @pl.when((lax.rem(n, 2) == 0) & (n > 0))
+                    cols.tick(n - 2 - n // 6)
+
+                @pl.when((n == 2) | (n == 6))
                 def _():
-                    downs.tick(1 + n // 2)
+                    downs.tick(2 + n // 6)
 
                 return carry
 
@@ -1598,8 +1606,6 @@
             vmem((half_rows, width), bf16), vmem((half_rows, width), f32),
         )
         back_out.start()
-        cols.tick(steps // 2)
-        downs.tick(1 + steps // 2)
 
     chunk = 2 * JOB
     chunks = width // chunk
@@ -1655,19 +1661,21 @@
                     def _():
                         wide_copy(send, k).start()
 
-                @pl.when(lax.rem(n, 2) == 1)
+                @pl.when(lax.rem(n, 3) == 0)
                 def _():
-                    cols.tick(5 + n // 2)
-
-                @pl.when(lax.rem(n, 2) == 0)
+                    downs.tick(4 + n // 3)
+
+                @pl.when(lax.rem(n, 3) == 2)
                 def _():
-                    downs.tick(6 + n // 2)
+                    cols.tick(5 + n // 3)
 
                 return carry
 
             lax.fori_loop(0, count, step, 0)
             for n in range(count - 2, count):
                 part_store(n, n % 2).wait()
+            cols.tick(7)
+            downs.tick(6)
             for k in range(chunks):
                 wide_copy(send, k).wait()
 
@@ -1696,6 +1704,7 @@
             kept = load(grad_nf.at[sublanes(me.core, half_rows), :], kept_h, 0)
             kept.start()
             cols.tick(8)
+            downs.tick(7)
             kept.wait()
 
         pl.run_scoped(
@@ -1722,7 +1731,7 @@
                 g_tile[slot] = dot(mixed_t[...], grad_attn[:, lanes(n)]).astype(bf16)
                 grad_store(g_tile, slot, g_o_h, n, 1).start()
 
-                @pl.when(lax.rem(n, 3) == 2)
+                @pl.when(lax.rem(n, 3) == 1)
                 def _():
                     cols.tick(9 + n // 3)
 
@@ -1750,13 +1759,13 @@
                 )
                 outs.tick(pair)
 
-                @pl.when(pair > 0)
+                @pl.when(lax.rem(pair, 3) != 2)
                 def _():
-                    cols.tick(10 + pair)
-
-                @pl.when(pair < 4)
+                    cols.tick(11 + pair - pair // 3)
+
+                @pl.when(lax.rem(pair, 3) != 1)
                 def _():
-                    downs.tick(9 + pair)
+                    downs.tick(8 + pair - lax.rem(pair, 3) // 2 - pair // 3)
 
                 return carry
 
@@ -1769,6 +1778,7 @@
 
         def projection_grads(normed_t, g_tile):
             fetch((normed_t_h, normed_t))
+            cols.tick(15)
             count = 3 * own_width // JOB
 
             def step(n, carry):
@@ -1785,9 +1795,9 @@
                 def _():
                     cols.tick(15 + n)
 
-                @pl.when(n < 7)
+                @pl.when(n >= 1)
                 def _():
-                    outs.tick(6 + n)
+                    outs.tick(5 + n)
 
                 return carry
 
@@ -1795,6 +1805,8 @@
             grad_store(g_tile, (count - 1) % 2, g_cols_h, ff_jobs + count - 1, 1).wait()
 
         pl.run_scoped(projection_grads, vmem((width, length), bf16), vmem((2, width, JOB), bf16))
+
+        cols.tick(24)
 
         def tokens_back(w_tile, send, total, x_rows, kept):
             def tile_load(n, slot):
@@ -1815,13 +1827,21 @@
 
                 send[:, lanes(n)] = nt(grads[sublanes(1 - me.core, half_rows), :], w_tile[slot]).astype(bf16)
                 total[:, lanes(n)] = nt(grads[sublanes(me.core, half_rows), :], w_tile[slot])
+
+                @pl.when((n == 1) | (n == 3))
+                def _():
+                    cols.tick(25 + n - 1)
+                    cols.tick(26 + n - 1)
+                    downs.tick(12 + n // 2)
+
                 return carry
 
             lax.fori_loop(0, count, step, 0)
             pl.semaphore_wait(half_free, 1)
             exchange = remote(send, half_recv, half_sem.at[0, 0], half_sem.at[1, 0], me.over_core, me.z)
             exchange.start()
-            cols.tick(15 + 3 * own_width // JOB)
+            cols.tick(29)
+            cols.tick(30)
             load(x_h.at[sublanes(me.core, half_rows), :], x_rows, 0).wait()
             load(kept_h, kept, 1).wait()
             exchange.wait()
@@ -1846,18 +1866,22 @@
 
     pl.run_scoped(attention, vmem((length, 3 * own_width), bf16))
 
-    first = 16 + 3 * own_width // JOB
+    downs.tick(14)
+    outs.tick(14)
+    downs.tick(15)
+    first = 31
 
     def rest(t, carry):
         cols.tick(t)
-        for k in range(GAIN_HOPS):
-            @pl.when(t == first + 1 + k)
+        for k in range(GAIN_HOPS - 1):
+            @pl.when(t == first + k)
             def _():
                 gains.step(k)
 
         return carry
 
     lax.fori_loop(first, cols.ticks, rest, 0)
+    gains.step(GAIN_HOPS - 1)
     gains.drain()
     back_out.drain()
     back_tokens.drain()
@@ -1873,7 +1897,7 @@
     )
 
 
-COLUMN_SLOTS = 10
+COLUMN_SLOTS = 12
 
 
 def backward(branch, slopes, hidden, turned, heads, lse, middle, x, g_down, weights, start, gain, cosine, sine):

time: 646 us -> 599 us (0.927)
  Pallas kernels: 619 us -> 573 us
    pallas_call x1, Pallas kernels: 378 us -> 332 us  [backward(): pl.pallas_call(backward_kernel, in_specs=[ANY] * 16 + [whole] * 4, out_sp...]
where the time goes in v6:
time: 599 us; the launch traced here: 595 us
  Pallas kernels  573 us (96%)
  other arithmetic  17.9 us (3%)
    pallas_call x1, Pallas kernels, backward(): pl.pallas_call(backward_kernel, in_specs=[ANY] * 16 + [whole] * 4, out_sp...  332 us
    pallas_call x1, Pallas kernels, gather_all(): pl.pallas_call(gather_kernel, in_specs=[ANY] * 4 + [whole] * 2 + [ANY] *...  241 us
    convert_element_type x5, other arithmetic, wide(): return value.astype(jnp.float32)  14.1 us

profile of v6, /device:TPU:0, one launch (start us, length us, event | category | flops | bytes accessed | tf_op | source)
XLA Modules:
  0.0 595.4 jit_solution(7163738652256531468)
XLA Ops:
  0.6 0.0 copy-start.6
  0.7 0.0 copy-start.7
  0.7 0.0 copy-start.5
  0.7 1.9 fusion
  2.6 1.8 pad_maximum_fusion
  4.5 0.0 copy-done.6
  4.5 0.0 copy-done.7
  4.5 0.3 dynamic_update_slice.3.gains
  4.9 0.0 copy-done.5
  4.9 0.0 copy-start.4
  4.9 0.6 reshape.34.segments
  5.5 0.0 copy-done.4
  5.5 240.8 %gather_all.1 = (bf16[1024,1536]{1,0:T(8,128)(2,1)}, s32[4,1,256]{2,1,0:T(1,128)}, bf16[1024,1536]{1,0:T(8,128)(2,1)}, bf16[8,2,1536]{2,1,0:T(2,128)(2,1)}, bf16...) custom-call(bf16[2,256,1536]{2,1,0:T(8,128)(2,1)} %tokens.1, ...), custom_call_target="tpu_custom_call" | custom-call | bytes 500000000 | tf_op jit(solution)/shard_map/gather_all/pallas_call | solution.py:955
  246.2 332.2 %backward.1 = (bf16[2,256,1536]{2,1,0:T(8,128)(2,1)}, bf16[2,256,1536]{2,1,0:T(8,128)(2,1)}, bf16[192,12800]{1,0:T(8,128)(2,1)}, bf16[192,1536]{1,0:T(8,128)(2,1...) custom-call(bf16[1024,1536]{1,0:T(8,128)(2,1)} %get-tuple-element.35, ...), custom_call_target="tpu_custom_call" | custom-call | bytes 800000000 | tf_op jit(solution)/shard_map/backward/pallas_call | solution.py:1936
  578.4 5.4 slice_convert_fusion
  583.8 0.0 copy-start.2
  583.8 3.5 slice_convert_fusion.2
  587.3 0.0 copy-start.1
  587.3 0.0 copy-done.2
  587.3 2.1 convert_element_type.46
  589.3 0.0 copy-start.3
  589.3 0.0 copy-done.1
  589.3 0.0 copy-start
  589.3 2.1 convert_element_type.53
  591.4 0.0 copy-done.3
  591.4 1.1 convert_element_type.50
  592.6 1.4 fusion.1
  594.0 0.0 copy-done
  594.0 1.1 copy.26
  (6 shorter events, 0.0 us)
Async XLA Ops:
  0.6 3.8 copy-start.6
  0.7 3.8 copy-start.7
  0.7 4.2 copy-start.5
  4.9 0.6 copy-start.4
  583.8 3.5 copy-start.2
  587.3 2.1 copy-start.1
  589.3 2.1 copy-start.3
  589.3 4.6 copy-start

commit v7 on v6

--- a/solution.py
+++ b/solution.py
@@ -577,28 +577,63 @@
             def _():
                 remote(half, mine, send.at[index, 4], recv.at[index, 4], me.over_core, me.z).start()
 
+    beside = me.z + 1 - 2 * lax.rem(me.z, 2)
+    corner = me.over_x + me.over_y - me.dp - me.core
+
+    def turn_of(index):
+        return lax.rem(index + me.z, 2)
+
+    last = 6
+
+    def hand_on(index, piece, came, slot, send_slot, dp, seq):
+        remote(piece, piece, send.at[index, send_slot], recv.at[index, came], dp, seq).wait_recv()
+        remote(piece, piece, send.at[index, send_slot], recv.at[index, slot], dp, seq).start()
+
+    def arrived(index, piece, slot):
+        remote(piece, piece, send.at[index, 5], recv.at[index, slot], me.over_core, me.z).wait_recv()
+
+    def left(index, piece, slot):
+        remote(piece, piece, send.at[index, slot], recv.at[index, 5], me.over_core, me.z).wait_send()
+
     def columns_relay(index):
-        piece = column_piece(index, me.over_x - me.core)
-        remote(piece, piece, send.at[index, 5], recv.at[index, 0], me.over_y, me.z).wait_recv()
-        begin(remote(piece, piece, send.at[index, 5], recv.at[index, 5], me.over_y, me.z))
-        piece = column_piece(index, me.over_y - me.core + 1)
-        remote(piece, piece, send.at[index, 6], recv.at[index, 3], me.over_x, me.z).wait_recv()
-        begin(remote(piece, piece, send.at[index, 6], recv.at[index, 6], me.over_x, me.z))
+        @pl.when(turn_of(index) == 0)
+        def _():
+            hand_on(index, column_piece(index, me.over_x - me.core), 0, 5, 5, me.over_y, me.z)
+
+        @pl.when(turn_of(index) == 1)
+        def _():
+            hand_on(index, column_piece(index, me.over_y - me.core + 1), 3, 6, 6, me.over_x, me.z)
+
+    def columns_forward(index):
+        @pl.when(turn_of(index) == 0)
+        def _():
+            hand_on(index, column_piece(index, corner), 5, 5, 6, me.dp, beside)
+
+        @pl.when(turn_of(index) == 1)
+        def _():
+            hand_on(index, column_piece(index, corner + 1), 6, 6, 5, me.dp, beside)
 
     def columns_finish(index):
         source, target, first = by_columns[index]
         width = source.shape[1] // 2
-        corner = me.over_x + me.over_y - me.dp - me.core
-        for slot, owner in (
-            (1, me.over_x - me.core + 1), (2, me.over_y - me.core), (4, me.over_core),
-            (5, corner), (6, corner + 1),
-        ):
-            piece = column_piece(index, owner)
-            remote(piece, piece, send.at[index, 5], recv.at[index, slot], me.over_core, me.z).wait_recv()
+        arrived(index, column_piece(index, me.over_x - me.core + 1), 1)
+        arrived(index, column_piece(index, me.over_y - me.core), 2)
+        arrived(index, column_piece(index, me.over_core), 4)
+
+        @pl.when(turn_of(index) == 0)
+        def _():
+            arrived(index, column_piece(index, me.over_y - me.core + 1), 3)
+            arrived(index, column_piece(index, corner + 1), 6)
+
+        @pl.when(turn_of(index) == 1)
+        def _():
+            arrived(index, column_piece(index, me.over_x - me.core), 0)
+            arrived(index, column_piece(index, corner), 5)
+
         mine = column_piece(index, me.dp)
         pltpu.make_async_copy(mine, mine, local.at[index]).wait()
-        half = source.at[:, pl.ds(0, width)]
-        remote(half, mine, send.at[index, 4], recv.at[index, 4], me.over_core, me.z).wait_send()
+        for slot in (4, 5, 6):
+            left(index, mine, slot)
 
     def row_piece(which, owner):
         source, target = by_rows[which]
@@ -625,46 +660,66 @@
     def rows_relay(which):
         index = 5 + which
 
-        @pl.when(me.core == me.y)
+        @pl.when((me.core == me.y) & ((index == last) | (turn_of(index) == 0)))
         def _():
-            piece = row_piece(which, me.over_x - me.core)
-            remote(piece, piece, send.at[index, 5], recv.at[index, 0], me.over_y, me.z).wait_recv()
-            remote(piece, piece, send.at[index, 5], recv.at[index, 5], me.over_y, me.z).start()
-
-        @pl.when(me.core != me.y)
+            hand_on(index, row_piece(which, me.over_x - me.core), 0, 5, 5, me.over_y, me.z)
+
+        @pl.when((me.core != me.y) & ((index == last) | (turn_of(index) == 1)))
         def _():
-            piece = row_piece(which, me.over_y - me.core + 1)
-            remote(piece, piece, send.at[index, 6], recv.at[index, 3], me.over_x, me.z).wait_recv()
-            remote(piece, piece, send.at[index, 6], recv.at[index, 6], me.over_x, me.z).start()
+            hand_on(index, row_piece(which, me.over_y - me.core + 1), 3, 6, 6, me.over_x, me.z)
+
+    def rows_forward(which):
+        index = 5 + which
+
+        @pl.when((me.core != me.y) & (turn_of(index) == 0))
+        def _():
+            hand_on(index, row_piece(which, corner), 5, 5, 6, me.dp, beside)
+
+        @pl.when((me.core != me.y) & (turn_of(index) == 1))
+        def _():
+            hand_on(index, row_piece(which, corner + 1), 6, 6, 5, me.dp, beside)
 
     def rows_finish(which):
         source, target = by_rows[which]
         index = 5 + which
-        corner = me.over_x + me.over_y - me.dp - me.core
-
-        def arrived(slot, owner):
-            piece = row_piece(which, owner)
-            remote(piece, piece, send.at[index, 5], recv.at[index, slot], me.over_core, me.z).wait_recv()
-
-        def left(slot):
-            piece = row_piece(which, me.dp)
-            remote(source, piece, send.at[index, slot], recv.at[index, slot], me.over_core, me.z).wait_send()
+        mine = row_piece(which, me.dp)
 
         @pl.when(me.core == me.y)
         def _():
-            arrived(1, me.over_x - me.core + 1)
-            arrived(4, me.over_core)
-            mine = row_piece(which, me.dp)
+            arrived(index, row_piece(which, me.over_x - me.core + 1), 1)
+            arrived(index, row_piece(which, me.over_core), 4)
             pltpu.make_async_copy(source, mine, local.at[index]).wait()
-            left(5)
+
+            @pl.when((index == last) | (turn_of(index) == 0))
+            def _():
+                left(index, mine, 5)
+
+            @pl.when((index != last) & (turn_of(index) == 1))
+            def _():
+                arrived(index, row_piece(which, me.over_x - me.core), 0)
 
         @pl.when(me.core != me.y)
         def _():
-            arrived(2, me.over_y - me.core)
-            arrived(5, corner)
-            arrived(6, corner + 1)
-            left(4)
-            left(6)
+            arrived(index, row_piece(which, me.over_y - me.core), 2)
+            left(index, mine, 4)
+            left(index, mine, 6)
+
+            @pl.when((index != last) & (turn_of(index) == 0))
+            def _():
+                arrived(index, row_piece(which, me.over_y - me.core + 1), 3)
+                arrived(index, row_piece(which, corner + 1), 6)
+
+            @pl.when((index == last) | (turn_of(index) == 1))
+            def _():
+                arrived(index, row_piece(which, corner), 5)
+
+            @pl.when(index == last)
+            def _():
+                arrived(index, row_piece(which, corner + 1), 6)
+
+            @pl.when((index != last) & (turn_of(index) == 1))
+            def _():
+                left(index, mine, 5)
 
     def load(source, target, k):
         return pltpu.make_async_copy(source, target, load_sem.at[k])
@@ -689,10 +744,10 @@
         begin(remote(gains, gains_out.at[me.dp], gain_send.at[k - 1], gain_recv.at[k - 1],
                      lax.rem(me.dp + k, 8), me.z))
     pltpu.make_async_copy(gains, gains_out.at[me.dp], gain_recv.at[7]).start()
-    row_copies(2)
     for index in range(3):
         columns_relay(index)
     rows_start(0)
+    columns_start(3)
     row_relay(0)
     row_relay(1)
     for k in range(1, 8):
@@ -733,10 +788,11 @@
     normed_store = store(turned_v, normed_t_out)
 
     for index in range(3):
+        columns_forward(index)
+    rows_relay(0)
+    columns_start(4)
+    for index in range(3):
         columns_finish(index)
-    columns_start(3)
-    columns_start(4)
-    rows_relay(0)
     tile = 256
     tiles = own_width // tile
     for t in range(tiles):
@@ -760,9 +816,10 @@
 
         lax.fori_loop(tile // 128 * t, tile // 128 * (t + 1), pair_step, 0)
         if t == 0:
-            row_relay(2)
+            row_copies(2)
         if t == 1:
-            rows_start(1)
+            rows_forward(0)
+            columns_relay(3)
     store(heads_v, heads_out)
     lse_t_v[...] = lse_v[...].T
     store(lse_t_v, lse_out)
@@ -771,8 +828,6 @@
 
     rows_finish(0)
     load(o_out, w_o_v, 0).start()
-    row_finish(2)
-    load(g_out, branch_v, 1).start()
     load(o_out, w_o_v, 0).wait()
     chunk = width // 3
 
@@ -789,8 +844,11 @@
             part_send[:, part] = product.astype(jnp.bfloat16)
             middle_v[:, part] = x_v[:, part].astype(jnp.float32) + product
         part_copy(k).start()
-    columns_relay(3)
+    row_relay(2)
     columns_relay(4)
+    rows_start(1)
+    row_finish(2)
+    load(g_out, branch_v, 1).start()
     for k in range(3):
         part_copy(k).wait_recv()
 
@@ -805,7 +863,8 @@
     turn(nf_v, turned_v)
     store(turned_v, nf_t_out)
     load(g_out, branch_v, 1).wait()
-    rows_relay(1)
+    columns_forward(3)
+    columns_forward(4)
     columns_finish(3)
     columns_finish(4)
 
@@ -858,6 +917,11 @@
         for kind in range(3):
             tile_store(n, slot, kind).start()
         grad_store(n, slot).start()
+
+        @pl.when(n == count // 4)
+        def _():
+            rows_relay(1)
+
         return carry
 
     lax.fori_loop(0, count, ff_step, 0)

time: 599 us -> 573 us (0.957)
  Pallas kernels: 573 us -> 543 us
    pallas_call x1, Pallas kernels: 241 us -> 207 us  [gather_all(): pl.pallas_call(gather_kernel, in_specs=[ANY] * 4 + [whole] * 2 + [ANY] *...]
where the time goes in v7:
time: 573 us; the launch traced here: 565 us
  Pallas kernels  543 us (95%)
  other arithmetic  17.9 us (3%)
    pallas_call x1, Pallas kernels, backward(): pl.pallas_call(backward_kernel, in_specs=[ANY] * 16 + [whole] * 4, out_sp...  335 us
    pallas_call x1, Pallas kernels, gather_all(): pl.pallas_call(gather_kernel, in_specs=[ANY] * 4 + [whole] * 2 + [ANY] *...  207 us
    convert_element_type x5, other arithmetic, wide(): return value.astype(jnp.float32)  14.1 us

profile of v7, /device:TPU:0, one launch (start us, length us, event | category | flops | bytes accessed | tf_op | source)
XLA Modules:
  0.0 565.2 jit_solution(852751321607429811)
XLA Ops:
  0.6 0.0 copy-start.6
  0.7 0.0 copy-start.7
  0.7 0.0 copy-start.5
  0.7 1.9 fusion
  2.6 1.8 pad_maximum_fusion
  4.5 0.0 copy-done.6
  4.5 0.0 copy-done.7
  4.5 0.3 dynamic_update_slice.3.gains
  4.9 0.0 copy-done.5
  4.9 0.0 copy-start.4
  4.9 0.6 reshape.34.segments
  5.5 0.0 copy-done.4
  5.5 207.5 %gather_all.1 = (bf16[1024,1536]{1,0:T(8,128)(2,1)}, s32[4,1,256]{2,1,0:T(1,128)}, bf16[1024,1536]{1,0:T(8,128)(2,1)}, bf16[8,2,1536]{2,1,0:T(2,128)(2,1)}, bf16...) custom-call(bf16[2,256,1536]{2,1,0:T(8,128)(2,1)} %tokens.1, ...), custom_call_target="tpu_custom_call" | custom-call | bytes 500000000 | tf_op jit(solution)/shard_map/gather_all/pallas_call | solution.py:1019
  213.0 335.3 %backward.1 = (bf16[2,256,1536]{2,1,0:T(8,128)(2,1)}, bf16[2,256,1536]{2,1,0:T(8,128)(2,1)}, bf16[192,12800]{1,0:T(8,128)(2,1)}, bf16[192,1536]{1,0:T(8,128)(2,1...) custom-call(bf16[1024,1536]{1,0:T(8,128)(2,1)} %get-tuple-element.35, ...), custom_call_target="tpu_custom_call" | custom-call | bytes 800000000 | tf_op jit(solution)/shard_map/backward/pallas_call | solution.py:2000
  548.3 5.4 slice_convert_fusion
  553.6 0.0 copy-start.2
  553.6 3.5 slice_convert_fusion.2
  557.1 0.0 copy-start.1
  557.1 0.0 copy-done.2
  557.1 2.1 convert_element_type.46
  559.1 0.0 copy-start.3
  559.1 0.0 copy-done.1
  559.2 0.0 copy-start
  559.2 2.1 convert_element_type.53
  561.2 0.0 copy-done.3
  561.2 1.1 convert_element_type.50
  562.4 1.4 fusion.1
  563.8 0.0 copy-done
  563.8 1.1 copy.26
  (6 shorter events, 0.0 us)
Async XLA Ops:
  0.6 3.8 copy-start.6
  0.7 3.8 copy-start.7
  0.7 4.2 copy-start.5
  4.9 0.6 copy-start.4
  553.6 3.5 copy-start.2
  557.1 2.1 copy-start.1
  559.1 2.1 copy-start.3
  559.2 4.6 copy-start

commit v8 on v7

--- a/solution.py
+++ b/solution.py
@@ -918,7 +918,7 @@
             tile_store(n, slot, kind).start()
         grad_store(n, slot).start()
 
-        @pl.when(n == count // 4)
+        @pl.when(n == 1)
         def _():
             rows_relay(1)
 
@@ -1193,13 +1193,12 @@
         self.count, self.ff_jobs = source.shape[1] // JOB, ff_jobs
         self.ff, self.d_model = ff, d_model
         self.stages = (
-            (0, self.start), (2, self.pass_second), (4, self.plane_and_ends), (6, self.across),
-            (8, self.back), (9, self.finish), (10, self.drain),
+            *zip(LATE["C"], (self.pass_second, self.plane_and_ends, self.across, self.back, self.finish, self.drain)),
         )
 
     def x_first(self, k):
         late = k // self.ff_jobs
-        return (1 - late) * ((k // (self.ff_jobs // 2)) % 2) * ((k + 1) % 2) + late * (k % 2)
+        return (1 - late) * ((k + self.ff_jobs // 2 - 2) // self.ff_jobs) * ((k + 1) % 2) + late * (k % 2)
 
     def first_copy(self, k, part):
         me, slot, x_first = self.me, self.slot(k), self.x_first(k)
@@ -1336,10 +1335,7 @@
         self.slots, self.rows = self.got.shape[0], source.shape[0] // 2
         self.count = source.shape[1] // JOB
         self.active = me.core == me.y
-        steps = (
-            self.start, self.load, self.pass_second, self.plane_and_ends, self.across, self.back, self.finish,
-            self.drain,
-        )
+        steps = (self.pass_second, self.plane_and_ends, self.across, self.back, self.finish, self.drain)
         self.stages = tuple(zip(lates, steps))
 
     def first_copy(self, k):
@@ -1362,14 +1358,13 @@
 
     def start(self, k):
         self.first_copy(k).start()
-
-    def load(self, k):
-        self.load_copy(k).start()
+        guard(k == 0, lambda: self.load_copy(k).start())
 
     def pass_second(self, k):
         self.load_copy(k).wait()
         self.first_copy(k).wait_recv()
         add_rows(self.got.at[self.slot(k)], 0, self.stage, self.rows)
+        guard(k + 1 < self.count, lambda: self.load_copy(k + 1).start())
         guard(jnp.logical_not(self.active), lambda: self.second_copy(k).start())
 
     def reduce_plane(self, k):
@@ -1412,6 +1407,55 @@
 
         guard(self.active, active)
         guard(jnp.logical_not(self.active), passive)
+
+
+PLAN = {
+    "s0": {"E": (0, 3)},
+    "a": {"E": (3, 4, 4, 4, 4, 4, 4, 4, 4), "S": (0, 1, 1, 2, 2, 4, 4, 5, 5), "C": (0, 0, 0, 0, 0, 1, 1, 1, 2), "D": (0, 0, 0, 1, 1, 1, 1, 2, 3)},
+    "l0": {"C": (2, 3)},
+    "l1": {"S": (5, 6), "C": (3, 4)},
+    "l2": {},
+    "i": {"E": (4, 4, 4, 6, 6, 6, 6), "S": (6, 6, 6, 6, 7, 7, 8), "C": (4, 4, 4, 4, 5, 5, 5)},
+    "n0": {"S": (8, 9), "C": (5, 6), "D": (3, 4)},
+    "n1": {"S": (9, 10), "C": (6, 7)},
+    "n2": {"F": (0, 1)},
+    "o": {"S": (10, 11, 11, 11, 11, 11, 12), "C": (7, 8, 8, 8, 8, 8, 9), "D": (4, 4, 5, 5, 6, 6, 6)},
+    "h": {"S": (12, 13, 14, 15, 15, 16, 16), "C": (9, 10, 11, 11, 12, 13, 14), "D": (6, 6, 6, 7, 8, 8, 9), "O": (0, 0, 0, 0, 0, 1, 1)},
+    "p": {"S": (16, 16, 17, 18, 19, 19, 19, 20, 20, 20), "C": (14, 14, 15, 15, 15, 15, 16, 16, 16, 16)},
+    "p9": {},
+    "t": {"S": (20, 20, 20, 20, 21, 21, 22), "C": (16, 17, 17, 18, 18, 18, 20), "D": (9, 10, 10, 11, 11, 11, 11)},
+    "t6": {"F": (1, 2)},
+}
+LATE = {"C": (0, 2, 4, 6, 7, 8), "D": (0, 2, 4, 6, 7, 8), "O": (0, 1, 2, 4, 5, 6)}
+
+
+class Pace:
+    def __init__(self, cols, downs, outs):
+        self.actions = {
+            "E": downs.start, "S": cols.start, "F": outs.start, "C": cols.tick, "D": downs.tick, "O": outs.tick,
+        }
+
+    def at(self, place, n=0):
+        for kind, bounds in PLAN[place].items():
+            action = self.actions[kind]
+
+            def one(t, carry, action=action):
+                action(t)
+                return carry
+
+            if isinstance(n, int):
+                low, high = bounds[n], bounds[n + 1]
+                if high - low == 1:
+                    action(low)
+                elif high > low:
+                    lax.fori_loop(low, high, one, 0)
+                continue
+            low, high = bounds[0], bounds[1]
+            for k in range(1, len(bounds) - 1):
+                reached = (n + 32 - k) // 32
+                low = low + (bounds[k] - bounds[k - 1]) * reached
+                high = high + (bounds[k + 1] - bounds[k]) * reached
+            lax.fori_loop(low, high, one, 0)
 
 
 GAIN_HOPS = 5
@@ -1546,9 +1590,9 @@
         (col_got, col_keep, col_second, col_over, col_sem, col_seq, col_credit),
     )
     downs = RowStream(
-        me, g_down_h, down_o, (0, 2, 3, 5, 7, 8, 9, 10), (down_got, down_second, down_over, down_stage, down_sem, down_seq)
-    )
-    outs = RowStream(me, g_o_h, o_o, (0, 1, 2, 4, 6, 7, 8, 9), (o_got, o_second, o_over, o_stage, o_sem, o_seq))
+        me, g_down_h, down_o, LATE["D"], (down_got, down_second, down_over, down_stage, down_sem, down_seq)
+    )
+    outs = RowStream(me, g_o_h, o_o, LATE["O"], (o_got, o_second, o_over, o_stage, o_sem, o_seq))
     back_out = RowsBack(me, rows_h.at[0], out_o, row_sem.at[0])
     back_tokens = RowsBack(me, rows_h.at[1], tokens_o, row_sem.at[1])
     gains = GainSums(me, gains_o, gain_buffer, gain_sem)
@@ -1571,7 +1615,8 @@
     def grad_store(buffer, slot, target, n, k):
         return pltpu.make_async_copy(buffer.at[slot], target.at[:, lanes(n)], store_sem.at[slot, k])
 
-    downs.tick(0)
+    pace = Pace(cols, downs, outs)
+    pace.at("s0")
 
     def feed_forward(grad_ff):
         steps = half_ff // JOB
@@ -1587,7 +1632,6 @@
             for copy in tile_loads(0, 0):
                 copy.start()
             fetch((branch_h, branch), (nf_t_h, nf_t))
-            downs.tick(1)
 
             def step(n, carry):
                 slot = lax.rem(n, 2)
@@ -1601,7 +1645,7 @@
 
                 grad_hidden = nt(branch[...], w_tile[slot])
 
-                @pl.when(n > 0)
+                @pl.when(n > 1)
                 def _():
                     for kind in range(2):
                         grad_store(g_tile, kind, g_cols_h, 2 * n - 2 + kind, 0).wait()
@@ -1612,13 +1656,12 @@
                     g_tile[kind] = dot(nf_t[...], grad).astype(bf16)
                     grad_store(g_tile, kind, g_cols_h, 2 * n + kind, 0).start()
 
-                @pl.when((n >= 2) & (n != 5))
+                @pl.when(n == 0)
                 def _():
-                    cols.tick(n - 2 - n // 6)
-
-                @pl.when((n == 2) | (n == 6))
-                def _():
-                    downs.tick(2 + n // 6)
+                    for kind in range(2):
+                        grad_store(g_tile, kind, g_cols_h, kind, 0).wait()
+
+                pace.at("a", n)
 
                 return carry
 
@@ -1643,6 +1686,7 @@
             lax.fori_loop(0, width // JOB, other_tile, 0)
             exchange = remote(send, half_recv, half_sem.at[0, 0], half_sem.at[1, 0], me.over_core, me.z)
             exchange.start()
+            pace.at("l0")
             fetch((hidden_h.at[sublanes(own, half_rows), :], hidden))
             load(middle_h.at[sublanes(own, half_rows), :], total, 2).wait()
 
@@ -1651,6 +1695,7 @@
                 return carry
 
             lax.fori_loop(0, width // JOB, own_tile, 0)
+            pace.at("l1")
             exchange.wait()
 
             def combine(k, carry):
@@ -1670,6 +1715,7 @@
             vmem((half_rows, width), bf16), vmem((half_rows, width), f32),
         )
         back_out.start()
+        pace.at("l2")
 
     chunk = 2 * JOB
     chunks = width // chunk
@@ -1725,21 +1771,14 @@
                     def _():
                         wide_copy(send, k).start()
 
-                @pl.when(lax.rem(n, 3) == 0)
-                def _():
-                    downs.tick(4 + n // 3)
-
-                @pl.when(lax.rem(n, 3) == 2)
-                def _():
-                    cols.tick(5 + n // 3)
+                pace.at("i", n)
 
                 return carry
 
             lax.fori_loop(0, count, step, 0)
             for n in range(count - 2, count):
                 part_store(n, n % 2).wait()
-            cols.tick(7)
-            downs.tick(6)
+            pace.at("n0")
             for k in range(chunks):
                 wide_copy(send, k).wait()
 
@@ -1767,8 +1806,7 @@
             gain_buffer[0, 0, 1:2, :] = 0.5 * total
             kept = load(grad_nf.at[sublanes(me.core, half_rows), :], kept_h, 0)
             kept.start()
-            cols.tick(8)
-            downs.tick(7)
+            pace.at("n1")
             kept.wait()
 
         pl.run_scoped(
@@ -1795,9 +1833,7 @@
                 g_tile[slot] = dot(mixed_t[...], grad_attn[:, lanes(n)]).astype(bf16)
                 grad_store(g_tile, slot, g_o_h, n, 1).start()
 
-                @pl.when(lax.rem(n, 3) == 1)
-                def _():
-                    cols.tick(9 + n // 3)
+                pace.at("o", n)
 
                 return carry
 
@@ -1812,6 +1848,7 @@
         )
 
     pl.run_scoped(to_attention, vmem((length, width), bf16))
+    pace.at("n2")
 
     def attention(grads):
         def heads_back(heads, lse, key_sum, value_sum, query_sum):
@@ -1821,16 +1858,7 @@
                 attend_back(
                     pair, own_width, heads, wide_recv, start_ref, lse, grads, key_sum, value_sum, query_sum, cosine, sine
                 )
-                outs.tick(pair)
-
-                @pl.when(lax.rem(pair, 3) != 2)
-                def _():
-                    cols.tick(11 + pair - pair // 3)
-
-                @pl.when(lax.rem(pair, 3) != 1)
-                def _():
-                    downs.tick(8 + pair - lax.rem(pair, 3) // 2 - pair // 3)
-
+                pace.at("h", pair)
                 return carry
 
             lax.fori_loop(0, own_width // 128, step, 0)
@@ -1842,7 +1870,6 @@
 
         def projection_grads(normed_t, g_tile):
             fetch((normed_t_h, normed_t))
-            cols.tick(15)
             count = 3 * own_width // JOB
 
             def step(n, carry):
@@ -1855,14 +1882,7 @@
 
                 grad_store(g_tile, slot, g_cols_h, ff_jobs + n, 1).start()
 
-                @pl.when(n >= 1)
-                def _():
-                    cols.tick(15 + n)
-
-                @pl.when(n >= 1)
-                def _():
-                    outs.tick(5 + n)
-
+                pace.at("p", n)
                 return carry
 
             lax.fori_loop(0, count, step, 0)
@@ -1870,7 +1890,7 @@
 
         pl.run_scoped(projection_grads, vmem((width, length), bf16), vmem((2, width, JOB), bf16))
 
-        cols.tick(24)
+        pace.at("p9")
 
         def tokens_back(w_tile, send, total, x_rows, kept):
             def tile_load(n, slot):
@@ -1892,20 +1912,14 @@
                 send[:, lanes(n)] = nt(grads[sublanes(1 - me.core, half_rows), :], w_tile[slot]).astype(bf16)
                 total[:, lanes(n)] = nt(grads[sublanes(me.core, half_rows), :], w_tile[slot])
 
-                @pl.when((n == 1) | (n == 3))
-                def _():
-                    cols.tick(25 + n - 1)
-                    cols.tick(26 + n - 1)
-                    downs.tick(12 + n // 2)
-
+                pace.at("t", n)
                 return carry
 
             lax.fori_loop(0, count, step, 0)
             pl.semaphore_wait(half_free, 1)
             exchange = remote(send, half_recv, half_sem.at[0, 0], half_sem.at[1, 0], me.over_core, me.z)
             exchange.start()
-            cols.tick(29)
-            cols.tick(30)
+            pace.at("t6")
             load(x_h.at[sublanes(me.core, half_rows), :], x_rows, 0).wait()
             load(kept_h, kept, 1).wait()
             exchange.wait()
@@ -1930,22 +1944,26 @@
 
     pl.run_scoped(attention, vmem((length, 3 * own_width), bf16))
 
-    downs.tick(14)
-    outs.tick(14)
-    downs.tick(15)
-    first = 31
+    first = {"E": 6, "S": 22, "F": 2, "C": 20, "D": 11, "O": 1}
+    steps = max(stream.ticks - first[kind] for kind, stream in (("C", cols), ("D", downs), ("O", outs)))
 
     def rest(t, carry):
-        cols.tick(t)
+        for kind, stream in (("E", downs), ("S", cols), ("F", outs)):
+            if first[kind] < stream.count:
+                guard(first[kind] + t < stream.count, functools.partial(stream.start, first[kind] + t))
+        for kind, stream in (("C", cols), ("D", downs), ("O", outs)):
+            if first[kind] < stream.ticks:
+                stream.tick(first[kind] + t)
         for k in range(GAIN_HOPS - 1):
-            @pl.when(t == first + k)
+            @pl.when(t == k)
             def _():
                 gains.step(k)
 
         return carry
 
-    lax.fori_loop(first, cols.ticks, rest, 0)
-    gains.step(GAIN_HOPS - 1)
+    lax.fori_loop(0, steps, rest, 0)
+    for k in range(min(steps, GAIN_HOPS - 1), GAIN_HOPS):
+        gains.step(k)
     gains.drain()
     back_out.drain()
     back_tokens.drain()
@@ -2032,6 +2050,37 @@
     return jnp.dot(a, b, preferred_element_type=jnp.float32)
 
 
+WIDEN_STEPS = 4
+
+
+def widen_kernel(cols, o, down, tokens, result, *outs):
+    first = 0
+    for out in outs[:5]:
+        out[...] = cols[:, first : first + out.shape[1]].astype(jnp.float32)
+        first += out.shape[1]
+    for source, out in zip((o, down, tokens, result), outs[5:]):
+        out[...] = source[...].astype(out.dtype)
+
+
+def widen(cols, o, down, tokens, result, ff):
+    depth, width = o.shape
+
+    def rows(count, columns):
+        return pl.BlockSpec((count // WIDEN_STEPS, columns), lambda i: (i, 0))
+
+    shapes = [(depth, ff)] * 2 + [(depth, width)] * 4 + [down.shape, tokens.shape, result.shape]
+    return pl.pallas_call(
+        widen_kernel,
+        grid=(WIDEN_STEPS,),
+        in_specs=[rows(*value.shape) for value in (cols, o, down, tokens, result)],
+        out_specs=[rows(*shape) for shape in shapes],
+        out_shape=[jax.ShapeDtypeStruct(shape, jnp.float32) for shape in shapes[:-1]]
+        + [jax.ShapeDtypeStruct(result.shape, result.dtype)],
+        compiler_params=pltpu.CompilerParams(vmem_limit_bytes=63 * 1024 * 1024),
+        name="widen",
+    )(cols, o, down, tokens, result)
+
+
 def column_device(
     tokens, segment_ids, out_grad, w_q, w_k, w_v, w_o, w_gate, w_up, w_down, gain_attn, gain_ffn
 ):
@@ -2044,9 +2093,11 @@
         dp_at * gain_attn.shape[0],
         1,
     )
-    cosine, sine = rope_tables(jnp.arange(length, dtype=jnp.int32), HD // 2)
-    cosine = jnp.concatenate([cosine] * 4, axis=1)
-    sine = jnp.concatenate([-sine, sine, -sine, sine], axis=1)
+    lane = jnp.arange(2 * HD, dtype=jnp.int32)
+    pace = jnp.exp((lane % (HD // 2)).astype(jnp.float32) * (-math.log(10000.0) / (HD // 2)))
+    angle = jnp.arange(length, dtype=jnp.float32)[:, None] * pace[None, :]
+    cosine = jnp.cos(angle)
+    sine = jnp.where(lane % HD < HD // 2, -1.0, 1.0)[None, :] * jnp.sin(angle)
     (
         x_low, docs, grad_branch, gains, full_qkv, full_o, full_ff, full_down, heads, lse, middle,
         slope_gate, slope_up, hidden, g_down, start, gain, normed_t, nf_t, mixed_t,
@@ -2059,19 +2110,13 @@
         (full_qkv, full_o, full_ff, full_down), start, gain, cosine, sine,
     )[:6]
     grad_gains = lax.dynamic_slice_in_dim(grad_gains, dp_at * (width // 8), width // 8, 1)
-    first = 2 * ff
+    flat = (2 * rows, width)
+    gate, up, query, key, value, out, down, grad_tokens, result = widen(
+        g_cols, g_o, g_down, grad_tokens.reshape(flat), result.reshape(flat), ff
+    )
+    result = result.reshape(2, rows, width)
     return (
-        result,
-        wide(grad_tokens),
-        wide(g_cols[:, first : first + width]),
-        wide(g_cols[:, first + width : first + 2 * width]),
-        wide(g_cols[:, first + 2 * width :]),
-        wide(g_o),
-        wide(g_cols[:, :ff]),
-        wide(g_cols[:, ff:first]),
-        wide(g_down),
-        grad_gains[0],
-        grad_gains[1],
+        result, grad_tokens.reshape(2, rows, width), query, key, value, out, gate, up, down, grad_gains[0], grad_gains[1]
     )
 
 

time: 573 us -> 564 us (0.984)
  other arithmetic: 17.9 us -> 2.84 us
    convert_element_type x6 -> x0, other arithmetic: 14.1 us -> none  [the longest x5 14.1 us: wide(): return value.astype(jnp.float32)]
    pallas_call x0 -> x1, Pallas kernels: none -> 10.7 us  [widen(): pl.pallas_call(widen_kernel, grid=(WIDEN_STEPS,), in_specs=[rows(*value.s...]
    pallas_call x1, Pallas kernels: 335 us -> 327 us  [backward(): pl.pallas_call(backward_kernel, in_specs=[ANY] * 16 + [whole] * 4, out_sp...]
where the time goes in v8:
time: 564 us; the launch traced here: 553 us
  Pallas kernels  545 us (97%)
    pallas_call x1, Pallas kernels, backward(): pl.pallas_call(backward_kernel, in_specs=[ANY] * 16 + [whole] * 4, out_sp...  327 us
    pallas_call x1, Pallas kernels, gather_all(): pl.pallas_call(gather_kernel, in_specs=[ANY] * 4 + [whole] * 2 + [ANY] *...  207 us

profile of v8, /device:TPU:0, one launch (start us, length us, event | category | flops | bytes accessed | tf_op | source)
XLA Modules:
  0.0 553.4 jit_solution(7783204541751854223)
XLA Ops:
  0.6 0.7 stack.10
  1.3 0.7 stack.9
  2.0 0.2 dynamic_update_slice.3.gains
  2.2 0.0 copy-start
  2.2 2.8 sine_multiply_fusion
  5.0 1.3 reshape.60.segments
  6.3 0.0 copy-done
  6.3 207.5 %gather_all.1 = (bf16[1024,1536]{1,0:T(8,128)(2,1)}, s32[4,1,256]{2,1,0:T(1,128)}, bf16[1024,1536]{1,0:T(8,128)(2,1)}, bf16[8,2,1536]{2,1,0:T(2,128)(2,1)}, bf16...) custom-call(bf16[2,256,1536]{2,1,0:T(8,128)(2,1)} %tokens.1, ...), custom_call_target="tpu_custom_call" | custom-call | bytes 500000000 | tf_op jit(solution)/shard_map/gather_all/pallas_call | solution.py:1019
  213.8 327.1 %backward.1 = (bf16[2,256,1536]{2,1,0:T(8,128)(2,1)}, bf16[2,256,1536]{2,1,0:T(8,128)(2,1)}, bf16[192,12800]{1,0:T(8,128)(2,1)}, bf16[192,1536]{1,0:T(8,128)(2,1...) custom-call(bf16[1024,1536]{1,0:T(8,128)(2,1)} %get-tuple-element.44, ...), custom_call_target="tpu_custom_call" | custom-call | bytes 800000000 | tf_op jit(solution)/shard_map/backward/pallas_call | solution.py:2018
  540.9 10.7 %widen.1 = (f32[192,4096]{1,0:T(8,128)}, f32[192,4096]{1,0:T(8,128)}, f32[192,1536]{1,0:T(8,128)}, f32[192,1536]{1,0:T(8,128)}, f32[192,1536]{1,0:T(8,128)}, /*i...) custom-call(bf16[192,12800]{1,0:T(8,128)(2,1)} %get-tuple-element.62.cols, ...), custom_call_target="tpu_custom_call" | custom-call | tf_op jit(solution)/shard_map/widen/pallas_call | solution.py:2072
  551.6 1.4 fusion.4
  (3 shorter events, 0.0 us)
Async XLA Ops:
  2.2 4.1 copy-start

commit v9 on v8

--- a/solution.py
+++ b/solution.py
@@ -799,27 +799,47 @@
         for kind in range(3):
             part = pl.ds(own_width * kind + tile * t, tile)
             pltpu.make_async_copy(qkv_out.at[:, part], w_qkv_v.at[:, part], w_sem.at[kind, t]).start()
-    for t in range(tiles):
-        for kind in range(3):
-            part = pl.ds(own_width * kind + tile * t, tile)
+    def tile_step(t, carry):
+        def kind_step(kind, carry):
+            first = own_width * kind + tile * t
+            part = pl.ds(pl.multiple_of(first, 128), tile)
             pltpu.make_async_copy(qkv_out.at[:, part], w_qkv_v.at[:, part], w_sem.at[kind, t]).wait()
             product = jnp.dot(normed_v[...], w_qkv_v[:, part], preferred_element_type=jnp.float32)
             for k in range(tile // 128):
                 piece = product[:, 128 * k : 128 * k + 128]
-                if kind < 2:
-                    piece = piece * cosine[...] + swap_halves(piece) * sine[...]
-                heads_v[:, pl.ds(own_width * kind + tile * t + 128 * k, 128)] = piece.astype(jnp.bfloat16)
+                cols = pl.ds(pl.multiple_of(first + 128 * k, 128), 128)
+
+                @pl.when(kind < 2)
+                def _():
+                    turned = piece * cosine[...] + swap_halves(piece) * sine[...]
+                    heads_v[:, cols] = turned.astype(jnp.bfloat16)
+
+                @pl.when(kind == 2)
+                def _():
+                    heads_v[:, cols] = piece.astype(jnp.bfloat16)
+
+            return carry
+
+        lax.fori_loop(0, 3, kind_step, 0)
 
         def pair_step(pair, carry):
             attend(pair, own_width, heads_v, start_v, mixed_v, lse_v)
             return carry
 
         lax.fori_loop(tile // 128 * t, tile // 128 * (t + 1), pair_step, 0)
-        if t == 0:
+
+        @pl.when(t == 0)
+        def _():
             row_copies(2)
-        if t == 1:
+
+        @pl.when(t == 1)
+        def _():
             rows_forward(0)
             columns_relay(3)
+
+        return carry
+
+    lax.fori_loop(0, tiles, tile_step, 0)
     store(heads_v, heads_out)
     lse_t_v[...] = lse_v[...].T
     store(lse_t_v, lse_out)
@@ -837,13 +857,19 @@
             part_send.at[:, part], part_recv.at[:, part], part_sem.at[0, k], part_sem.at[1, k], me.over_core, me.z
         )
 
-    for k in range(3):
-        for at in range(chunk * k, chunk * (k + 1), tile):
-            part = pl.ds(at, tile)
-            product = jnp.dot(mixed_v[...], w_o_v[:, part], preferred_element_type=jnp.float32)
-            part_send[:, part] = product.astype(jnp.bfloat16)
-            middle_v[:, part] = x_v[:, part].astype(jnp.float32) + product
-        part_copy(k).start()
+    def out_step(n, carry):
+        part = pl.ds(pl.multiple_of(tile * n, 128), tile)
+        product = jnp.dot(mixed_v[...], w_o_v[:, part], preferred_element_type=jnp.float32)
+        part_send[:, part] = product.astype(jnp.bfloat16)
+        middle_v[:, part] = x_v[:, part].astype(jnp.float32) + product
+        for k in range(3):
+            @pl.when(tile * (n + 1) == chunk * (k + 1))
+            def _():
+                part_copy(k).start()
+
+        return carry
+
+    lax.fori_loop(0, width // tile, out_step, 0)
     row_relay(2)
     columns_relay(4)
     rows_start(1)
@@ -918,7 +944,7 @@
             tile_store(n, slot, kind).start()
         grad_store(n, slot).start()
 
-        @pl.when(n == 1)
+        @pl.when(n == 0)
         def _():
             rows_relay(1)
 
@@ -942,8 +968,12 @@
 
 
 def turn(source, target):
-    for k in range(source.shape[1] // 256):
-        target[256 * k : 256 * (k + 1), :] = source[:, 256 * k : 256 * (k + 1)].T
+    def step(k, carry):
+        first = pl.multiple_of(256 * k, 256)
+        target[pl.ds(first, 256), :] = source[:, pl.ds(first, 256)].T
+        return carry
+
+    lax.fori_loop(0, source.shape[1] // 256, step, 0)
 
 
 def norm_rows(read, gain, target, length, step=64):
@@ -1411,22 +1441,22 @@
 
 PLAN = {
     "s0": {"E": (0, 3)},
-    "a": {"E": (3, 4, 4, 4, 4, 4, 4, 4, 4), "S": (0, 1, 1, 2, 2, 4, 4, 5, 5), "C": (0, 0, 0, 0, 0, 1, 1, 1, 2), "D": (0, 0, 0, 1, 1, 1, 1, 2, 3)},
-    "l0": {"C": (2, 3)},
-    "l1": {"S": (5, 6), "C": (3, 4)},
-    "l2": {},
-    "i": {"E": (4, 4, 4, 6, 6, 6, 6), "S": (6, 6, 6, 6, 7, 7, 8), "C": (4, 4, 4, 4, 5, 5, 5)},
-    "n0": {"S": (8, 9), "C": (5, 6), "D": (3, 4)},
-    "n1": {"S": (9, 10), "C": (6, 7)},
-    "n2": {"F": (0, 1)},
-    "o": {"S": (10, 11, 11, 11, 11, 11, 12), "C": (7, 8, 8, 8, 8, 8, 9), "D": (4, 4, 5, 5, 6, 6, 6)},
-    "h": {"S": (12, 13, 14, 15, 15, 16, 16), "C": (9, 10, 11, 11, 12, 13, 14), "D": (6, 6, 6, 7, 8, 8, 9), "O": (0, 0, 0, 0, 0, 1, 1)},
-    "p": {"S": (16, 16, 17, 18, 19, 19, 19, 20, 20, 20), "C": (14, 14, 15, 15, 15, 15, 16, 16, 16, 16)},
+    "a": {"E": (3, 4, 4, 5, 5, 5, 6, 6, 6), "S": (0, 1, 2, 3, 3, 5, 5, 5, 5), "C": (0, 0, 0, 0, 0, 1, 1, 2, 2), "D": (0, 0, 0, 0, 1, 1, 1, 1, 1)},
+    "l0": {"D": (1, 2)},
+    "l1": {"S": (5, 6), "D": (2, 3)},
+    "l2": {"S": (6, 8)},
+    "i": {"S": (8, 8, 8, 8, 9, 9, 10), "C": (2, 2, 2, 2, 3, 3, 3), "D": (3, 3, 3, 3, 4, 4, 4)},
+    "n0": {"S": (10, 12), "C": (3, 5)},
+    "n1": {"C": (5, 6)},
+    "n2": {"C": (8, 9)},
+    "o": {"C": (6, 7, 7, 7, 8, 8, 8), "D": (4, 4, 4, 4, 4, 4, 5)},
+    "h": {"S": (12, 13, 13, 14, 14, 15, 15), "C": (9, 10, 11, 12, 13, 13, 13), "D": (5, 6, 7, 7, 7, 8, 9)},
+    "t": {"S": (15, 16, 16, 16, 16, 16, 16), "F": (0, 0, 1, 1, 2, 3, 3), "C": (13, 14, 14, 15, 15, 15, 16), "D": (9, 10, 10, 10, 10, 10, 11)},
+    "t6": {"F": (3, 4)},
+    "p": {"S": (16, 16, 17, 18, 19, 20, 20, 20, 20, 20), "O": (0, 0, 1, 1, 1, 2, 3, 3, 3, 3)},
     "p9": {},
-    "t": {"S": (20, 20, 20, 20, 21, 21, 22), "C": (16, 17, 17, 18, 18, 18, 20), "D": (9, 10, 10, 11, 11, 11, 11)},
-    "t6": {"F": (1, 2)},
 }
-LATE = {"C": (0, 2, 4, 6, 7, 8), "D": (0, 2, 4, 6, 7, 8), "O": (0, 1, 2, 4, 5, 6)}
+LATE = {"C": (0, 2, 4, 6, 7, 8), "D": (0, 2, 4, 6, 7, 8), "O": (0, 2, 4, 6, 7, 8)}
 
 
 class Pace:
@@ -1815,10 +1845,12 @@
 
         def out_projection(w_o, mixed_t, g_tile, grad_mixed):
             fetch((w_o_h, w_o), (mixed_t_h, mixed_t))
-            for n in range(own_width // JOB):
-                grad_mixed[:, JOB * n : JOB * (n + 1)] = nt(
-                    grad_attn[...], w_o[JOB * n : JOB * (n + 1), :]
-                ).astype(bf16)
+
+            def mixed_step(n, carry):
+                grad_mixed[:, lanes(n)] = nt(grad_attn[...], w_o[sublanes(n, JOB), :]).astype(bf16)
+                return carry
+
+            lax.fori_loop(0, own_width // JOB, mixed_step, 0)
             placed = load(grad_mixed, wide_recv.at[:, pl.ds(0, own_width)], 3)
             placed.start()
             count = width // JOB
@@ -1867,30 +1899,6 @@
             heads_back, vmem((length, 3 * own_width), bf16), vmem((128, length), f32),
             *[vmem((length, 128), f32)] * 3,
         )
-
-        def projection_grads(normed_t, g_tile):
-            fetch((normed_t_h, normed_t))
-            count = 3 * own_width // JOB
-
-            def step(n, carry):
-                slot = lax.rem(n, 2)
-                g_tile[slot] = dot(normed_t[...], grads[:, lanes(n)]).astype(bf16)
-
-                @pl.when(n >= 1)
-                def _():
-                    grad_store(g_tile, 1 - slot, g_cols_h, ff_jobs + n - 1, 1).wait()
-
-                grad_store(g_tile, slot, g_cols_h, ff_jobs + n, 1).start()
-
-                pace.at("p", n)
-                return carry
-
-            lax.fori_loop(0, count, step, 0)
-            grad_store(g_tile, (count - 1) % 2, g_cols_h, ff_jobs + count - 1, 1).wait()
-
-        pl.run_scoped(projection_grads, vmem((width, length), bf16), vmem((2, width, JOB), bf16))
-
-        pace.at("p9")
 
         def tokens_back(w_tile, send, total, x_rows, kept):
             def tile_load(n, slot):
@@ -1942,15 +1950,41 @@
         )
         back_tokens.start()
 
+        def projection_grads(normed_t, g_tile):
+            fetch((normed_t_h, normed_t))
+            count = 3 * own_width // JOB
+
+            def step(n, carry):
+                slot = lax.rem(n, 2)
+                g_tile[slot] = dot(normed_t[...], grads[:, lanes(n)]).astype(bf16)
+
+                @pl.when(n >= 1)
+                def _():
+                    grad_store(g_tile, 1 - slot, g_cols_h, ff_jobs + n - 1, 1).wait()
+
+                grad_store(g_tile, slot, g_cols_h, ff_jobs + n, 1).start()
+
+                pace.at("p", n)
+                return carry
+
+            lax.fori_loop(0, count, step, 0)
+            grad_store(g_tile, (count - 1) % 2, g_cols_h, ff_jobs + count - 1, 1).wait()
+
+        pl.run_scoped(projection_grads, vmem((width, length), bf16), vmem((2, width, JOB), bf16))
+
+        pace.at("p9")
+
     pl.run_scoped(attention, vmem((length, 3 * own_width), bf16))
 
-    first = {"E": 6, "S": 22, "F": 2, "C": 20, "D": 11, "O": 1}
+    first = {"E": 6, "S": 20, "F": 4, "C": 16, "D": 11, "O": 3}
+    later = max(0, first["S"] - first["C"] - cols.slots + LATE["C"][-1] + 1)
     steps = max(stream.ticks - first[kind] for kind, stream in (("C", cols), ("D", downs), ("O", outs)))
 
     def rest(t, carry):
         for kind, stream in (("E", downs), ("S", cols), ("F", outs)):
             if first[kind] < stream.count:
-                guard(first[kind] + t < stream.count, functools.partial(stream.start, first[kind] + t))
+                k = first[kind] + t - (later if kind == "S" else 0)
+                guard((k >= first[kind]) & (k < stream.count), functools.partial(stream.start, k))
         for kind, stream in (("C", cols), ("D", downs), ("O", outs)):
             if first[kind] < stream.ticks:
                 stream.tick(first[kind] + t)

time: 564 us -> 551 us (0.977); the launches traced: 553 us -> 549 us
  no operation moved by 1% of the time
where the time goes in v9:
time: 551 us; the launch traced here: 549 us
  Pallas kernels  542 us (98%)
    pallas_call x1, Pallas kernels, backward(): pl.pallas_call(backward_kernel, in_specs=[ANY] * 16 + [whole] * 4, out_sp...  323 us
    pallas_call x1, Pallas kernels, gather_all(): pl.pallas_call(gather_kernel, in_specs=[ANY] * 4 + [whole] * 2 + [ANY] *...  207 us

profile of v9, /device:TPU:0, one launch (start us, length us, event | category | flops | bytes accessed | tf_op | source)
XLA Modules:
  0.0 549.2 jit_solution(13078494622250793331)
XLA Ops:
  0.6 0.7 stack.10
  1.3 0.7 stack.9
  2.0 0.2 dynamic_update_slice.3.gains
  2.2 0.0 copy-start
  2.2 2.8 sine_multiply_fusion
  5.0 1.3 reshape.60.segments
  6.3 0.0 copy-done
  6.3 207.5 %gather_all.1 = (bf16[1024,1536]{1,0:T(8,128)(2,1)}, s32[4,1,256]{2,1,0:T(1,128)}, bf16[1024,1536]{1,0:T(8,128)(2,1)}, bf16[8,2,1536]{2,1,0:T(2,128)(2,1)}, bf16...) custom-call(bf16[2,256,1536]{2,1,0:T(8,128)(2,1)} %tokens.1, ...), custom_call_target="tpu_custom_call" | custom-call | bytes 500000000 | tf_op jit(solution)/shard_map/gather_all/pallas_call | solution.py:1049
  213.8 323.3 %backward.1 = (bf16[2,256,1536]{2,1,0:T(8,128)(2,1)}, bf16[2,256,1536]{2,1,0:T(8,128)(2,1)}, bf16[192,12800]{1,0:T(8,128)(2,1)}, bf16[192,1536]{1,0:T(8,128)(2,1...) custom-call(bf16[1024,1536]{1,0:T(8,128)(2,1)} %get-tuple-element.44, ...), custom_call_target="tpu_custom_call" | custom-call | bytes 800000000 | tf_op jit(solution)/shard_map/backward/pallas_call | solution.py:2052
  537.1 10.7 %widen.1 = (f32[192,4096]{1,0:T(8,128)}, f32[192,4096]{1,0:T(8,128)}, f32[192,1536]{1,0:T(8,128)}, f32[192,1536]{1,0:T(8,128)}, f32[192,1536]{1,0:T(8,128)}, /*i...) custom-call(bf16[192,12800]{1,0:T(8,128)(2,1)} %get-tuple-element.62.cols, ...), custom_call_target="tpu_custom_call" | custom-call | tf_op jit(solution)/shard_map/widen/pallas_call | solution.py:2106
  547.8 1.4 fusion.4
  (3 shorter events, 0.0 us)
Async XLA Ops:
  2.2 4.1 copy-start

commit v10 on v9

--- a/solution.py
+++ b/solution.py
@@ -453,13 +453,13 @@
 
 
 def gather_kernel(
-    tokens, segments, out_grad, gains, cosine, sine, w_q, w_k, w_v, w_o, w_gate, w_up, w_down,
+    tokens, segments, out_grad, gains, rotary, w_q, w_k, w_v, w_o, w_gate, w_up, w_down,
     x_out, seg_out, g_out, gains_out, qkv_out, o_out, ff_out, down_out,
     heads_out, lse_out, middle_out, slope_gate_out, slope_up_out, hidden_out, g_down_out, start_out,
-    gain_out, normed_t_out, nf_t_out, mixed_t_out,
+    gain_out, normed_t_out, nf_t_out, mixed_t_out, cosine_out, sine_out,
     send, recv, local, row_send, row_recv, row_local, gain_send, gain_recv,
     x_v, seg_v, gains_v, normed_v, w_qkv_v, heads_v, mixed_v, w_o_v, middle_v, part_send, part_recv,
-    nf_v, w_ff_v, branch_v, tile_v, g_tile_v, lse_v, start_v, lse_t_v, start_row_v, gain_v, turned_v, mixed_t_v,
+    nf_v, w_ff_v, branch_v, tile_v, g_tile_v, lse_v, start_v, lse_t_v, start_row_v, gain_v, turned_v, mixed_t_v, cosine, sine,
     part_sem, load_sem, w_sem, tile_sem, store_sem,
 ):
     me = Place()
@@ -744,6 +744,9 @@
         begin(remote(gains, gains_out.at[me.dp], gain_send.at[k - 1], gain_recv.at[k - 1],
                      lax.rem(me.dp + k, 8), me.z))
     pltpu.make_async_copy(gains, gains_out.at[me.dp], gain_recv.at[7]).start()
+    fill_rotary(rotary, cosine, sine)
+    store(cosine, cosine_out)
+    store(sine, sine_out)
     for index in range(3):
         columns_relay(index)
     rows_start(0)
@@ -912,6 +915,7 @@
     count = half_ff // tile
     for kind in range(2):
         ff_load(0, 0, kind).start()
+    rows_relay(1)
 
     def ff_step(n, carry):
         slot = lax.rem(n, 2)
@@ -943,10 +947,6 @@
         for kind in range(3):
             tile_store(n, slot, kind).start()
         grad_store(n, slot).start()
-
-        @pl.when(n == 0)
-        def _():
-            rows_relay(1)
 
         return carry
 
@@ -974,6 +974,34 @@
         return carry
 
     lax.fori_loop(0, source.shape[1] // 256, step, 0)
+
+
+ROTARY_STEP = 32
+
+
+def rotary_parts(length):
+    lane = np.arange(2 * HD)
+    pace = np.exp(-(lane % (HD // 2)) * (math.log(10000.0) / (HD // 2)))
+    sign = np.where(lane % HD < HD // 2, -1.0, 1.0)
+    far = np.arange(0, length, ROTARY_STEP)[:, None] * pace
+    near = np.arange(ROTARY_STEP)[:, None] * pace
+    parts = (np.cos(far), np.sin(far), sign * np.cos(far), sign * np.sin(far), np.cos(near), np.sin(near))
+    return np.concatenate(parts).astype(np.float32)
+
+
+def fill_rotary(parts, cosine, sine):
+    steps = cosine.shape[0] // ROTARY_STEP
+    near_cos = parts[4 * steps : 4 * steps + ROTARY_STEP, :]
+    near_sin = parts[4 * steps + ROTARY_STEP : 4 * steps + 2 * ROTARY_STEP, :]
+
+    def step(k, carry):
+        far_cos, far_sin, sign_cos, sign_sin = (parts[pl.ds(steps * which + k, 1), :] for which in range(4))
+        rows = pl.ds(pl.multiple_of(ROTARY_STEP * k, ROTARY_STEP), ROTARY_STEP)
+        cosine[rows, :] = far_cos * near_cos - far_sin * near_sin
+        sine[rows, :] = sign_sin * near_cos + sign_cos * near_sin
+        return carry
+
+    lax.fori_loop(0, steps, step, 0)
 
 
 def norm_rows(read, gain, target, length, step=64):
@@ -1013,7 +1041,7 @@
         lse[own_rows, :] = kept
 
 
-def gather_all(tokens, segments, out_grad, gains, cosine, sine, weights):
+def gather_all(tokens, segments, out_grad, gains, weights):
     rows, width = tokens.shape[1], tokens.shape[2]
     length, half, ff = 4 * rows, width // 2, weights[4].shape[1]
     half_ff = ff // 2
@@ -1043,12 +1071,14 @@
         shape(width, length),
         shape(width, length),
         shape(half, length),
+        shape(length, 128, dtype=jnp.float32),
+        shape(length, 128, dtype=jnp.float32),
     ]
     dma, vmem = pltpu.SemaphoreType.DMA, pltpu.VMEM
     whole = pl.BlockSpec(memory_space=pltpu.VMEM)
     return pl.pallas_call(
         gather_kernel,
-        in_specs=[ANY] * 4 + [whole] * 2 + [ANY] * 7,
+        in_specs=[ANY] * 4 + [whole] + [ANY] * 7,
         out_specs=[ANY] * len(shapes),
         out_shape=shapes,
         scratch_shapes=[
@@ -1076,14 +1106,16 @@
             vmem((2, width), jnp.float32),
             vmem((width, length), low),
             vmem((half, length), low),
-            dma((2, 3)), dma((3,)), dma((3, 3)), dma((3, 2, 3)), dma((9,)),
+            vmem((length, 128), jnp.float32),
+            vmem((length, 128), jnp.float32),
+            dma((2, 3)), dma((3,)), dma((3, 3)), dma((3, 2, 3)), dma((11,)),
         ],
         compiler_params=pltpu.CompilerParams(
             collective_id=0, has_side_effects=True, vmem_limit_bytes=61 * 1024 * 1024
         ),
         cost_estimate=pl.CostEstimate(flops=0, bytes_accessed=500_000_000, transcendentals=0),
         name="gather_all",
-    )(tokens, segments, out_grad, gains, cosine, sine, *weights)
+    )(tokens, segments, out_grad, gains, jnp.asarray(rotary_parts(length)), *weights)
 
 
 def guard(condition, action):
@@ -1219,8 +1251,8 @@
     def __init__(self, me, source, target, ff_jobs, d_model, ff, refs):
         self.me, self.source, self.target = me, source, target
         self.got, self.keep, self.second, self.over, self.sem, self.seq_sem, self.credit = refs
-        self.slots, self.rows = self.got.shape[0], source.shape[0] // 4
-        self.count, self.ff_jobs = source.shape[1] // JOB, ff_jobs
+        self.slots, self.rows = self.got.shape[0], source.shape[1] // 4
+        self.count, self.ff_jobs = source.shape[0], ff_jobs
         self.ff, self.d_model = ff, d_model
         self.stages = (
             *zip(LATE["C"], (self.pass_second, self.plane_and_ends, self.across, self.back, self.finish, self.drain)),
@@ -1233,7 +1265,7 @@
     def first_copy(self, k, part):
         me, slot, x_first = self.me, self.slot(k), self.x_first(k)
         block = x_first * (2 * part + 1 - me.x) + (1 - x_first) * (2 * (1 - me.y) + part)
-        sent = self.source.at[pl.ds(pl.multiple_of(self.rows * block, self.rows), self.rows), self.column(k)]
+        sent = self.source.at[k, pl.ds(pl.multiple_of(self.rows * block, self.rows), self.rows)]
         to = x_first * me.over_x + (1 - x_first) * me.over_y
         return remote(
             sent, self.got.at[slot, pl.ds(self.rows * part, self.rows)],
@@ -1243,7 +1275,7 @@
     def keep_copy(self, k, part):
         me, slot, x_first = self.me, self.slot(k), self.x_first(k)
         block = x_first * (2 * part + me.x) + (1 - x_first) * (2 * me.y + part)
-        kept = self.source.at[pl.ds(pl.multiple_of(self.rows * block, self.rows), self.rows), self.column(k)]
+        kept = self.source.at[k, pl.ds(pl.multiple_of(self.rows * block, self.rows), self.rows)]
         return pltpu.make_async_copy(
             kept, self.keep.at[slot, pl.ds(self.rows * part, self.rows)], self.sem.at[slot, 2, part]
         )
@@ -1362,22 +1394,22 @@
     def __init__(self, me, source, target, lates, refs):
         self.me, self.source, self.target = me, source, target
         self.got, self.second, self.over, self.stage, self.sem, self.seq_sem = refs
-        self.slots, self.rows = self.got.shape[0], source.shape[0] // 2
-        self.count = source.shape[1] // JOB
+        self.slots, self.rows = self.got.shape[0], self.got.shape[1]
+        self.count = self.slots
         self.active = me.core == me.y
         steps = (self.pass_second, self.plane_and_ends, self.across, self.back, self.finish, self.drain)
         self.stages = tuple(zip(lates, steps))
 
     def first_copy(self, k):
         me, slot = self.me, self.slot(k)
-        sent = self.source.at[pl.ds(pl.multiple_of(self.rows * (1 - me.x), self.rows), self.rows), self.column(k)]
-        return remote(sent, self.got.at[slot], self.sem.at[slot, 0, 0], self.sem.at[slot, 1, 0], me.over_x, me.z)
+        return remote(self.part(k, 1 - me.x), self.got.at[slot], self.sem.at[slot, 0, 0], self.sem.at[slot, 1, 0], me.over_x, me.z)
+
+    def part(self, k, x):
+        rows = pl.ds(pl.multiple_of(self.rows * x, self.rows), self.rows)
+        return self.source.at[k, rows] if len(self.source.shape) == 3 else self.source.at[rows, self.column(k)]
 
     def load_copy(self, k):
-        kept = self.source.at[
-            pl.ds(pl.multiple_of(self.rows * self.me.x, self.rows), self.rows), self.column(k)
-        ]
-        return pltpu.make_async_copy(kept, self.stage, self.sem.at[self.slot(k), 2, 0])
+        return pltpu.make_async_copy(self.part(k, self.me.x), self.stage, self.sem.at[self.slot(k), 2, 0])
 
     def second_copy(self, k):
         me, slot = self.me, self.slot(k)
@@ -1643,7 +1675,7 @@
         return pl.ds(pl.multiple_of(n * size, size), size)
 
     def grad_store(buffer, slot, target, n, k):
-        return pltpu.make_async_copy(buffer.at[slot], target.at[:, lanes(n)], store_sem.at[slot, k])
+        return pltpu.make_async_copy(buffer.at[slot], target.at[n], store_sem.at[slot, k])
 
     pace = Pace(cols, downs, outs)
     pace.at("s0")
@@ -1661,7 +1693,8 @@
 
             for copy in tile_loads(0, 0):
                 copy.start()
-            fetch((branch_h, branch), (nf_t_h, nf_t))
+            load(nf_t_h, nf_t, 1).start()
+            fetch((branch_h, branch))
 
             def step(n, carry):
                 slot = lax.rem(n, 2)
@@ -1674,6 +1707,10 @@
                         copy.start()
 
                 grad_hidden = nt(branch[...], w_tile[slot])
+
+                @pl.when(n == 0)
+                def _():
+                    load(nf_t_h, nf_t, 1).wait()
 
                 @pl.when(n > 1)
                 def _():
@@ -1706,10 +1743,17 @@
 
         def layer_out(hidden, w_down, send, total):
             other, own = 1 - me.core, me.core
-            fetch((w_down_h, w_down), (hidden_h.at[sublanes(other, half_rows), :], hidden))
+            def w_load(n):
+                return load(w_down_h.at[:, lanes(n)], w_down.at[:, lanes(n)], 4 + n)
+
+            load(hidden_h.at[sublanes(other, half_rows), :], hidden, 0).start()
+            for n in range(width // JOB):
+                w_load(n).start()
+            load(hidden_h.at[sublanes(other, half_rows), :], hidden, 0).wait()
             load(middle_h.at[sublanes(own, half_rows), :], total, 2).start()
 
             def other_tile(n, carry):
+                w_load(n).wait()
                 send[:, lanes(n)] = dot(hidden[...], w_down[:, lanes(n)]).astype(bf16)
                 return carry
 
@@ -1820,7 +1864,17 @@
 
     def to_attention(grad_attn):
         def norm_back(grad_nf, middle, branch):
-            fetch((middle_h, middle), (branch_h, branch), (grad_nf_h, grad_nf))
+            def quarter(q):
+                part = sublanes(q, length // 4)
+                pairs = ((middle_h, middle), (branch_h, branch), (grad_nf_h, grad_nf))
+                return [
+                    load(source.at[part, :], target.at[part, :], 4 + 3 * q + k)
+                    for k, (source, target) in enumerate(pairs)
+                ]
+
+            for q in range(4):
+                for copy in quarter(q):
+                    copy.start()
             gain = gain_ref[1:2, :]
 
             def rows(k, total):
@@ -1832,7 +1886,12 @@
                 grad_attn[part, :] = values.astype(bf16)
                 return total + gained
 
-            total = lax.fori_loop(0, length // 64, rows, jnp.zeros((1, width), f32))
+            def quarter_rows(q, total):
+                for copy in quarter(q):
+                    copy.wait()
+                return lax.fori_loop(length // 256 * q, length // 256 * (q + 1), rows, total)
+
+            total = lax.fori_loop(0, 4, quarter_rows, jnp.zeros((1, width), f32))
             gain_buffer[0, 0, 1:2, :] = 0.5 * total
             kept = load(grad_nf.at[sublanes(me.core, half_rows), :], kept_h, 0)
             kept.start()
@@ -2033,8 +2092,8 @@
         shape(width // 8, width),
         shape(half_ff // 4, width),
         shape(2, width, dtype=f32),
-        shape(width, columns),
-        shape(half, width),
+        shape(columns // JOB, width, JOB),
+        shape(width // JOB, half, JOB),
         shape(length // 2, width, dtype=f32),
         shape(2, length // 2, width),
         shape(length, width, dtype=f32),
@@ -2063,7 +2122,7 @@
         + [
             vmem((length, width), bf16), vmem((length // 2, width), bf16), pltpu.SemaphoreType.REGULAR,
             dma((2, 3)), dma((2, 1)),
-            vmem((GAIN_HOPS, 2, 2, width), f32), dma((2, GAIN_HOPS)), dma((2, 3, 2)), dma((4,)), dma((2, 3)),
+            vmem((GAIN_HOPS, 2, 2, width), f32), dma((2, GAIN_HOPS)), dma((2, 3, 2)), dma((16,)), dma((2, 3)),
             dma((2, 2)),
         ],
         compiler_params=pltpu.CompilerParams(
@@ -2127,16 +2186,12 @@
         dp_at * gain_attn.shape[0],
         1,
     )
-    lane = jnp.arange(2 * HD, dtype=jnp.int32)
-    pace = jnp.exp((lane % (HD // 2)).astype(jnp.float32) * (-math.log(10000.0) / (HD // 2)))
-    angle = jnp.arange(length, dtype=jnp.float32)[:, None] * pace[None, :]
-    cosine = jnp.cos(angle)
-    sine = jnp.where(lane % HD < HD // 2, -1.0, 1.0)[None, :] * jnp.sin(angle)
     (
         x_low, docs, grad_branch, gains, full_qkv, full_o, full_ff, full_down, heads, lse, middle,
         slope_gate, slope_up, hidden, g_down, start, gain, normed_t, nf_t, mixed_t,
+        cosine, sine,
     ) = gather_all(
-        tokens, segment_ids.reshape(2, 1, rows), out_grad, gains, cosine, sine,
+        tokens, segment_ids.reshape(2, 1, rows), out_grad, gains,
         (w_q, w_k, w_v, w_o, w_gate, w_up, w_down),
     )
     result, grad_tokens, g_cols, g_o, g_down, grad_gains = backward(

time: 551 us -> 546 us (level)
  no operation moved by 1% of the time
where the time goes in v10:
time: 546 us; the launch traced here: 545 us
  Pallas kernels  541 us (99%)
    pallas_call x1, Pallas kernels, backward(): pl.pallas_call(backward_kernel, in_specs=[ANY] * 16 + [whole] * 4, out_sp...  320 us
    pallas_call x1, Pallas kernels, gather_all(): pl.pallas_call(gather_kernel, in_specs=[ANY] * 4 + [whole] + [ANY] * 7, o...  209 us

profile of v10, /device:TPU:0, one launch (start us, length us, event | category | flops | bytes accessed | tf_op | source)
XLA Modules:
  0.0 545.4 jit_solution(9760792242040741624)
XLA Ops:
  0.6 0.7 stack.10
  1.3 0.7 stack.9
  2.0 0.2 dynamic_update_slice.3.gains
  2.2 0.0 copy-start
  2.2 1.3 reshape.37.segments
  3.4 0.0 copy-done
  3.4 209.5 %gather_all.1 = (bf16[1024,1536]{1,0:T(8,128)(2,1)}, s32[4,1,256]{2,1,0:T(1,128)}, bf16[1024,1536]{1,0:T(8,128)(2,1)}, bf16[8,2,1536]{2,1,0:T(2,128)(2,1)}, bf16...) custom-call(bf16[2,256,1536]{2,1,0:T(8,128)(2,1)} %tokens.1, ...), custom_call_target="tpu_custom_call" | custom-call | bytes 500000000 | tf_op jit(solution)/shard_map/gather_all/pallas_call | solution.py:1079
  212.9 320.4 %backward.1 = (bf16[2,256,1536]{2,1,0:T(8,128)(2,1)}, bf16[2,256,1536]{2,1,0:T(8,128)(2,1)}, bf16[192,12800]{1,0:T(8,128)(2,1)}, bf16[192,1536]{1,0:T(8,128)(2,1...) custom-call(bf16[1024,1536]{1,0:T(8,128)(2,1)} %get-tuple-element.46, ...), custom_call_target="tpu_custom_call" | custom-call | bytes 800000000 | tf_op jit(solution)/shard_map/backward/pallas_call | solution.py:2111
  533.3 10.7 %widen.1 = (f32[192,4096]{1,0:T(8,128)}, f32[192,4096]{1,0:T(8,128)}, f32[192,1536]{1,0:T(8,128)}, f32[192,1536]{1,0:T(8,128)}, f32[192,1536]{1,0:T(8,128)}, /*i...) custom-call(bf16[192,12800]{1,0:T(8,128)(2,1)} %get-tuple-element.66.cols, ...), custom_call_target="tpu_custom_call" | custom-call | tf_op jit(solution)/shard_map/widen/pallas_call | solution.py:2165
  544.0 1.4 fusion
  (2 shorter events, 0.0 us)
Async XLA Ops:
  2.2 1.3 copy-start

commit v11 on v10

--- a/solution.py
+++ b/solution.py
@@ -2143,7 +2143,7 @@
     return jnp.dot(a, b, preferred_element_type=jnp.float32)
 
 
-WIDEN_STEPS = 4
+WIDEN_STEPS = 2
 
 
 def widen_kernel(cols, o, down, tokens, result, *outs):

time: 546 us -> 545 us (level)
  no operation moved by 1% of the time
where the time goes in v11:
time: 545 us; the launch traced here: 544 us
  Pallas kernels  539 us (99%)
    pallas_call x1, Pallas kernels, backward(): pl.pallas_call(backward_kernel, in_specs=[ANY] * 16 + [whole] * 4, out_sp...  320 us
    pallas_call x1, Pallas kernels, gather_all(): pl.pallas_call(gather_kernel, in_specs=[ANY] * 4 + [whole] + [ANY] * 7, o...  209 us

profile of v11, /device:TPU:0, one launch (start us, length us, event | category | flops | bytes accessed | tf_op | source)
XLA Modules:
  0.0 544.2 jit_solution(16314577579974204422)
XLA Ops:
  0.6 0.7 stack.10
  1.3 0.7 stack.9
  2.0 0.2 dynamic_update_slice.3.gains
  2.2 0.0 copy-start
  2.2 1.3 reshape.37.segments
  3.4 0.0 copy-done
  3.4 209.5 %gather_all.1 = (bf16[1024,1536]{1,0:T(8,128)(2,1)}, s32[4,1,256]{2,1,0:T(1,128)}, bf16[1024,1536]{1,0:T(8,128)(2,1)}, bf16[8,2,1536]{2,1,0:T(2,128)(2,1)}, bf16...) custom-call(bf16[2,256,1536]{2,1,0:T(8,128)(2,1)} %tokens.1, ...), custom_call_target="tpu_custom_call" | custom-call | bytes 500000000 | tf_op jit(solution)/shard_map/gather_all/pallas_call | solution.py:1079
  212.9 320.4 %backward.1 = (bf16[2,256,1536]{2,1,0:T(8,128)(2,1)}, bf16[2,256,1536]{2,1,0:T(8,128)(2,1)}, bf16[192,12800]{1,0:T(8,128)(2,1)}, bf16[192,1536]{1,0:T(8,128)(2,1...) custom-call(bf16[1024,1536]{1,0:T(8,128)(2,1)} %get-tuple-element.46, ...), custom_call_target="tpu_custom_call" | custom-call | bytes 800000000 | tf_op jit(solution)/shard_map/backward/pallas_call | solution.py:2111
  533.3 9.5 %widen.1 = (f32[192,4096]{1,0:T(8,128)}, f32[192,4096]{1,0:T(8,128)}, f32[192,1536]{1,0:T(8,128)}, f32[192,1536]{1,0:T(8,128)}, f32[192,1536]{1,0:T(8,128)}, /*i...) custom-call(bf16[192,12800]{1,0:T(8,128)(2,1)} %get-tuple-element.66.cols, ...), custom_call_target="tpu_custom_call" | custom-call | tf_op jit(solution)/shard_map/widen/pallas_call | solution.py:2165
  542.8 1.4 fusion
  (2 shorter events, 0.0 us)
Async XLA Ops:
  2.2 1.3 copy-start
